TPU v7x, 32 devices: a whole 2x2x4 slice. The times are simulated.
32 devices in a mesh: dp: 2 (over x), wide: 4 (over z), narrow: 4 (over y, core).
Axes of the slice: x: 2, y: 2, z: 4, core: 2. Of those that a mesh axis runs over, the one named last changes fastest.
Arguments:
- tokens: bfloat16 [8192, 2048], P(('dp', 'wide'), 'narrow'), may hold values from -6 to 6
- continuation_lengths: int32 [2, 8], P('dp'), may hold values from 1 to 511, 2048 in all within a row
- attention_gain: float32 [2048], replicated, may hold values from 0.5 to 1.5
- query_weight: bfloat16 [2048, 2048], P('narrow', 'wide'), may hold values from -0.125 to 0.125
- key_weight: bfloat16 [2048, 1024], P('narrow', 'wide'), may hold values from -0.125 to 0.125
- value_weight: bfloat16 [2048, 1024], P('narrow', 'wide'), may hold values from -0.125 to 0.125
- head_gate: bfloat16 [2048, 16], P('narrow', 'wide'), may hold values from -0.125 to 0.125
- query_gain: float32 [128], replicated, may hold values from 0.5 to 1.5
- key_gain: float32 [128], replicated, may hold values from 0.5 to 1.5
- output_weight: bfloat16 [2048, 2048], P('wide', 'narrow'), may hold values from -2 to 2
- feedforward_gain: float32 [2048], replicated, may hold values from 0.5 to 1.5
- gate_weight: bfloat16 [2048, 6144], P('narrow', 'wide'), may hold values from -0.125 to 0.125
- up_weight: bfloat16 [2048, 6144], P('narrow', 'wide'), may hold values from -0.125 to 0.125
- down_weight: bfloat16 [6144, 2048], P('wide', 'narrow'), may hold values from -0.078125 to 0.078125
- cotangent: bfloat16 [8192, 2048], P(('dp', 'wide'), 'narrow'), may hold values from -6 to 6
Outputs:
- layer_output: bfloat16 [8192, 2048], P(('dp', 'wide'), 'narrow')
- tokens_gradient: float32 [8192, 2048], P(('dp', 'wide'), 'narrow')
- attention_gain_gradient: float32 [2048], replicated
- query_gradient: float32 [2048, 2048], P('narrow', 'wide')
- key_gradient: float32 [2048, 1024], P('narrow', 'wide')
- value_gradient: float32 [2048, 1024], P('narrow', 'wide')
- head_gate_gradient: float32 [2048, 16], P('narrow', 'wide')
- query_gain_gradient: float32 [128], replicated
- key_gain_gradient: float32 [128], replicated
- output_gradient: float32 [2048, 2048], P('wide', 'narrow')
- feedforward_gain_gradient: float32 [2048], replicated
- gate_gradient: float32 [2048, 6144], P('narrow', 'wide')
- up_gradient: float32 [2048, 6144], P('narrow', 'wide')
- down_gradient: float32 [6144, 2048], P('wide', 'narrow')
Inputs may be any that keep to these rules, and one draw needn't show every extreme that they name: `continuation_lengths`: each group's 8 lengths sum to 2048, and one of them is exactly 511.
All inputs are finite; a program needn't handle non-finite values.
Results may differ from a plain program's by a relative error of at most 0.018.
Values may be sent and summed in bfloat16 or wider, within the bound.
A program may use at most 320 MiB of HBM per device.

v0:
```python
import jax
import jax.numpy as jnp
from jax import lax
from jax.sharding import PartitionSpec as P

PROMPT = 2048


EPS = 1e-06
THETA = 1000000.0


def dot_rows(left, right):
    return jnp.dot(left, right, preferred_element_type=jnp.float32)


def dot_trans(left, right):
    return lax.dot_general(
        left, right, (((1,), (1,)), ((), ())), preferred_element_type=jnp.float32
    )


def dot_inner(left, right):
    return lax.dot_general(
        left, right, (((0,), (0,)), ((), ())), preferred_element_type=jnp.float32
    )


def expand(local_rows, weight, transpose):
    gathered = lax.all_gather(local_rows, "wide", axis=0, tiled=True)

    def expand_partial_term():
        if transpose:
            return dot_trans(gathered, weight)
        return dot_rows(gathered, weight)

    return (
        gathered,
        lax.psum_scatter(expand_partial_term(), "narrow", scatter_dimension=0, tiled=True),
    )


def contract(local_rows, weight, transpose):
    gathered = lax.all_gather(local_rows, "narrow", axis=0, tiled=True)

    def contract_partial_term():
        if transpose:
            return dot_trans(gathered, weight)
        return dot_rows(gathered, weight)

    return (
        gathered,
        lax.psum_scatter(contract_partial_term(), "wide", scatter_dimension=0, tiled=True),
    )


def row_total(values):
    return lax.psum(values, "narrow")


def layout(lengths, group_rows):
    ends = jnp.cumsum(lengths)
    starts = ends - lengths
    index = jnp.arange(group_rows, dtype=jnp.int32)
    offset = index - PROMPT
    member = ((offset[:, None] >= starts[None, :]) & (offset[:, None] < ends[None, :])).astype(
        jnp.int32
    )
    numbers = jnp.arange(1, lengths.shape[0] + 1, dtype=jnp.int32)
    segment = jnp.sum(member * numbers[None, :], axis=1)
    position = index - jnp.sum(member * starts[None, :], axis=1)
    return (index, segment, position)


def rope_tables(position, head_size):
    frequency = THETA ** (-2.0 * jnp.arange(head_size // 2, dtype=jnp.float32) / head_size)
    angle = position.astype(jnp.float32)[:, None] * frequency[None, :]
    return (jnp.cos(angle)[:, None, :], jnp.sin(angle)[:, None, :])


def rotate(values, cosine, sine):
    half = values.shape[-1] // 2
    first = values[..., :half]
    second = values[..., half:]
    return jnp.concatenate(
        [first * cosine - second * sine, second * cosine + first * sine], axis=-1
    )


def rotate_back(upstream, cosine, sine):
    half = upstream.shape[-1] // 2
    first = upstream[..., :half]
    second = upstream[..., half:]
    return jnp.concatenate(
        [first * cosine + second * sine, second * cosine - first * sine], axis=-1
    )


def head_norm(raw, gain):
    inverse = lax.rsqrt(jnp.mean(raw * raw, axis=-1, keepdims=True) + EPS)
    normal = raw * inverse
    return (normal, inverse, normal * gain)


def head_norm_back(upstream, normal, inverse, gain):
    scaled = upstream * gain
    gain_term = jnp.sum(upstream * normal, axis=(0, 1))
    inner = jnp.mean(scaled * normal, axis=-1, keepdims=True)
    return (inverse * (scaled - normal * inner), gain_term)


def visible(row_index, row_segment, index, segment):
    return (index[None, :] <= row_index[:, None]) & (
        (segment[None, :] == 0) | (segment[None, :] == row_segment[:, None])
    )


def block_scores(grouped, keys_all, allowed, scale):
    scores = (
        jnp.einsum("bkrd,tkd->krbt", grouped, keys_all, preferred_element_type=jnp.float32) * scale
    )
    return jnp.where(allowed[None, None], scores, -1e30)


def on_device(
    tokens,
    continuation_lengths,
    attention_gain,
    query_weight,
    key_weight,
    value_weight,
    head_gate,
    query_gain,
    key_gain,
    output_weight,
    feedforward_gain,
    gate_weight,
    up_weight,
    down_weight,
    cotangent,
):
    rows_wide, width_local = tokens.shape
    width_full = attention_gain.shape[0]
    head_size = query_gain.shape[0]
    heads_local = head_gate.shape[1]
    pair_heads = key_weight.shape[1] // head_size
    hidden_local = gate_weight.shape[1]
    group_rows = rows_wide * lax.axis_size("wide")
    rows_narrow = group_rows // lax.axis_size("narrow")
    narrow_index = lax.axis_index("narrow")
    repeat = heads_local // pair_heads
    block = 512
    blocks = rows_narrow // block
    scale = head_size ** (-0.5)
    query_cols = heads_local * head_size
    key_cols = pair_heads * head_size
    index, segment, position = layout(continuation_lengths[0], group_rows)
    my_start = narrow_index * rows_narrow
    my_index = lax.dynamic_slice_in_dim(index, my_start, rows_narrow)
    my_segment = lax.dynamic_slice_in_dim(segment, my_start, rows_narrow)
    my_position = lax.dynamic_slice_in_dim(position, my_start, rows_narrow)
    cosine, sine = rope_tables(my_position, head_size)
    gain_one = lax.dynamic_slice_in_dim(attention_gain, narrow_index * width_local, width_local)
    gain_two = lax.dynamic_slice_in_dim(feedforward_gain, narrow_index * width_local, width_local)
    inputs = tokens.astype(jnp.float32)
    inverse_one = lax.rsqrt(row_total(jnp.sum(inputs * inputs, axis=1)) / width_full + EPS)[:, None]
    hat_one = inputs * inverse_one
    normed = (hat_one * gain_one).astype(jnp.bfloat16)
    joined_weight = jnp.concatenate([query_weight, key_weight, value_weight, head_gate], axis=1)
    normed_all, projected = expand(normed, joined_weight, False)
    query_raw = projected[:, :query_cols].reshape(rows_narrow, heads_local, head_size)
    key_raw = projected[:, query_cols : query_cols + key_cols].reshape(
        rows_narrow, pair_heads, head_size
    )
    value_raw = projected[:, query_cols + key_cols : query_cols + 2 * key_cols]
    gate_logit = projected[:, query_cols + 2 * key_cols :]
    query_hat, query_inverse, query_normed = head_norm(query_raw, query_gain)
    key_hat, key_inverse, key_normed = head_norm(key_raw, key_gain)
    queries = rotate(query_normed, cosine, sine).astype(jnp.bfloat16)
    keys_local = rotate(key_normed, cosine, sine).astype(jnp.bfloat16)
    values_local = value_raw.reshape(rows_narrow, pair_heads, head_size).astype(jnp.bfloat16)
    keys_all, values_all = (
        lax.all_gather(keys_local, "narrow", axis=0, tiled=True),
        lax.all_gather(values_local, "narrow", axis=0, tiled=True),
    )

    def attend(block_inputs):
        query_block, row_index, row_segment = block_inputs
        grouped = query_block.reshape(block, pair_heads, repeat, head_size)
        scores = block_scores(
            grouped, keys_all, visible(row_index, row_segment, index, segment), scale
        )
        peak = jnp.max(scores, axis=-1, keepdims=True)
        weights = jnp.exp(scores - peak)
        total = jnp.sum(weights, axis=-1, keepdims=True)
        probs = weights / total
        context_block = jnp.einsum(
            "krbt,tkd->bkrd",
            probs.astype(jnp.bfloat16),
            values_all,
            preferred_element_type=jnp.float32,
        )
        return (
            context_block.reshape(block, heads_local, head_size),
            (peak + jnp.log(total))[..., 0],
        )

    query_blocks = queries.reshape(blocks, block, heads_local, head_size)
    index_blocks = my_index.reshape(blocks, block)
    segment_blocks = my_segment.reshape(blocks, block)
    context, log_total = lax.map(attend, (query_blocks, index_blocks, segment_blocks))
    context = context.reshape(rows_narrow, heads_local, head_size)
    gate = jax.nn.sigmoid(gate_logit)
    gated = (context * gate[:, :, None]).astype(jnp.bfloat16).reshape(rows_narrow, query_cols)
    context_all, attention_term = contract(gated, output_weight, False)
    middle = inputs + attention_term
    inverse_two = lax.rsqrt(row_total(jnp.sum(middle * middle, axis=1)) / width_full + EPS)[:, None]
    hat_two = middle * inverse_two
    normed_two = (hat_two * gain_two).astype(jnp.bfloat16)
    gate_up_weight = jnp.concatenate([gate_weight, up_weight], axis=1)
    normed_two_all, gate_up = expand(normed_two, gate_up_weight, False)
    gate_pre = gate_up[:, :hidden_local]
    up_pre = gate_up[:, hidden_local:]
    hidden = (jax.nn.silu(gate_pre) * up_pre).astype(jnp.bfloat16)
    hidden_all, mlp_term = contract(hidden, down_weight, False)
    layer_output = (middle + mlp_term).astype(jnp.bfloat16)
    upstream_all, hidden_grad = expand(cotangent, down_weight, True)
    down_grad = dot_inner(hidden_all, upstream_all)
    gate_sigmoid = jax.nn.sigmoid(gate_pre)
    gate_grad = hidden_grad * up_pre * gate_sigmoid * (1.0 + gate_pre * (1.0 - gate_sigmoid))
    up_grad = hidden_grad * jax.nn.silu(gate_pre)
    gate_up_low = jnp.concatenate([gate_grad, up_grad], axis=1).astype(jnp.bfloat16)
    gate_up_all, normed_two_grad = contract(gate_up_low, gate_up_weight, True)
    gate_up_grad = dot_inner(normed_two_all, gate_up_all)
    gain_two_term = jnp.sum(normed_two_grad * hat_two, axis=0)
    scaled_two = normed_two_grad * gain_two
    inner_two = row_total(jnp.sum(scaled_two * hat_two, axis=1))[:, None] / width_full
    middle_grad = cotangent.astype(jnp.float32) + inverse_two * (scaled_two - hat_two * inner_two)
    middle_low = middle_grad.astype(jnp.bfloat16)
    middle_all, gated_grad = expand(middle_low, output_weight, True)
    output_grad = dot_inner(context_all, middle_all)
    gated_grad = gated_grad.reshape(rows_narrow, heads_local, head_size)
    context_grad = (gated_grad * gate[:, :, None]).astype(jnp.bfloat16)
    gate_logit_grad = jnp.sum(gated_grad * context, axis=2) * gate * (1.0 - gate)

    def attend_back(carry, block_inputs):
        key_sum, value_sum = carry
        query_block, grad_block, log_block, row_index, row_segment = block_inputs
        grouped = query_block.reshape(block, pair_heads, repeat, head_size)
        grad_grouped = grad_block.reshape(block, pair_heads, repeat, head_size)
        scores = block_scores(
            grouped, keys_all, visible(row_index, row_segment, index, segment), scale
        )
        probs = jnp.exp(scores - log_block[..., None])
        prob_grads = jnp.einsum(
            "bkrd,tkd->krbt", grad_grouped, values_all, preferred_element_type=jnp.float32
        )
        inner = jnp.sum(probs * prob_grads, axis=-1, keepdims=True)
        score_grads = (probs * (prob_grads - inner)).astype(jnp.bfloat16)
        query_part = (
            jnp.einsum("krbt,tkd->bkrd", score_grads, keys_all, preferred_element_type=jnp.float32)
            * scale
        )
        key_sum = (
            key_sum
            + jnp.einsum("krbt,bkrd->tkd", score_grads, grouped, preferred_element_type=jnp.float32)
            * scale
        )
        value_sum = value_sum + jnp.einsum(
            "krbt,bkrd->tkd",
            probs.astype(jnp.bfloat16),
            grad_grouped,
            preferred_element_type=jnp.float32,
        )
        return ((key_sum, value_sum), query_part.reshape(block, heads_local, head_size))

    empty = jnp.zeros((group_rows, pair_heads, head_size), jnp.float32)
    grad_blocks = context_grad.reshape(blocks, block, heads_local, head_size)
    (key_sum, value_sum), query_grads = lax.scan(
        attend_back,
        (empty, empty),
        (query_blocks, grad_blocks, log_total, index_blocks, segment_blocks),
    )
    query_grads = query_grads.reshape(rows_narrow, heads_local, head_size)
    key_mine, value_mine = (
        lax.psum_scatter(
            key_sum.astype(jnp.bfloat16), "narrow", scatter_dimension=0, tiled=True
        ).astype(jnp.float32),
        lax.psum_scatter(
            value_sum.astype(jnp.bfloat16), "narrow", scatter_dimension=0, tiled=True
        ).astype(jnp.float32),
    )
    query_raw_grad, query_gain_term = head_norm_back(
        rotate_back(query_grads, cosine, sine), query_hat, query_inverse, query_gain
    )
    key_raw_grad, key_gain_term = head_norm_back(
        rotate_back(key_mine, cosine, sine), key_hat, key_inverse, key_gain
    )
    joined_low = jnp.concatenate(
        [
            query_raw_grad.reshape(rows_narrow, query_cols),
            key_raw_grad.reshape(rows_narrow, key_cols),
            value_mine.reshape(rows_narrow, key_cols),
            gate_logit_grad,
        ],
        axis=1,
    ).astype(jnp.bfloat16)
    joined_all, normed_grad = contract(joined_low, joined_weight, True)
    joined_grad = dot_inner(normed_all, joined_all)
    gain_one_term = jnp.sum(normed_grad * hat_one, axis=0)
    scaled_one = normed_grad * gain_one
    inner_one = row_total(jnp.sum(scaled_one * hat_one, axis=1))[:, None] / width_full
    tokens_gradient = middle_grad + inverse_one * (scaled_one - hat_one * inner_one)
    joined_grad, output_grad, gate_up_grad, down_grad = (
        lax.psum(joined_grad.astype(jnp.bfloat16), "dp").astype(jnp.float32),
        lax.psum(output_grad.astype(jnp.bfloat16), "dp").astype(jnp.float32),
        lax.psum(gate_up_grad.astype(jnp.bfloat16), "dp").astype(jnp.float32),
        lax.psum(down_grad.astype(jnp.bfloat16), "dp").astype(jnp.float32),
    )
    gain_one_full = lax.dynamic_update_slice_in_dim(
        jnp.zeros_like(attention_gain), gain_one_term, narrow_index * width_local, 0
    )
    gain_two_full = lax.dynamic_update_slice_in_dim(
        jnp.zeros_like(feedforward_gain), gain_two_term, narrow_index * width_local, 0
    )
    gain_one_full, gain_two_full, query_gain_term, key_gain_term = lax.psum(
        (gain_one_full, gain_two_full, query_gain_term, key_gain_term), ("dp", "wide", "narrow")
    )
    query_gradient = joined_grad[:, :query_cols]
    key_gradient = joined_grad[:, query_cols : query_cols + key_cols]
    value_gradient = joined_grad[:, query_cols + key_cols : query_cols + 2 * key_cols]
    head_gate_gradient = joined_grad[:, query_cols + 2 * key_cols :]
    gate_gradient = gate_up_grad[:, :hidden_local]
    up_gradient = gate_up_grad[:, hidden_local:]
    return (
        layer_output,
        tokens_gradient,
        gain_one_full,
        query_gradient,
        key_gradient,
        value_gradient,
        head_gate_gradient,
        query_gain_term,
        key_gain_term,
        output_grad,
        gain_two_full,
        gate_gradient,
        up_gradient,
        down_grad,
    )


def solution(mesh):
    return jax.shard_map(
        on_device,
        mesh=mesh,
        in_specs=(
            P(("dp", "wide"), "narrow"),
            P("dp", None),
            P(),
            P("narrow", "wide"),
            P("narrow", "wide"),
            P("narrow", "wide"),
            P("narrow", "wide"),
            P(),
            P(),
            P("wide", "narrow"),
            P(),
            P("narrow", "wide"),
            P("narrow", "wide"),
            P("wide", "narrow"),
            P(("dp", "wide"), "narrow"),
        ),
        out_specs=(
            P(("dp", "wide"), "narrow"),
            P(("dp", "wide"), "narrow"),
            P(),
            P("narrow", "wide"),
            P("narrow", "wide"),
            P("narrow", "wide"),
            P("narrow", "wide"),
            P(),
            P(),
            P("wide", "narrow"),
            P(),
            P("narrow", "wide"),
            P("narrow", "wide"),
            P("wide", "narrow"),
        ),
        check_vma=False,
    )
```

profile of v0, /device:TPU:0, one launch (start us, length us, event | category | flops | bytes accessed | tf_op | source)
XLA Modules:
  0.0 2702.8 jit_solution(11104213106023687378)
XLA Ops:
  21.5 80.9 %all-gather.11.cloned.1.call-done = bf16[4096,512]{1,0:T(8,128)(2,1)} async-done(((bf16[1024,512]{1,0:T(8,128)(2,1)}), bf16[4096,512]{1,0:T(8,128)(2,1)}) %all-gather.11.cloned.1.call-update) | async-done | bytes 4194320 | tf_op jit(solution)/shard_map/all_gather | solution.py:30
  117.1 122.4 %reduce-scatter.11.cloned.1.call-done = f32[1024,1028]{0,1:T(8,128)} async-done(((f32[4096,1028]{0,1:T(8,128)}), f32[1024,1028]{0,1:T(8,128)}) %reduce-scatter.11.cloned.1.call-update) | async-done | bytes 4210704 | tf_op jit(solution)/shard_map/reduce_scatter | solution.py:39
  272.0 18.6 all-gather.15.cloned.1.call-done
  290.6 100.4 %while.28 = (s32[]{:T(128)}, f32[2,512,4,128]{3,1,2,0:T(8,128)}, f32[2,2,2,512]{3,2,1,0:T(2,128)S(1)}, s32[2,512]{1,0:T(2,128)S(1)}, s32[4096]{0:T(1024)S(1)}, /...) while((s32[]{:T(128)}, f32[2,512,4,128]{3,1,2,0:T(8,128)}, ...), condition=%wide.region_11.12_spmd.clone, body=%wide.region_8.11_spmd.clone.sunk | while | flops 4404021248 | bytes 134860992 | solution.py:211
  374.1 15.7 fusion.136
  397.0 34.2 %all-gather.17.cloned.1.call-done = bf16[4096,512]{1,0:T(8,128)(2,1)} async-done(((bf16[1024,512]{1,0:T(8,128)(2,1)}), bf16[4096,512]{1,0:T(8,128)(2,1)}) %all-gather.17.cloned.1.call-update) | async-done | bytes 4194320 | tf_op jit(solution)/shard_map/all_gather | solution.py:44
  440.6 143.2 %reduce-scatter.13.cloned.1.call-done = f32[1024,512]{1,0:T(8,128)} async-done(((f32[4096,512]{1,0:T(8,128)}), f32[1024,512]{1,0:T(8,128)}) %reduce-scatter.13.cloned.1.call-update) | async-done | bytes 2097168 | tf_op jit(solution)/shard_map/reduce_scatter | solution.py:53
  596.3 70.5 %all-gather.23.cloned.1.call-done = bf16[4096,512]{1,0:T(8,128)(2,1)} async-done(((bf16[1024,512]{1,0:T(8,128)(2,1)}), bf16[4096,512]{1,0:T(8,128)(2,1)}) %all-gather.23.cloned.1.call-update) | async-done | bytes 4194320 | tf_op jit(solution)/shard_map/all_gather | solution.py:30
  685.5 62.6 %all-gather.19.cloned.1.call-done = bf16[4096,512]{1,0:T(8,128)(2,1)} async-done(((bf16[1024,512]{1,0:T(8,128)(2,1)}), bf16[4096,512]{1,0:T(8,128)(2,1)}) %all-gather.19.cloned.1.call-update) | async-done | bytes 4194320 | tf_op jit(solution)/shard_map/all_gather | solution.py:30
  748.1 36.5 %fusion.76 = f32[4096,3072]{1,0:T(8,128)} fusion(bf16[4096,512]{1,0:T(8,128)(2,1)} %all-gather.19.cloned.1.call-done, bf16[512,3072]{1,0:T(8,128)(2,1)} %constant_dynamic-update-slice_fusion.2), kind=kOutput, calls=%fused_computation.169 | convolution fusion | flops 12884901888 | bytes 57671680 | tf_op jit(solution)/shard_map/dot_general | solution.py:14
  784.9 146.3 %reduce-scatter.19.cloned.1.call-done = f32[1024,1536]{1,0:T(8,128)} async-done(((f32[4096,1536]{1,0:T(8,128)}), f32[1024,1536]{1,0:T(8,128)}) %reduce-scatter.19.cloned.1.call-update) | async-done | bytes 6291472 | tf_op jit(solution)/shard_map/reduce_scatter | solution.py:39
  931.2 349.0 %reduce-scatter.15.cloned.1.call-done = f32[1024,3072]{1,0:T(8,128)} async-done(((f32[4096,3072]{1,0:T(8,128)}), f32[1024,3072]{1,0:T(8,128)}) %reduce-scatter.15.cloned.1.call-update) | async-done | bytes 12582928 | tf_op jit(solution)/shard_map/reduce_scatter | solution.py:39
  1293.5 154.9 %all-gather.25.cloned.1.call-done = bf16[4096,3072]{1,0:T(8,128)(2,1)} async-done(((bf16[1024,3072]{1,0:T(8,128)(2,1)}), bf16[4096,3072]{1,0:T(8,128)(2,1)}) %all-gather.25.cloned.1.call-update) | async-done | bytes 25165840 | tf_op jit(solution)/shard_map/all_gather | solution.py:44
  1448.4 21.0 fusion.79
  1469.4 144.7 %reduce-scatter.21.cloned.1.call-done = f32[1024,512]{1,0:T(8,128)} async-done(((f32[4096,512]{1,0:T(8,128)}), f32[1024,512]{1,0:T(8,128)}) %reduce-scatter.21.cloned.1.call-update) | async-done | bytes 2097168 | tf_op jit(solution)/shard_map/reduce_scatter | solution.py:53
  1628.2 81.2 %all-gather.27.cloned.1.call-done = bf16[4096,512]{1,0:T(8,128)(2,1)} async-done(((bf16[1024,512]{1,0:T(8,128)(2,1)}), bf16[4096,512]{1,0:T(8,128)(2,1)}) %all-gather.27.cloned.1.call-update) | async-done | bytes 4194320 | tf_op jit(solution)/shard_map/all_gather | solution.py:30
  1717.3 70.0 %reduce-scatter.23.cloned.1.call-done = f32[1024,512]{1,0:T(8,128)} async-done(((f32[4096,512]{1,0:T(8,128)}), f32[1024,512]{1,0:T(8,128)}) %reduce-scatter.23.cloned.1.call-update) | async-done | bytes 2097168 | tf_op jit(solution)/shard_map/reduce_scatter | solution.py:39
  1793.1 223.9 %while.29 = (s32[]{:T(128)}, f32[4096,2,128]{0,2,1:T(8,128)}, f32[4096,2,128]{0,2,1:T(8,128)}, f32[2,512,4,128]{3,1,0,2:T(8,128)}, bf16[2,512,4,128]{3,1,2,0:T(8...) while((s32[]{:T(128)}, f32[4096,2,128]{0,2,1:T(8,128)}, ...), condition=%wide.region_24.25_spmd.clone, body=%wide.region_22.24_spmd.clone.sunk | while | flops 10877143040 | bytes 349286720 | solution.py:279
  1811.8 17.4 fusion.151
  1829.2 25.2 fusion.148
  1854.3 28.4 %fusion.149 = bf16[2,2,512,4096]{3,2,1,0:T(8,128)(2,1)} fusion(f32[2,512,2,4096]{3,1,2,0:T(8,128)} %get-tuple-element.583, f32[2,512,2,4096]{3,1,2,0:T(8,128)} %fusion.146, f32[2,2,512]{2,1,0:T(2,128)S(1)} %get-tuple-element.584, f32[2,2,512]{2,1,0:T(2,128)S(1)} %dynamic-slice_bitcast_fusion.2, pred[512,4096]{1,0:T(8,128)(4,1)} %fusion.147), kind=kLoop, calls=%fused_computation.26.clone.1 | loop fusion | flops 50331648 | bytes 85999616 | tf_op jit(solution)/shard_map/while/body/eval_jaxpr/convert_element_type | solution.py:259
  1922.9 18.5 fusion.151
  1941.4 25.2 fusion.148
  1966.6 28.4 %fusion.149 = bf16[2,2,512,4096]{3,2,1,0:T(8,128)(2,1)} fusion(f32[2,512,2,4096]{3,1,2,0:T(8,128)} %get-tuple-element.583, f32[2,512,2,4096]{3,1,2,0:T(8,128)} %fusion.146, f32[2,2,512]{2,1,0:T(2,128)S(1)} %get-tuple-element.584, f32[2,2,512]{2,1,0:T(2,128)S(1)} %dynamic-slice_bitcast_fusion.2, pred[512,4096]{1,0:T(8,128)(4,1)} %fusion.147), kind=kLoop, calls=%fused_computation.26.clone.1 | loop fusion | flops 50331648 | bytes 85999616 | tf_op jit(solution)/shard_map/while/body/eval_jaxpr/convert_element_type | solution.py:259
  2056.6 29.1 %reduce-scatter.27.cloned.1.call-done = bf16[1024,2,128]{0,2,1:T(8,128)(2,1)} async-done(((bf16[4096,2,128]{0,2,1:T(8,128)(2,1)}), bf16[1024,2,128]{0,2,1:T(8,128)(2,1)}) %reduce-scatter.27.cloned.1.call-update) | async-done | bytes 524304 | tf_op jit(solution)/shard_map/reduce_scatter | solution.py:289
  2088.3 81.5 %all-gather.21.cloned.1.call-done = bf16[4096,1536]{1,0:T(8,128)(2,1)} async-done(((bf16[1024,1536]{1,0:T(8,128)(2,1)}), bf16[4096,1536]{1,0:T(8,128)(2,1)}) %all-gather.21.cloned.1.call-update) | async-done | bytes 12582928 | tf_op jit(solution)/shard_map/all_gather | solution.py:44
  2181.7 20.8 convolution_convert_fusion
  2205.7 24.7 all-gather.29.cloned.1.call-done
  2266.7 127.6 %all-reduce.4.cloned.1.call-done = (bf16[512,1028]{0,1:T(8,128)(2,1)}, bf16[512,3072]{1,0:T(8,128)(2,1)}, bf16[512,512]{1,0:T(8,128)(2,1)}, bf16[1536,512]{1,0:T(8,128)(2,1)}) async-done(((bf16[512,1028]{0,1:T(8,128)(2,1)}, bf16[512,3072]{1,0:T(8,128)(2,1)}, bf16[512,512]{1,0:T(8,128)(2,1)}, bf16[1536,512]{1,0:T(8,128)(2,1)}), (bf16[512,1028]{0,1:T(8,128)(2,1)}, bf16[512,3072]{1,0:T(8,128)(2,1)}, ...) | async-done | bytes 6295568 | tf_op jit(solution)/shard_map/psum | solution.py:315
  2410.7 131.0 %reduce-scatter.29.cloned.1.call-done = f32[1024,512]{1,0:T(8,128)} async-done(((f32[4096,512]{1,0:T(8,128)}), f32[1024,512]{1,0:T(8,128)}) %reduce-scatter.29.cloned.1.call-update) | async-done | bytes 2097168 | tf_op jit(solution)/shard_map/reduce_scatter | solution.py:53
  2544.3 46.1 %all-reduce = (f32[2048]{0:T(1024)}, f32[128]{0:T(128)}, f32[128]{0:T(128)}, f32[2048]{0:T(1024)}) all-reduce(f32[2048]{0:T(1024)S(1)} %dynamic_update_slice.17, f32[128]{0:T(128)S(1)} %bitcast_reduce_fusion.1, f32[128]{0:T(128)S(1)} %bitcast_reduce_fusion.2, ...), channel_id=1, replica_groups=mesh['dp'=2,'wide'=4,'narrow'=4] {'dp','wide','narrow'}, use_global_device_ids=true, to_apply=%region_34.35 | all-reduce | flops 4352 | bytes 34816 | tf_op jit(solution)/shard_map/psum | solution.py:326
  2596.6 93.6 %reduce-scatter.17.cloned.1.call-done = f32[1024,512]{1,0:T(8,128)} async-done(((f32[4096,512]{1,0:T(8,128)}), f32[1024,512]{1,0:T(8,128)}) %reduce-scatter.17.cloned.1.call-update) | async-done | bytes 2097168 | tf_op jit(solution)/shard_map/reduce_scatter | solution.py:53
  (330 shorter events, 437.6 us)
Async XLA Ops:
  7.2 659.6 %copy-start = (bf16[1536,512]{1,0:T(8,128)(2,1)S(1)}, bf16[1536,512]{1,0:T(8,128)(2,1)}, u32[]{:S(2)}) copy-start(bf16[1536,512]{1,0:T(8,128)(2,1)} %param.32) | copy-start | bytes 4718596
  7.2 95.2 %all-gather.11.cloned.1.call-start = ((), (), s32[]{:S(2)}) async-start(), calls=%async_computation.10 | async-start | bytes 5242880 | tf_op jit(solution)/shard_map/all_gather | solution.py:30
  21.2 218.3 %reduce-scatter.11.cloned.1.call-start = ((), (), s32[]{:S(2)}) async-start(), calls=%async_computation.11 | async-start | bytes 21135360 | tf_op jit(solution)/shard_map/reduce_scatter | solution.py:39
  115.0 152.9 %all-gather.13.cloned.1.call-start = ((), (), s32[]{:S(2)}) async-start(), calls=%async_computation.12 | async-start | bytes 2621440 | tf_op jit(solution)/shard_map/all_gather | solution.py:183
  243.3 47.3 %all-gather.15.cloned.1.call-start = ((), (), s32[]{:S(2)}) async-start(), calls=%async_computation.13 | async-start | bytes 2621440 | tf_op jit(solution)/shard_map/all_gather | solution.py:184
  245.7 185.5 %all-gather.17.cloned.1.call-start = ((), (), s32[]{:S(2)}) async-start(), calls=%async_computation.14 | async-start | bytes 5242880 | tf_op jit(solution)/shard_map/all_gather | solution.py:44
  396.6 187.2 %reduce-scatter.13.cloned.1.call-start = ((), (), s32[]{:S(2)}) async-start(), calls=%async_computation.15 | async-start | bytes 10485760 | tf_op jit(solution)/shard_map/reduce_scatter | solution.py:53
  439.0 144.8 %copy-start.6 = (bf16[1024,512]{1,0:T(8,128)(2,1)S(1)}, bf16[1024,512]{1,0:T(8,128)(2,1)}, u32[]{:S(2)}) copy-start(bf16[1024,512]{1,0:T(8,128)(2,1)} %param.19) | copy-start | bytes 3145732
  439.0 227.7 %all-gather.23.cloned.1.call-start = ((), (), s32[]{:S(2)}) async-start(), calls=%async_computation.20 | async-start | bytes 5242880 | tf_op jit(solution)/shard_map/all_gather | solution.py:30
  439.8 308.4 %all-gather.19.cloned.1.call-start = ((), (), s32[]{:S(2)}) async-start(), calls=%async_computation.16 | async-start | bytes 5242880 | tf_op jit(solution)/shard_map/all_gather | solution.py:30
  440.6 1183.1 %copy-start.44 = (f32[512]{0:T(512)}, f32[512]{0:T(512)S(1)}, u32[]{:S(2)}) copy-start(f32[512]{0:T(512)S(1)} %dynamic_slice.46) | copy-start | bytes 6148
  593.1 1030.6 %copy-start.40 = (f32[1024]{0:T(1024)}, f32[1024]{0:T(1024)S(1)}, u32[]{:S(2)}) copy-start(f32[1024]{0:T(1024)S(1)} %add_rsqrt_fusion.2) | copy-start | bytes 12292
  596.2 335.0 %reduce-scatter.19.cloned.1.call-start = ((), (), s32[]{:S(2)}) async-start(), calls=%async_computation.21 | async-start | bytes 31457280 | tf_op jit(solution)/shard_map/reduce_scatter | solution.py:39
  681.4 598.7 %reduce-scatter.15.cloned.1.call-start = ((), (), s32[]{:S(2)}) async-start(), calls=%async_computation.17 | async-start | bytes 62914560 | tf_op jit(solution)/shard_map/reduce_scatter | solution.py:39
  784.7 663.7 %all-gather.25.cloned.1.call-start = ((), (), s32[]{:S(2)}) async-start(), calls=%async_computation.22 | async-start | bytes 31457280 | tf_op jit(solution)/shard_map/all_gather | solution.py:44
  1293.4 320.7 %reduce-scatter.21.cloned.1.call-start = ((), (), s32[]{:S(2)}) async-start(), calls=%async_computation.23 | async-start | bytes 10485760 | tf_op jit(solution)/shard_map/reduce_scatter | solution.py:53
  1469.4 155.0 %copy-start.11 = (bf16[1024,512]{1,0:T(8,128)(2,1)S(1)}, bf16[1024,512]{1,0:T(8,128)(2,1)}, u32[]{:S(2)}) copy-start(bf16[1024,512]{1,0:T(8,128)(2,1)} %param.33) | copy-start | bytes 3145732
  1469.4 240.0 %all-gather.27.cloned.1.call-start = ((), (), s32[]{:S(2)}) async-start(), calls=%async_computation.24 | async-start | bytes 5242880 | tf_op jit(solution)/shard_map/all_gather | solution.py:30
  1628.1 159.2 %reduce-scatter.23.cloned.1.call-start = ((), (), s32[]{:S(2)}) async-start(), calls=%async_computation.25 | async-start | bytes 10485760 | tf_op jit(solution)/shard_map/reduce_scatter | solution.py:39
  1717.2 334.9 %reduce-scatter.25.cloned.1.call-start = ((), (), s32[]{:S(2)}) async-start(), calls=%async_computation.26 | async-start | bytes 2621440 | tf_op jit(solution)/shard_map/reduce_scatter | solution.py:286
  2020.8 64.9 %reduce-scatter.27.cloned.1.call-start = ((), (), s32[]{:S(2)}) async-start(), calls=%async_computation.27 | async-start | bytes 2621440 | tf_op jit(solution)/shard_map/reduce_scatter | solution.py:289
  2024.7 145.1 %all-gather.21.cloned.1.call-start = ((), (), s32[]{:S(2)}) async-start(), calls=%async_computation.18 | async-start | bytes 15728640 | tf_op jit(solution)/shard_map/all_gather | solution.py:44
  2025.3 205.2 %all-gather.29.cloned.1.call-start = ((), (), s32[]{:S(2)}) async-start(), calls=%async_computation.28 | async-start | bytes 10567680 | tf_op jit(solution)/shard_map/all_gather | solution.py:44
  2088.3 306.0 %all-reduce.4.cloned.1.call-start = ((), (), s32[]{:S(2)}) async-start(), calls=%async_computation.30 | async-start | bytes 12599296 | tf_op jit(solution)/shard_map/psum | solution.py:315
  2240.7 301.0 %reduce-scatter.29.cloned.1.call-start = ((), (), s32[]{:S(2)}) async-start(), calls=%async_computation.29 | async-start | bytes 10485760 | tf_op jit(solution)/shard_map/reduce_scatter | solution.py:53
  2254.1 436.1 %reduce-scatter.17.cloned.1.call-start = ((), (), s32[]{:S(2)}) async-start(), calls=%async_computation.19 | async-start | bytes 10485760 | tf_op jit(solution)/shard_map/reduce_scatter | solution.py:53
  2407.1 134.6 %copy-start.7 = (bf16[1024,512]{1,0:T(8,128)(2,1)S(1)}, bf16[1024,512]{1,0:T(8,128)(2,1)}, u32[]{:S(2)}) copy-start(bf16[1024,512]{1,0:T(8,128)(2,1)} %param.19) | copy-start | bytes 3145732
  2407.1 134.6 %copy-start.43 = (f32[1024]{0:T(1024)S(1)}, f32[1024]{0:T(1024)}, u32[]{:S(2)}) copy-start(f32[1024]{0:T(1024)} %copy-done.42) | copy-start | bytes 12292
  2407.1 134.6 %copy-start.49 = (f32[512]{0:T(512)S(1)}, f32[512]{0:T(512)}, u32[]{:S(2)}) copy-start(f32[512]{0:T(512)} %copy-done.48) | copy-start | bytes 6148
  2410.7 279.6 %copy-start.41 = (f32[1024]{0:T(1024)S(1)}, f32[1024]{0:T(1024)}, u32[]{:S(2)}) copy-start(f32[1024]{0:T(1024)} %copy-done.40) | copy-start | bytes 12292
  2410.7 279.6 %copy-start.45 = (f32[512]{0:T(512)S(1)}, f32[512]{0:T(512)}, u32[]{:S(2)}) copy-start(f32[512]{0:T(512)} %copy-done.44) | copy-start | bytes 6148
  2410.7 279.6 %copy-start.47 = (f32[1024]{0:T(1024)S(1)}, f32[1024]{0:T(1024)}, u32[]{:S(2)}) copy-start(f32[1024]{0:T(1024)} %copy-done.46) | copy-start | bytes 12292
  (60 other events, 1155.9 us)
Sparse Core Ops, SparseCore 0:
  21.4 81.0 all-gather.10
  115.2 124.2 reduce-scatter.10
  243.4 22.5 all-gather.12
  268.0 22.5 all-gather.14
  396.7 34.4 all-gather.16
  439.1 144.6 reduce-scatter.12
  585.4 81.3 all-gather.22
  668.9 79.2 all-gather.18
  750.7 180.4 reduce-scatter.18
  933.6 346.4 reduce-scatter.14
  1293.5 154.7 all-gather.24
  1469.5 144.6 reduce-scatter.20
  1628.2 81.0 all-gather.26
  1717.3 69.9 reduce-scatter.22
  2020.9 31.1 reduce-scatter.24
  2054.5 31.1 reduce-scatter.26
  2087.7 82.0 all-gather.20
  2171.8 58.6 all-gather.28
  2240.8 153.4 all-reduce.3
  2396.5 145.1 reduce-scatter.28
  2544.1 146.1 reduce-scatter.16
where the time goes:
time: 2710 us; the launch traced here: 2700 us
  waiting for transfers between devices  1980 us (73%)
  matrix products  380 us (14%)
  other arithmetic  184 us (7%)
  blocking collectives  73.1 us (3%)
  local copies, waits for them, and re-layouts  70.3 us (3%)
    reduce_scatter x4, waiting for transfers between devices, expand(): lax.psum_scatter(expand_partial_term(), 'narrow', scatter_dimension=0, ti...  688 us
    reduce_scatter x4, waiting for transfers between devices, contract(): lax.psum_scatter(contract_partial_term(), 'wide', scatter_dimension=0, ti...  513 us
    all_gather x4, waiting for transfers between devices, contract(): gathered = lax.all_gather(local_rows, 'narrow', axis=0, tiled=True)  295 us
    all_gather x4, waiting for transfers between devices, expand(): gathered = lax.all_gather(local_rows, 'wide', axis=0, tiled=True)  295 us
    psum x1, waiting for transfers between devices, on_device(): lax.psum(joined_grad.astype(jnp.bfloat16), 'dp').astype(jnp.float32)  128 us
    dot_general x4, matrix products, dot_rows(): return jnp.dot(left, right, preferred_element_type=jnp.float32)  68.6 us
    convert_element_type x2, other arithmetic, attend_back(): score_grads = (probs * (prob_grads - inner)).astype(jnp.bfloat16)  56.9 us
    dot_general x4, matrix products, dot_trans(): lax.dot_general(left, right, (((1,), (1,)), ((), ())), preferred_element_...  55.7 us
  transfers between devices with their start and end apart: 21, of which 20 were waited for; matrix products, arithmetic and copies ran while one was open for 7% of the time, Pallas kernels for 0%

commit v1 on v0

v1 whole, which is shorter than its diff:
```python
import functools
import math

import jax
import jax.numpy as jnp
from jax import lax
from jax.experimental import pallas as pl
from jax.experimental.pallas import tpu as pltpu
from jax.sharding import PartitionSpec as P

PROMPT = 2048
EPS = 1e-06
THETA = 1000000.0
RELATIVE = (0, 2, 1, 3)
BF16 = jnp.bfloat16
F32 = jnp.float32
VMEM_LIMIT = 56 * 1024 * 1024


def dot_rows(left, right):
    return jnp.dot(left, right, preferred_element_type=F32)


def dot_trans(left, right):
    return lax.dot_general(left, right, (((1,), (1,)), ((), ())), preferred_element_type=F32)


def dot_inner(left, right):
    return lax.dot_general(left, right, (((0,), (0,)), ((), ())), preferred_element_type=F32)


def partner(values, distance, size):
    return lax.ppermute(values, "narrow", [(i, i ^ distance) for i in range(size)])


def gather_relative(values, size, axis):
    pair = jnp.concatenate([values, partner(values, 2, size)], axis=axis)
    return jnp.concatenate([pair, partner(pair, 1, size)], axis=axis)


def after(values, *others):
    return lax.optimization_barrier((values,) + others)[0]


def post_kernel(raw_ref, cos_ref, sin_ref, query_gain_ref, key_gain_ref, q_ref, kv_ref, *, heads, pairs, size, factor):
    cosine = cos_ref[...]
    sine = sin_ref[...]

    def turned(value, gain):
        inverse = lax.rsqrt(jnp.mean(value * value, axis=-1, keepdims=True) + EPS)
        normal = value * inverse * gain
        return normal * cosine + pltpu.roll(normal, size // 2, 1) * sine

    for h in range(heads):
        value = raw_ref[:, h * size : (h + 1) * size]
        q_ref[:, h * size : (h + 1) * size] = (turned(value, query_gain_ref[...]) * factor).astype(BF16)
    for h in range(pairs):
        at = (heads + h) * size
        kv_ref[:, h * size : (h + 1) * size] = turned(raw_ref[:, at : at + size], key_gain_ref[...]).astype(BF16)
        at = (heads + pairs + h) * size
        to = (pairs + h) * size
        kv_ref[:, to : to + size] = raw_ref[:, at : at + size].astype(BF16)


def post(raw, cosine, sine, query_gain, key_gain, heads, pairs, size, factor):
    rows, width = raw.shape
    step = 256
    return pl.pallas_call(
        functools.partial(post_kernel, heads=heads, pairs=pairs, size=size, factor=factor),
        grid=(rows // step,),
        in_specs=[
            pl.BlockSpec((step, width), lambda i: (i, 0)),
            pl.BlockSpec((step, size), lambda i: (i, 0)),
            pl.BlockSpec((step, size), lambda i: (i, 0)),
            pl.BlockSpec((1, size), lambda i: (0, 0)),
            pl.BlockSpec((1, size), lambda i: (0, 0)),
        ],
        out_specs=[
            pl.BlockSpec((step, heads * size), lambda i: (i, 0)),
            pl.BlockSpec((step, 2 * pairs * size), lambda i: (i, 0)),
        ],
        out_shape=[
            jax.ShapeDtypeStruct((rows, heads * size), BF16),
            jax.ShapeDtypeStruct((rows, 2 * pairs * size), BF16),
        ],
        cost_estimate=pl.CostEstimate(flops=rows * width * 20, bytes_accessed=rows * width * 8, transcendentals=0),
        name="post",
    )(raw, cosine, sine, query_gain[None], key_gain[None])


def back_kernel(
    dq_ref, dkv_ref, raw_ref, cos_ref, sin_ref, query_gain_ref, key_gain_ref, logit_ref, out_ref, gq_ref, gk_ref, *, heads, pairs, size, factor_q, factor_k
):
    cosine = cos_ref[...]
    sine = sin_ref[...]

    @pl.when(pl.program_id(0) == 0)
    def _():
        gq_ref[...] = jnp.zeros_like(gq_ref)
        gk_ref[...] = jnp.zeros_like(gk_ref)

    def back(up, value, gain, total_ref):
        up = up * cosine - pltpu.roll(up, size // 2, 1) * sine
        inverse = lax.rsqrt(jnp.mean(value * value, axis=-1, keepdims=True) + EPS)
        hat = value * inverse
        total_ref[...] += jnp.sum(up * hat, axis=0, keepdims=True)
        scaled = up * gain
        return inverse * (scaled - hat * jnp.mean(scaled * hat, axis=-1, keepdims=True))

    for h in range(heads):
        cols = slice(h * size, (h + 1) * size)
        out_ref[:, cols] = back(dq_ref[:, cols] * factor_q, raw_ref[:, cols], query_gain_ref[...], gq_ref).astype(BF16)
    for h in range(pairs):
        at = (heads + h) * size
        up = dkv_ref[:, h * size : (h + 1) * size].astype(F32) * factor_k
        out_ref[:, at : at + size] = back(up, raw_ref[:, at : at + size], key_gain_ref[...], gk_ref).astype(BF16)
        to = (pairs + h) * size
        at = (heads + pairs + h) * size
        out_ref[:, at : at + size] = dkv_ref[:, to : to + size].astype(BF16)
    at = (heads + 2 * pairs) * size
    out_ref[:, at : at + heads] = logit_ref[...].astype(BF16)


def project_back(dq, dkv, raw, cosine, sine, query_gain, key_gain, logit_grad, heads, pairs, size, factor_q, factor_k):
    rows, width = raw.shape
    step = 256
    row = lambda cols: pl.BlockSpec((step, cols), lambda i: (i, 0))
    one = pl.BlockSpec((1, size), lambda i: (0, 0))
    return pl.pallas_call(
        functools.partial(back_kernel, heads=heads, pairs=pairs, size=size, factor_q=factor_q, factor_k=factor_k),
        grid=(rows // step,),
        in_specs=[row(heads * size), row(2 * pairs * size), row(width), row(size), row(size), one, one, row(heads)],
        out_specs=[row(width), one, one],
        out_shape=[
            jax.ShapeDtypeStruct((rows, width), BF16),
            jax.ShapeDtypeStruct((1, size), F32),
            jax.ShapeDtypeStruct((1, size), F32),
        ],
        cost_estimate=pl.CostEstimate(flops=rows * width * 30, bytes_accessed=rows * width * 12, transcendentals=0),
        name="project_back",
    )(dq, dkv, raw, cosine, sine, query_gain[None], key_gain[None], logit_grad)


def forward_kernel(table_ref, q_ref, kv_ref, row_ref, start_ref, logit_ref, gated_ref, context_ref, inverse_ref, *, pairs, repeat, size, step):
    stripe = pl.program_id(0)
    wide_blocks = table_ref[stripe, 0]
    low = table_ref[stripe, 1]
    high = table_ref[stripe, 2]
    rows = row_ref[...]
    starts = start_ref[...]
    rows = jnp.concatenate([rows] * repeat, axis=0)
    starts = jnp.concatenate([starts] * repeat, axis=0)
    for k in range(pairs):
        heads = [k * repeat + r for r in range(repeat)]
        query = jnp.concatenate([q_ref[:, h * size : (h + 1) * size] for h in heads], axis=0)
        key_cols = slice(k * size, (k + 1) * size)
        value_cols = slice((pairs + k) * size, (pairs + k + 1) * size)

        def seen(i, total, length, mask):
            at = pl.ds(pl.multiple_of(i * length, length), length)
            scores = dot_trans(query, kv_ref[at, key_cols])
            weights = jnp.exp2(scores)
            if mask:
                keys = i * length + lax.broadcasted_iota(jnp.int32, scores.shape, 1)
                weights = jnp.where((keys <= rows) & (keys >= starts), weights, 0.0)
            values = kv_ref[at, value_cols]
            values = jnp.concatenate([values, jnp.ones_like(values)], axis=1)
            return total + dot_rows(weights.astype(BF16), values)

        total = jnp.zeros((query.shape[0], 2 * size), F32)
        total = lax.fori_loop(0, wide_blocks, lambda i, t: seen(i, t, 2 * step, False), total)
        total = lax.fori_loop(low, high + 1, lambda i, t: seen(i, t, step, True), total)
        inverse = 1.0 / total[:, size:]
        context = total[:, :size] * inverse
        for r, h in enumerate(heads):
            part = context[r * step : (r + 1) * step]
            cols = slice(h * size, (h + 1) * size)
            gate = jax.nn.sigmoid(logit_ref[:, h : h + 1])
            gated_ref[:, cols] = (part * gate).astype(BF16)
            context_ref[:, cols] = part
            inverse_ref[:, cols] = inverse[r * step : (r + 1) * step]


def attend(table, q, kv, rows, starts, logit, pairs, size):
    length, cols = q.shape
    heads = cols // size
    step = length // table.shape[0]
    block = lambda width: pl.BlockSpec((step, width), lambda i, t: (i, 0))
    return pl.pallas_call(
        functools.partial(forward_kernel, pairs=pairs, repeat=heads // pairs, size=size, step=step),
        grid_spec=pltpu.PrefetchScalarGridSpec(
            num_scalar_prefetch=1,
            grid=(length // step,),
            in_specs=[
                block(cols),
                pl.BlockSpec(kv.shape, lambda i, t: (0, 0), pipeline_mode=pl.Buffered(1)),
                block(1),
                block(1),
                block(heads),
            ],
            out_specs=[block(cols), block(cols), block(cols)],
        ),
        out_shape=[
            jax.ShapeDtypeStruct((length, cols), BF16),
            jax.ShapeDtypeStruct((length, cols), F32),
            jax.ShapeDtypeStruct((length, cols), F32),
        ],
        compiler_params=pltpu.CompilerParams(vmem_limit_bytes=VMEM_LIMIT),
        cost_estimate=pl.CostEstimate(flops=15 * 10**9, bytes_accessed=12 * 10**6, transcendentals=7 * 10**6),
        name="attend",
    )(table, q, kv, rows, starts, logit)


def backward_kernel(
    table_ref, q_ref, kv_ref, row_ref, start_ref, logit_ref, context_ref, inverse_ref, grad_ref,
    dq_ref, dkv_ref, dlogit_ref, sums_ref, *, pairs, repeat, size, step,
):
    stripe = pl.program_id(0)
    wide_blocks = table_ref[stripe, 0]
    low = table_ref[stripe, 1]
    high = table_ref[stripe, 2]

    @pl.when(stripe == 0)
    def _():
        sums_ref[...] = jnp.zeros_like(sums_ref)

    rows = jnp.concatenate([row_ref[0]] * repeat, axis=1)
    starts = jnp.concatenate([start_ref[0]] * repeat, axis=1)
    for k in range(pairs):
        heads = [k * repeat + r for r in range(repeat)]
        query = jnp.concatenate([q_ref[:, h * size : (h + 1) * size] for h in heads], axis=0)
        grads, inners = [], []
        for h in heads:
            cols = slice(h * size, (h + 1) * size)
            up = grad_ref[:, cols]
            gate = jax.nn.sigmoid(logit_ref[:, h : h + 1])
            product = jnp.sum(up * context_ref[:, cols], axis=1, keepdims=True)
            dlogit_ref[:, h : h + 1] = product * gate * (1.0 - gate)
            inverse = inverse_ref[:, cols]
            grads.append((up * gate * inverse).astype(BF16))
            inners.append(product * gate * inverse)
        grad = jnp.concatenate(grads, axis=0)
        inner = jnp.transpose(jnp.concatenate(inners, axis=0))[0:1]
        key_cols = slice(k * size, (k + 1) * size)
        value_cols = slice((pairs + k) * size, (pairs + k + 1) * size)

        def seen(i, total, length, mask):
            at = pl.ds(pl.multiple_of(i * length, length), length)
            keys_block = kv_ref[at, key_cols]
            weights = jnp.exp2(dot_trans(keys_block, query))
            if mask:
                keys = i * length + lax.broadcasted_iota(jnp.int32, weights.shape, 0)
                weights = jnp.where((keys <= rows) & (keys >= starts), weights, 0.0)
            changes = dot_trans(kv_ref[at, value_cols], grad)
            changes = (weights * (changes - inner)).astype(BF16)
            sums_ref[at, value_cols] += dot_rows(weights.astype(BF16), grad)
            sums_ref[at, key_cols] += dot_rows(changes, query)
            return total + dot_inner(changes, keys_block)

        total = jnp.zeros((query.shape[0], size), F32)
        total = lax.fori_loop(0, wide_blocks, lambda i, t: seen(i, t, 2 * step, False), total)
        total = lax.fori_loop(low, high + 1, lambda i, t: seen(i, t, step, True), total)
        for r, h in enumerate(heads):
            dq_ref[:, h * size : (h + 1) * size] = total[r * step : (r + 1) * step]

    @pl.when(stripe == pl.num_programs(0) - 1)
    def _():
        dkv_ref[...] = sums_ref[...].astype(BF16)


def attend_back(table, q, kv, rows, starts, logit, context, inverse, grad, pairs, size):
    length, cols = q.shape
    heads = cols // size
    step = length // table.shape[0]
    block = lambda width: pl.BlockSpec((step, width), lambda i, t: (i, 0))
    whole = pl.BlockSpec(kv.shape, lambda i, t: (0, 0), pipeline_mode=pl.Buffered(1))
    lane = pl.BlockSpec((1, 1, step), lambda i, t: (i, 0, 0))
    return pl.pallas_call(
        functools.partial(backward_kernel, pairs=pairs, repeat=heads // pairs, size=size, step=step),
        grid_spec=pltpu.PrefetchScalarGridSpec(
            num_scalar_prefetch=1,
            grid=(length // step,),
            in_specs=[block(cols), whole, lane, lane, block(heads), block(cols), block(cols), block(cols)],
            out_specs=[block(cols), whole, block(heads)],
            scratch_shapes=[pltpu.VMEM(kv.shape, F32)],
        ),
        out_shape=[
            jax.ShapeDtypeStruct((length, cols), F32),
            jax.ShapeDtypeStruct(kv.shape, BF16),
            jax.ShapeDtypeStruct((length, heads), F32),
        ],
        compiler_params=pltpu.CompilerParams(vmem_limit_bytes=VMEM_LIMIT),
        cost_estimate=pl.CostEstimate(flops=38 * 10**9, bytes_accessed=20 * 10**6, transcendentals=7 * 10**6),
        name="attend_back",
    )(table, q, kv, rows.reshape(-1, 1, step), starts.reshape(-1, 1, step), logit, context, inverse, grad)


def layout(lengths, group_rows):
    ends = jnp.cumsum(lengths)
    begins = ends - lengths
    index = jnp.arange(group_rows, dtype=jnp.int32)
    offset = index - PROMPT
    member = ((offset[:, None] >= begins[None, :]) & (offset[:, None] < ends[None, :])).astype(jnp.int32)
    shift = jnp.sum(member * begins[None, :], axis=1)
    start = jnp.where(offset >= 0, PROMPT + shift, 0)
    return index, start, index - shift


def make(sizes):
    n_dp, n_wide, n_narrow = sizes["dp"], sizes["wide"], sizes["narrow"]

    def gather_rows(values):
        return lax.all_gather(values, "wide", axis=0, tiled=True)

    def scatter_rows(values):
        return lax.psum_scatter(values.astype(BF16), "wide", scatter_dimension=0, tiled=True).astype(F32)

    def reduce_weight(first, second, axis):
        half = first.shape[axis] // 2
        come = partner(second.astype(BF16), 1, n_narrow)
        total = first + come.astype(F32)
        mine = lax.slice_in_dim(total, 0, half, axis=axis)
        theirs = lax.slice_in_dim(total, half, 2 * half, axis=axis)
        come = partner(theirs.astype(BF16), 2, n_narrow)
        total = (mine + come.astype(F32)).astype(BF16)
        if n_dp == 2:
            come = lax.ppermute(total, "dp", [(0, 1), (1, 0)])
            return total.astype(F32) + come.astype(F32)
        return lax.psum(total, "dp").astype(F32)

    def on_device(
        tokens, continuation_lengths, attention_gain, query_weight, key_weight, value_weight, head_gate, query_gain, key_gain,
        output_weight, feedforward_gain, gate_weight, up_weight, down_weight, cotangent,
    ):
        rows_wide, width_local = tokens.shape
        width = attention_gain.shape[0]
        size = query_gain.shape[0]
        heads = head_gate.shape[1]
        pairs = key_weight.shape[1] // size
        hidden_local = gate_weight.shape[1]
        group_rows = rows_wide * n_wide
        rows_local = rows_wide // n_narrow
        narrow = lax.axis_index("narrow")
        query_cols = heads * size
        key_cols = pairs * size
        scale = size ** (-0.5)
        factor = scale * math.log2(math.e)

        def to_local(values):
            send = [lax.dynamic_slice_in_dim(values, (narrow ^ r) * rows_local, rows_local) for r in RELATIVE]
            parts = [send[0]] + [partner(s, r, n_narrow) for s, r in zip(send[1:], RELATIVE[1:])]
            return jnp.concatenate(parts, axis=1)

        def from_local(values):
            out = jnp.zeros((rows_wide, width_local), values.dtype)
            for i, r in enumerate(RELATIVE):
                part = values[:, i * width_local : (i + 1) * width_local]
                if r:
                    part = partner(part, r, n_narrow)
                out = lax.dynamic_update_slice_in_dim(out, part, (narrow ^ r) * rows_local, 0)
            return out

        def relative_vector(vector):
            return jnp.concatenate(
                [lax.dynamic_slice_in_dim(vector, (narrow ^ r) * width_local, width_local) for r in RELATIVE]
            )

        def absolute_vector(vector):
            out = jnp.zeros((width,), vector.dtype)
            for i, r in enumerate(RELATIVE):
                part = vector[i * width_local : (i + 1) * width_local]
                out = lax.dynamic_update_slice_in_dim(out, part, (narrow ^ r) * width_local, 0)
            return out

        def norm(values, gain):
            inverse = lax.rsqrt(jnp.mean(values * values, axis=1, keepdims=True) + EPS)
            hat = values * inverse
            return inverse, hat, (hat * gain).astype(BF16)

        def norm_back(grad, hat, inverse, gain):
            scaled = grad * gain
            inner = jnp.mean(scaled * hat, axis=1, keepdims=True)
            return jnp.sum(grad * hat, axis=0), inverse * (scaled - hat * inner)

        inputs = to_local(tokens)
        joined = jnp.concatenate([query_weight, key_weight, value_weight, head_gate], axis=1)
        joined_weight = gather_relative(joined, n_narrow, 0)
        upstream = to_local(after(cotangent, joined_weight))
        out_weight = gather_relative(after(output_weight, joined_weight), n_narrow, 1)
        gate_up = jnp.concatenate([gate_weight, up_weight], axis=1)
        gate_up_weight = gather_relative(after(gate_up, out_weight), n_narrow, 0)
        down = gather_relative(after(down_weight, gate_up_weight), n_narrow, 1)

        index, start, position = layout(continuation_lengths[0], group_rows)

        def mine(vector):
            return lax.dynamic_slice_in_dim(
                vector.reshape(n_wide, n_narrow, rows_local), narrow, 1, axis=1
            ).reshape(rows_wide)

        my_index, my_start, my_position = mine(index), mine(start), mine(position)
        frequency = THETA ** (-2.0 * jnp.arange(size // 2, dtype=F32) / size)
        angle = my_position.astype(F32)[:, None] * frequency[None, :]
        cosine, sine = jnp.cos(angle), jnp.sin(angle)
        cosine = jnp.concatenate([cosine, cosine], axis=1)
        sine = jnp.concatenate([-sine, sine], axis=1)
        block = my_index[::rows_local] // rows_local
        first = my_start[::rows_local] // rows_local
        prompt_blocks = PROMPT // rows_local
        in_prompt = block < prompt_blocks
        table = jnp.stack(
            [
                jnp.where(in_prompt, block // 2, prompt_blocks // 2),
                jnp.where(in_prompt, block // 2 * 2, first),
                block,
            ],
            axis=1,
        ).astype(jnp.int32)

        gain_one, gain_two = relative_vector(attention_gain), relative_vector(feedforward_gain)
        inputs = inputs.astype(F32)
        inverse_one, hat_one, normed = norm(inputs, gain_one)
        normed_all = gather_rows(normed)
        upstream_all = gather_rows(after(upstream, normed_all))
        raw = dot_rows(normed_all, joined_weight)
        q, kv = post(raw, cosine, sine, query_gain, key_gain, heads, pairs, size, factor)
        logit = raw[:, query_cols + 2 * key_cols :]
        kv_parts = gather_relative(kv[None], n_narrow, 0)
        kv_all = jnp.zeros((n_wide, n_narrow, rows_local, 2 * key_cols), BF16)
        for i, r in enumerate(RELATIVE):
            kv_all = lax.dynamic_update_slice_in_dim(
                kv_all, kv_parts[i].reshape(n_wide, 1, rows_local, 2 * key_cols), narrow ^ r, 1
            )
        kv_all = kv_all.reshape(group_rows, 2 * key_cols)
        gated, context, inverse_total = attend(
            table, q, kv_all, my_index[:, None], my_start[:, None], logit, pairs, size
        )
        middle = inputs + scatter_rows(dot_rows(gated, out_weight))
        inverse_two, hat_two, normed_two = norm(middle, gain_two)
        normed_two_all = gather_rows(normed_two)
        both = dot_rows(normed_two_all, gate_up_weight)
        gate_pre, up_pre = both[:, :hidden_local], both[:, hidden_local:]
        gate_sigmoid = jax.nn.sigmoid(gate_pre)
        silu = gate_pre * gate_sigmoid
        hidden = (silu * up_pre).astype(BF16)
        hidden_grad = dot_trans(upstream_all, down)
        gate_grad = hidden_grad * up_pre * gate_sigmoid * (1.0 + gate_pre * (1.0 - gate_sigmoid))
        up_grad = hidden_grad * silu
        gate_up_low = jnp.concatenate([gate_grad, up_grad], axis=1).astype(BF16)
        normed_two_grad = scatter_rows(dot_trans(gate_up_low, gate_up_weight))
        gain_two_term, change = norm_back(normed_two_grad, hat_two, inverse_two, gain_two)
        upstream_rows = upstream.astype(F32)
        middle_grad = upstream_rows + change
        middle_low = middle_grad.astype(BF16)
        middle_all = gather_rows(middle_low)
        mlp_term = scatter_rows(after(dot_rows(hidden, down).astype(BF16), middle_all))
        layer_output = from_local((middle + mlp_term).astype(BF16))
        gated_grad = dot_trans(middle_all, out_weight)
        dq, dkv, logit_grad = attend_back(
            table, q, kv_all, my_index, my_start, logit, context, inverse_total, gated_grad, pairs, size
        )
        half = width // 2
        down_gradient = reduce_weight(
            dot_inner(hidden, upstream_all[:, :half]), dot_inner(hidden, upstream_all[:, half:]), 1
        )
        gate_up_gradient = reduce_weight(
            dot_inner(normed_two_all[:, :half], gate_up_low), dot_inner(normed_two_all[:, half:], gate_up_low), 0
        )
        output_gradient = reduce_weight(
            dot_inner(gated, middle_all[:, :half]), dot_inner(gated, middle_all[:, half:]), 1
        )
        dkv = dkv.reshape(n_wide, n_narrow, rows_local, 2 * key_cols)
        pick = lambda r: lax.dynamic_slice_in_dim(dkv, narrow ^ r, 1, axis=1).reshape(rows_wide, 2 * key_cols)
        come = partner(jnp.concatenate([pick(1), pick(3)], axis=0), 1, n_narrow).astype(F32)
        theirs = (pick(2).astype(F32) + come[rows_wide:]).astype(BF16)
        dkv_mine = pick(0).astype(F32) + come[:rows_wide] + partner(theirs, 2, n_narrow).astype(F32)
        low, query_gain_term, key_gain_term = project_back(
            dq, dkv_mine, raw, cosine, sine, query_gain, key_gain, logit_grad, heads, pairs, size, scale, math.log(2.0)
        )
        normed_grad = scatter_rows(dot_trans(low, joined_weight))
        joined_gradient = reduce_weight(
            dot_inner(normed_all[:, :half], low), dot_inner(normed_all[:, half:], low), 0
        )
        gain_one_term, change = norm_back(normed_grad, hat_one, inverse_one, gain_one)
        tokens_gradient = from_local((middle_grad + change).astype(BF16)).astype(F32)
        gains = lax.psum(
            (absolute_vector(gain_one_term), absolute_vector(gain_two_term), query_gain_term[0], key_gain_term[0]),
            ("dp", "wide", "narrow"),
        )
        return (
            layer_output,
            tokens_gradient,
            gains[0],
            joined_gradient[:, :query_cols],
            joined_gradient[:, query_cols : query_cols + key_cols],
            joined_gradient[:, query_cols + key_cols : query_cols + 2 * key_cols],
            joined_gradient[:, query_cols + 2 * key_cols :],
            gains[2],
            gains[3],
            output_gradient,
            gains[1],
            gate_up_gradient[:, :hidden_local],
            gate_up_gradient[:, hidden_local:],
            down_gradient,
        )

    return on_device


def solution(mesh):
    rows, up, down = P(("dp", "wide"), "narrow"), P("narrow", "wide"), P("wide", "narrow")
    return jax.shard_map(
        make(dict(mesh.shape)),
        mesh=mesh,
        in_specs=(rows, P("dp", None), P(), up, up, up, up, P(), P(), down, P(), up, up, down, rows),
        out_specs=(rows, rows, P(), up, up, up, up, P(), P(), down, P(), up, up, down),
        check_vma=False,
    )
```

time: 2710 us -> 1060 us (0.39)
  waiting for transfers between devices: 1980 us -> 599 us
  matrix products: 380 us -> 144 us
  other arithmetic: 184 us -> 70.9 us
  Pallas kernels: 0 us -> 72.3 us
  starting transfers between devices: 1.63 us -> 48.7 us
  blocking collectives: 73.1 us -> 45.2 us
    reduce_scatter x10 -> x4, waiting for transfers between devices: 1240 us -> 77.8 us  [scatter_rows(): lax.psum_scatter(values.astype(BF16), 'wide', scatter_dimension=0, tiled=...]
    all_gather x10 -> x4, waiting for transfers between devices: 609 us -> 159 us  [gather_rows(): return lax.all_gather(values, 'wide', axis=0, tiled=True)]
    ppermute x0 -> x36, waiting for transfers between devices: none -> 362 us  [the longest x32 288 us: partner(): lax.ppermute(values, 'narrow', [(i, i ^ distance) for i in range(size)])]
    dot_general x18 -> x4, matrix products: 278 us -> 46.3 us  [dot_rows(): return jnp.dot(left, right, preferred_element_type=F32)]
    psum x1 -> x0, waiting for transfers between devices: 128 us -> none  [on_device(): lax.psum(joined_grad.astype(jnp.bfloat16), 'dp').astype(jnp.float32)]
    pallas_call x0 -> x4, Pallas kernels: none -> 72.3 us  [the longest x1 34.1 us: attend_back(): pl.pallas_call(functools.partial(backward_kernel, pairs=pairs, repeat=hea...]
    convert_element_type x13 -> x12, other arithmetic: 84 us -> 24.2 us  [the longest x4 8.49 us: reduce_weight(): total = (mine + come.astype(F32)).astype(BF16)]
    ppermute x0 -> x36, starting transfers between devices: none -> 48.2 us  [the longest x32 39.4 us: partner(): lax.ppermute(values, 'narrow', [(i, i ^ distance) for i in range(size)])]
  transfers between devices with their start and end apart: 21 -> 44, of which waited for: 20 -> 22; matrix products, arithmetic and copies ran while one was open for 7% -> 19% of each run, Pallas kernels for 0% -> 4%
where the time goes in v1:
time: 1060 us
  waiting for transfers between devices  599 us (57%)
  matrix products  144 us (14%)
  Pallas kernels  72.3 us (7%)
  other arithmetic  70.9 us (7%)
  local copies, waits for them, and re-layouts  63.5 us (6%)
  starting transfers between devices  48.7 us (5%)
  blocking collectives  45.2 us (4%)
  between operations  15.3 us (1%)
    ppermute x32, waiting for transfers between devices, partner(): lax.ppermute(values, 'narrow', [(i, i ^ distance) for i in range(size)])  288 us
    all_gather x4, waiting for transfers between devices, gather_rows(): return lax.all_gather(values, 'wide', axis=0, tiled=True)  159 us
    reduce_scatter x4, waiting for transfers between devices, scatter_rows(): lax.psum_scatter(values.astype(BF16), 'wide', scatter_dimension=0, tiled=...  77.8 us
    ppermute x4, waiting for transfers between devices, reduce_weight(): come = lax.ppermute(total, 'dp', [(0, 1), (1, 0)])  73.5 us
    dot_general x4, matrix products, dot_trans(): lax.dot_general(left, right, (((1,), (1,)), ((), ())), preferred_element_...  50.9 us
    dot_general x8, matrix products, dot_inner(): lax.dot_general(left, right, (((0,), (0,)), ((), ())), preferred_element_...  46.6 us
    dot_general x4, matrix products, dot_rows(): return jnp.dot(left, right, preferred_element_type=F32)  46.3 us
    psum x1, blocking collectives, on_device(): lax.psum((absolute_vector(gain_one_term), absolute_vector(gain_two_term),...  45.2 us
  transfers between devices with their start and end apart: 44, of which 22 were waited for; matrix products, arithmetic and copies ran while one was open for 19% of the time, Pallas kernels for 4%

profile of v1, /device:TPU:0, one launch (start us, length us, event | category | flops | bytes accessed | tf_op | source)
XLA Modules:
  0.0 1058.5 jit_solution(14878729986015078229)
XLA Ops:
  28.3 23.6 %collective-permute-done.3 = bf16[512,1028]{0,1:T(8,128)(2,1)S(1)} collective-permute-done((bf16[512,1028]{0,1:T(8,128)(2,1)S(1)}, bf16[512,1028]{0,1:T(8,128)(2,1)S(1)}, u32[]{:S(2)}, u32[]{:S(2)}) %collective-permute-start.3) | collective-permute-done | bytes 1052704 | tf_op jit(solution)/shard_map/ppermute | solution.py:33
  58.0 10.7 %pad_maximum_fusion.2 = bf16[2048,1028]{0,1:T(8,128)(2,1)} fusion(bf16[1024,1028]{0,1:T(8,128)(2,1)} %collective-permute-done.4, bf16[512,1028]{0,1:T(8,128)(2,1)S(1)} %collective-permute-done.3, bf16[512,4]{0,1:T(4,128)(2,1)S(1)} %copy-done.33, bf16[512,256]{0,1:T(8,128)(2,1)S(1)} %copy.94, bf16[512,256]{0,1:T(8,128)(2,1)S(1)} %copy.93, ...), kind=kLoop, calls=%fused_computation.15 | loop fusion | flops 25264128 | bytes 8421376 | tf_op jit(solution)/shard_map/concatenate | solution.py:38
  68.7 39.4 %all-gather.5.cloned.1.call-done = bf16[1024,2048]{1,0:T(8,128)(2,1)} async-done(((bf16[256,2048]{1,0:T(8,128)(2,1)}), bf16[1024,2048]{1,0:T(8,128)(2,1)}) %all-gather.5.cloned.1.call-update) | async-done | bytes 4194320 | tf_op jit(solution)/shard_map/all_gather | solution.py:313
  108.1 10.1 fusion.60.raw_ref
  118.2 6.3 post.1
  126.6 24.2 %collective-permute-done.5 = bf16[1,1024,512]{2,1,0:T(8,128)(2,1)S(1)} collective-permute-done((bf16[1,1024,512]{2,1,0:T(8,128)(2,1)}, bf16[1,1024,512]{2,1,0:T(8,128)(2,1)S(1)}, u32[]{:S(2)}, u32[]{:S(2)}) %collective-permute-start.5) | collective-permute-done | bytes 1048608 | tf_op jit(solution)/shard_map/ppermute | solution.py:33
  153.5 7.2 collective-permute-done.7
  174.3 23.6 %attend.1 = (bf16[1024,512]{1,0:T(8,128)(2,1)}, f32[1024,512]{1,0:T(8,128)}, f32[1024,512]{1,0:T(8,128)}) custom-call(s32[4,3]{1,0:T(4,128)} %pad_add_fusion.table_ref, bf16[1024,512]{1,0:T(8,128)(2,1)} %get-tuple-element.31.q_ref, bf16[4096,512]{1,0:T(8,128)(2,1)} %bitcast.75, s32[1024,1]{1,0:T(8,128)} %copy.101.row_ref, s32[1024,1]{1,0:T(8,128)} %copy.102.start_ref, ...), custom_call_target="tpu_custom_call" | custom-call | flops 15000000512 | bytes 12000000 | tf_op jit(solution)/shard_map/attend/pallas_call | solution.py:189
  211.2 66.5 %collective-permute-done.9 = bf16[512,3072]{1,0:T(8,128)(2,1)S(1)} collective-permute-done((bf16[512,3072]{1,0:T(8,128)(2,1)S(1)}, bf16[512,3072]{1,0:T(8,128)(2,1)S(1)}, u32[]{:S(2)}, u32[]{:S(2)}) %collective-permute-start.9) | collective-permute-done | bytes 3145760 | tf_op jit(solution)/shard_map/ppermute | solution.py:33
  295.7 6.6 constant_dynamic-update-slice_fusion.3
  303.6 34.2 %collective-permute-done.11 = bf16[1536,512]{1,0:T(8,128)(2,1)S(1)} collective-permute-done((bf16[1536,512]{1,0:T(8,128)(2,1)S(1)}, bf16[1536,512]{1,0:T(8,128)(2,1)S(1)}, u32[]{:S(2)}, u32[]{:S(2)}) %collective-permute-start.11) | collective-permute-done | bytes 1572896 | tf_op jit(solution)/shard_map/ppermute | solution.py:33
  363.7 7.6 all-gather.7.cloned.1.call-done
  371.3 19.0 %fusion.61 = f32[1024,3072]{1,0:T(8,128)} fusion(bf16[1024,2048]{1,0:T(8,128)(2,1)} %all-gather.7.cloned.1.call-done, bf16[2048,3072]{1,0:T(8,128)(2,1)} %constant_dynamic-update-slice_fusion.3), kind=kOutput, calls=%fused_computation.180 | convolution fusion | flops 12884901888 | bytes 29360128 | tf_op jit(solution)/shard_map/dot_general | solution.py:21
  390.3 62.3 %all-gather.9.cloned.1.call-done = bf16[1024,2048]{1,0:T(8,128)(2,1)} async-done(((bf16[256,2048]{1,0:T(8,128)(2,1)}), bf16[1024,2048]{1,0:T(8,128)(2,1)}) %all-gather.9.cloned.1.call-update) | async-done | bytes 4194320 | tf_op jit(solution)/shard_map/all_gather | solution.py:313
  452.5 16.4 %multiply_convert_fusion.1 = (bf16[1024,1536]{1,0:T(8,128)(2,1)S(1)}, bf16[1024,1536]{1,0:T(8,128)(2,1)}, bf16[1024,1536]{1,0:T(8,128)(2,1)}) fusion(f32[1024,3072]{1,0:T(8,128)} %fusion.61, bf16[1024,2048]{1,0:T(8,128)(2,1)} %all-gather.9.cloned.1.call-done, bf16[1536,2048]{1,0:T(8,128)(2,1)} %constant_dynamic-update-slice_fusion.6), kind=kOutput, calls=%fused_computation.9 | convolution fusion | flops 6466043904 | bytes 32505856 | tf_op jit(solution)/shard_map/dot_general | solution.py:25
  470.6 18.5 %convolution_convert_fusion.1 = bf16[1024,2048]{1,0:T(8,128)(2,1)} fusion(bf16[2048,3072]{1,0:T(8,128)(2,1)} %constant_dynamic-update-slice_fusion.3, bf16[1024,1536]{1,0:T(8,128)(2,1)} %get-tuple-element.118, bf16[1024,1536]{1,0:T(8,128)(2,1)S(1)} %get-tuple-element.117), kind=kOutput, calls=%fused_computation.16 | convolution fusion | flops 12899581952 | bytes 23068672 | tf_op jit(solution)/shard_map/dot_general | solution.py:25
  489.3 75.2 %reduce-scatter.7.cloned.1.call-done = bf16[256,2048]{1,0:T(8,128)(2,1)} async-done(((bf16[1024,2048]{1,0:T(8,128)(2,1)}), bf16[256,2048]{1,0:T(8,128)(2,1)}) %reduce-scatter.7.cloned.1.call-update) | async-done | bytes 1048592 | tf_op jit(solution)/shard_map/reduce_scatter | solution.py:316
  569.9 12.0 %convolution_convert_fusion = bf16[1024,3072]{1,0:T(8,128)(2,1)} fusion(bf16[1024,2048]{1,0:T(8,128)(2,1)} %all-gather.7.cloned.1.call-done, bf16[1024,1536]{1,0:T(8,128)(2,1)} %get-tuple-element.118, bf16[1024,1536]{1,0:T(8,128)(2,1)} %copy-done.14), kind=kOutput, calls=%fused_computation.13 | convolution fusion | flops 6458179584 | bytes 14680064 | tf_op jit(solution)/shard_map/dot_general | solution.py:29
  581.9 11.0 %convolution_convert_fusion.2 = bf16[1024,2048]{1,0:T(8,128)(2,1)} fusion(bf16[1024,1536]{1,0:T(8,128)(2,1)S(1)} %copy-done.47, bf16[1536,2048]{1,0:T(8,128)(2,1)} %constant_dynamic-update-slice_fusion.6), kind=kOutput, calls=%fused_computation.17 | convolution fusion | flops 6444548096 | bytes 13631488 | tf_op jit(solution)/shard_map/dot_general | solution.py:21
  592.9 7.8 convolution_convert_fusion.5
  601.1 50.1 %all-gather.11.cloned.1.call-done = bf16[1024,2048]{1,0:T(8,128)(2,1)} async-done(((bf16[256,2048]{1,0:T(8,128)(2,1)}), bf16[1024,2048]{1,0:T(8,128)(2,1)}) %all-gather.11.cloned.1.call-update) | async-done | bytes 4194320 | tf_op jit(solution)/shard_map/all_gather | solution.py:313
  651.3 6.5 fusion.62.grad_ref
  657.8 34.1 %attend_back.1 = (f32[1024,512]{1,0:T(8,128)}, bf16[4096,512]{1,0:T(8,128)(2,1)}, f32[1024,4]{1,0:T(8,128)}) custom-call(s32[4,3]{1,0:T(4,128)} %pad_add_fusion.table_ref, bf16[1024,512]{1,0:T(8,128)(2,1)} %get-tuple-element.31.q_ref, bf16[4096,512]{1,0:T(8,128)(2,1)} %bitcast.76, s32[4,1,256]{2,1,0:T(1,128)} %copy-done.34, s32[4,1,256]{2,1,0:T(1,128)} %copy-done.35, ...), custom_call_target="tpu_custom_call" | custom-call | flops 38000001024 | bytes 20000000 | tf_op jit(solution)/shard_map/attend_back/pallas_call | solution.py:278
  712.9 11.9 %convert_add_fusion = f32[1024,3072]{1,0:T(8,128)S(1)} fusion(bf16[1024,3072]{1,0:T(8,128)(2,1)} %collective-permute-done.30, bf16[1024,2048]{1,0:T(8,128)(2,1)} %all-gather.7.cloned.1.call-done, bf16[1024,1536]{1,0:T(8,128)(2,1)} %get-tuple-element.118, bf16[1024,1536]{1,0:T(8,128)(2,1)} %copy-done.14), kind=kOutput, calls=%fused_computation | convolution fusion | flops 6461325312 | bytes 27262976 | tf_op jit(solution)/shard_map/dot_general | solution.py:29
  735.7 11.9 %collective-permute-done.34 = bf16[1536,512]{1,0:T(8,128)(2,1)} collective-permute-done((bf16[1536,512]{1,0:T(8,128)(2,1)}, bf16[1536,512]{1,0:T(8,128)(2,1)}, u32[]{:S(2)}, u32[]{:S(2)}) %collective-permute-start.34) | collective-permute-done | bytes 1572896 | tf_op jit(solution)/shard_map/ppermute | solution.py:33
  753.4 84.0 %collective-permute-done.20 = bf16[1024,512]{1,0:T(8,128)(2,1)S(1)} collective-permute-done((bf16[1024,512]{1,0:T(8,128)(2,1)S(1)}, bf16[1024,512]{1,0:T(8,128)(2,1)S(1)}, u32[]{:S(2)}, u32[]{:S(2)}) %collective-permute-start.20) | collective-permute-done | bytes 1048608 | tf_op jit(solution)/shard_map/ppermute | solution.py:33
  839.2 8.3 project_back.1
  847.5 9.4 convolution_convert_fusion.6
  879.6 53.9 %collective-permute-done.32 = bf16[512,3072]{1,0:T(8,128)(2,1)S(1)} collective-permute-done((bf16[512,3072]{1,0:T(8,128)(2,1)S(1)}, bf16[512,3072]{1,0:T(8,128)(2,1)S(1)}, u32[]{:S(2)}, u32[]{:S(2)}) %collective-permute-start.32) | collective-permute-done | bytes 3145760 | tf_op jit(solution)/shard_map/ppermute | solution.py:327
  941.5 9.8 collective-permute-done.28
  956.2 19.6 %collective-permute-done.29 = bf16[512,512]{1,0:T(8,128)(2,1)S(1)} collective-permute-done((bf16[512,512]{1,0:T(8,128)(2,1)S(1)}, bf16[512,512]{1,0:T(8,128)(2,1)S(1)}, u32[]{:S(2)}, u32[]{:S(2)}) %collective-permute-start.29) | collective-permute-done | bytes 524320 | tf_op jit(solution)/shard_map/ppermute | solution.py:327
  998.0 45.2 %all-reduce = (f32[2048]{0:T(1024)}, f32[128]{0:T(128)}, f32[128]{0:T(128)}, f32[2048]{0:T(1024)}) all-reduce(f32[2048]{0:T(1024)S(1)} %slice_dynamic-update-slice_fusion.6, f32[128]{0:T(128)S(1)} %bitcast.98, f32[128]{0:T(128)S(1)} %bitcast.99, ...), channel_id=1, replica_groups=mesh['dp'=2,'wide'=4,'narrow'=4] {'dp','wide','narrow'}, use_global_device_ids=true, to_apply=%region_11.12 | all-reduce | flops 4352 | bytes 34816 | tf_op jit(solution)/shard_map/psum | solution.py:486
  (299 shorter events, 216.4 us)
Async XLA Ops:
  7.2 100.9 %all-gather.5.cloned.1.call-start = ((), (), s32[]{:S(2)}) async-start(), calls=%async_computation.4 | async-start | bytes 5242880 | tf_op jit(solution)/shard_map/all_gather | solution.py:313
  25.2 261.5 %reduce-scatter.5.cloned.1.call-start = ((), (), s32[]{:S(2)}) async-start(), calls=%async_computation.5 | async-start | bytes 5242880 | tf_op jit(solution)/shard_map/reduce_scatter | solution.py:316
  25.9 26.0 %collective-permute-start.3 = (bf16[512,1028]{0,1:T(8,128)(2,1)S(1)}, bf16[512,1028]{0,1:T(8,128)(2,1)S(1)}, u32[]{:S(2)}, u32[]{:S(2)}) collective-permute-start(bf16[512,1028]{0,1:T(8,128)(2,1)S(1)} %pad_maximum_fusion.11), channel_id=1, source_target_pairs={{0,2},{1,3},{2,0},{3,1},{4,6},{5,7},{6,4},{7,5},{8,10},{9,11},{10,... | collective-permute-start | bytes 3158024 | tf_op jit(solution)/shard_map/ppermute | solution.py:33
  124.5 26.2 %collective-permute-start.5 = (bf16[1,1024,512]{2,1,0:T(8,128)(2,1)}, bf16[1,1024,512]{2,1,0:T(8,128)(2,1)S(1)}, u32[]{:S(2)}, u32[]{:S(2)}) collective-permute-start(bf16[1,1024,512]{2,1,0:T(8,128)(2,1)} %bitcast.79), channel_id=1, source_target_pairs={{0,2},{1,3},{2,0},{3,1},{4,6},{5,7},{6,4},{7,5},{8,10},{9,11},{10,... | collective-permute-start | bytes 3145736 | tf_op jit(solution)/shard_map/ppermute | solution.py:33
  126.0 34.7 %collective-permute-start.7 = (bf16[512,512]{1,0:T(8,128)(2,1)S(1)}, bf16[512,512]{1,0:T(8,128)(2,1)S(1)}, u32[]{:S(2)}, u32[]{:S(2)}) collective-permute-start(bf16[512,512]{1,0:T(8,128)(2,1)S(1)} %copy-done.21), channel_id=1, source_target_pairs={{0,2},{1,3},{2,0},{3,1},{4,6},{5,7},{6,4},{7,5},{8,10},{9,11},{10,... | collective-permute-start | bytes 1572872 | tf_op jit(solution)/shard_map/ppermute | solution.py:33
  153.5 16.8 %collective-permute-start.6 = (bf16[2,1024,512]{2,1,0:T(8,128)(2,1)}, bf16[2,1024,512]{2,1,0:T(8,128)(2,1)}, u32[]{:S(2)}, u32[]{:S(2)}) collective-permute-start(bf16[2,1024,512]{2,1,0:T(8,128)(2,1)} %pad_maximum_fusion.6), channel_id=1, source_target_pairs={{0,1},{1,0},{2,3},{3,2},{4,5},{5,4},{6,7},{7,6},{8,9},{9,8},{10,11... | collective-permute-start | bytes 6291464 | tf_op jit(solution)/shard_map/ppermute | solution.py:33
  204.1 167.2 %all-gather.7.cloned.1.call-start = ((), (), s32[]{:S(2)}) async-start(), calls=%async_computation.6 | async-start | bytes 5242880 | tf_op jit(solution)/shard_map/all_gather | solution.py:313
  206.4 71.3 %collective-permute-start.9 = (bf16[512,3072]{1,0:T(8,128)(2,1)S(1)}, bf16[512,3072]{1,0:T(8,128)(2,1)S(1)}, u32[]{:S(2)}, u32[]{:S(2)}) collective-permute-start(bf16[512,3072]{1,0:T(8,128)(2,1)S(1)} %pad_maximum_fusion.3), channel_id=1, source_target_pairs={{0,2},{1,3},{2,0},{3,1},{4,6},{5,7},{6,4},{7,5},{8,10},{9,11},{10,... | collective-permute-start | bytes 9437192 | tf_op jit(solution)/shard_map/ppermute | solution.py:33
  289.9 162.6 %all-gather.9.cloned.1.call-start = ((), (), s32[]{:S(2)}) async-start(), calls=%async_computation.7 | async-start | bytes 5242880 | tf_op jit(solution)/shard_map/all_gather | solution.py:313
  302.3 35.5 %collective-permute-start.11 = (bf16[1536,512]{1,0:T(8,128)(2,1)S(1)}, bf16[1536,512]{1,0:T(8,128)(2,1)S(1)}, u32[]{:S(2)}, u32[]{:S(2)}) collective-permute-start(bf16[1536,512]{1,0:T(8,128)(2,1)S(1)} %copy-done.7), channel_id=1, source_target_pairs={{0,2},{1,3},{2,0},{3,1},{4,6},{5,7},{6,4},{7,5},{8,10},{9,11},{10,... | collective-permute-start | bytes 4718600 | tf_op jit(solution)/shard_map/ppermute | solution.py:33
  340.0 19.7 %collective-permute-start.12 = (bf16[1536,1024]{1,0:T(8,128)(2,1)}, bf16[1536,1024]{1,0:T(8,128)(2,1)}, u32[]{:S(2)}, u32[]{:S(2)}) collective-permute-start(bf16[1536,1024]{1,0:T(8,128)(2,1)} %pad_maximum_fusion.4), channel_id=1, source_target_pairs={{0,1},{1,0},{2,3},{3,2},{4,5},{5,4},{6,7},{7,6},{8,9},{9,8},{10,11... | collective-permute-start | bytes 9437192 | tf_op jit(solution)/shard_map/ppermute | solution.py:33
  355.6 209.0 %reduce-scatter.7.cloned.1.call-start = ((), (), s32[]{:S(2)}) async-start(), calls=%async_computation.8 | async-start | bytes 5242880 | tf_op jit(solution)/shard_map/reduce_scatter | solution.py:316
  489.1 162.1 %all-gather.11.cloned.1.call-start = ((), (), s32[]{:S(2)}) async-start(), calls=%async_computation.9 | async-start | bytes 5242880 | tf_op jit(solution)/shard_map/all_gather | solution.py:313
  569.8 418.6 %reduce-scatter.9.cloned.1.call-start = ((), (), s32[]{:S(2)}) async-start(), calls=%async_computation.10 | async-start | bytes 5242880 | tf_op jit(solution)/shard_map/reduce_scatter | solution.py:316
  581.9 131.0 %collective-permute-start.30 = (bf16[1024,3072]{1,0:T(8,128)(2,1)}, bf16[1024,3072]{1,0:T(8,128)(2,1)}, u32[]{:S(2)}, u32[]{:S(2)}) collective-permute-start(bf16[1024,3072]{1,0:T(8,128)(2,1)} %convolution_convert_fusion), channel_id=1, source_target_pairs={{0,1},{1,0},{2,3},{3,2},{4,5},{5,4},{6,7},{7,6},{8,9},{9,8},{10,11... | collective-permute-start | bytes 18874376 | tf_op jit(solution)/shard_map/ppermute | solution.py:33
  600.6 99.1 %collective-permute-start.33 = (bf16[1536,1024]{1,0:T(8,128)(2,1)}, bf16[1536,1024]{1,0:T(8,128)(2,1)}, u32[]{:S(2)}, u32[]{:S(2)}) collective-permute-start(bf16[1536,1024]{1,0:T(8,128)(2,1)} %convolution_convert_fusion.5), channel_id=1, source_target_pairs={{0,1},{1,0},{2,3},{3,2},{4,5},{5,4},{6,7},{7,6},{8,9},{9,8},{10,11... | collective-permute-start | bytes 9437192 | tf_op jit(solution)/shard_map/ppermute | solution.py:33
  651.2 337.1 %reduce-scatter.11.cloned.1.call-start = ((), (), s32[]{:S(2)}) async-start(), calls=%async_computation.11 | async-start | bytes 5242880 | tf_op jit(solution)/shard_map/reduce_scatter | solution.py:316
  696.3 32.1 %collective-permute-start.19 = (bf16[2048,512]{1,0:T(8,128)(2,1)}, bf16[2048,512]{1,0:T(8,128)(2,1)}, u32[]{:S(2)}, u32[]{:S(2)}) collective-permute-start(bf16[2048,512]{1,0:T(8,128)(2,1)} %pad_maximum_fusion.7), channel_id=1, source_target_pairs={{0,1},{1,0},{2,3},{3,2},{4,5},{5,4},{6,7},{7,6},{8,9},{9,8},{10,11... | collective-permute-start | bytes 6291464 | tf_op jit(solution)/shard_map/ppermute | solution.py:33
  706.7 40.9 %collective-permute-start.34 = (bf16[1536,512]{1,0:T(8,128)(2,1)}, bf16[1536,512]{1,0:T(8,128)(2,1)}, u32[]{:S(2)}, u32[]{:S(2)}) collective-permute-start(bf16[1536,512]{1,0:T(8,128)(2,1)} %slice.300), channel_id=1, source_target_pairs={{0,2},{1,3},{2,0},{3,1},{4,6},{5,7},{6,4},{7,5},{8,10},{9,11},{10,... | collective-permute-start | bytes 4718600 | tf_op jit(solution)/shard_map/ppermute | solution.py:33
  726.9 130.0 %collective-permute-start.31 = (bf16[512,3072]{1,0:T(8,128)(2,1)}, bf16[512,3072]{1,0:T(8,128)(2,1)}, u32[]{:S(2)}, u32[]{:S(2)}) collective-permute-start(bf16[512,3072]{1,0:T(8,128)(2,1)} %slice.299), channel_id=1, source_target_pairs={{0,2},{1,3},{2,0},{3,1},{4,6},{5,7},{6,4},{7,5},{8,10},{9,11},{10,... | collective-permute-start | bytes 9437192 | tf_op jit(solution)/shard_map/ppermute | solution.py:33
  734.9 102.5 %collective-permute-start.20 = (bf16[1024,512]{1,0:T(8,128)(2,1)S(1)}, bf16[1024,512]{1,0:T(8,128)(2,1)S(1)}, u32[]{:S(2)}, u32[]{:S(2)}) collective-permute-start(bf16[1024,512]{1,0:T(8,128)(2,1)S(1)} %fusion.38), channel_id=1, source_target_pairs={{0,2},{1,3},{2,0},{3,1},{4,6},{5,7},{6,4},{7,5},{8,10},{9,11},{10,... | collective-permute-start | bytes 3145736 | tf_op jit(solution)/shard_map/ppermute | solution.py:33
  750.7 116.8 %collective-permute-start.35 = (bf16[1536,512]{1,0:T(8,128)(2,1)}, bf16[1536,512]{1,0:T(8,128)(2,1)}, u32[]{:S(2)}, u32[]{:S(2)}) collective-permute-start(bf16[1536,512]{1,0:T(8,128)(2,1)} %fusion.2), channel_id=1, source_target_pairs={{0,16},{16,0},{1,17},{17,1},{2,18},{18,2},{3,19},{19,3},{4,20},{20... | collective-permute-start | bytes 4718600 | tf_op jit(solution)/shard_map/ppermute | solution.py:327
  861.8 71.7 %collective-permute-start.32 = (bf16[512,3072]{1,0:T(8,128)(2,1)S(1)}, bf16[512,3072]{1,0:T(8,128)(2,1)S(1)}, u32[]{:S(2)}, u32[]{:S(2)}) collective-permute-start(bf16[512,3072]{1,0:T(8,128)(2,1)S(1)} %fusion), channel_id=1, source_target_pairs={{0,16},{16,0},{1,17},{17,1},{2,18},{18,2},{3,19},{19,3},{4,20},{20... | collective-permute-start | bytes 9437192 | tf_op jit(solution)/shard_map/ppermute | solution.py:327
  874.6 60.1 %collective-permute-start.27 = (bf16[512,1024]{1,0:T(8,128)(2,1)}, bf16[512,1024]{1,0:T(8,128)(2,1)}, u32[]{:S(2)}, u32[]{:S(2)}) collective-permute-start(bf16[512,1024]{1,0:T(8,128)(2,1)} %fusion.41), channel_id=1, source_target_pairs={{0,1},{1,0},{2,3},{3,2},{4,5},{5,4},{6,7},{7,6},{8,9},{9,8},{10,11... | collective-permute-start | bytes 3145736 | tf_op jit(solution)/shard_map/ppermute | solution.py:33
  877.2 62.2 %collective-permute-start.25 = (bf16[512,1028]{0,1:T(8,128)(2,1)S(1)}, bf16[512,1028]{0,1:T(8,128)(2,1)S(1)}, u32[]{:S(2)}, u32[]{:S(2)}) collective-permute-start(bf16[512,1028]{0,1:T(8,128)(2,1)S(1)} %slice.301), channel_id=1, source_target_pairs={{0,2},{1,3},{2,0},{3,1},{4,6},{5,7},{6,4},{7,5},{8,10},{9,11},{10,... | collective-permute-start | bytes 3158024 | tf_op jit(solution)/shard_map/ppermute | solution.py:33
  939.7 37.2 %collective-permute-start.26 = (bf16[512,1028]{0,1:T(8,128)(2,1)S(1)}, bf16[512,1028]{0,1:T(8,128)(2,1)S(1)}, u32[]{:S(2)}, u32[]{:S(2)}) collective-permute-start(bf16[512,1028]{0,1:T(8,128)(2,1)S(1)} %fusion.10), channel_id=1, source_target_pairs={{0,16},{16,0},{1,17},{17,1},{2,18},{18,2},{3,19},{19,3},{4,20},{20... | collective-permute-start | bytes 3158024 | tf_op jit(solution)/shard_map/ppermute | solution.py:327
  951.5 24.3 %collective-permute-start.29 = (bf16[512,512]{1,0:T(8,128)(2,1)S(1)}, bf16[512,512]{1,0:T(8,128)(2,1)S(1)}, u32[]{:S(2)}, u32[]{:S(2)}) collective-permute-start(bf16[512,512]{1,0:T(8,128)(2,1)S(1)} %fusion.44), channel_id=1, source_target_pairs={{0,16},{16,0},{1,17},{17,1},{2,18},{18,2},{3,19},{19,3},{4,20},{20... | collective-permute-start | bytes 1572872 | tf_op jit(solution)/shard_map/ppermute | solution.py:327
  992.3 53.4 %collective-permute-start.16 = (bf16[256,512]{1,0:T(8,128)(2,1)}, bf16[256,512]{1,0:T(8,128)(2,1)}, u32[]{:S(2)}, u32[]{:S(2)}) collective-permute-start(bf16[256,512]{1,0:T(8,128)(2,1)} %get-tuple-element.137), channel_id=1, source_target_pairs={{0,2},{1,3},{2,0},{3,1},{4,6},{5,7},{6,4},{7,5},{8,10},{9,11},{10,... | collective-permute-start | bytes 786440 | tf_op jit(solution)/shard_map/ppermute | solution.py:33
  992.6 54.0 %collective-permute-start.17 = (bf16[256,512]{1,0:T(8,128)(2,1)}, bf16[256,512]{1,0:T(8,128)(2,1)}, u32[]{:S(2)}, u32[]{:S(2)}) collective-permute-start(bf16[256,512]{1,0:T(8,128)(2,1)} %get-tuple-element.136), channel_id=1, source_target_pairs={{0,1},{1,0},{2,3},{3,2},{4,5},{5,4},{6,7},{7,6},{8,9},{9,8},{10,11... | collective-permute-start | bytes 786440 | tf_op jit(solution)/shard_map/ppermute | solution.py:33
  995.4 47.7 %collective-permute-start.21 = (bf16[256,512]{1,0:T(8,128)(2,1)S(1)}, bf16[256,512]{1,0:T(8,128)(2,1)S(1)}, u32[]{:S(2)}, u32[]{:S(2)}) collective-permute-start(bf16[256,512]{1,0:T(8,128)(2,1)S(1)} %get-tuple-element.132), channel_id=1, source_target_pairs={{0,2},{1,3},{2,0},{3,1},{4,6},{5,7},{6,4},{7,5},{8,10},{9,11},{10,... | collective-permute-start | bytes 786440 | tf_op jit(solution)/shard_map/ppermute | solution.py:33
  996.6 47.4 %collective-permute-start.22 = (bf16[256,512]{1,0:T(8,128)(2,1)S(1)}, bf16[256,512]{1,0:T(8,128)(2,1)S(1)}, u32[]{:S(2)}, u32[]{:S(2)}) collective-permute-start(bf16[256,512]{1,0:T(8,128)(2,1)S(1)} %get-tuple-element.131), channel_id=1, source_target_pairs={{0,1},{1,0},{2,3},{3,2},{4,5},{5,4},{6,7},{7,6},{8,9},{9,8},{10,11... | collective-permute-start | bytes 786440 | tf_op jit(solution)/shard_map/ppermute | solution.py:33
  996.8 47.2 %collective-permute-start.23 = (bf16[256,512]{1,0:T(8,128)(2,1)S(1)}, bf16[256,512]{1,0:T(8,128)(2,1)S(1)}, u32[]{:S(2)}, u32[]{:S(2)}) collective-permute-start(bf16[256,512]{1,0:T(8,128)(2,1)S(1)} %get-tuple-element.130), channel_id=1, source_target_pairs={{0,3},{1,2},{2,1},{3,0},{4,7},{5,6},{6,5},{7,4},{8,11},{9,10},{10,... | collective-permute-start | bytes 786440 | tf_op jit(solution)/shard_map/ppermute | solution.py:33
  (63 other events, 705.9 us)
Sparse Core Ops, SparseCore 0:
  25.3 82.7 all-gather.4
  204.2 82.4 reduce-scatter.4
  290.0 81.2 all-gather.6
  373.3 79.2 all-gather.8
  489.2 75.2 reduce-scatter.6
  569.9 81.2 all-gather.10
  653.5 75.2 reduce-scatter.8
  857.0 78.0 reduce-scatter.10

commit v2 on v1

v2 whole, which is shorter than its diff:
```python
import functools
import math

import jax
import jax.numpy as jnp
from jax import lax
from jax.experimental import pallas as pl
from jax.experimental.pallas import tpu as pltpu
from jax.sharding import PartitionSpec as P

PROMPT = 2048
EPS = 1e-06
THETA = 1000000.0
RELATIVE = (0, 2, 1, 3)
BF16 = jnp.bfloat16
F32 = jnp.float32
VMEM_LIMIT = 56 * 1024 * 1024
LANES = 128


def dot_rows(left, right):
    return jnp.dot(left, right, preferred_element_type=F32)


def dot_trans(left, right):
    return lax.dot_general(left, right, (((1,), (1,)), ((), ())), preferred_element_type=F32)


def dot_inner(left, right):
    return lax.dot_general(left, right, (((0,), (0,)), ((), ())), preferred_element_type=F32)


def exchange(values, axis, distance, size):
    return lax.ppermute(values, axis, [(i, i ^ distance) for i in range(size)])


def join(parts, axis=0):
    return jnp.concatenate(parts, axis=axis)


def cut(values, at, length, axis):
    return lax.dynamic_slice_in_dim(values, at, length, axis=axis)


def turn_pairs(values):
    step = values.shape[1] // 4
    return join([values[:, i * step : (i + 1) * step] for i in (1, 0, 3, 2)], 1)


def after(values, *others):
    return lax.optimization_barrier((values,) + others)[0]


def columns(heads, pairs, size):
    query, pair = heads // 2, pairs // 2
    block = (query + 2 * pair) * size
    of = lambda i, count, before: (i // count) * block + (before + i % count) * size
    return (
        [of(h, query, 0) for h in range(heads)],
        [of(p, pair, query) for p in range(pairs)],
        [of(p, pair, query + pair) for p in range(pairs)],
        2 * block,
    )


def post_kernel(raw_ref, cos_ref, sin_ref, query_gain_ref, key_gain_ref, q_ref, kv_ref, *, heads, pairs, size, factor):
    cosine = cos_ref[...]
    sine = sin_ref[...]
    query_at, key_at, value_at, _ = columns(heads, pairs, size)

    def turned(value, gain):
        inverse = lax.rsqrt(jnp.mean(value * value, axis=-1, keepdims=True) + EPS)
        normal = value * inverse * gain
        return normal * cosine + pltpu.roll(normal, size // 2, 1) * sine

    for h, at in enumerate(query_at):
        value = raw_ref[:, at : at + size]
        q_ref[:, h * size : (h + 1) * size] = (turned(value, query_gain_ref[...]) * factor).astype(BF16)
    for p, at in enumerate(key_at):
        kv_ref[:, p * size : (p + 1) * size] = turned(raw_ref[:, at : at + size], key_gain_ref[...]).astype(BF16)
    for p, at in enumerate(value_at):
        to = (pairs + p) * size
        kv_ref[:, to : to + size] = raw_ref[:, at : at + size].astype(BF16)


def post(raw, cosine, sine, query_gain, key_gain, heads, pairs, size, factor):
    rows, width = raw.shape
    step = 256
    return pl.pallas_call(
        functools.partial(post_kernel, heads=heads, pairs=pairs, size=size, factor=factor),
        grid=(rows // step,),
        in_specs=[
            pl.BlockSpec((step, width), lambda i: (i, 0)),
            pl.BlockSpec((step, size), lambda i: (i, 0)),
            pl.BlockSpec((step, size), lambda i: (i, 0)),
            pl.BlockSpec((1, size), lambda i: (0, 0)),
            pl.BlockSpec((1, size), lambda i: (0, 0)),
        ],
        out_specs=[
            pl.BlockSpec((step, heads * size), lambda i: (i, 0)),
            pl.BlockSpec((step, 2 * pairs * size), lambda i: (i, 0)),
        ],
        out_shape=[
            jax.ShapeDtypeStruct((rows, heads * size), BF16),
            jax.ShapeDtypeStruct((rows, 2 * pairs * size), BF16),
        ],
        cost_estimate=pl.CostEstimate(flops=rows * width * 20, bytes_accessed=rows * width * 8, transcendentals=0),
        name="post",
    )(raw, cosine, sine, query_gain[None], key_gain[None])


def back_kernel(
    dq_ref, dkv_ref, raw_ref, cos_ref, sin_ref, query_gain_ref, key_gain_ref, logit_ref, out_ref, gq_ref, gk_ref, *, heads, pairs, size, factor_q, factor_k
):
    cosine = cos_ref[...]
    sine = sin_ref[...]
    query_at, key_at, value_at, logit_at = columns(heads, pairs, size)

    @pl.when(pl.program_id(0) == 0)
    def _():
        gq_ref[...] = jnp.zeros_like(gq_ref)
        gk_ref[...] = jnp.zeros_like(gk_ref)

    def back(up, value, gain, total_ref):
        up = up * cosine - pltpu.roll(up, size // 2, 1) * sine
        inverse = lax.rsqrt(jnp.mean(value * value, axis=-1, keepdims=True) + EPS)
        hat = value * inverse
        total_ref[...] += jnp.sum(up * hat, axis=0, keepdims=True)
        scaled = up * gain
        return inverse * (scaled - hat * jnp.mean(scaled * hat, axis=-1, keepdims=True))

    for h, at in enumerate(query_at):
        up = dq_ref[:, h * size : (h + 1) * size] * factor_q
        out_ref[:, at : at + size] = back(up, raw_ref[:, at : at + size], query_gain_ref[...], gq_ref).astype(BF16)
    for p, at in enumerate(key_at):
        up = dkv_ref[:, p * size : (p + 1) * size].astype(F32) * factor_k
        out_ref[:, at : at + size] = back(up, raw_ref[:, at : at + size], key_gain_ref[...], gk_ref).astype(BF16)
    for p, at in enumerate(value_at):
        to = (pairs + p) * size
        out_ref[:, at : at + size] = dkv_ref[:, to : to + size].astype(BF16)
    out_ref[:, logit_at:] = logit_ref[...].astype(BF16)


def project_back(dq, dkv, raw, cosine, sine, query_gain, key_gain, logit_grad, heads, pairs, size, factor_q, factor_k):
    rows, width = raw.shape
    step = 256
    row = lambda cols: pl.BlockSpec((step, cols), lambda i: (i, 0))
    one = pl.BlockSpec((1, size), lambda i: (0, 0))
    return pl.pallas_call(
        functools.partial(back_kernel, heads=heads, pairs=pairs, size=size, factor_q=factor_q, factor_k=factor_k),
        grid=(rows // step,),
        in_specs=[row(heads * size), row(2 * pairs * size), row(width), row(size), row(size), one, one, row(LANES)],
        out_specs=[row(width), one, one],
        out_shape=[
            jax.ShapeDtypeStruct((rows, width), BF16),
            jax.ShapeDtypeStruct((1, size), F32),
            jax.ShapeDtypeStruct((1, size), F32),
        ],
        cost_estimate=pl.CostEstimate(flops=rows * width * 30, bytes_accessed=rows * width * 12, transcendentals=0),
        name="project_back",
    )(dq, dkv, raw, cosine, sine, query_gain[None], key_gain[None], logit_grad)


def places(table_ref, stripe, step, length):
    turn = table_ref[stripe, 3]
    core = table_ref[stripe, 4]
    half = length // 2
    blocks = half // step

    def pair(i):
        at = jnp.bitwise_xor(i, turn) * step
        return pl.ds(pl.multiple_of(at, step), step), pl.ds(pl.multiple_of(at + half // 2, step), step)

    def single(b):
        part = b // blocks
        inner = b - part * blocks
        at = part * half + jnp.bitwise_xor(inner % 2, core) * (half // 2) + jnp.bitwise_xor(inner // 2, turn) * step
        return (pl.ds(pl.multiple_of(at, step), step),)

    return pair, single


def forward_kernel(table_ref, q_ref, kv_ref, row_ref, start_ref, logit_ref, gated_ref, context_ref, inverse_ref, *, pairs, repeat, size, step):
    stripe = pl.program_id(0)
    wide_blocks = table_ref[stripe, 0]
    low = table_ref[stripe, 1]
    high = table_ref[stripe, 2]
    pair, single = places(table_ref, stripe, step, kv_ref.shape[0])
    rows = row_ref[...]
    starts = start_ref[...]
    rows = jnp.concatenate([rows] * repeat, axis=0)
    starts = jnp.concatenate([starts] * repeat, axis=0)
    for k in range(pairs):
        heads = [k * repeat + r for r in range(repeat)]
        query = jnp.concatenate([q_ref[:, h * size : (h + 1) * size] for h in heads], axis=0)
        key_cols = slice(k * size, (k + 1) * size)
        value_cols = slice((pairs + k) * size, (pairs + k + 1) * size)

        def seen(total, where, first):
            keys = join([kv_ref[at, key_cols] for at in where])
            weights = jnp.exp2(dot_trans(query, keys))
            if first is not None:
                index = first + lax.broadcasted_iota(jnp.int32, weights.shape, 1)
                weights = jnp.where((index <= rows) & (index >= starts), weights, 0.0)
            values = join([kv_ref[at, value_cols] for at in where])
            values = jnp.concatenate([values, jnp.ones_like(values)], axis=1)
            return total + dot_rows(weights.astype(BF16), values)

        total = jnp.zeros((query.shape[0], 2 * size), F32)
        total = lax.fori_loop(0, wide_blocks, lambda i, t: seen(t, pair(i), None), total)
        total = lax.fori_loop(low, high + 1, lambda i, t: seen(t, single(i), i * step), total)
        inverse = 1.0 / total[:, size:]
        context = total[:, :size] * inverse
        for r, h in enumerate(heads):
            part = context[r * step : (r + 1) * step]
            cols = slice(h * size, (h + 1) * size)
            gate = jax.nn.sigmoid(logit_ref[:, h : h + 1])
            gated_ref[:, cols] = (part * gate).astype(BF16)
            context_ref[:, cols] = part
            inverse_ref[:, cols] = inverse[r * step : (r + 1) * step]


def attend(table, q, kv, rows, starts, raw, pairs, size):
    length, cols = q.shape
    heads = cols // size
    step = length // table.shape[0]
    block = lambda width: pl.BlockSpec((step, width), lambda i, t: (i, 0))
    logit_block = raw.shape[1] // LANES - 1
    return pl.pallas_call(
        functools.partial(forward_kernel, pairs=pairs, repeat=heads // pairs, size=size, step=step),
        grid_spec=pltpu.PrefetchScalarGridSpec(
            num_scalar_prefetch=1,
            grid=(length // step,),
            in_specs=[
                block(cols),
                pl.BlockSpec(kv.shape, lambda i, t: (0, 0), pipeline_mode=pl.Buffered(1)),
                block(1),
                block(1),
                pl.BlockSpec((step, LANES), lambda i, t: (i, logit_block)),
            ],
            out_specs=[block(cols), block(cols), block(cols)],
        ),
        out_shape=[
            jax.ShapeDtypeStruct((length, cols), BF16),
            jax.ShapeDtypeStruct((length, cols), F32),
            jax.ShapeDtypeStruct((length, cols), F32),
        ],
        compiler_params=pltpu.CompilerParams(vmem_limit_bytes=VMEM_LIMIT),
        cost_estimate=pl.CostEstimate(flops=20 * 10**9, bytes_accessed=12 * 10**6, transcendentals=7 * 10**6),
        name="attend",
    )(table, q, kv, rows, starts, raw)


def backward_kernel(
    table_ref, q_ref, kv_ref, row_ref, start_ref, logit_ref, context_ref, inverse_ref, grad_ref,
    dq_ref, dkv_ref, dlogit_ref, sums_ref, *, pairs, repeat, size, step,
):
    stripe = pl.program_id(0)
    wide_blocks = table_ref[stripe, 0]
    low = table_ref[stripe, 1]
    high = table_ref[stripe, 2]
    pair, single = places(table_ref, stripe, step, kv_ref.shape[0])

    @pl.when(stripe == 0)
    def _():
        sums_ref[...] = jnp.zeros_like(sums_ref)

    dlogit_ref[...] = jnp.zeros_like(dlogit_ref)
    rows = jnp.concatenate([row_ref[0]] * repeat, axis=1)
    starts = jnp.concatenate([start_ref[0]] * repeat, axis=1)
    for k in range(pairs):
        heads = [k * repeat + r for r in range(repeat)]
        query = jnp.concatenate([q_ref[:, h * size : (h + 1) * size] for h in heads], axis=0)
        grads, inners = [], []
        for h in heads:
            cols = slice(h * size, (h + 1) * size)
            up = grad_ref[:, cols]
            gate = jax.nn.sigmoid(logit_ref[:, h : h + 1])
            product = jnp.sum(up * context_ref[:, cols], axis=1, keepdims=True)
            dlogit_ref[:, h : h + 1] = product * gate * (1.0 - gate)
            inverse = inverse_ref[:, cols]
            grads.append((up * gate * inverse).astype(BF16))
            inners.append(product * gate * inverse)
        grad = jnp.concatenate(grads, axis=0)
        inner = jnp.transpose(jnp.concatenate(inners, axis=0))[0:1]
        key_cols = slice(k * size, (k + 1) * size)
        value_cols = slice((pairs + k) * size, (pairs + k + 1) * size)

        def seen(total, where, first):
            keys = join([kv_ref[at, key_cols] for at in where])
            weights = jnp.exp2(dot_trans(keys, query))
            if first is not None:
                index = first + lax.broadcasted_iota(jnp.int32, weights.shape, 0)
                weights = jnp.where((index <= rows) & (index >= starts), weights, 0.0)
            changes = dot_trans(join([kv_ref[at, value_cols] for at in where]), grad)
            changes = (weights * (changes - inner)).astype(BF16)
            value_sums = dot_rows(weights.astype(BF16), grad)
            key_sums = dot_rows(changes, query)
            for i, at in enumerate(where):
                sums_ref[at, value_cols] += value_sums[i * step : (i + 1) * step]
                sums_ref[at, key_cols] += key_sums[i * step : (i + 1) * step]
            return total + dot_inner(changes, keys)

        total = jnp.zeros((query.shape[0], size), F32)
        total = lax.fori_loop(0, wide_blocks, lambda i, t: seen(t, pair(i), None), total)
        total = lax.fori_loop(low, high + 1, lambda i, t: seen(t, single(i), i * step), total)
        for r, h in enumerate(heads):
            dq_ref[:, h * size : (h + 1) * size] = total[r * step : (r + 1) * step]

    @pl.when(stripe == pl.num_programs(0) - 1)
    def _():
        dkv_ref[...] = sums_ref[...].astype(BF16)


def attend_back(table, q, kv, rows, starts, raw, context, inverse, grad, pairs, size):
    length, cols = q.shape
    heads = cols // size
    step = length // table.shape[0]
    block = lambda width: pl.BlockSpec((step, width), lambda i, t: (i, 0))
    whole = pl.BlockSpec(kv.shape, lambda i, t: (0, 0), pipeline_mode=pl.Buffered(1))
    lane = pl.BlockSpec((1, 1, step), lambda i, t: (i, 0, 0))
    logit_block = raw.shape[1] // LANES - 1
    logit = pl.BlockSpec((step, LANES), lambda i, t: (i, logit_block))
    return pl.pallas_call(
        functools.partial(backward_kernel, pairs=pairs, repeat=heads // pairs, size=size, step=step),
        grid_spec=pltpu.PrefetchScalarGridSpec(
            num_scalar_prefetch=1,
            grid=(length // step,),
            in_specs=[block(cols), whole, lane, lane, logit, block(cols), block(cols), block(cols)],
            out_specs=[block(cols), whole, block(LANES)],
            scratch_shapes=[pltpu.VMEM(kv.shape, F32)],
        ),
        out_shape=[
            jax.ShapeDtypeStruct((length, cols), F32),
            jax.ShapeDtypeStruct(kv.shape, BF16),
            jax.ShapeDtypeStruct((length, LANES), F32),
        ],
        compiler_params=pltpu.CompilerParams(vmem_limit_bytes=VMEM_LIMIT),
        cost_estimate=pl.CostEstimate(flops=50 * 10**9, bytes_accessed=20 * 10**6, transcendentals=7 * 10**6),
        name="attend_back",
    )(table, q, kv, rows.reshape(-1, 1, step), starts.reshape(-1, 1, step), raw, context, inverse, grad)


def layout(lengths, group_rows):
    ends = jnp.cumsum(lengths)
    begins = ends - lengths
    index = jnp.arange(group_rows, dtype=jnp.int32)
    offset = index - PROMPT
    member = ((offset[:, None] >= begins[None, :]) & (offset[:, None] < ends[None, :])).astype(jnp.int32)
    shift = jnp.sum(member * begins[None, :], axis=1)
    start = jnp.where(offset >= 0, PROMPT + shift, 0)
    return index, start, index - shift


def make(sizes):
    n_dp, n_wide, n_narrow = sizes["dp"], sizes["wide"], sizes["narrow"]

    def over_y(values):
        return exchange(values, "narrow", 2, n_narrow)

    def over_core(values):
        return exchange(values, "narrow", 1, n_narrow)

    def over_z(values):
        return exchange(values, "wide", 1, n_wide)

    def over_far(values):
        return exchange(values, "wide", 2, n_wide)

    def over_x(values):
        return exchange(values, "dp", 1, n_dp)

    def gather_rows(values):
        half = values.shape[0] // 2
        first, second = values[:half], values[half:]
        turned = turn_pairs(values)
        first_y = over_y(turned[:half])
        second_z = over_z(second)
        come = over_z(join([first, first_y]))
        first_z, first_d = come[:half], come[half:]
        come = over_y(join([turned[half:], turn_pairs(second_z)]))
        second_y, second_d = come[:half], come[half:]
        return join([first, second, first_y, second_y, first_z, second_z, first_d, second_d])

    def scatter_rows(partial):
        half = partial.shape[0] // 8
        part = lambda i: partial[i * half : (i + 1) * half]
        come = over_z(join([part(4), part(6)]))
        first = part(0).astype(F32) + come[:half]
        first_y = (part(2).astype(F32) + come[half:]).astype(BF16)
        come = over_y(turn_pairs(join([part(3), part(7)])))
        second = part(1).astype(F32) + come[:half]
        second_z = (part(5).astype(F32) + come[half:]).astype(BF16)
        first = first + over_y(turn_pairs(first_y)).astype(F32)
        second = second + over_z(second_z).astype(F32)
        return join([first, second])

    def all_sum(values):
        for axis, size in (("narrow", n_narrow), ("wide", n_wide), ("dp", n_dp)):
            distance = 1
            while distance < size:
                values = values + exchange(values, axis, distance, size)
                distance *= 2
        return values

    def on_device(
        tokens, continuation_lengths, attention_gain, query_weight, key_weight, value_weight, head_gate, query_gain, key_gain,
        output_weight, feedforward_gain, gate_weight, up_weight, down_weight, cotangent,
    ):
        rows_wide, width_local = tokens.shape
        width = attention_gain.shape[0]
        size = query_gain.shape[0]
        heads = head_gate.shape[1]
        pairs = key_weight.shape[1] // size
        group_rows = rows_wide * n_wide
        rows_local = rows_wide // n_narrow
        x = lax.axis_index("dp") % 2
        z = lax.axis_index("wide")
        narrow = lax.axis_index("narrow")
        y, core = narrow // 2, narrow % 2
        z_near, z_far = z % 2, z // 2
        quarter = width_local // 2
        scale = size ** (-0.5)
        factor = scale * math.log2(math.e)
        log_two = math.log(2.0)

        def by_x(values, axis):
            half = values.shape[axis] // 2
            low = lax.slice_in_dim(values, 0, half, axis=axis)
            high = lax.slice_in_dim(values, half, 2 * half, axis=axis)
            return join([jnp.where(x == 0, low, high), jnp.where(x == 0, high, low)], axis)

        def to_local(values):
            values = by_x(values, 1)
            send = [cut(values, (narrow ^ r) * rows_local, rows_local, 0) for r in RELATIVE]
            parts = [send[0]] + [exchange(s, "narrow", r, n_narrow) for s, r in zip(send[1:], RELATIVE[1:])]
            return join(parts, 1)

        def from_local(values):
            out = jnp.zeros((rows_wide, width_local), values.dtype)
            for i, r in enumerate(RELATIVE):
                part = by_x(values[:, i * width_local : (i + 1) * width_local], 1)
                if r:
                    part = exchange(part, "narrow", r, n_narrow)
                out = lax.dynamic_update_slice_in_dim(out, part, (narrow ^ r) * rows_local, 0)
            return out

        def relative_vector(vector):
            return join([by_x(cut(vector, (narrow ^ r) * width_local, width_local, 0), 0) for r in RELATIVE])

        def absolute_vector(vector):
            out = jnp.zeros((width,), vector.dtype)
            for i, r in enumerate(RELATIVE):
                part = by_x(vector[i * width_local : (i + 1) * width_local], 0)
                out = lax.dynamic_update_slice_in_dim(out, part, (narrow ^ r) * width_local, 0)
            return out

        def norm(values, gain):
            inverse = lax.rsqrt(jnp.mean(values * values, axis=1, keepdims=True) + EPS)
            hat = values * inverse
            return inverse, hat, (hat * gain).astype(BF16)

        def norm_back(grad, hat, inverse, gain):
            scaled = grad * gain
            inner = jnp.mean(scaled * hat, axis=1, keepdims=True)
            return jnp.sum(grad * hat, axis=0), inverse * (scaled - hat * inner)

        def pieces(weights, axis):
            across = 1 - axis
            half = lambda i: join([cut(w, i * (w.shape[across] // 2), w.shape[across] // 2, across) for w in weights], across)
            mine = half(y)
            return (
                cut(mine, x * quarter, quarter, axis),
                cut(mine, (1 - x) * quarter, quarter, axis),
                cut(half(1 - y), x * quarter, quarter, axis),
            )

        def send_far(mine, from_y, axis):
            return over_far(join([mine, from_y], axis))

        def assemble(mine, rest, from_y, from_far, axis):
            far_first = lax.slice_in_dim(from_far, 0, quarter, axis=axis)
            far_second = lax.slice_in_dim(from_far, quarter, 2 * quarter, axis=axis)
            their_y, their_far = over_x(from_y), over_x(from_far)
            their_first = lax.slice_in_dim(their_far, 0, quarter, axis=axis)
            their_second = lax.slice_in_dim(their_far, quarter, 2 * quarter, axis=axis)
            own = join([mine, rest, from_y, their_y], axis)
            other = join([far_first, their_first, far_second, their_second], axis)
            block = join([own, other], 1 - axis)
            return block, over_core(block)

        def reduce_weight(first, second, axis, widths, kind=BF16):
            across = 1 - axis
            step = first.shape[axis] // 4
            piece = lambda v, i: lax.slice_in_dim(v, i * step, (i + 1) * step, axis=axis)
            total = first + over_core(second.astype(kind)).astype(F32)
            come = over_x(join([piece(total, 1), piece(total, 3)], axis).astype(kind))
            total = join([piece(total, 0), piece(total, 2)], axis) + come.astype(F32)
            distance = 2
            while distance < n_dp:
                total = total + exchange(total.astype(kind), "dp", distance, n_dp).astype(F32)
                distance *= 2
            count = sum(widths)
            come = over_far(lax.slice_in_dim(total, count, 2 * count, axis=across).astype(kind))
            total = (lax.slice_in_dim(total, 0, count, axis=across) + come.astype(F32)).astype(kind)
            ours = join([piece(total, 0), over_y(piece(total, 1))], across)
            theirs = over_x(ours)
            outs, at = [], 0
            for length in widths:
                sides = []
                for v in (ours, theirs):
                    a = lax.slice_in_dim(v, at, at + length, axis=across)
                    b = lax.slice_in_dim(v, count + at, count + at + length, axis=across)
                    sides.append(join([jnp.where(y == 0, a, b), jnp.where(y == 0, b, a)], across))
                a, b = sides
                outs.append(join([jnp.where(x == 0, a, b), jnp.where(x == 0, b, a)], axis).astype(F32))
                at += length
            return outs

        inputs = to_local(tokens)
        qkv_mine, qkv_rest, send = pieces([query_weight, key_weight, value_weight], 0)
        qkv_y = over_y(send)
        qkv_far = send_far(qkv_mine, qkv_y, 0)
        gates = lax.all_gather(lax.all_gather(head_gate, "wide", axis=1, tiled=True), "narrow", axis=0, tiled=True)
        gates = join([by_x(cut(gates, (narrow ^ r) * width_local, width_local, 0), 0) for r in RELATIVE])
        gates = join([cut(gates, v * heads + y * (heads // 2), heads // 2, 1) for v in (z, z ^ 2)], 1)
        gates = jnp.pad(gates, ((0, 0), (0, LANES - heads)))
        qkv_block, qkv_core = assemble(qkv_mine, qkv_rest, qkv_y, qkv_far, 0)
        joined_weight = join([join([qkv_block, qkv_core], 0), gates], 1)

        out_mine, out_rest, send = pieces([after(output_weight, qkv_y)], 1)
        out_y = over_y(send)
        down_mine, down_rest, send = pieces([after(down_weight, out_y)], 1)
        down_y = over_y(send)
        out_far = send_far(after(out_mine, qkv_far), out_y, 1)
        down_far = send_far(after(down_mine, out_far), down_y, 1)
        out_weight = join(assemble(out_mine, out_rest, out_y, out_far, 1), 1)
        down = join(assemble(down_mine, down_rest, down_y, down_far, 1), 1)

        index, start, position = layout(continuation_lengths[0], group_rows)
        square = [(z ^ (i // 2), narrow ^ (2 * (i % 2))) for i in range(4)]
        mine = lambda vector: join([cut(vector, (i * n_narrow + j) * rows_local, rows_local, 0) for i, j in square])
        my_index, my_start, my_position = mine(index), mine(start), mine(position)
        frequency = THETA ** (-2.0 * jnp.arange(size // 2, dtype=F32) / size)
        angle = my_position.astype(F32)[:, None] * frequency[None, :]
        cosine, sine = jnp.cos(angle), jnp.sin(angle)
        cosine = jnp.concatenate([cosine, cosine], axis=1)
        sine = jnp.concatenate([-sine, sine], axis=1)
        block = my_index[::rows_local] // rows_local
        first = my_start[::rows_local] // rows_local
        prompt_blocks = PROMPT // rows_local
        in_prompt = block < prompt_blocks
        table = jnp.stack(
            [
                jnp.where(in_prompt, block // 2, prompt_blocks // 2),
                jnp.where(in_prompt, block // 2 * 2, first),
                block,
                jnp.full_like(block, 2 * z_near + y),
                jnp.full_like(block, core),
            ],
            axis=1,
        ).astype(jnp.int32)

        gain_one, gain_two = relative_vector(attention_gain), relative_vector(feedforward_gain)
        inputs = inputs.astype(F32)
        inverse_one, hat_one, normed = norm(inputs, gain_one)
        normed_all = gather_rows(normed)
        raw = dot_rows(normed_all, joined_weight)
        q, kv = post(raw, cosine, sine, query_gain, key_gain, heads, pairs, size, factor)
        kv = after(kv, out_far, down_far)

        kv_core = over_core(kv)
        near = [i for i in range(n_wide) if i & 2 == 0]
        far_kv = lax.ppermute(turn_pairs(kv), "wide", [(i, i + 2) for i in near])
        far_core = over_core(far_kv)
        kv_all = join([jnp.where(z_far == 0, kv, far_kv), jnp.where(z_far == 0, kv_core, far_core), kv, kv_core])

        upstream = to_local(after(cotangent, kv))
        upstream_all = gather_rows(upstream)
        gate_mine, gate_rest, send = pieces([after(gate_weight, down_y)], 0)
        gate_y = over_y(send)
        up_mine, up_rest, send = pieces([after(up_weight, gate_y)], 0)
        up_y = over_y(send)
        gate_far = send_far(after(gate_mine, far_kv), gate_y, 0)
        up_far = send_far(after(up_mine, gate_far), up_y, 0)

        gated, context, inverse_total = attend(
            table, q, kv_all, my_index[:, None], my_start[:, None], raw, pairs, size
        )
        partial = dot_rows(after(gated, upstream_all, gate_far), out_weight).astype(BF16)
        middle = inputs + scatter_rows(partial)
        gate_full = join(assemble(gate_mine, gate_rest, gate_y, gate_far, 0), 0)
        up_full = join(assemble(up_mine, up_rest, up_y, up_far, 0), 0)
        inverse_two, hat_two, normed_two = norm(middle, gain_two)
        normed_two_all = gather_rows(normed_two)
        gate_pre = dot_rows(normed_two_all, gate_full)
        up_pre = dot_rows(normed_two_all, up_full)
        gate_sigmoid = jax.nn.sigmoid(gate_pre)
        silu = gate_pre * gate_sigmoid
        hidden = (silu * up_pre).astype(BF16)
        hidden_grad = dot_trans(upstream_all, down)
        gate_grad = (hidden_grad * up_pre * gate_sigmoid * (1.0 + gate_pre * (1.0 - gate_sigmoid))).astype(BF16)
        up_grad = (hidden_grad * silu).astype(BF16)
        partial = (dot_trans(gate_grad, gate_full) + dot_trans(up_grad, up_full)).astype(BF16)
        normed_two_grad = scatter_rows(partial)
        gain_two_term, change = norm_back(normed_two_grad, hat_two, inverse_two, gain_two)
        middle_grad = upstream.astype(F32) + change
        middle_low = middle_grad.astype(BF16)
        middle_all = gather_rows(middle_low)
        half = width // 2
        hidden_cols = gate_weight.shape[1] // 2
        down_gradient, = reduce_weight(
            dot_inner(hidden, upstream_all[:, :half]), dot_inner(hidden, upstream_all[:, half:]), 1, [hidden_cols]
        )
        gate_gradient, = reduce_weight(
            dot_inner(normed_two_all[:, :half], gate_grad), dot_inner(normed_two_all[:, half:], gate_grad), 0, [hidden_cols]
        )
        up_gradient, = reduce_weight(
            dot_inner(normed_two_all[:, :half], up_grad), dot_inner(normed_two_all[:, half:], up_grad), 0, [hidden_cols]
        )
        gated_grad = dot_trans(middle_all, out_weight)
        dq, dkv, logit_grad = attend_back(
            table, q, kv_all, my_index, my_start, raw, context, inverse_total, gated_grad, pairs, size
        )
        mlp_term = scatter_rows(dot_rows(after(hidden, middle_all), down).astype(BF16))
        layer_output = from_local((middle + mlp_term).astype(BF16))
        output_gradient, = reduce_weight(
            dot_inner(gated, middle_all[:, :half]), dot_inner(gated, middle_all[:, half:]), 1, [output_weight.shape[0] // 2]
        )

        part = lambda i: dkv[i * rows_wide : (i + 1) * rows_wide]
        come = over_core(join([part(1), part(3)]))
        prompt = part(0).astype(F32) + come[:rows_wide].astype(F32)
        rest = part(2).astype(F32) + come[rows_wide:].astype(F32)
        come = lax.ppermute(turn_pairs(prompt.astype(BF16)), "wide", [(i + 2, i) for i in near])
        dkv_mine = jnp.where(z_far == 0, prompt + come.astype(F32), rest)
        low, query_gain_term, key_gain_term = project_back(
            dq, dkv_mine, raw, cosine, sine, query_gain, key_gain, logit_grad, heads, pairs, size, scale, log_two
        )
        normed_grad = scatter_rows(dot_trans(low, joined_weight).astype(BF16))
        wide = low.shape[1] - LANES
        query_cols, key_cols = heads // 2 * size, pairs // 2 * size
        query_gradient, key_gradient, value_gradient = reduce_weight(
            dot_inner(normed_all[:, :half], low[:, :wide]), dot_inner(normed_all[:, half:], low[:, :wide]), 0,
            [query_cols, key_cols, key_cols],
        )
        gates_term = dot_inner(low[:, wide:], normed_all)[:heads]
        head_gate_gradient, = reduce_weight(gates_term[:, :half], gates_term[:, half:], 1, [heads // 2], F32)
        gain_one_term, change = norm_back(normed_grad, hat_one, inverse_one, gain_one)
        tokens_gradient = from_local((middle_grad + change).astype(BF16)).astype(F32)
        gains = all_sum(
            join([absolute_vector(gain_one_term), absolute_vector(gain_two_term), query_gain_term[0], key_gain_term[0]])
        )
        return (
            layer_output,
            tokens_gradient,
            gains[:width],
            query_gradient,
            key_gradient,
            value_gradient,
            head_gate_gradient.T,
            gains[2 * width : 2 * width + size],
            gains[2 * width + size :],
            output_gradient,
            gains[width : 2 * width],
            gate_gradient,
            up_gradient,
            down_gradient,
        )

    return on_device


def solution(mesh):
    rows, up, down = P(("dp", "wide"), "narrow"), P("narrow", "wide"), P("wide", "narrow")
    return jax.shard_map(
        make(dict(mesh.shape)),
        mesh=mesh,
        in_specs=(rows, P("dp", None), P(), up, up, up, up, P(), P(), down, P(), up, up, down, rows),
        out_specs=(rows, rows, P(), up, up, up, up, P(), P(), down, P(), up, up, down),
        check_vma=False,
    )
```

time: 1060 us -> 1070 us (level)
  waiting for transfers between devices: 599 us -> 466 us
  starting transfers between devices: 48.7 us -> 179 us
  other arithmetic: 70.9 us -> 155 us
  blocking collectives: 45.2 us -> 18.7 us
  local copies, waits for them, and re-layouts: 63.5 us -> 39.4 us
  Pallas kernels: 72.3 us -> 59.7 us
  between operations: 15.3 us -> 4.44 us
    all_gather x4 -> x0, waiting for transfers between devices: 159 us -> none  [gather_rows(): return lax.all_gather(values, 'wide', axis=0, tiled=True)]
    ppermute x36 -> x109, starting transfers between devices: 48.2 us -> 179 us  [the longest x107 173 us: exchange(): return lax.ppermute(values, axis, [(i, i ^ distance) for i in range(size)])]
    ppermute x36 -> x109, waiting for transfers between devices: 362 us -> 466 us  [the longest x107 466 us: exchange(): return lax.ppermute(values, axis, [(i, i ^ distance) for i in range(size)])]
    concatenate x12 -> x74, other arithmetic: 26.7 us -> 109 us  [join(): return jnp.concatenate(parts, axis=axis)]
    reduce_scatter x4 -> x0, waiting for transfers between devices: 77.8 us -> none  [scatter_rows(): lax.psum_scatter(values.astype(BF16), 'wide', scatter_dimension=0, tiled=...]
    psum x1 -> x0, blocking collectives: 45.2 us -> none  [on_device(): lax.psum((absolute_vector(gain_one_term), absolute_vector(gain_two_term),...]
    all_gather x0 -> x2, blocking collectives: none -> 18.7 us  [the longest x1 13.4 us: on_device(): lax.all_gather(head_gate, 'wide', axis=1, tiled=True)]
    concatenate x3 -> x4, local copies, waits for them, and re-layouts: 11.8 us -> 0.15 us  [join(): return jnp.concatenate(parts, axis=axis)]
  transfers between devices with their start and end apart: 44 -> 109, of which waited for: 22 -> 49; matrix products, arithmetic and copies ran while one was open for 19% -> 24% of each run, Pallas kernels for 4% -> 5%
where the time goes in v2:
time: 1070 us; the launch traced here: 1060 us
  waiting for transfers between devices  466 us (44%)
  starting transfers between devices  179 us (17%)
  other arithmetic  155 us (14%)
  matrix products  140 us (13%)
  Pallas kernels  59.7 us (6%)
  local copies, waits for them, and re-layouts  39.4 us (4%)
  blocking collectives  18.7 us (2%)
    ppermute x107, waiting for transfers between devices, exchange(): return lax.ppermute(values, axis, [(i, i ^ distance) for i in range(size)])  466 us
    ppermute x107, starting transfers between devices, exchange(): return lax.ppermute(values, axis, [(i, i ^ distance) for i in range(size)])  173 us
    concatenate x74, other arithmetic, join(): return jnp.concatenate(parts, axis=axis)  109 us
    dot_general x5, matrix products, dot_trans(): lax.dot_general(left, right, (((1,), (1,)), ((), ())), preferred_element_...  50.1 us
    dot_general x5, matrix products, dot_rows(): return jnp.dot(left, right, preferred_element_type=F32)  46.8 us
    dot_general x11, matrix products, dot_inner(): lax.dot_general(left, right, (((0,), (0,)), ((), ())), preferred_element_...  42.8 us
    pallas_call x1, Pallas kernels, attend_back(): pl.pallas_call(functools.partial(backward_kernel, pairs=pairs, repeat=hea...  26.2 us
  transfers between devices with their start and end apart: 109, of which 49 were waited for; matrix products, arithmetic and copies ran while one was open for 24% of the time, Pallas kernels for 5%

profile of v2, /device:TPU:0, one launch (start us, length us, event | category | flops | bytes accessed | tf_op | source)
XLA Modules:
  0.0 1062.1 jit_solution(1837198709989181203)
XLA Ops:
  9.9 13.4 %all-gather = bf16[4,4,512]{2,1,0:T(4,128)(2,1)S(1)} all-gather(bf16[1,4,512]{2,1,0:T(4,128)(2,1)S(1)} %bitcast.67), channel_id=1, replica_groups=mesh['dp'=2,'wide'=4,'narrow'=4] {'wide'}, dimensions={0}, use_global_device_ids=true | all-gather | bytes 20480 | tf_op jit(solution)/shard_map/all_gather | solution.py:524
  52.9 13.0 %collective-permute-done.9 = bf16[512,512]{1,0:T(8,128)(2,1)S(1)} collective-permute-done((bf16[512,512]{1,0:T(8,128)(2,1)S(1)}, bf16[512,512]{1,0:T(8,128)(2,1)S(1)}, u32[]{:S(2)}, u32[]{:S(2)}) %collective-permute-start.9) | collective-permute-done | bytes 524320 | tf_op jit(solution)/shard_map/ppermute | solution.py:34
  91.7 12.6 %maximum_maximum_fusion.3 = bf16[1024,1024]{1,0:T(8,128)(2,1)S(1)} fusion(bf16[256,512]{1,0:T(8,128)(2,1)S(1)} %get-tuple-element.356, bf16[256,512]{1,0:T(8,128)(2,1)S(1)} %get-tuple-element.354, bf16[256,512]{1,0:T(8,128)(2,1)S(1)} %get-tuple-element.355, bf16[256,512]{1,0:T(8,128)(2,1)S(1)} %get-tuple-element.353, ...), kind=kLoop, calls=%fused_computation.63 | loop fusion | flops 16777216 | bytes 4194304 | tf_op jit(solution)/shard_map/concatenate | solution.py:38
  104.9 17.4 %collective-permute-done.15 = bf16[768,512]{1,0:T(8,128)(2,1)S(1)} collective-permute-done((bf16[768,512]{1,0:T(8,128)(2,1)S(1)}, bf16[768,512]{1,0:T(8,128)(2,1)S(1)}, u32[]{:S(2)}, u32[]{:S(2)}) %collective-permute-start.15) | collective-permute-done | bytes 786464 | tf_op jit(solution)/shard_map/ppermute | solution.py:34
  124.1 12.2 %collective-permute-done.48 = bf16[768,512]{1,0:T(8,128)(2,1)S(1)} collective-permute-done((bf16[768,512]{1,0:T(8,128)(2,1)S(1)}, bf16[768,512]{1,0:T(8,128)(2,1)S(1)}, u32[]{:S(2)}, u32[]{:S(2)}) %collective-permute-start.48) | collective-permute-done | bytes 786464 | tf_op jit(solution)/shard_map/ppermute | solution.py:34
  178.0 17.6 %maximum_maximum_fusion.2 = bf16[1536,1024]{1,0:T(8,128)(2,1)} fusion(bf16[768,256]{1,0:T(8,128)(2,1)S(1)} %copy-done.26, bf16[768,256]{1,0:T(8,128)(2,1)S(1)} %copy-done.24, bf16[768,256]{1,0:T(8,128)(2,1)S(1)} %copy-done.25, bf16[768,256]{1,0:T(8,128)(2,1)S(1)} %copy-done.23, bf16[768,256]{1,0:T(8,128)(2,1)} %collective-permute-done.47, ...), kind=kLoop, calls=%fused_computation.25 | loop fusion | flops 25165824 | bytes 6291456 | tf_op jit(solution)/shard_map/concatenate | solution.py:38
  195.7 10.0 collective-permute-done.23
  209.8 29.9 %collective-permute-start.25 = (bf16[256,2048]{1,0:T(8,128)(2,1)S(1)}, bf16[256,2048]{1,0:T(8,128)(2,1)S(1)}, u32[]{:S(2)}, u32[]{:S(2)}) collective-permute-start(bf16[256,2048]{1,0:T(8,128)(2,1)S(1)} %pad_maximum_fusion.16), channel_id=1, source_target_pairs={{0,4},{4,0},{8,12},{12,8},{1,5},{5,1},{9,13},{13,9},{2,6},{6,2},{1... | collective-permute-start | bytes 3145736 | tf_op jit(solution)/shard_map/ppermute | solution.py:34
  242.6 20.3 %collective-permute-done.25 = bf16[256,2048]{1,0:T(8,128)(2,1)S(1)} collective-permute-done((bf16[256,2048]{1,0:T(8,128)(2,1)S(1)}, bf16[256,2048]{1,0:T(8,128)(2,1)S(1)}, u32[]{:S(2)}, u32[]{:S(2)}) %collective-permute-start.25) | collective-permute-done | bytes 1048608 | tf_op jit(solution)/shard_map/ppermute | solution.py:34
  265.6 17.0 %collective-permute-start.44 = (bf16[512,768]{1,0:T(8,128)(2,1)}, bf16[512,768]{1,0:T(8,128)(2,1)}, u32[]{:S(2)}, u32[]{:S(2)}) collective-permute-start(bf16[512,768]{1,0:T(8,128)(2,1)} %pad_maximum_fusion.30), channel_id=1, source_target_pairs={{0,8},{4,12},{8,0},{12,4},{1,9},{5,13},{9,1},{13,5},{2,10},{6,14},... | collective-permute-start | bytes 2359304 | tf_op jit(solution)/shard_map/ppermute | solution.py:34
  285.0 18.4 %attend.1 = (bf16[1024,512]{1,0:T(8,128)(2,1)}, f32[1024,512]{1,0:T(8,128)}, f32[1024,512]{1,0:T(8,128)}) custom-call(s32[4,5]{1,0:T(4,128)} %stack.15.table_ref, bf16[1024,512]{1,0:T(8,128)(2,1)} %get-tuple-element.37.q_ref, bf16[4096,512]{1,0:T(8,128)(2,1)} %pad_maximum_fusion.3.kv_ref, s32[1024,1]{1,0:T(8,128)} %copy.55.row_ref, ...), custom_call_target="tpu_custom_call" | custom-call | flops 20000000000 | bytes 12000000 | tf_op jit(solution)/shard_map/attend/pallas_call | solution.py:229
  309.9 14.8 %pad_maximum_fusion.2 = bf16[1536,2048]{1,0:T(8,128)(2,1)S(1)} fusion(bf16[1536,1024]{1,0:T(8,128)(2,1)} %collective-permute-done.49, bf16[768,256]{1,0:T(8,128)(2,1)S(1)} %copy-done.26, bf16[768,256]{1,0:T(8,128)(2,1)S(1)} %copy-done.24, bf16[768,256]{1,0:T(8,128)(2,1)S(1)} %copy-done.25, bf16[768,256]{1,0:T(8,128)(2,1)S(1)} %copy-done.23, ...), kind=kLoop, calls=%fused_computation.5 | loop fusion | flops 56623104 | bytes 12582912 | tf_op jit(solution)/shard_map/concatenate | solution.py:38
  324.7 15.2 %collective-permute-done.31 = bf16[256,2048]{1,0:T(8,128)(2,1)S(1)} collective-permute-done((bf16[256,2048]{1,0:T(8,128)(2,1)S(1)}, bf16[256,2048]{1,0:T(8,128)(2,1)S(1)}, u32[]{:S(2)}, u32[]{:S(2)}) %collective-permute-start.31) | collective-permute-done | bytes 1048608 | tf_op jit(solution)/shard_map/ppermute | solution.py:34
  355.8 13.7 %collective-permute-done.40 = bf16[512,768]{1,0:T(8,128)(2,1)S(1)} collective-permute-done((bf16[512,768]{1,0:T(8,128)(2,1)S(1)}, bf16[512,768]{1,0:T(8,128)(2,1)S(1)}, u32[]{:S(2)}, u32[]{:S(2)}) %collective-permute-start.40) | collective-permute-done | bytes 786464 | tf_op jit(solution)/shard_map/ppermute | solution.py:34
  369.6 15.9 %collective-permute-done.45 = bf16[512,768]{1,0:T(8,128)(2,1)S(1)} collective-permute-done((bf16[512,768]{1,0:T(8,128)(2,1)}, bf16[512,768]{1,0:T(8,128)(2,1)S(1)}, u32[]{:S(2)}, u32[]{:S(2)}) %collective-permute-start.45) | collective-permute-done | bytes 786464 | tf_op jit(solution)/shard_map/ppermute | solution.py:34
  388.7 18.3 %maximum_maximum_fusion.1 = bf16[1024,1536]{1,0:T(8,128)(2,1)S(1)} fusion(bf16[256,768]{1,0:T(8,128)(2,1)S(1)} %get-tuple-element.307, bf16[256,768]{1,0:T(8,128)(2,1)S(1)} %get-tuple-element.305, bf16[256,768]{1,0:T(8,128)(2,1)S(1)} %get-tuple-element.306, bf16[256,768]{1,0:T(8,128)(2,1)S(1)} %get-tuple-element.304, ...), kind=kLoop, calls=%fused_computation.24 | loop fusion | flops 25165824 | bytes 6291456 | tf_op jit(solution)/shard_map/concatenate | solution.py:38
  409.9 15.7 %maximum_maximum_fusion = bf16[1024,1536]{1,0:T(8,128)(2,1)S(1)} fusion(bf16[256,768]{1,0:T(8,128)(2,1)S(1)} %get-tuple-element.303, bf16[256,768]{1,0:T(8,128)(2,1)S(1)} %copy-done.40, bf16[256,768]{1,0:T(8,128)(2,1)S(1)} %get-tuple-element.302, bf16[256,768]{1,0:T(8,128)(2,1)S(1)} %copy-done.38, bf16[256,768]{1,0:T(8,128)(2,1)} %collective-permute-done.39, ...), kind=kLoop, calls=%fused_computation.23 | loop fusion | flops 25165824 | bytes 6291456 | tf_op jit(solution)/shard_map/concatenate | solution.py:38
  447.6 19.7 %multiply_convert_fusion.1 = (bf16[1024,1536]{1,0:T(8,128)(2,1)}, bf16[1024,1536]{1,0:T(8,128)(2,1)S(1)}, bf16[1024,1536]{1,0:T(8,128)(2,1)}) fusion(f32[1024,1536]{1,0:T(8,128)} %fusion.163, f32[1024,1536]{1,0:T(8,128)} %fusion.162, bf16[1024,2048]{1,0:T(8,128)(2,1)} %copy-done.84, bf16[1024,1536]{1,0:T(8,128)(2,1)} %collective-permute-done.41, ...), kind=kOutput, calls=%fused_computation.10 | convolution fusion | flops 6522667008 | bytes 32505856 | tf_op jit(solution)/shard_map/dot_general | solution.py:22
  476.3 19.1 %add_convert_fusion = bf16[1024,2048]{1,0:T(8,128)(2,1)} fusion(f32[1024,2048]{1,0:T(8,128)} %fusion.164, bf16[1024,1536]{1,0:T(8,128)(2,1)} %get-tuple-element.132, bf16[1024,1536]{1,0:T(8,128)(2,1)} %collective-permute-done.41, bf16[256,768]{1,0:T(8,128)(2,1)} %copy-done.44, bf16[256,768]{1,0:T(8,128)(2,1)S(1)} %copy-done.42, ...), kind=kOutput, calls=%fused_computation.2 | convolution fusion | flops 6503268352 | bytes 22020096 | tf_op jit(solution)/shard_map/dot_general | solution.py:26
  506.0 16.0 %collective-permute-done.50 = bf16[256,2048]{1,0:T(8,128)(2,1)S(1)} collective-permute-done((bf16[256,2048]{1,0:T(8,128)(2,1)S(1)}, bf16[256,2048]{1,0:T(8,128)(2,1)S(1)}, u32[]{:S(2)}, u32[]{:S(2)}) %collective-permute-start.50) | collective-permute-done | bytes 1048608 | tf_op jit(solution)/shard_map/ppermute | solution.py:34
  554.2 9.5 collective-permute-done.55
  616.7 26.2 %attend_back.1 = (f32[1024,512]{1,0:T(8,128)}, bf16[4096,512]{1,0:T(8,128)(2,1)}, f32[1024,128]{1,0:T(8,128)}) custom-call(s32[4,5]{1,0:T(4,128)} %stack.15.table_ref, bf16[1024,512]{1,0:T(8,128)(2,1)} %get-tuple-element.37.q_ref, bf16[4096,512]{1,0:T(8,128)(2,1)} %pad_maximum_fusion.3.kv_ref, s32[4,1,256]{2,1,0:T(1,128)} %get-tuple-element.446.row_ref, ...), custom_call_target="tpu_custom_call" | custom-call | flops 49999998976 | bytes 20000000 | tf_op jit(solution)/shard_map/attend_back/pallas_call | solution.py:324
  657.3 17.7 %collective-permute-done.105 = bf16[1536,512]{0,1:T(8,128)(2,1)} collective-permute-done((bf16[1536,512]{0,1:T(8,128)(2,1)}, bf16[1536,512]{0,1:T(8,128)(2,1)}, u32[]{:S(2)}, u32[]{:S(2)}) %collective-permute-start.105) | collective-permute-done | bytes 1572896 | tf_op jit(solution)/shard_map/ppermute | solution.py:34
  675.0 14.2 %collective-permute-start.96 = (bf16[512,768]{1,0:T(8,128)(2,1)S(1)}, bf16[512,768]{1,0:T(8,128)(2,1)S(1)}, u32[]{:S(2)}, u32[]{:S(2)}) collective-permute-start(bf16[512,768]{1,0:T(8,128)(2,1)S(1)} %slice.1996), channel_id=1, source_target_pairs={{0,8},{4,12},{8,0},{12,4},{1,9},{5,13},{9,1},{13,5},{2,10},{6,14},... | collective-permute-start | bytes 2359304 | tf_op jit(solution)/shard_map/ppermute | solution.py:34
  704.0 97.9 %collective-permute-done.91 = bf16[256,512]{1,0:T(8,128)(2,1)S(1)} collective-permute-done((bf16[256,512]{1,0:T(8,128)(2,1)S(1)}, bf16[256,512]{1,0:T(8,128)(2,1)S(1)}, u32[]{:S(2)}, u32[]{:S(2)}) %collective-permute-start.91) | collective-permute-done | bytes 262176 | tf_op jit(solution)/shard_map/ppermute | solution.py:34
  843.1 11.1 %collective-permute-done.98 = bf16[256,1536]{1,0:T(8,128)(2,1)S(1)} collective-permute-done((bf16[256,1536]{1,0:T(8,128)(2,1)S(1)}, bf16[256,1536]{1,0:T(8,128)(2,1)S(1)}, u32[]{:S(2)}, u32[]{:S(2)}) %collective-permute-start.98) | collective-permute-done | bytes 786464 | tf_op jit(solution)/shard_map/ppermute | solution.py:34
  854.2 16.8 %collective-permute-done.103 = bf16[256,1536]{1,0:T(8,128)(2,1)S(1)} collective-permute-done((bf16[256,1536]{1,0:T(8,128)(2,1)S(1)}, bf16[256,1536]{1,0:T(8,128)(2,1)S(1)}, u32[]{:S(2)}, u32[]{:S(2)}) %collective-permute-start.103) | collective-permute-done | bytes 786464 | tf_op jit(solution)/shard_map/ppermute | solution.py:34
  871.6 13.2 %collective-permute-done.108 = bf16[1536,256]{0,1:T(8,128)(2,1)S(1)} collective-permute-done((bf16[1536,256]{0,1:T(8,128)(2,1)S(1)}, bf16[1536,256]{0,1:T(8,128)(2,1)S(1)}, u32[]{:S(2)}, u32[]{:S(2)}) %collective-permute-start.108) | collective-permute-done | bytes 786464 | tf_op jit(solution)/shard_map/ppermute | solution.py:34
  922.6 18.7 %collective-permute-done.86 = f32[2,512]{1,0:T(2,128)S(1)} collective-permute-done((f32[2,512]{1,0:T(2,128)S(1)}, f32[2,512]{1,0:T(2,128)S(1)}, u32[]{:S(2)}, u32[]{:S(2)}) %collective-permute-start.86) | collective-permute-done | bytes 4128 | tf_op jit(solution)/shard_map/ppermute | solution.py:34
  950.1 18.9 %collective-permute-done.69 = bf16[256,2048]{1,0:T(8,128)(2,1)} collective-permute-done((bf16[256,2048]{1,0:T(8,128)(2,1)}, bf16[256,2048]{1,0:T(8,128)(2,1)}, u32[]{:S(2)}, u32[]{:S(2)}) %collective-permute-start.69) | collective-permute-done | bytes 1048608 | tf_op jit(solution)/shard_map/ppermute | solution.py:34
  969.0 9.1 collective-permute-done.68
  1015.7 19.5 %collective-permute-done.77 = f32[4352]{0:T(1024)S(1)} collective-permute-done((f32[4352]{0:T(1024)S(1)}, f32[4352]{0:T(1024)S(1)}, u32[]{:S(2)}, u32[]{:S(2)}) %collective-permute-start.77) | collective-permute-done | bytes 17440 | tf_op jit(solution)/shard_map/ppermute | solution.py:34
  (774 shorter events, 454.7 us)
Async XLA Ops:
  51.4 39.8 %collective-permute-start.8 = (bf16[256,512]{1,0:T(8,128)(2,1)S(1)}, bf16[256,512]{1,0:T(8,128)(2,1)S(1)}, u32[]{:S(2)}, u32[]{:S(2)}) collective-permute-start(bf16[256,512]{1,0:T(8,128)(2,1)S(1)} %collective-permute-done.7), channel_id=1, source_target_pairs={{0,16},{16,0},{1,17},{17,1},{2,18},{18,2},{3,19},{19,3},{4,20},{20... | collective-permute-start | bytes 786440 | tf_op jit(solution)/shard_map/ppermute | solution.py:34
  84.9 38.1 %collective-permute-start.6 = (bf16[256,2048]{1,0:T(8,128)(2,1)S(1)}, bf16[256,2048]{1,0:T(8,128)(2,1)S(1)}, u32[]{:S(2)}, u32[]{:S(2)}) collective-permute-start(bf16[256,2048]{1,0:T(8,128)(2,1)S(1)} %pad_maximum_fusion.13), channel_id=1, source_target_pairs={{0,4},{4,0},{8,12},{12,8},{1,5},{5,1},{9,13},{13,9},{2,6},{6,2},{1... | collective-permute-start | bytes 3145736 | tf_op jit(solution)/shard_map/ppermute | solution.py:34
  88.6 89.4 %collective-permute-start.47 = (bf16[768,256]{1,0:T(8,128)(2,1)S(1)}, bf16[768,256]{1,0:T(8,128)(2,1)}, u32[]{:S(2)}, u32[]{:S(2)}) collective-permute-start(bf16[768,256]{1,0:T(8,128)(2,1)S(1)} %collective-permute-done.14), channel_id=1, source_target_pairs={{0,16},{16,0},{1,17},{17,1},{2,18},{18,2},{3,19},{19,3},{4,20},{20... | collective-permute-start | bytes 1179656 | tf_op jit(solution)/shard_map/ppermute | solution.py:34
  91.2 148.7 %collective-permute-start.42 = (bf16[256,768]{1,0:T(8,128)(2,1)}, bf16[256,768]{1,0:T(8,128)(2,1)}, u32[]{:S(2)}, u32[]{:S(2)}) collective-permute-start(bf16[256,768]{1,0:T(8,128)(2,1)} %get-tuple-element.192), channel_id=1, source_target_pairs={{0,2},{1,3},{2,0},{3,1},{4,6},{5,7},{6,4},{7,5},{8,10},{9,11},{10,... | collective-permute-start | bytes 1179656 | tf_op jit(solution)/shard_map/ppermute | solution.py:34
  166.0 243.8 %collective-permute-start.39 = (bf16[256,768]{1,0:T(8,128)(2,1)}, bf16[256,768]{1,0:T(8,128)(2,1)}, u32[]{:S(2)}, u32[]{:S(2)}) collective-permute-start(bf16[256,768]{1,0:T(8,128)(2,1)} %collective-permute-done.26), channel_id=1, source_target_pairs={{0,16},{16,0},{1,17},{17,1},{2,18},{18,2},{3,19},{19,3},{4,20},{20... | collective-permute-start | bytes 1179656 | tf_op jit(solution)/shard_map/ppermute | solution.py:34
  166.7 39.2 %collective-permute-start.16 = (bf16[1024,512]{1,0:T(8,128)(2,1)S(1)}, bf16[1024,512]{1,0:T(8,128)(2,1)S(1)}, u32[]{:S(2)}, u32[]{:S(2)}) collective-permute-start(bf16[1024,512]{1,0:T(8,128)(2,1)S(1)} %pad_maximum_fusion.14), channel_id=1, source_target_pairs={{0,8},{4,12},{1,9},{5,13},{2,10},{6,14},{3,11},{7,15},{16,24},{20,... | collective-permute-start | bytes 3145736 | tf_op jit(solution)/shard_map/ppermute | solution.py:574
  205.9 36.6 %collective-permute-start.24 = (bf16[256,2048]{1,0:T(8,128)(2,1)S(1)}, bf16[256,2048]{1,0:T(8,128)(2,1)S(1)}, u32[]{:S(2)}, u32[]{:S(2)}) collective-permute-start(bf16[256,2048]{1,0:T(8,128)(2,1)S(1)} %maximum_maximum_fusion.5), channel_id=1, source_target_pairs={{0,2},{1,3},{2,0},{3,1},{4,6},{5,7},{6,4},{7,5},{8,10},{9,11},{10,... | collective-permute-start | bytes 3145736 | tf_op jit(solution)/shard_map/ppermute | solution.py:34
  209.8 53.1 %collective-permute-start.25 = (bf16[256,2048]{1,0:T(8,128)(2,1)S(1)}, bf16[256,2048]{1,0:T(8,128)(2,1)S(1)}, u32[]{:S(2)}, u32[]{:S(2)}) collective-permute-start(bf16[256,2048]{1,0:T(8,128)(2,1)S(1)} %pad_maximum_fusion.16), channel_id=1, source_target_pairs={{0,4},{4,0},{8,12},{12,8},{1,5},{5,1},{9,13},{13,9},{2,6},{6,2},{1... | collective-permute-start | bytes 3145736 | tf_op jit(solution)/shard_map/ppermute | solution.py:34
  239.9 63.5 %collective-permute-start.30 = (bf16[512,1024]{1,0:T(8,128)(2,1)}, bf16[512,1024]{1,0:T(8,128)(2,1)}, u32[]{:S(2)}, u32[]{:S(2)}) collective-permute-start(bf16[512,1024]{1,0:T(8,128)(2,1)} %maximum_maximum_fusion.6), channel_id=1, source_target_pairs={{0,1},{1,0},{2,3},{3,2},{4,5},{5,4},{6,7},{7,6},{8,9},{9,8},{10,11... | collective-permute-start | bytes 3145736 | tf_op jit(solution)/shard_map/ppermute | solution.py:34
  240.0 148.7 %collective-permute-start.43 = (bf16[256,768]{1,0:T(8,128)(2,1)}, bf16[256,768]{1,0:T(8,128)(2,1)S(1)}, u32[]{:S(2)}, u32[]{:S(2)}) collective-permute-start(bf16[256,768]{1,0:T(8,128)(2,1)} %collective-permute-done.42), channel_id=1, source_target_pairs={{0,16},{16,0},{1,17},{17,1},{2,18},{18,2},{3,19},{19,3},{4,20},{20... | collective-permute-start | bytes 1179656 | tf_op jit(solution)/shard_map/ppermute | solution.py:34
  265.0 44.7 %collective-permute-start.49 = (bf16[1536,1024]{1,0:T(8,128)(2,1)}, bf16[1536,1024]{1,0:T(8,128)(2,1)}, u32[]{:S(2)}, u32[]{:S(2)}) collective-permute-start(bf16[1536,1024]{1,0:T(8,128)(2,1)} %maximum_maximum_fusion.2), channel_id=1, source_target_pairs={{0,1},{1,0},{2,3},{3,2},{4,5},{5,4},{6,7},{7,6},{8,9},{9,8},{10,11... | collective-permute-start | bytes 9437192 | tf_op jit(solution)/shard_map/ppermute | solution.py:34
  265.6 83.4 %collective-permute-start.44 = (bf16[512,768]{1,0:T(8,128)(2,1)}, bf16[512,768]{1,0:T(8,128)(2,1)}, u32[]{:S(2)}, u32[]{:S(2)}) collective-permute-start(bf16[512,768]{1,0:T(8,128)(2,1)} %pad_maximum_fusion.30), channel_id=1, source_target_pairs={{0,8},{4,12},{8,0},{12,4},{1,9},{5,13},{9,1},{13,5},{2,10},{6,14},... | collective-permute-start | bytes 2359304 | tf_op jit(solution)/shard_map/ppermute | solution.py:34
  309.8 40.7 %collective-permute-start.33 = (bf16[256,2048]{1,0:T(8,128)(2,1)S(1)}, bf16[256,2048]{1,0:T(8,128)(2,1)S(1)}, u32[]{:S(2)}, u32[]{:S(2)}) collective-permute-start(bf16[256,2048]{1,0:T(8,128)(2,1)S(1)} %fusion.55), channel_id=1, source_target_pairs={{0,2},{1,3},{2,0},{3,1},{4,6},{5,7},{6,4},{7,5},{8,10},{9,11},{10,... | collective-permute-start | bytes 3145736 | tf_op jit(solution)/shard_map/ppermute | solution.py:34
  506.0 59.7 %collective-permute-start.94 = (bf16[1024,1536]{1,0:T(8,128)(2,1)}, bf16[1024,1536]{1,0:T(8,128)(2,1)S(1)}, u32[]{:S(2)}, u32[]{:S(2)}) collective-permute-start(bf16[1024,1536]{1,0:T(8,128)(2,1)} %convolution_convert_fusion.5), channel_id=1, source_target_pairs={{0,1},{1,0},{2,3},{3,2},{4,5},{5,4},{6,7},{7,6},{8,9},{9,8},{10,11... | collective-permute-start | bytes 9437192 | tf_op jit(solution)/shard_map/ppermute | solution.py:34
  528.9 43.1 %collective-permute-start.99 = (bf16[1024,1536]{1,0:T(8,128)(2,1)}, bf16[1024,1536]{1,0:T(8,128)(2,1)}, u32[]{:S(2)}, u32[]{:S(2)}) collective-permute-start(bf16[1024,1536]{1,0:T(8,128)(2,1)} %convolution_convert_fusion.4), channel_id=1, source_target_pairs={{0,1},{1,0},{2,3},{3,2},{4,5},{5,4},{6,7},{7,6},{8,9},{9,8},{10,11... | collective-permute-start | bytes 9437192 | tf_op jit(solution)/shard_map/ppermute | solution.py:34
  541.9 40.5 %collective-permute-start.104 = (bf16[1536,1024]{0,1:T(8,128)(2,1)}, bf16[1536,1024]{0,1:T(8,128)(2,1)}, u32[]{:S(2)}, u32[]{:S(2)}) collective-permute-start(bf16[1536,1024]{0,1:T(8,128)(2,1)} %convolution_convert_fusion.3), channel_id=1, source_target_pairs={{0,1},{1,0},{2,3},{3,2},{4,5},{5,4},{6,7},{7,6},{8,9},{9,8},{10,11... | collective-permute-start | bytes 9437192 | tf_op jit(solution)/shard_map/ppermute | solution.py:34
  570.7 77.4 %collective-permute-start.95 = (bf16[512,1536]{1,0:T(8,128)(2,1)}, bf16[512,1536]{1,0:T(8,128)(2,1)}, u32[]{:S(2)}, u32[]{:S(2)}) collective-permute-start(bf16[512,1536]{1,0:T(8,128)(2,1)} %pad_maximum_fusion.8), channel_id=1, source_target_pairs={{0,16},{16,0},{1,17},{17,1},{2,18},{18,2},{3,19},{19,3},{4,20},{20... | collective-permute-start | bytes 4718600 | tf_op jit(solution)/shard_map/ppermute | solution.py:34
  579.8 74.3 %collective-permute-start.100 = (bf16[512,1536]{1,0:T(8,128)(2,1)}, bf16[512,1536]{1,0:T(8,128)(2,1)}, u32[]{:S(2)}, u32[]{:S(2)}) collective-permute-start(bf16[512,1536]{1,0:T(8,128)(2,1)} %pad_maximum_fusion.9), channel_id=1, source_target_pairs={{0,16},{16,0},{1,17},{17,1},{2,18},{18,2},{3,19},{19,3},{4,20},{20... | collective-permute-start | bytes 4718600 | tf_op jit(solution)/shard_map/ppermute | solution.py:34
  591.8 83.2 %collective-permute-start.105 = (bf16[1536,512]{0,1:T(8,128)(2,1)}, bf16[1536,512]{0,1:T(8,128)(2,1)}, u32[]{:S(2)}, u32[]{:S(2)}) collective-permute-start(bf16[1536,512]{0,1:T(8,128)(2,1)} %pad_maximum_fusion.10), channel_id=1, source_target_pairs={{0,16},{16,0},{1,17},{17,1},{2,18},{18,2},{3,19},{19,3},{4,20},{20... | collective-permute-start | bytes 4718600 | tf_op jit(solution)/shard_map/ppermute | solution.py:34
  607.7 43.2 %collective-permute-start.58 = (bf16[256,2048]{1,0:T(8,128)(2,1)}, bf16[256,2048]{1,0:T(8,128)(2,1)}, u32[]{:S(2)}, u32[]{:S(2)}) collective-permute-start(bf16[256,2048]{1,0:T(8,128)(2,1)} %pad_maximum_fusion.24), channel_id=1, source_target_pairs={{0,4},{4,0},{8,12},{12,8},{1,5},{5,1},{9,13},{13,9},{2,6},{6,2},{1... | collective-permute-start | bytes 3145736 | tf_op jit(solution)/shard_map/ppermute | solution.py:34
  609.7 89.7 %collective-permute-start.60 = (bf16[256,2048]{1,0:T(8,128)(2,1)}, bf16[256,2048]{1,0:T(8,128)(2,1)}, u32[]{:S(2)}, u32[]{:S(2)}) collective-permute-start(bf16[256,2048]{1,0:T(8,128)(2,1)} %fusion.59), channel_id=1, source_target_pairs={{0,2},{1,3},{2,0},{3,1},{4,6},{5,7},{6,4},{7,5},{8,10},{9,11},{10,... | collective-permute-start | bytes 3145736 | tf_op jit(solution)/shard_map/ppermute | solution.py:34
  650.9 159.4 %collective-permute-start.65 = (bf16[2048,512]{1,0:T(8,128)(2,1)S(1)}, bf16[2048,512]{1,0:T(8,128)(2,1)S(1)}, u32[]{:S(2)}, u32[]{:S(2)}) collective-permute-start(bf16[2048,512]{1,0:T(8,128)(2,1)S(1)} %pad_maximum_fusion.6), channel_id=1, source_target_pairs={{0,1},{1,0},{2,3},{3,2},{4,5},{5,4},{6,7},{7,6},{8,9},{9,8},{10,11... | collective-permute-start | bytes 6291464 | tf_op jit(solution)/shard_map/ppermute | solution.py:34
  652.7 46.8 %collective-permute-start.59 = (bf16[128,2048]{1,0:T(8,128)(2,1)S(1)}, bf16[128,2048]{1,0:T(8,128)(2,1)S(1)}, u32[]{:S(2)}, u32[]{:S(2)}) collective-permute-start(bf16[128,2048]{1,0:T(8,128)(2,1)S(1)} %pad_maximum_fusion.46), channel_id=1, source_target_pairs={{0,2},{1,3},{2,0},{3,1},{4,6},{5,7},{6,4},{7,5},{8,10},{9,11},{10,... | collective-permute-start | bytes 1572872 | tf_op jit(solution)/shard_map/ppermute | solution.py:34
  654.2 37.3 %collective-permute-start.90 = (bf16[512,512]{1,0:T(8,128)(2,1)S(1)}, bf16[512,512]{1,0:T(8,128)(2,1)S(1)}, u32[]{:S(2)}, u32[]{:S(2)}) collective-permute-start(bf16[512,512]{1,0:T(8,128)(2,1)S(1)} %pad_maximum_fusion.49), channel_id=1, source_target_pairs={{0,16},{16,0},{1,17},{17,1},{2,18},{18,2},{3,19},{19,3},{4,20},{20... | collective-permute-start | bytes 1572872 | tf_op jit(solution)/shard_map/ppermute | solution.py:34
  675.0 127.1 %collective-permute-start.96 = (bf16[512,768]{1,0:T(8,128)(2,1)S(1)}, bf16[512,768]{1,0:T(8,128)(2,1)S(1)}, u32[]{:S(2)}, u32[]{:S(2)}) collective-permute-start(bf16[512,768]{1,0:T(8,128)(2,1)S(1)} %slice.1996), channel_id=1, source_target_pairs={{0,8},{4,12},{8,0},{12,4},{1,9},{5,13},{9,1},{13,5},{2,10},{6,14},... | collective-permute-start | bytes 2359304 | tf_op jit(solution)/shard_map/ppermute | solution.py:34
  691.4 112.7 %collective-permute-start.101 = (bf16[512,768]{1,0:T(8,128)(2,1)S(1)}, bf16[512,768]{1,0:T(8,128)(2,1)S(1)}, u32[]{:S(2)}, u32[]{:S(2)}) collective-permute-start(bf16[512,768]{1,0:T(8,128)(2,1)S(1)} %slice.1995), channel_id=1, source_target_pairs={{0,8},{4,12},{8,0},{12,4},{1,9},{5,13},{9,1},{13,5},{2,10},{6,14},... | collective-permute-start | bytes 2359304 | tf_op jit(solution)/shard_map/ppermute | solution.py:34
  699.4 105.4 %collective-permute-start.106 = (bf16[768,512]{0,1:T(8,128)(2,1)S(1)}, bf16[768,512]{0,1:T(8,128)(2,1)S(1)}, u32[]{:S(2)}, u32[]{:S(2)}) collective-permute-start(bf16[768,512]{0,1:T(8,128)(2,1)S(1)} %slice.1994), channel_id=1, source_target_pairs={{0,8},{4,12},{8,0},{12,4},{1,9},{5,13},{9,1},{13,5},{2,10},{6,14},... | collective-permute-start | bytes 2359304 | tf_op jit(solution)/shard_map/ppermute | solution.py:34
  699.5 102.5 %collective-permute-start.91 = (bf16[256,512]{1,0:T(8,128)(2,1)S(1)}, bf16[256,512]{1,0:T(8,128)(2,1)S(1)}, u32[]{:S(2)}, u32[]{:S(2)}) collective-permute-start(bf16[256,512]{1,0:T(8,128)(2,1)S(1)} %slice.1998), channel_id=1, source_target_pairs={{0,8},{4,12},{8,0},{12,4},{1,9},{5,13},{9,1},{13,5},{2,10},{6,14},... | collective-permute-start | bytes 786440 | tf_op jit(solution)/shard_map/ppermute | solution.py:34
  839.3 51.1 %collective-permute-start.66 = (bf16[1024,512]{1,0:T(8,128)(2,1)S(1)}, bf16[1024,512]{1,0:T(8,128)(2,1)S(1)}, u32[]{:S(2)}, u32[]{:S(2)}) collective-permute-start(bf16[1024,512]{1,0:T(8,128)(2,1)S(1)} %pad_maximum_fusion.25), channel_id=1, source_target_pairs={{8,0},{12,4},{9,1},{13,5},{10,2},{14,6},{11,3},{15,7},{24,16},{28,... | collective-permute-start | bytes 3145736 | tf_op jit(solution)/shard_map/ppermute | solution.py:635
  840.7 44.2 %collective-permute-start.108 = (bf16[1536,256]{0,1:T(8,128)(2,1)S(1)}, bf16[1536,256]{0,1:T(8,128)(2,1)S(1)}, u32[]{:S(2)}, u32[]{:S(2)}) collective-permute-start(bf16[1536,256]{0,1:T(8,128)(2,1)S(1)} %pad_maximum_fusion.38), channel_id=1, source_target_pairs={{0,16},{16,0},{1,17},{17,1},{2,18},{18,2},{3,19},{19,3},{4,20},{20... | collective-permute-start | bytes 2359304 | tf_op jit(solution)/shard_map/ppermute | solution.py:34
  944.4 39.7 %collective-permute-start.79 = (bf16[1024,1024]{1,0:T(8,128)(2,1)}, bf16[1024,1024]{1,0:T(8,128)(2,1)}, u32[]{:S(2)}, u32[]{:S(2)}) collective-permute-start(bf16[1024,1024]{1,0:T(8,128)(2,1)} %fusion.37), channel_id=1, source_target_pairs={{0,1},{1,0},{2,3},{3,2},{4,5},{5,4},{6,7},{7,6},{8,9},{9,8},{10,11... | collective-permute-start | bytes 6291464 | tf_op jit(solution)/shard_map/ppermute | solution.py:34
  998.9 42.4 %collective-permute-start.71 = (bf16[256,512]{1,0:T(8,128)(2,1)S(1)}, bf16[256,512]{1,0:T(8,128)(2,1)S(1)}, u32[]{:S(2)}, u32[]{:S(2)}) collective-permute-start(bf16[256,512]{1,0:T(8,128)(2,1)S(1)} %pad_maximum_fusion.54), channel_id=1, source_target_pairs={{0,2},{1,3},{2,0},{3,1},{4,6},{5,7},{6,4},{7,5},{8,10},{9,11},{10,... | collective-permute-start | bytes 786440 | tf_op jit(solution)/shard_map/ppermute | solution.py:34
  (194 other events, 4303.7 us)

commit v3 on v2

--- a/solution.py
+++ b/solution.py
@@ -53,13 +53,13 @@
 
 def columns(heads, pairs, size):
     query, pair = heads // 2, pairs // 2
-    block = (query + 2 * pair) * size
+    block = (query + 2 * pair) * size + LANES
     of = lambda i, count, before: (i // count) * block + (before + i % count) * size
     return (
         [of(h, query, 0) for h in range(heads)],
         [of(p, pair, query) for p in range(pairs)],
         [of(p, pair, query + pair) for p in range(pairs)],
-        2 * block,
+        [block - LANES, 2 * block - LANES],
     )
 
 
@@ -138,7 +138,8 @@
     for p, at in enumerate(value_at):
         to = (pairs + p) * size
         out_ref[:, at : at + size] = dkv_ref[:, to : to + size].astype(BF16)
-    out_ref[:, logit_at:] = logit_ref[...].astype(BF16)
+    for i, at in enumerate(logit_at):
+        out_ref[:, at : at + LANES] = logit_ref[:, i * LANES : (i + 1) * LANES].astype(BF16)
 
 
 def project_back(dq, dkv, raw, cosine, sine, query_gain, key_gain, logit_grad, heads, pairs, size, factor_q, factor_k):
@@ -149,7 +150,7 @@
     return pl.pallas_call(
         functools.partial(back_kernel, heads=heads, pairs=pairs, size=size, factor_q=factor_q, factor_k=factor_k),
         grid=(rows // step,),
-        in_specs=[row(heads * size), row(2 * pairs * size), row(width), row(size), row(size), one, one, row(LANES)],
+        in_specs=[row(heads * size), row(2 * pairs * size), row(width), row(size), row(size), one, one, row(2 * LANES)],
         out_specs=[row(width), one, one],
         out_shape=[
             jax.ShapeDtypeStruct((rows, width), BF16),
@@ -180,7 +181,18 @@
     return pair, single
 
 
-def forward_kernel(table_ref, q_ref, kv_ref, row_ref, start_ref, logit_ref, gated_ref, context_ref, inverse_ref, *, pairs, repeat, size, step):
+def logit_of(head, heads, own_ref, other_ref):
+    half = heads // 2
+    at = head % half
+    return (own_ref if head < half else other_ref)[:, at : at + 1]
+
+
+def logit_specs(raw, heads, pairs, size, step):
+    spec = lambda i: pl.BlockSpec((step, LANES), lambda s, t: (s, i))
+    return [spec(at // LANES) for at in columns(heads, pairs, size)[3]]
+
+
+def forward_kernel(table_ref, q_ref, kv_ref, row_ref, start_ref, own_ref, other_ref, gated_ref, context_ref, inverse_ref, *, pairs, repeat, size, step):
     stripe = pl.program_id(0)
     wide_blocks = table_ref[stripe, 0]
     low = table_ref[stripe, 1]
@@ -214,7 +226,7 @@
         for r, h in enumerate(heads):
             part = context[r * step : (r + 1) * step]
             cols = slice(h * size, (h + 1) * size)
-            gate = jax.nn.sigmoid(logit_ref[:, h : h + 1])
+            gate = jax.nn.sigmoid(logit_of(h, pairs * repeat, own_ref, other_ref))
             gated_ref[:, cols] = (part * gate).astype(BF16)
             context_ref[:, cols] = part
             inverse_ref[:, cols] = inverse[r * step : (r + 1) * step]
@@ -225,7 +237,6 @@
     heads = cols // size
     step = length // table.shape[0]
     block = lambda width: pl.BlockSpec((step, width), lambda i, t: (i, 0))
-    logit_block = raw.shape[1] // LANES - 1
     return pl.pallas_call(
         functools.partial(forward_kernel, pairs=pairs, repeat=heads // pairs, size=size, step=step),
         grid_spec=pltpu.PrefetchScalarGridSpec(
@@ -236,7 +247,7 @@
                 pl.BlockSpec(kv.shape, lambda i, t: (0, 0), pipeline_mode=pl.Buffered(1)),
                 block(1),
                 block(1),
-                pl.BlockSpec((step, LANES), lambda i, t: (i, logit_block)),
+                *logit_specs(raw, heads, pairs, size, step),
             ],
             out_specs=[block(cols), block(cols), block(cols)],
         ),
@@ -248,11 +259,11 @@
         compiler_params=pltpu.CompilerParams(vmem_limit_bytes=VMEM_LIMIT),
         cost_estimate=pl.CostEstimate(flops=20 * 10**9, bytes_accessed=12 * 10**6, transcendentals=7 * 10**6),
         name="attend",
-    )(table, q, kv, rows, starts, raw)
+    )(table, q, kv, rows, starts, raw, raw)
 
 
 def backward_kernel(
-    table_ref, q_ref, kv_ref, row_ref, start_ref, logit_ref, context_ref, inverse_ref, grad_ref,
+    table_ref, q_ref, kv_ref, row_ref, start_ref, own_ref, other_ref, context_ref, inverse_ref, grad_ref,
     dq_ref, dkv_ref, dlogit_ref, sums_ref, *, pairs, repeat, size, step,
 ):
     stripe = pl.program_id(0)
@@ -275,9 +286,11 @@
         for h in heads:
             cols = slice(h * size, (h + 1) * size)
             up = grad_ref[:, cols]
-            gate = jax.nn.sigmoid(logit_ref[:, h : h + 1])
+            gate = jax.nn.sigmoid(logit_of(h, pairs * repeat, own_ref, other_ref))
             product = jnp.sum(up * context_ref[:, cols], axis=1, keepdims=True)
-            dlogit_ref[:, h : h + 1] = product * gate * (1.0 - gate)
+            half = pairs * repeat // 2
+            at = h // half * LANES + h % half
+            dlogit_ref[:, at : at + 1] = product * gate * (1.0 - gate)
             inverse = inverse_ref[:, cols]
             grads.append((up * gate * inverse).astype(BF16))
             inners.append(product * gate * inverse)
@@ -319,26 +332,377 @@
     block = lambda width: pl.BlockSpec((step, width), lambda i, t: (i, 0))
     whole = pl.BlockSpec(kv.shape, lambda i, t: (0, 0), pipeline_mode=pl.Buffered(1))
     lane = pl.BlockSpec((1, 1, step), lambda i, t: (i, 0, 0))
-    logit_block = raw.shape[1] // LANES - 1
-    logit = pl.BlockSpec((step, LANES), lambda i, t: (i, logit_block))
+    logits = logit_specs(raw, heads, pairs, size, step)
     return pl.pallas_call(
         functools.partial(backward_kernel, pairs=pairs, repeat=heads // pairs, size=size, step=step),
         grid_spec=pltpu.PrefetchScalarGridSpec(
             num_scalar_prefetch=1,
             grid=(length // step,),
-            in_specs=[block(cols), whole, lane, lane, logit, block(cols), block(cols), block(cols)],
-            out_specs=[block(cols), whole, block(LANES)],
+            in_specs=[block(cols), whole, lane, lane, *logits, block(cols), block(cols), block(cols)],
+            out_specs=[block(cols), whole, block(2 * LANES)],
             scratch_shapes=[pltpu.VMEM(kv.shape, F32)],
         ),
         out_shape=[
             jax.ShapeDtypeStruct((length, cols), F32),
             jax.ShapeDtypeStruct(kv.shape, BF16),
-            jax.ShapeDtypeStruct((length, LANES), F32),
+            jax.ShapeDtypeStruct((length, 2 * LANES), F32),
         ],
         compiler_params=pltpu.CompilerParams(vmem_limit_bytes=VMEM_LIMIT),
         cost_estimate=pl.CostEstimate(flops=50 * 10**9, bytes_accessed=20 * 10**6, transcendentals=7 * 10**6),
         name="attend_back",
-    )(table, q, kv, rows.reshape(-1, 1, step), starts.reshape(-1, 1, step), raw, context, inverse, grad)
+    )(table, q, kv, rows.reshape(-1, 1, step), starts.reshape(-1, 1, step), raw, raw, context, inverse, grad)
+
+
+class Wires:
+    def __init__(self, send_sems, recv_sems, local_sems, sizes):
+        self.send_sems, self.recv_sems, self.local_sems = send_sems, recv_sems, local_sems
+        self.sizes = sizes
+        self.sent, self.local, self.open = [], [], []
+        self.locals_used = 0
+        self.dp, self.wide, self.narrow = (lax.axis_index(a) for a in ("dp", "wide", "narrow"))
+        self.y, self.core = self.narrow // 2, self.narrow % 2
+        self.x, self.far = self.dp % 2, self.wide // 2
+
+    def peer(self, axis, distance):
+        at = {"dp": self.dp, "wide": self.wide, "narrow": self.narrow}[axis]
+        bit = at // distance % 2
+        return {axis: at + distance * (1 - 2 * bit) if distance < 3 else 3 - at}
+
+    def greet(self, peers):
+        barrier = pltpu.get_barrier_semaphore()
+        for to in peers:
+            pl.semaphore_signal(barrier, inc=1, device_id=self.peer(*to), device_id_type=pl.DeviceIdType.MESH)
+        pl.semaphore_wait(barrier, len(peers))
+
+    def make(self, source, target, to):
+        i = len(self.sent)
+        copy = pltpu.make_async_remote_copy(
+            src_ref=source, dst_ref=target, send_sem=self.send_sems.at[i], recv_sem=self.recv_sems.at[i],
+            device_id=self.peer(*to), device_id_type=pl.DeviceIdType.MESH,
+        )
+        self.sent.append(copy)
+        return copy
+
+    def send(self, source, target, to):
+        copy = self.make(source, target, to)
+        copy.start()
+        self.open.append(copy)
+        return copy
+
+    def arrived(self, copy):
+        copy.wait_recv()
+        self.open = [other for other in self.open if other is not copy]
+
+    def copy(self, source, target):
+        copy = pltpu.make_async_copy(source, target, self.local_sems.at[self.locals_used])
+        self.locals_used += 1
+        copy.start()
+        self.local.append(copy)
+        return copy
+
+    def finish(self):
+        for copy in list(self.open):
+            self.arrived(copy)
+        for copy in self.sent:
+            copy.wait_send()
+        for copy in self.local:
+            copy.wait()
+
+
+Y, CORE, CORNER, NEAR, FAR, X = ("narrow", 2), ("narrow", 1), ("narrow", 3), ("wide", 1), ("wide", 2), ("dp", 1)
+
+
+def local_flow(net, values_ref, rows_ref):
+    rows, width = rows_ref.shape[0], values_ref.shape[1]
+    half = width // 2
+    out = []
+    for distance, to in ((0, None), (1, CORE), (2, Y), (3, CORNER)):
+        target = net.narrow if to is None else net.peer(*to)["narrow"]
+        at = (2 * (distance % 2) + net.y) * width
+        for j in range(2):
+            sub = net.x if j == 0 else 1 - net.x
+            source = values_ref.at[pl.ds(pl.multiple_of(target * rows, rows), rows), pl.ds(pl.multiple_of(sub * half, half), half)]
+            goal = rows_ref.at[:, pl.ds(pl.multiple_of(at + j * half, half), half)]
+            out.append(net.copy(source, goal) if to is None else net.send(source, goal, to))
+    return out
+
+
+def gather_flow(net, values_ref, all_ref):
+    rows = values_ref.shape[0]
+    half = rows // 2
+    part = lambda i: all_ref.at[pl.ds(i * half, half), :]
+    first, second = values_ref.at[pl.ds(0, half), :], values_ref.at[pl.ds(half, half), :]
+    first_y = net.send(first, part(2), Y)
+    second_z = net.send(second, part(5), NEAR)
+    net.send(first, part(4), NEAR)
+    net.send(second, part(3), Y)
+    net.copy(values_ref, all_ref.at[pl.ds(0, rows), :])
+    yield
+    net.arrived(first_y)
+    net.send(part(2), part(6), NEAR)
+    yield
+    net.arrived(second_z)
+    net.send(part(5), part(7), Y)
+    yield
+
+
+def weight_flow(net, source_ref, out_ref, axis, own, other, across, from_y=None, from_far=None):
+    step = source_ref.shape[axis] // 2
+    count = source_ref.shape[axis]
+
+    def window(ref, at, start):
+        long, wide = pl.ds(pl.multiple_of(at, step), step), pl.ds(start, across)
+        return ref.at[long, wide] if axis == 0 else ref.at[wide, long]
+
+    y, x = net.y, net.x
+    piece = lambda sub, half: window(source_ref, sub * step, pl.multiple_of(half * across, across))
+    place = lambda slot, j, start: window(out_ref, slot * count + j * step, start)
+    mine, rest = piece(x, y), piece(1 - x, y)
+    net.copy(mine, place(y, 0, own))
+    net.copy(rest, place(y, 1, own))
+    if from_y is None:
+        come_y = net.send(piece(x, 1 - y), place(y, 0, own), Y)
+    else:
+        net.copy(from_y, place(1 - y, 0, own))
+    if from_far is None:
+        come_far = net.send(mine, place(y, 0, other), FAR)
+    else:
+        net.copy(from_far, place(y, 0, other))
+    net.send(mine, place(2 + y, 0, own), CORE)
+    net.send(rest, place(2 + y, 1, own), CORE)
+    if from_y is None:
+        yield
+        net.arrived(come_y)
+        from_y = place(1 - y, 0, own)
+    come_both = net.send(from_y, place(1 - y, 0, other), FAR)
+    their_y = net.send(from_y, place(1 - y, 1, own), X)
+    net.send(from_y, place(3 - y, 0, own), CORE)
+    if from_far is None:
+        yield
+        net.arrived(come_far)
+        from_far = place(y, 0, other)
+    their_far = net.send(from_far, place(y, 1, other), X)
+    net.send(from_far, place(2 + y, 0, other), CORE)
+    yield
+    net.arrived(come_both)
+    both = place(1 - y, 0, other)
+    their_both = net.send(both, place(1 - y, 1, other), X)
+    net.send(both, place(3 - y, 0, other), CORE)
+    yield
+    for copy, slot, start in ((their_y, 1 - y, own), (their_far, y, other), (their_both, 1 - y, other)):
+        net.arrived(copy)
+        net.send(place(slot, 1, start), place(slot + 2, 1, start), CORE)
+    yield
+
+
+def run(flow):
+    return next(flow, None)
+
+
+def by_rows(count, body):
+    step = 16
+    lax.fori_loop(0, count // step, lambda i, _: (body(pl.ds(pl.multiple_of(i * step, step), step)), 0)[1], 0)
+
+
+def begin_kernel(tokens_ref, gain_ref, qkv_ref, out_ref, x_ref, all_ref, joined_ref, output_ref, here, normed, send, recv, local, *, sizes):
+    net = Wires(send, recv, local, sizes)
+    net.greet([Y, CORE, CORNER, NEAR, FAR, X])
+    rows = local_flow(net, tokens_ref, here)
+    across = qkv_ref.shape[1] // 2
+    joined = weight_flow(net, qkv_ref, joined_ref, 0, 0, across, across)
+    run(joined)
+    rows[0].wait()
+    rows[1].wait()
+    net.local = net.local[2:]
+    for copy in rows[2:]:
+        net.arrived(copy)
+
+    def norm(at):
+        values = here[at, :].astype(F32)
+        inverse = lax.rsqrt(jnp.mean(values * values, axis=1, keepdims=True) + EPS)
+        normed[at, :] = (values * inverse * gain_ref[...]).astype(BF16)
+        x_ref[at, :] = here[at, :]
+
+    by_rows(here.shape[0], norm)
+    gather = gather_flow(net, normed, all_ref)
+    run(gather)
+    across = out_ref.shape[0] // 2
+    output = weight_flow(net, out_ref, output_ref, 1, 0, across, across)
+    for flow in (joined, output, gather, joined, gather, joined, output, joined, output, output, output):
+        run(flow)
+    net.finish()
+
+
+ANY = pl.BlockSpec(memory_space=pl.ANY)
+VMEM = pl.BlockSpec(memory_space=pltpu.VMEM)
+
+
+def sems(sends, locals_):
+    return [pltpu.SemaphoreType.DMA((sends,)), pltpu.SemaphoreType.DMA((sends,)), pltpu.SemaphoreType.DMA((locals_,))]
+
+
+def wire_call(kernel, name, number, specs, out_specs, shapes, scratch, sizes, cost, *args):
+    return pl.pallas_call(
+        functools.partial(kernel, sizes=sizes),
+        in_specs=specs,
+        out_specs=out_specs,
+        out_shape=[jax.ShapeDtypeStruct(*shape) for shape in shapes],
+        scratch_shapes=scratch,
+        compiler_params=pltpu.CompilerParams(collective_id=number, has_side_effects=True, vmem_limit_bytes=VMEM_LIMIT),
+        cost_estimate=pl.CostEstimate(flops=0, bytes_accessed=cost * 3 * 10**6, transcendentals=0),
+        name=name,
+    )(*args)
+
+
+def begin(tokens, gain, qkv, out, sizes):
+    rows, width = tokens.shape[0] // sizes["narrow"], gain.shape[0]
+    return wire_call(
+        begin_kernel, "begin", 1, [ANY, VMEM, VMEM, VMEM], [VMEM, ANY, ANY, ANY],
+        [((rows, width), BF16), ((4 * rows, width), BF16), ((width, qkv.shape[1]), BF16), ((out.shape[0], width), BF16)],
+        [pltpu.VMEM((rows, width), BF16), pltpu.VMEM((rows, width), BF16), *sems(48, 8)], sizes, 55,
+        tokens, gain[None], qkv, out,
+    )
+
+
+def keys_kernel(kv_ref, cotangent_ref, keys_ref, rows_ref, all_ref, here, send, recv, local, *, sizes):
+    net = Wires(send, recv, local, sizes)
+    net.greet([Y, CORE, CORNER, NEAR, FAR])
+    count, width = kv_ref.shape
+    size = width // 4
+    part = lambda i, j: keys_ref.at[pl.ds(i, count), pl.ds(j * size, size)]
+    base = pl.multiple_of(net.far * 2 * count, count)
+    far = [net.make(kv_ref.at[:, pl.ds(j * size, size)], part(0, j ^ 1), FAR) for j in range(4)]
+
+    @pl.when(net.far == 0)
+    def _():
+        for copy in far:
+            copy.start()
+
+    rows = local_flow(net, cotangent_ref, here)
+    net.copy(kv_ref, keys_ref.at[pl.ds(base, count), :])
+    net.send(kv_ref, keys_ref.at[pl.ds(base + count, count), :], CORE)
+    rows[0].wait()
+    rows[1].wait()
+    net.local = net.local[2:]
+    for copy in rows[2:]:
+        net.arrived(copy)
+    net.copy(here, rows_ref)
+    gather = gather_flow(net, here, all_ref)
+    for _ in range(3):
+        run(gather)
+    on = [net.make(part(0, j ^ 1), part(count, j ^ 1), CORE) for j in range(4)]
+
+    @pl.when(net.far == 1)
+    def _():
+        for copy, forward in zip(far, on):
+            copy.wait_recv()
+            forward.start()
+        for forward in on:
+            forward.wait()
+
+    @pl.when(net.far == 0)
+    def _():
+        for copy in far:
+            copy.wait_send()
+
+    net.sent = [copy for copy in net.sent if all(copy is not other for other in far + on)]
+    net.finish()
+
+
+def exchange_keys(kv, cotangent, width, sizes):
+    rows = cotangent.shape[0] // sizes["narrow"]
+    return wire_call(
+        keys_kernel, "keys", 2, [VMEM, ANY], [ANY, ANY, ANY],
+        [((4 * kv.shape[0], kv.shape[1]), BF16), ((rows, width), BF16), ((4 * rows, width), BF16)],
+        [pltpu.VMEM((rows, width), BF16), *sems(24, 8)], sizes, 55, kv, cotangent,
+    )
+
+
+def scatter_flow(net, partial_ref, first_ref, second_ref, send_ref, last_ref, total_ref):
+    half = partial_ref.shape[0] // 8
+    part = lambda i: partial_ref.at[pl.ds(i * half, half), :]
+    slot = lambda ref, i: ref.at[pl.ds(i * half, half), :]
+    to_z = [net.send(part(6), slot(first_ref, 1), NEAR), net.send(part(4), slot(first_ref, 0), NEAR)]
+    to_y = [net.send(part(7), slot(second_ref, 1), Y), net.send(part(3), slot(second_ref, 0), Y)]
+    yield
+
+    def add(out_ref, to, i, ref, j):
+        def body(at):
+            move = lambda start: pl.ds(pl.multiple_of(at.start + start, 16), at.size)
+            value = partial_ref[move(i * half), :].astype(F32) + ref[move(j * half), :].astype(F32)
+            out_ref[move(to), :] = value.astype(out_ref.dtype)
+
+        by_rows(half, body)
+
+    net.arrived(to_z[0])
+    add(send_ref, 0, 2, first_ref, 1)
+    last_y = net.send(slot(send_ref, 0), slot(last_ref, 0), Y)
+    net.arrived(to_y[0])
+    add(send_ref, half, 5, second_ref, 1)
+    last_z = net.send(slot(send_ref, 1), slot(last_ref, 1), NEAR)
+    yield
+    net.arrived(to_z[1])
+    add(total_ref, 0, 0, first_ref, 0)
+    net.arrived(to_y[1])
+    add(total_ref, half, 1, second_ref, 0)
+    yield
+    net.arrived(last_y)
+    net.arrived(last_z)
+    yield
+
+
+def middle_kernel(
+    partial_ref, x_ref, gain_ref, gate_ref, up_ref, down_ref, gate_y_ref, up_y_ref, down_y_ref, gate_far_ref, up_far_ref, down_far_ref,
+    middle_ref, all_ref, both_ref, last_ref,
+    first, second, sums, last, total, normed, send, recv, local, *, sizes,
+):
+    net = Wires(send, recv, local, sizes)
+    net.greet([Y, CORE, NEAR, FAR, X])
+    scatter = scatter_flow(net, partial_ref, first, second, sums, last, total)
+    run(scatter)
+    across = gate_ref.shape[1] // 2
+    flows = [
+        weight_flow(net, gate_ref, both_ref, 0, 0, across, across, gate_y_ref, gate_far_ref),
+        weight_flow(net, up_ref, both_ref, 0, 2 * across, 3 * across, across, up_y_ref, up_far_ref),
+        weight_flow(net, down_ref, last_ref, 1, 0, across, across, down_y_ref, down_far_ref),
+    ]
+    for flow in flows:
+        run(flow)
+    run(scatter)
+    run(scatter)
+    run(scatter)
+
+    def norm(at):
+        values = x_ref[at, :].astype(F32) + total[at, :] + last[at, :].astype(F32)
+        middle_ref[at, :] = values
+        inverse = lax.rsqrt(jnp.mean(values * values, axis=1, keepdims=True) + EPS)
+        normed[at, :] = (values * inverse * gain_ref[...]).astype(BF16)
+
+    by_rows(normed.shape[0], norm)
+    gather = gather_flow(net, normed, all_ref)
+    run(gather)
+    run(flows[0])
+    run(gather)
+    run(gather)
+    run(flows[1])
+    run(flows[2])
+    for flow in flows:
+        run(flow)
+    net.finish()
+
+
+def to_middle(partial, x, gain, gate, up, down, pieces, sizes):
+    rows, width = x.shape
+    buffer = lambda n, kind: pltpu.VMEM((n, width), kind)
+    return wire_call(
+        middle_kernel, "middle", 3, [VMEM] * 12, [VMEM, ANY, ANY, ANY],
+        [((rows, width), F32), ((4 * rows, width), BF16), ((width, 2 * gate.shape[1]), BF16), ((down.shape[0], width), BF16)],
+        [
+            buffer(rows, BF16), buffer(rows, BF16), buffer(rows, BF16), buffer(rows, BF16), buffer(rows, F32), buffer(rows, BF16),
+            *sems(64, 16),
+        ],
+        sizes, 80, partial, x, gain[None], gate, up, down, *pieces,
+    )
 
 
 def layout(lengths, group_rows):
@@ -373,12 +737,10 @@
     def gather_rows(values):
         half = values.shape[0] // 2
         first, second = values[:half], values[half:]
-        turned = turn_pairs(values)
-        first_y = over_y(turned[:half])
-        second_z = over_z(second)
+        first_y, second_z = over_y(first), over_z(second)
         come = over_z(join([first, first_y]))
         first_z, first_d = come[:half], come[half:]
-        come = over_y(join([turned[half:], turn_pairs(second_z)]))
+        come = over_y(join([second, second_z]))
         second_y, second_d = come[:half], come[half:]
         return join([first, second, first_y, second_y, first_z, second_z, first_d, second_d])
 
@@ -388,15 +750,15 @@
         come = over_z(join([part(4), part(6)]))
         first = part(0).astype(F32) + come[:half]
         first_y = (part(2).astype(F32) + come[half:]).astype(BF16)
-        come = over_y(turn_pairs(join([part(3), part(7)])))
+        come = over_y(join([part(3), part(7)]))
         second = part(1).astype(F32) + come[:half]
         second_z = (part(5).astype(F32) + come[half:]).astype(BF16)
-        first = first + over_y(turn_pairs(first_y)).astype(F32)
+        first = first + over_y(first_y).astype(F32)
         second = second + over_z(second_z).astype(F32)
         return join([first, second])
 
     def all_sum(values):
-        for axis, size in (("narrow", n_narrow), ("wide", n_wide), ("dp", n_dp)):
+        for axis, size in (("dp", n_dp), ("narrow", n_narrow), ("wide", n_wide)):
             distance = 1
             while distance < size:
                 values = values + exchange(values, axis, distance, size)
@@ -430,29 +792,26 @@
             high = lax.slice_in_dim(values, half, 2 * half, axis=axis)
             return join([jnp.where(x == 0, low, high), jnp.where(x == 0, high, low)], axis)
 
-        def to_local(values):
-            values = by_x(values, 1)
-            send = [cut(values, (narrow ^ r) * rows_local, rows_local, 0) for r in RELATIVE]
-            parts = [send[0]] + [exchange(s, "narrow", r, n_narrow) for s, r in zip(send[1:], RELATIVE[1:])]
-            return join(parts, 1)
+        owners = [2 * (i % 2) + (core ^ (i // 2)) for i in range(4)]
 
         def from_local(values):
             out = jnp.zeros((rows_wide, width_local), values.dtype)
-            for i, r in enumerate(RELATIVE):
-                part = by_x(values[:, i * width_local : (i + 1) * width_local], 1)
+            for r in RELATIVE:
+                slot = 2 * (r % 2) + (y ^ (r // 2))
+                part = by_x(cut(values, slot * width_local, width_local, 1), 1)
                 if r:
                     part = exchange(part, "narrow", r, n_narrow)
                 out = lax.dynamic_update_slice_in_dim(out, part, (narrow ^ r) * rows_local, 0)
             return out
 
         def relative_vector(vector):
-            return join([by_x(cut(vector, (narrow ^ r) * width_local, width_local, 0), 0) for r in RELATIVE])
+            return join([by_x(cut(vector, i * width_local, width_local, 0), 0) for i in owners])
 
         def absolute_vector(vector):
             out = jnp.zeros((width,), vector.dtype)
-            for i, r in enumerate(RELATIVE):
-                part = by_x(vector[i * width_local : (i + 1) * width_local], 0)
-                out = lax.dynamic_update_slice_in_dim(out, part, (narrow ^ r) * width_local, 0)
+            for at, i in enumerate(owners):
+                part = by_x(vector[at * width_local : (at + 1) * width_local], 0)
+                out = lax.dynamic_update_slice_in_dim(out, part, i * width_local, 0)
             return out
 
         def norm(values, gain):
@@ -465,47 +824,41 @@
             inner = jnp.mean(scaled * hat, axis=1, keepdims=True)
             return jnp.sum(grad * hat, axis=0), inverse * (scaled - hat * inner)
 
-        def pieces(weights, axis):
-            across = 1 - axis
-            half = lambda i: join([cut(w, i * (w.shape[across] // 2), w.shape[across] // 2, across) for w in weights], across)
-            mine = half(y)
-            return (
-                cut(mine, x * quarter, quarter, axis),
-                cut(mine, (1 - x) * quarter, quarter, axis),
-                cut(half(1 - y), x * quarter, quarter, axis),
-            )
-
-        def send_far(mine, from_y, axis):
-            return over_far(join([mine, from_y], axis))
-
-        def assemble(mine, rest, from_y, from_far, axis):
-            far_first = lax.slice_in_dim(from_far, 0, quarter, axis=axis)
-            far_second = lax.slice_in_dim(from_far, quarter, 2 * quarter, axis=axis)
-            their_y, their_far = over_x(from_y), over_x(from_far)
-            their_first = lax.slice_in_dim(their_far, 0, quarter, axis=axis)
-            their_second = lax.slice_in_dim(their_far, quarter, 2 * quarter, axis=axis)
-            own = join([mine, rest, from_y, their_y], axis)
-            other = join([far_first, their_first, far_second, their_second], axis)
-            block = join([own, other], 1 - axis)
-            return block, over_core(block)
-
-        def reduce_weight(first, second, axis, widths, kind=BF16):
-            across = 1 - axis
+        def piece_of(weight, i, axis):
+            half = weight.shape[1 - axis] // 2
+            return cut(cut(weight, x * quarter, quarter, axis), i * half, half, 1 - axis)
+
+        def reduce_first(first, second, axis, *ready):
             step = first.shape[axis] // 4
             piece = lambda v, i: lax.slice_in_dim(v, i * step, (i + 1) * step, axis=axis)
-            total = first + over_core(second.astype(kind)).astype(F32)
-            come = over_x(join([piece(total, 1), piece(total, 3)], axis).astype(kind))
+            total = first + over_core(second.astype(BF16)).astype(F32)
+            send = join([piece(total, 1), piece(total, 3)], axis).astype(BF16)
+            come = over_x(after(send, *ready) if ready else send)
             total = join([piece(total, 0), piece(total, 2)], axis) + come.astype(F32)
             distance = 2
             while distance < n_dp:
-                total = total + exchange(total.astype(kind), "dp", distance, n_dp).astype(F32)
+                total = total + exchange(total.astype(BF16), "dp", distance, n_dp).astype(F32)
                 distance *= 2
+            return total, come
+
+        def reduce_second(total, axis, *ready):
+            across = 1 - axis
+            count = total.shape[across] // 2
+            send = lax.slice_in_dim(total, count, 2 * count, axis=across).astype(BF16)
+            come = over_far(after(send, *ready) if ready else send)
+            return (lax.slice_in_dim(total, 0, count, axis=across) + come.astype(F32)).astype(BF16)
+
+        def reduce_third(total, axis, *ready):
+            step = total.shape[axis] // 2
+            piece = lambda i: cut(total, i * step, step, axis)
+            send = piece(1 - y)
+            ours = join([piece(y), over_y(after(send, *ready) if ready else send)], 1 - axis)
+            return ours, over_x(ours)
+
+        def reduce_last(ours, theirs, axis, widths):
+            across = 1 - axis
+            outs, at = [], 0
             count = sum(widths)
-            come = over_far(lax.slice_in_dim(total, count, 2 * count, axis=across).astype(kind))
-            total = (lax.slice_in_dim(total, 0, count, axis=across) + come.astype(F32)).astype(kind)
-            ours = join([piece(total, 0), over_y(piece(total, 1))], across)
-            theirs = over_x(ours)
-            outs, at = [], 0
             for length in widths:
                 sides = []
                 for v in (ours, theirs):
@@ -517,25 +870,15 @@
                 at += length
             return outs
 
-        inputs = to_local(tokens)
-        qkv_mine, qkv_rest, send = pieces([query_weight, key_weight, value_weight], 0)
-        qkv_y = over_y(send)
-        qkv_far = send_far(qkv_mine, qkv_y, 0)
-        gates = lax.all_gather(lax.all_gather(head_gate, "wide", axis=1, tiled=True), "narrow", axis=0, tiled=True)
-        gates = join([by_x(cut(gates, (narrow ^ r) * width_local, width_local, 0), 0) for r in RELATIVE])
-        gates = join([cut(gates, v * heads + y * (heads // 2), heads // 2, 1) for v in (z, z ^ 2)], 1)
-        gates = jnp.pad(gates, ((0, 0), (0, LANES - heads)))
-        qkv_block, qkv_core = assemble(qkv_mine, qkv_rest, qkv_y, qkv_far, 0)
-        joined_weight = join([join([qkv_block, qkv_core], 0), gates], 1)
-
-        out_mine, out_rest, send = pieces([after(output_weight, qkv_y)], 1)
-        out_y = over_y(send)
-        down_mine, down_rest, send = pieces([after(down_weight, out_y)], 1)
-        down_y = over_y(send)
-        out_far = send_far(after(out_mine, qkv_far), out_y, 1)
-        down_far = send_far(after(down_mine, out_far), down_y, 1)
-        out_weight = join(assemble(out_mine, out_rest, out_y, out_far, 1), 1)
-        down = join(assemble(down_mine, down_rest, down_y, down_far, 1), 1)
+        gain_one, gain_two = relative_vector(attention_gain), relative_vector(feedforward_gain)
+        lane_pad = ((0, 0), (0, LANES - heads // 2))
+        halves = lambda w, i: w[:, i * (w.shape[1] // 2) : (i + 1) * (w.shape[1] // 2)]
+        packed = join(
+            [v for i in range(2) for v in (
+                halves(query_weight, i), halves(key_weight, i), halves(value_weight, i), jnp.pad(halves(head_gate, i), lane_pad)
+            )], 1
+        )
+        inputs, normed_all, joined_weight, out_weight = begin(tokens, gain_one, packed, output_weight, sizes)
 
         index, start, position = layout(continuation_lengths[0], group_rows)
         square = [(z ^ (i // 2), narrow ^ (2 * (i % 2))) for i in range(4)]
@@ -561,96 +904,99 @@
             axis=1,
         ).astype(jnp.int32)
 
-        gain_one, gain_two = relative_vector(attention_gain), relative_vector(feedforward_gain)
-        inputs = inputs.astype(F32)
-        inverse_one, hat_one, normed = norm(inputs, gain_one)
-        normed_all = gather_rows(normed)
         raw = dot_rows(normed_all, joined_weight)
         q, kv = post(raw, cosine, sine, query_gain, key_gain, heads, pairs, size, factor)
-        kv = after(kv, out_far, down_far)
-
-        kv_core = over_core(kv)
+        send = after((gate_weight, up_weight, down_weight), normed_all)
+        axes = (0, 0, 1)
+        from_y = [over_y(piece_of(w, 1 - y, axis)) for w, axis in zip(send, axes)]
         near = [i for i in range(n_wide) if i & 2 == 0]
-        far_kv = lax.ppermute(turn_pairs(kv), "wide", [(i, i + 2) for i in near])
-        far_core = over_core(far_kv)
-        kv_all = join([jnp.where(z_far == 0, kv, far_kv), jnp.where(z_far == 0, kv_core, far_core), kv, kv_core])
-
-        upstream = to_local(after(cotangent, kv))
-        upstream_all = gather_rows(upstream)
-        gate_mine, gate_rest, send = pieces([after(gate_weight, down_y)], 0)
-        gate_y = over_y(send)
-        up_mine, up_rest, send = pieces([after(up_weight, gate_y)], 0)
-        up_y = over_y(send)
-        gate_far = send_far(after(gate_mine, far_kv), gate_y, 0)
-        up_far = send_far(after(up_mine, gate_far), up_y, 0)
+        kv_all, upstream, upstream_all = exchange_keys(after(kv, *from_y), cotangent, width, sizes)
+        send = after((gate_weight, up_weight, down_weight), kv_all)
+        from_far = [over_far(piece_of(w, y, axis)) for w, axis in zip(send, axes)]
 
         gated, context, inverse_total = attend(
             table, q, kv_all, my_index[:, None], my_start[:, None], raw, pairs, size
         )
-        partial = dot_rows(after(gated, upstream_all, gate_far), out_weight).astype(BF16)
-        middle = inputs + scatter_rows(partial)
-        gate_full = join(assemble(gate_mine, gate_rest, gate_y, gate_far, 0), 0)
-        up_full = join(assemble(up_mine, up_rest, up_y, up_far, 0), 0)
-        inverse_two, hat_two, normed_two = norm(middle, gain_two)
-        normed_two_all = gather_rows(normed_two)
-        gate_pre = dot_rows(normed_two_all, gate_full)
-        up_pre = dot_rows(normed_two_all, up_full)
+        partial = dot_rows(gated, out_weight).astype(BF16)
+        middle, normed_two_all, gate_up, down = to_middle(
+            partial, inputs, gain_two, gate_weight, up_weight, down_weight, from_y + from_far, sizes
+        )
+        inputs = inputs.astype(F32)
+        inverse_one, hat_one, _ = norm(inputs, gain_one)
+        inverse_two, hat_two, _ = norm(middle, gain_two)
+        both = dot_rows(normed_two_all, gate_up)
+        hidden_cols = gate_weight.shape[1]
+        gate_pre, up_pre = both[:, :hidden_cols], both[:, hidden_cols:]
         gate_sigmoid = jax.nn.sigmoid(gate_pre)
         silu = gate_pre * gate_sigmoid
         hidden = (silu * up_pre).astype(BF16)
         hidden_grad = dot_trans(upstream_all, down)
-        gate_grad = (hidden_grad * up_pre * gate_sigmoid * (1.0 + gate_pre * (1.0 - gate_sigmoid))).astype(BF16)
-        up_grad = (hidden_grad * silu).astype(BF16)
-        partial = (dot_trans(gate_grad, gate_full) + dot_trans(up_grad, up_full)).astype(BF16)
-        normed_two_grad = scatter_rows(partial)
+        gate_grad = hidden_grad * up_pre * gate_sigmoid * (1.0 + gate_pre * (1.0 - gate_sigmoid))
+        up_grad = hidden_grad * silu
+        gate_up_low = join([gate_grad, up_grad], 1).astype(BF16)
+        normed_two_grad = scatter_rows(dot_trans(gate_up_low, gate_up).astype(BF16))
         gain_two_term, change = norm_back(normed_two_grad, hat_two, inverse_two, gain_two)
         middle_grad = upstream.astype(F32) + change
         middle_low = middle_grad.astype(BF16)
         middle_all = gather_rows(middle_low)
         half = width // 2
-        hidden_cols = gate_weight.shape[1] // 2
-        down_gradient, = reduce_weight(
-            dot_inner(hidden, upstream_all[:, :half]), dot_inner(hidden, upstream_all[:, half:]), 1, [hidden_cols]
-        )
-        gate_gradient, = reduce_weight(
-            dot_inner(normed_two_all[:, :half], gate_grad), dot_inner(normed_two_all[:, half:], gate_grad), 0, [hidden_cols]
-        )
-        up_gradient, = reduce_weight(
-            dot_inner(normed_two_all[:, :half], up_grad), dot_inner(normed_two_all[:, half:], up_grad), 0, [hidden_cols]
+        down_total, down_x = reduce_first(
+            dot_inner(hidden, upstream_all[:, :half]), dot_inner(hidden, upstream_all[:, half:]), 1
+        )
+        gate_low, up_low = gate_up_low[:, :hidden_cols], gate_up_low[:, hidden_cols:]
+        gate_total, gate_x = reduce_first(
+            dot_inner(normed_two_all[:, :half], gate_low), dot_inner(normed_two_all[:, half:], gate_low), 0, down_x
+        )
+        up_total, up_x = reduce_first(
+            dot_inner(normed_two_all[:, :half], up_low), dot_inner(normed_two_all[:, half:], up_low), 0, gate_x
         )
         gated_grad = dot_trans(middle_all, out_weight)
         dq, dkv, logit_grad = attend_back(
             table, q, kv_all, my_index, my_start, raw, context, inverse_total, gated_grad, pairs, size
         )
+        down_total = reduce_second(down_total, 1)
+        gate_total = reduce_second(gate_total, 0, down_total)
         mlp_term = scatter_rows(dot_rows(after(hidden, middle_all), down).astype(BF16))
         layer_output = from_local((middle + mlp_term).astype(BF16))
-        output_gradient, = reduce_weight(
-            dot_inner(gated, middle_all[:, :half]), dot_inner(gated, middle_all[:, half:]), 1, [output_weight.shape[0] // 2]
+        out_total, _ = reduce_first(
+            dot_inner(gated, middle_all[:, :half]), dot_inner(gated, middle_all[:, half:]), 1, up_x
         )
 
         part = lambda i: dkv[i * rows_wide : (i + 1) * rows_wide]
         come = over_core(join([part(1), part(3)]))
         prompt = part(0).astype(F32) + come[:rows_wide].astype(F32)
         rest = part(2).astype(F32) + come[rows_wide:].astype(F32)
-        come = lax.ppermute(turn_pairs(prompt.astype(BF16)), "wide", [(i + 2, i) for i in near])
-        dkv_mine = jnp.where(z_far == 0, prompt + come.astype(F32), rest)
+        far_grad = lax.ppermute(turn_pairs(prompt.astype(BF16)), "wide", [(i + 2, i) for i in near])
+        down_ours, down_theirs = reduce_third(down_total, 1, dkv)
+        gate_ours, gate_theirs = reduce_third(gate_total, 0, down_ours)
+        far_grad = after(far_grad, down_theirs, gate_theirs)
+        dkv_mine = jnp.where(z_far == 0, prompt + far_grad.astype(F32), rest)
         low, query_gain_term, key_gain_term = project_back(
             dq, dkv_mine, raw, cosine, sine, query_gain, key_gain, logit_grad, heads, pairs, size, scale, log_two
         )
+        up_total = reduce_second(up_total, 0, far_grad)
+        out_total = reduce_second(out_total, 1, far_grad)
         normed_grad = scatter_rows(dot_trans(low, joined_weight).astype(BF16))
-        wide = low.shape[1] - LANES
-        query_cols, key_cols = heads // 2 * size, pairs // 2 * size
-        query_gradient, key_gradient, value_gradient = reduce_weight(
-            dot_inner(normed_all[:, :half], low[:, :wide]), dot_inner(normed_all[:, half:], low[:, :wide]), 0,
-            [query_cols, key_cols, key_cols],
-        )
-        gates_term = dot_inner(low[:, wide:], normed_all)[:heads]
-        head_gate_gradient, = reduce_weight(gates_term[:, :half], gates_term[:, half:], 1, [heads // 2], F32)
+        qkv_total, _ = reduce_first(
+            dot_inner(normed_all[:, :half], low), dot_inner(normed_all[:, half:], low), 0
+        )
+        qkv_total = reduce_second(qkv_total, 0, up_total, out_total)
+        up_ours, up_theirs = reduce_third(up_total, 0, low)
+        out_ours, out_theirs = reduce_third(out_total, 1, low)
         gain_one_term, change = norm_back(normed_grad, hat_one, inverse_one, gain_one)
         tokens_gradient = from_local((middle_grad + change).astype(BF16)).astype(F32)
         gains = all_sum(
             join([absolute_vector(gain_one_term), absolute_vector(gain_two_term), query_gain_term[0], key_gain_term[0]])
         )
+        qkv_ours, qkv_theirs = reduce_third(qkv_total, 0)
+        query_gradient, key_gradient, value_gradient, gates_gradient = reduce_last(
+            qkv_ours, qkv_theirs, 0, [heads // 2 * size, pairs // 2 * size, pairs // 2 * size, LANES]
+        )
+        head_gate_gradient = join([gates_gradient[:, : heads // 2], gates_gradient[:, LANES : LANES + heads // 2]], 1)
+        down_gradient, = reduce_last(down_ours, down_theirs, 1, [hidden_cols // 2])
+        gate_gradient, = reduce_last(gate_ours, gate_theirs, 0, [hidden_cols // 2])
+        up_gradient, = reduce_last(up_ours, up_theirs, 0, [hidden_cols // 2])
+        output_gradient, = reduce_last(out_ours, out_theirs, 1, [output_weight.shape[0] // 2])
         return (
             layer_output,
             tokens_gradient,
@@ -658,7 +1004,7 @@
             query_gradient,
             key_gradient,
             value_gradient,
-            head_gate_gradient.T,
+            head_gate_gradient,
             gains[2 * width : 2 * width + size],
             gains[2 * width + size :],
             output_gradient,

time: 1070 us -> 929 us (0.87)
  Pallas kernels: 59.7 us -> 307 us
  waiting for transfers between devices: 466 us -> 291 us
  other arithmetic: 155 us -> 49.7 us
  starting transfers between devices: 179 us -> 89.1 us
  blocking collectives: 18.7 us -> 0 us
    pallas_call x0 -> x3, Pallas kernels: none -> 247 us  [wire_call(): pl.pallas_call(functools.partial(kernel, sizes=sizes), in_specs=specs, ou...]
    ppermute x107 -> x59, waiting for transfers between devices: 466 us -> 288 us  [exchange(): return lax.ppermute(values, axis, [(i, i ^ distance) for i in range(size)])]
    concatenate x74 -> x32, other arithmetic: 109 us -> 8.15 us  [join(): return jnp.concatenate(parts, axis=axis)]
    ppermute x107 -> x59, starting transfers between devices: 173 us -> 87.8 us  [exchange(): return lax.ppermute(values, axis, [(i, i ^ distance) for i in range(size)])]
    all_gather x2 -> x0, blocking collectives: 18.7 us -> none  [the longest x1 13.4 us: on_device(): lax.all_gather(head_gate, 'wide', axis=1, tiled=True)]
    unnamed x257 -> x119, local copies, waits for them, and re-layouts: 14.5 us -> 22.2 us
    dot_general x5 -> x4, matrix products: 50.1 us -> 44.6 us  [dot_trans(): lax.dot_general(left, right, (((1,), (1,)), ((), ())), preferred_element_...]
    dot_general x5 -> x4, matrix products: 46.8 us -> 44.1 us  [dot_rows(): return jnp.dot(left, right, preferred_element_type=F32)]
  transfers between devices with their start and end apart: 109 -> 60, of which waited for: 49 -> 30; matrix products, arithmetic and copies ran while one was open for 24% -> 16% of each run, Pallas kernels for 5% -> 6%
where the time goes in v3:
time: 929 us; the launch traced here: 919 us
  Pallas kernels  307 us (33%)
  waiting for transfers between devices  291 us (31%)
  matrix products  134 us (14%)
  starting transfers between devices  89.1 us (10%)
  other arithmetic  49.7 us (5%)
  local copies, waits for them, and re-layouts  45.1 us (5%)
    ppermute x59, waiting for transfers between devices, exchange(): return lax.ppermute(values, axis, [(i, i ^ distance) for i in range(size)])  288 us
    pallas_call x3, Pallas kernels, wire_call(): pl.pallas_call(functools.partial(kernel, sizes=sizes), in_specs=specs, ou...  247 us
    ppermute x59, starting transfers between devices, exchange(): return lax.ppermute(values, axis, [(i, i ^ distance) for i in range(size)])  87.8 us
    dot_general x10, matrix products, dot_inner(): lax.dot_general(left, right, (((0,), (0,)), ((), ())), preferred_element_...  45.4 us
    dot_general x4, matrix products, dot_trans(): lax.dot_general(left, right, (((1,), (1,)), ((), ())), preferred_element_...  44.6 us
    dot_general x4, matrix products, dot_rows(): return jnp.dot(left, right, preferred_element_type=F32)  44.1 us
    pallas_call x1, Pallas kernels, attend_back(): pl.pallas_call(functools.partial(backward_kernel, pairs=pairs, repeat=hea...  26 us
    unnamed x119, local copies, waits for them, and re-layouts  22.2 us
  transfers between devices with their start and end apart: 60, of which 30 were waited for; matrix products, arithmetic and copies ran while one was open for 16% of the time, Pallas kernels for 6%

profile of v3, /device:TPU:0, one launch (start us, length us, event | category | flops | bytes accessed | tf_op | source)
XLA Modules:
  0.0 918.5 jit_solution(10326307503550819632)
XLA Ops:
  9.9 69.8 %begin.1 = (bf16[256,2048]{1,0:T(8,128)(2,1)}, bf16[1024,2048]{1,0:T(8,128)(2,1)}, bf16[2048,1280]{1,0:T(8,128)(2,1)}, bf16[512,2048]{1,0:T(8,128)(2,1)}) custom-call(bf16[1024,512]{1,0:T(8,128)(2,1)} %tokens_ref.1, f32[1,2048]{1,0:T(1,128)} %bitcast.54, bf16[512,1280]{1,0:T(8,128)(2,1)} %copy-done.16, bf16[512,512]{1,0:T(8,128)(2,1)} %out_ref.1), custom_call_target="tpu_custom_call" | custom-call | bytes 165000000 | tf_op jit(solution)/shard_map/begin/pallas_call | solution.py:545
  86.0 10.5 %fusion.83.raw_ref.own_ref.other_ref = f32[1024,1280]{1,0:T(8,128)} fusion(bf16[1024,2048]{1,0:T(8,128)(2,1)} %get-tuple-element.56, bf16[2048,1280]{1,0:T(8,128)(2,1)} %get-tuple-element.57), kind=kOutput, calls=%fused_computation.353 | convolution fusion | flops 5368709120 | bytes 14680064 | tf_op jit(solution)/shard_map/dot_general | solution.py:22
  110.8 68.3 %keys.1 = (bf16[4096,512]{1,0:T(8,128)(2,1)}, bf16[256,2048]{1,0:T(8,128)(2,1)}, bf16[1024,2048]{1,0:T(8,128)(2,1)}) custom-call(bf16[1024,512]{1,0:T(8,128)(2,1)} %get-tuple-element.63.kv_ref, bf16[1024,512]{1,0:T(8,128)(2,1)} %cotangent_ref.1), custom_call_target="tpu_custom_call" | custom-call | bytes 165000000 | tf_op jit(solution)/shard_map/keys/pallas_call | solution.py:545
  179.4 12.4 %collective-permute-start.3 = (bf16[256,768]{1,0:T(8,128)(2,1)S(1)}, bf16[256,768]{1,0:T(8,128)(2,1)S(1)}, u32[]{:S(2)}, u32[]{:S(2)}) collective-permute-start(bf16[256,768]{1,0:T(8,128)(2,1)S(1)} %dynamic_slice.161), channel_id=1, source_target_pairs={{0,8},{4,12},{8,0},{12,4},{1,9},{5,13},{9,1},{13,5},{2,10},{6,14},... | collective-permute-start | bytes 1179656 | tf_op jit(solution)/shard_map/ppermute | solution.py:34
  197.4 18.5 %attend.1 = (bf16[1024,512]{1,0:T(8,128)(2,1)}, f32[1024,512]{1,0:T(8,128)}, f32[1024,512]{1,0:T(8,128)}) custom-call(s32[4,5]{1,0:T(4,128)} %stack.15.table_ref, bf16[1024,512]{1,0:T(8,128)(2,1)} %get-tuple-element.58.q_ref, bf16[4096,512]{1,0:T(8,128)(2,1)} %get-tuple-element.64.kv_ref, s32[1024,1]{1,0:T(8,128)} %copy.63.row_ref, ...), custom_call_target="tpu_custom_call" | custom-call | flops 20000000000 | bytes 12000000 | tf_op jit(solution)/shard_map/attend/pallas_call | solution.py:240
  227.1 8.4 collective-permute-done.4.up_far_ref
  235.5 8.0 collective-permute-done.5.down_far_ref
  244.2 109.2 %middle.1 = (f32[256,2048]{1,0:T(8,128)}, bf16[1024,2048]{1,0:T(8,128)(2,1)}, bf16[2048,3072]{1,0:T(8,128)(2,1)}, bf16[1536,2048]{1,0:T(8,128)(2,1)}) custom-call(bf16[1024,2048]{1,0:T(8,128)(2,1)} %convolution_convert_fusion.2.partial_ref, bf16[256,2048]{1,0:T(8,128)(2,1)} %get-tuple-element.67.x_ref, f32[1,2048]{1,0:T(1,128)} %bitcast.55, ...), custom_call_target="tpu_custom_call" | custom-call | bytes 240000000 | tf_op jit(solution)/shard_map/middle/pallas_call | solution.py:545
  353.5 19.1 %fusion.84 = f32[1024,3072]{1,0:T(8,128)} fusion(bf16[1024,2048]{1,0:T(8,128)(2,1)} %get-tuple-element.72, bf16[2048,3072]{1,0:T(8,128)(2,1)} %get-tuple-element.73), kind=kOutput, calls=%fused_computation.354 | convolution fusion | flops 12884901888 | bytes 29360128 | tf_op jit(solution)/shard_map/dot_general | solution.py:22
  372.6 14.1 %multiply_convert_fusion.1 = (bf16[1024,1536]{1,0:T(8,128)(2,1)}, bf16[1024,1536]{1,0:T(8,128)(2,1)}, bf16[1024,1536]{1,0:T(8,128)(2,1)}) fusion(f32[1024,3072]{1,0:T(8,128)} %fusion.84, bf16[1024,2048]{1,0:T(8,128)(2,1)S(1)} %copy-done.40, bf16[1536,2048]{1,0:T(8,128)(2,1)S(1)} %copy-done.38), kind=kOutput, calls=%fused_computation.8 | convolution fusion | flops 6466043904 | bytes 32505856 | tf_op jit(solution)/shard_map/dot_general | solution.py:26
  386.7 17.8 %fusion.5 = bf16[1024,2048]{1,0:T(8,128)(2,1)S(1)} fusion(bf16[2048,3072]{1,0:T(8,128)(2,1)} %get-tuple-element.73, bf16[1024,1536]{1,0:T(8,128)(2,1)} %get-tuple-element.173, bf16[1024,1536]{1,0:T(8,128)(2,1)} %get-tuple-element.172), kind=kOutput, calls=%fused_computation.14 | convolution fusion | flops 12899581952 | bytes 23068672 | tf_op jit(solution)/shard_map/dot_general | solution.py:26
  416.1 15.0 %collective-permute-done.6 = bf16[256,2048]{1,0:T(8,128)(2,1)} collective-permute-done((bf16[256,2048]{1,0:T(8,128)(2,1)S(1)}, bf16[256,2048]{1,0:T(8,128)(2,1)}, u32[]{:S(2)}, u32[]{:S(2)}) %collective-permute-start.6) | collective-permute-done | bytes 1048608 | tf_op jit(solution)/shard_map/ppermute | solution.py:34
  437.6 7.1 collective-permute-done.7
  464.1 9.1 collective-permute-done.10
  510.6 26.0 %attend_back.1 = (f32[1024,512]{1,0:T(8,128)}, bf16[4096,512]{1,0:T(8,128)(2,1)}, f32[1024,256]{1,0:T(8,128)}) custom-call(s32[4,5]{1,0:T(4,128)} %stack.15.table_ref, bf16[1024,512]{1,0:T(8,128)(2,1)} %get-tuple-element.58.q_ref, bf16[4096,512]{1,0:T(8,128)(2,1)} %get-tuple-element.64.kv_ref, s32[4,1,256]{2,1,0:T(1,128)} %get-tuple-element.336.row_ref, ...), custom_call_target="tpu_custom_call" | custom-call | flops 49999998976 | bytes 20000000 | tf_op jit(solution)/shard_map/attend_back/pallas_call | solution.py:336
  540.1 9.0 convolution_convert_fusion
  556.4 20.4 %collective-permute-start.25 = (bf16[768,512]{0,1:T(8,128)(2,1)S(1)}, bf16[768,512]{0,1:T(8,128)(2,1)S(1)}, u32[]{:S(2)}, u32[]{:S(2)}) collective-permute-start(bf16[768,512]{0,1:T(8,128)(2,1)S(1)} %slice.1098), channel_id=1, source_target_pairs={{0,8},{4,12},{8,0},{12,4},{1,9},{5,13},{9,1},{13,5},{2,10},{6,14},... | collective-permute-start | bytes 2359304 | tf_op jit(solution)/shard_map/ppermute | solution.py:34
  580.3 9.6 %collective-permute-done.15 = bf16[128,2048]{1,0:T(8,128)(2,1)S(1)} collective-permute-done((bf16[128,2048]{1,0:T(8,128)(2,1)S(1)}, bf16[128,2048]{1,0:T(8,128)(2,1)S(1)}, u32[]{:S(2)}, u32[]{:S(2)}) %collective-permute-start.15) | collective-permute-done | bytes 524320 | tf_op jit(solution)/shard_map/ppermute | solution.py:34
  593.2 17.5 %collective-permute-done.25 = bf16[768,512]{0,1:T(8,128)(2,1)S(1)} collective-permute-done((bf16[768,512]{0,1:T(8,128)(2,1)S(1)}, bf16[768,512]{0,1:T(8,128)(2,1)S(1)}, u32[]{:S(2)}, u32[]{:S(2)}) %collective-permute-start.25) | collective-permute-done | bytes 786464 | tf_op jit(solution)/shard_map/ppermute | solution.py:34
  624.1 7.2 collective-permute-start.30
  634.8 8.9 collective-permute-done.27
  643.8 45.2 %collective-permute-done.30 = bf16[512,768]{1,0:T(8,128)(2,1)S(1)} collective-permute-done((bf16[512,768]{1,0:T(8,128)(2,1)S(1)}, bf16[512,768]{1,0:T(8,128)(2,1)S(1)}, u32[]{:S(2)}, u32[]{:S(2)}) %collective-permute-start.30) | collective-permute-done | bytes 786464 | tf_op jit(solution)/shard_map/ppermute | solution.py:34
  710.6 11.4 %collective-permute-done.32 = bf16[256,1536]{1,0:T(8,128)(2,1)S(1)} collective-permute-done((bf16[256,1536]{1,0:T(8,128)(2,1)S(1)}, bf16[256,1536]{1,0:T(8,128)(2,1)S(1)}, u32[]{:S(2)}, u32[]{:S(2)}) %collective-permute-start.32) | collective-permute-done | bytes 786464 | tf_op jit(solution)/shard_map/ppermute | solution.py:34
  725.5 8.4 project_back.1
  739.4 8.7 convolution_convert_fusion.1
  754.2 18.5 %collective-permute-done.52 = bf16[256,512]{1,0:T(8,128)(2,1)S(1)} collective-permute-done((bf16[256,512]{1,0:T(8,128)(2,1)S(1)}, bf16[256,512]{1,0:T(8,128)(2,1)S(1)}, u32[]{:S(2)}, u32[]{:S(2)}) %collective-permute-start.52) | collective-permute-done | bytes 262176 | tf_op jit(solution)/shard_map/ppermute | solution.py:34
  786.9 8.2 collective-permute-done.33
  798.2 10.9 %collective-permute-done.34 = bf16[128,2048]{1,0:T(8,128)(2,1)S(1)} collective-permute-done((bf16[128,2048]{1,0:T(8,128)(2,1)S(1)}, bf16[128,2048]{1,0:T(8,128)(2,1)S(1)}, u32[]{:S(2)}, u32[]{:S(2)}) %collective-permute-start.34) | collective-permute-done | bytes 524320 | tf_op jit(solution)/shard_map/ppermute | solution.py:34
  831.8 26.1 %collective-permute-done.46 = bf16[512,1280]{1,0:T(8,128)(2,1)S(1)} collective-permute-done((bf16[512,1280]{1,0:T(8,128)(2,1)S(1)}, bf16[512,1280]{1,0:T(8,128)(2,1)S(1)}, u32[]{:S(2)}, u32[]{:S(2)}) %collective-permute-start.46) | collective-permute-done | bytes 1310752 | tf_op jit(solution)/shard_map/ppermute | solution.py:34
  874.6 13.4 %collective-permute-done.44 = f32[4352]{0:T(1024)S(1)} collective-permute-done((f32[4352]{0:T(1024)S(1)}, f32[4352]{0:T(1024)S(1)}, u32[]{:S(2)}, u32[]{:S(2)}) %collective-permute-start.44) | collective-permute-done | bytes 17440 | tf_op jit(solution)/shard_map/ppermute | solution.py:34
  890.4 7.9 collective-permute-done.54
  900.6 13.3 %collective-permute-done.55 = bf16[256,1280]{1,0:T(8,128)(2,1)S(1)} collective-permute-done((bf16[256,1280]{1,0:T(8,128)(2,1)S(1)}, bf16[256,1280]{1,0:T(8,128)(2,1)S(1)}, u32[]{:S(2)}, u32[]{:S(2)}) %collective-permute-start.55) | collective-permute-done | bytes 655392 | tf_op jit(solution)/shard_map/ppermute | solution.py:34
  (442 shorter events, 257.4 us)
Async XLA Ops:
  80.0 30.8 %collective-permute-start = (bf16[256,768]{1,0:T(8,128)(2,1)S(1)}, bf16[256,768]{1,0:T(8,128)(2,1)}, u32[]{:S(2)}, u32[]{:S(2)}) collective-permute-start(bf16[256,768]{1,0:T(8,128)(2,1)S(1)} %dynamic_slice.154), channel_id=1, source_target_pairs={{0,2},{1,3},{2,0},{3,1},{4,6},{5,7},{6,4},{7,5},{8,10},{9,11},{10,... | collective-permute-start | bytes 1179656 | tf_op jit(solution)/shard_map/ppermute | solution.py:34
  81.8 29.0 %collective-permute-start.1 = (bf16[256,768]{1,0:T(8,128)(2,1)S(1)}, bf16[256,768]{1,0:T(8,128)(2,1)}, u32[]{:S(2)}, u32[]{:S(2)}) collective-permute-start(bf16[256,768]{1,0:T(8,128)(2,1)S(1)} %dynamic_slice.155), channel_id=1, source_target_pairs={{0,2},{1,3},{2,0},{3,1},{4,6},{5,7},{6,4},{7,5},{8,10},{9,11},{10,... | collective-permute-start | bytes 1179656 | tf_op jit(solution)/shard_map/ppermute | solution.py:34
  85.4 25.4 %collective-permute-start.2 = (bf16[768,256]{1,0:T(8,128)(2,1)}, bf16[768,256]{1,0:T(8,128)(2,1)}, u32[]{:S(2)}, u32[]{:S(2)}) collective-permute-start(bf16[768,256]{1,0:T(8,128)(2,1)} %dynamic_slice.156), channel_id=1, source_target_pairs={{0,2},{1,3},{2,0},{3,1},{4,6},{5,7},{6,4},{7,5},{8,10},{9,11},{10,... | collective-permute-start | bytes 1179656 | tf_op jit(solution)/shard_map/ppermute | solution.py:34
  179.4 47.7 %collective-permute-start.3 = (bf16[256,768]{1,0:T(8,128)(2,1)S(1)}, bf16[256,768]{1,0:T(8,128)(2,1)S(1)}, u32[]{:S(2)}, u32[]{:S(2)}) collective-permute-start(bf16[256,768]{1,0:T(8,128)(2,1)S(1)} %dynamic_slice.161), channel_id=1, source_target_pairs={{0,8},{4,12},{8,0},{12,4},{1,9},{5,13},{9,1},{13,5},{2,10},{6,14},... | collective-permute-start | bytes 1179656 | tf_op jit(solution)/shard_map/ppermute | solution.py:34
  193.1 42.4 %collective-permute-start.4 = (bf16[256,768]{1,0:T(8,128)(2,1)S(1)}, bf16[256,768]{1,0:T(8,128)(2,1)S(1)}, u32[]{:S(2)}, u32[]{:S(2)}) collective-permute-start(bf16[256,768]{1,0:T(8,128)(2,1)S(1)} %dynamic_slice.162), channel_id=1, source_target_pairs={{0,8},{4,12},{8,0},{12,4},{1,9},{5,13},{9,1},{13,5},{2,10},{6,14},... | collective-permute-start | bytes 1179656 | tf_op jit(solution)/shard_map/ppermute | solution.py:34
  194.5 49.0 %collective-permute-start.5 = (bf16[768,256]{1,0:T(8,128)(2,1)S(1)}, bf16[768,256]{1,0:T(8,128)(2,1)S(1)}, u32[]{:S(2)}, u32[]{:S(2)}) collective-permute-start(bf16[768,256]{1,0:T(8,128)(2,1)S(1)} %dynamic_slice.163), channel_id=1, source_target_pairs={{0,8},{4,12},{8,0},{12,4},{1,9},{5,13},{9,1},{13,5},{2,10},{6,14},... | collective-permute-start | bytes 1179656 | tf_op jit(solution)/shard_map/ppermute | solution.py:34
  406.5 24.6 %collective-permute-start.6 = (bf16[256,2048]{1,0:T(8,128)(2,1)S(1)}, bf16[256,2048]{1,0:T(8,128)(2,1)}, u32[]{:S(2)}, u32[]{:S(2)}) collective-permute-start(bf16[256,2048]{1,0:T(8,128)(2,1)S(1)} %pad_maximum_fusion.7), channel_id=1, source_target_pairs={{0,4},{4,0},{8,12},{12,8},{1,5},{5,1},{9,13},{13,9},{2,6},{6,2},{1... | collective-permute-start | bytes 3145736 | tf_op jit(solution)/shard_map/ppermute | solution.py:34
  407.6 30.1 %collective-permute-start.8 = (bf16[256,2048]{1,0:T(8,128)(2,1)S(1)}, bf16[256,2048]{1,0:T(8,128)(2,1)S(1)}, u32[]{:S(2)}, u32[]{:S(2)}) collective-permute-start(bf16[256,2048]{1,0:T(8,128)(2,1)S(1)} %pad_maximum_fusion.8), channel_id=1, source_target_pairs={{0,2},{1,3},{2,0},{3,1},{4,6},{5,7},{6,4},{7,5},{8,10},{9,11},{10,... | collective-permute-start | bytes 3145736 | tf_op jit(solution)/shard_map/ppermute | solution.py:34
  450.4 26.5 %collective-permute-start.23 = (bf16[1536,1024]{0,1:T(8,128)(2,1)S(1)}, bf16[1536,1024]{0,1:T(8,128)(2,1)S(1)}, u32[]{:S(2)}, u32[]{:S(2)}) collective-permute-start(bf16[1536,1024]{0,1:T(8,128)(2,1)S(1)} %convolution_convert_fusion.6), channel_id=1, source_target_pairs={{0,1},{1,0},{2,3},{3,2},{4,5},{5,4},{6,7},{7,6},{8,9},{9,8},{10,11... | collective-permute-start | bytes 9437192 | tf_op jit(solution)/shard_map/ppermute | solution.py:34
  450.4 33.8 %collective-permute-start.47 = (bf16[1024,1536]{1,0:T(8,128)(2,1)S(1)}, bf16[1024,1536]{1,0:T(8,128)(2,1)}, u32[]{:S(2)}, u32[]{:S(2)}) collective-permute-start(bf16[1024,1536]{1,0:T(8,128)(2,1)S(1)} %convolution_convert_fusion.3), channel_id=1, source_target_pairs={{0,1},{1,0},{2,3},{3,2},{4,5},{5,4},{6,7},{7,6},{8,9},{9,8},{10,11... | collective-permute-start | bytes 9437192 | tf_op jit(solution)/shard_map/ppermute | solution.py:34
  450.9 42.2 %collective-permute-start.28 = (bf16[1024,1536]{1,0:T(8,128)(2,1)}, bf16[1024,1536]{1,0:T(8,128)(2,1)}, u32[]{:S(2)}, u32[]{:S(2)}) collective-permute-start(bf16[1024,1536]{1,0:T(8,128)(2,1)} %convolution_convert_fusion.5), channel_id=1, source_target_pairs={{0,1},{1,0},{2,3},{3,2},{4,5},{5,4},{6,7},{7,6},{8,9},{9,8},{10,11... | collective-permute-start | bytes 9437192 | tf_op jit(solution)/shard_map/ppermute | solution.py:34
  473.3 31.7 %collective-permute-start.13 = (bf16[256,2048]{1,0:T(8,128)(2,1)S(1)}, bf16[256,2048]{1,0:T(8,128)(2,1)S(1)}, u32[]{:S(2)}, u32[]{:S(2)}) collective-permute-start(bf16[256,2048]{1,0:T(8,128)(2,1)S(1)} %pad_maximum_fusion.10), channel_id=1, source_target_pairs={{0,4},{4,0},{8,12},{12,8},{1,5},{5,1},{9,13},{13,9},{2,6},{6,2},{1... | collective-permute-start | bytes 3145736 | tf_op jit(solution)/shard_map/ppermute | solution.py:34
  474.2 30.8 %collective-permute-start.12 = (bf16[256,2048]{1,0:T(8,128)(2,1)S(1)}, bf16[256,2048]{1,0:T(8,128)(2,1)S(1)}, u32[]{:S(2)}, u32[]{:S(2)}) collective-permute-start(bf16[256,2048]{1,0:T(8,128)(2,1)S(1)} %pad_maximum_fusion.9), channel_id=1, source_target_pairs={{0,2},{1,3},{2,0},{3,1},{4,6},{5,7},{6,4},{7,5},{8,10},{9,11},{10,... | collective-permute-start | bytes 3145736 | tf_op jit(solution)/shard_map/ppermute | solution.py:34
  483.8 69.4 %collective-permute-start.24 = (bf16[1536,512]{0,1:T(8,128)(2,1)}, bf16[1536,512]{0,1:T(8,128)(2,1)}, u32[]{:S(2)}, u32[]{:S(2)}) collective-permute-start(bf16[1536,512]{0,1:T(8,128)(2,1)} %pad_maximum_fusion.3), channel_id=1, source_target_pairs={{0,16},{16,0},{1,17},{17,1},{2,18},{18,2},{3,19},{19,3},{4,20},{20... | collective-permute-start | bytes 4718600 | tf_op jit(solution)/shard_map/ppermute | solution.py:34
  538.4 76.1 %collective-permute-start.21 = (bf16[2048,512]{1,0:T(8,128)(2,1)S(1)}, bf16[2048,512]{1,0:T(8,128)(2,1)S(1)}, u32[]{:S(2)}, u32[]{:S(2)}) collective-permute-start(bf16[2048,512]{1,0:T(8,128)(2,1)S(1)} %pad_maximum_fusion.1), channel_id=1, source_target_pairs={{0,1},{1,0},{2,3},{3,2},{4,5},{5,4},{6,7},{7,6},{8,9},{9,8},{10,11... | collective-permute-start | bytes 6291464 | tf_op jit(solution)/shard_map/ppermute | solution.py:34
  549.5 27.3 %collective-permute-start.14 = (bf16[256,2048]{1,0:T(8,128)(2,1)S(1)}, bf16[256,2048]{1,0:T(8,128)(2,1)S(1)}, u32[]{:S(2)}, u32[]{:S(2)}) collective-permute-start(bf16[256,2048]{1,0:T(8,128)(2,1)S(1)} %pad_maximum_fusion.11), channel_id=1, source_target_pairs={{0,4},{4,0},{8,12},{12,8},{1,5},{5,1},{9,13},{13,9},{2,6},{6,2},{1... | collective-permute-start | bytes 3145736 | tf_op jit(solution)/shard_map/ppermute | solution.py:34
  553.1 27.2 %collective-permute-start.16 = (bf16[256,2048]{1,0:T(8,128)(2,1)S(1)}, bf16[256,2048]{1,0:T(8,128)(2,1)S(1)}, u32[]{:S(2)}, u32[]{:S(2)}) collective-permute-start(bf16[256,2048]{1,0:T(8,128)(2,1)S(1)} %pad_maximum_fusion.12), channel_id=1, source_target_pairs={{0,2},{1,3},{2,0},{3,1},{4,6},{5,7},{6,4},{7,5},{8,10},{9,11},{10,... | collective-permute-start | bytes 3145736 | tf_op jit(solution)/shard_map/ppermute | solution.py:34
  556.4 54.4 %collective-permute-start.25 = (bf16[768,512]{0,1:T(8,128)(2,1)S(1)}, bf16[768,512]{0,1:T(8,128)(2,1)S(1)}, u32[]{:S(2)}, u32[]{:S(2)}) collective-permute-start(bf16[768,512]{0,1:T(8,128)(2,1)S(1)} %slice.1098), channel_id=1, source_target_pairs={{0,8},{4,12},{8,0},{12,4},{1,9},{5,13},{9,1},{13,5},{2,10},{6,14},... | collective-permute-start | bytes 2359304 | tf_op jit(solution)/shard_map/ppermute | solution.py:34
  576.8 46.6 %collective-permute-start.29 = (bf16[512,1536]{1,0:T(8,128)(2,1)S(1)}, bf16[512,1536]{1,0:T(8,128)(2,1)S(1)}, u32[]{:S(2)}, u32[]{:S(2)}) collective-permute-start(bf16[512,1536]{1,0:T(8,128)(2,1)S(1)} %copy-done.17), channel_id=1, source_target_pairs={{0,16},{16,0},{1,17},{17,1},{2,18},{18,2},{3,19},{19,3},{4,20},{20... | collective-permute-start | bytes 4718600 | tf_op jit(solution)/shard_map/ppermute | solution.py:34
  624.1 64.9 %collective-permute-start.30 = (bf16[512,768]{1,0:T(8,128)(2,1)S(1)}, bf16[512,768]{1,0:T(8,128)(2,1)S(1)}, u32[]{:S(2)}, u32[]{:S(2)}) collective-permute-start(bf16[512,768]{1,0:T(8,128)(2,1)S(1)} %slice.1097), channel_id=1, source_target_pairs={{0,8},{4,12},{8,0},{12,4},{1,9},{5,13},{9,1},{13,5},{2,10},{6,14},... | collective-permute-start | bytes 2359304 | tf_op jit(solution)/shard_map/ppermute | solution.py:34
  633.0 77.6 %collective-permute-start.22 = (bf16[1024,512]{1,0:T(8,128)(2,1)}, bf16[1024,512]{1,0:T(8,128)(2,1)}, u32[]{:S(2)}, u32[]{:S(2)}) collective-permute-start(bf16[1024,512]{1,0:T(8,128)(2,1)} %pad_maximum_fusion.13), channel_id=1, source_target_pairs={{8,0},{12,4},{9,1},{13,5},{10,2},{14,6},{11,3},{15,7},{24,16},{28,... | collective-permute-start | bytes 3145736 | tf_op jit(solution)/shard_map/ppermute | solution.py:969
  634.4 69.4 %collective-permute-start.48 = (bf16[512,1536]{1,0:T(8,128)(2,1)}, bf16[512,1536]{1,0:T(8,128)(2,1)}, u32[]{:S(2)}, u32[]{:S(2)}) collective-permute-start(bf16[512,1536]{1,0:T(8,128)(2,1)} %pad_maximum_fusion.5), channel_id=1, source_target_pairs={{0,16},{16,0},{1,17},{17,1},{2,18},{18,2},{3,19},{19,3},{4,20},{20... | collective-permute-start | bytes 4718600 | tf_op jit(solution)/shard_map/ppermute | solution.py:34
  706.9 42.8 %collective-permute-start.51 = (bf16[512,512]{1,0:T(8,128)(2,1)}, bf16[512,512]{1,0:T(8,128)(2,1)}, u32[]{:S(2)}, u32[]{:S(2)}) collective-permute-start(bf16[512,512]{1,0:T(8,128)(2,1)} %pad_maximum_fusion.28), channel_id=1, source_target_pairs={{0,16},{16,0},{1,17},{17,1},{2,18},{18,2},{3,19},{19,3},{4,20},{20... | collective-permute-start | bytes 1572872 | tf_op jit(solution)/shard_map/ppermute | solution.py:34
  748.1 37.5 %collective-permute-start.49 = (bf16[512,768]{1,0:T(8,128)(2,1)S(1)}, bf16[512,768]{1,0:T(8,128)(2,1)S(1)}, u32[]{:S(2)}, u32[]{:S(2)}) collective-permute-start(bf16[512,768]{1,0:T(8,128)(2,1)S(1)} %copy-done.21), channel_id=1, source_target_pairs={{0,8},{4,12},{8,0},{12,4},{1,9},{5,13},{9,1},{13,5},{2,10},{6,14},... | collective-permute-start | bytes 2359304 | tf_op jit(solution)/shard_map/ppermute | solution.py:34
  748.2 77.9 %collective-permute-start.45 = (bf16[1024,1280]{1,0:T(8,128)(2,1)S(1)}, bf16[1024,1280]{1,0:T(8,128)(2,1)S(1)}, u32[]{:S(2)}, u32[]{:S(2)}) collective-permute-start(bf16[1024,1280]{1,0:T(8,128)(2,1)S(1)} %convolution_convert_fusion.4), channel_id=1, source_target_pairs={{0,1},{1,0},{2,3},{3,2},{4,5},{5,4},{6,7},{7,6},{8,9},{9,8},{10,11... | collective-permute-start | bytes 7864328 | tf_op jit(solution)/shard_map/ppermute | solution.py:34
  748.5 49.7 %collective-permute-start.35 = (bf16[256,2048]{1,0:T(8,128)(2,1)S(1)}, bf16[256,2048]{1,0:T(8,128)(2,1)S(1)}, u32[]{:S(2)}, u32[]{:S(2)}) collective-permute-start(bf16[256,2048]{1,0:T(8,128)(2,1)S(1)} %pad_maximum_fusion.15), channel_id=1, source_target_pairs={{0,2},{1,3},{2,0},{3,1},{4,6},{5,7},{6,4},{7,5},{8,10},{9,11},{10,... | collective-permute-start | bytes 3145736 | tf_op jit(solution)/shard_map/ppermute | solution.py:34
  754.0 41.1 %collective-permute-start.33 = (bf16[256,2048]{1,0:T(8,128)(2,1)S(1)}, bf16[256,2048]{1,0:T(8,128)(2,1)S(1)}, u32[]{:S(2)}, u32[]{:S(2)}) collective-permute-start(bf16[256,2048]{1,0:T(8,128)(2,1)S(1)} %pad_maximum_fusion.14), channel_id=1, source_target_pairs={{0,4},{4,0},{8,12},{12,8},{1,5},{5,1},{9,13},{13,9},{2,6},{6,2},{1... | collective-permute-start | bytes 3145736 | tf_op jit(solution)/shard_map/ppermute | solution.py:34
  829.2 28.8 %collective-permute-start.46 = (bf16[512,1280]{1,0:T(8,128)(2,1)S(1)}, bf16[512,1280]{1,0:T(8,128)(2,1)S(1)}, u32[]{:S(2)}, u32[]{:S(2)}) collective-permute-start(bf16[512,1280]{1,0:T(8,128)(2,1)S(1)} %pad_maximum_fusion.6), channel_id=1, source_target_pairs={{0,16},{16,0},{1,17},{17,1},{2,18},{18,2},{3,19},{19,3},{4,20},{20... | collective-permute-start | bytes 3932168 | tf_op jit(solution)/shard_map/ppermute | solution.py:34
  831.6 27.0 %collective-permute-start.41 = (f32[4352]{0:T(1024)S(1)}, f32[4352]{0:T(1024)S(1)}, u32[]{:S(2)}, u32[]{:S(2)}) collective-permute-start(f32[4352]{0:T(1024)S(1)} %fusion.53), channel_id=1, source_target_pairs={{0,1},{1,0},{2,3},{3,2},{4,5},{5,4},{6,7},{7,6},{8,9},{9,8},{10,11... | collective-permute-start | bytes 52232 | tf_op jit(solution)/shard_map/ppermute | solution.py:34
  858.4 30.3 %collective-permute-start.53 = (bf16[512,640]{1,0:T(8,128)(2,1)S(1)}, bf16[512,640]{1,0:T(8,128)(2,1)S(1)}, u32[]{:S(2)}, u32[]{:S(2)}) collective-permute-start(bf16[512,640]{1,0:T(8,128)(2,1)S(1)} %slice.1099), channel_id=1, source_target_pairs={{0,8},{4,12},{8,0},{12,4},{1,9},{5,13},{9,1},{13,5},{2,10},{6,14},... | collective-permute-start | bytes 1966088 | tf_op jit(solution)/shard_map/ppermute | solution.py:34
  858.5 40.3 %collective-permute-start.39 = (bf16[256,512]{1,0:T(8,128)(2,1)S(1)}, bf16[256,512]{1,0:T(8,128)(2,1)S(1)}, u32[]{:S(2)}, u32[]{:S(2)}) collective-permute-start(bf16[256,512]{1,0:T(8,128)(2,1)S(1)} %pad_maximum_fusion.34), channel_id=1, source_target_pairs={{0,3},{1,2},{2,1},{3,0},{4,7},{5,6},{6,5},{7,4},{8,11},{9,10},{10,... | collective-permute-start | bytes 786440 | tf_op jit(solution)/shard_map/ppermute | solution.py:34
  859.6 39.2 %collective-permute-start.38 = (bf16[256,512]{1,0:T(8,128)(2,1)S(1)}, bf16[256,512]{1,0:T(8,128)(2,1)S(1)}, u32[]{:S(2)}, u32[]{:S(2)}) collective-permute-start(bf16[256,512]{1,0:T(8,128)(2,1)S(1)} %pad_maximum_fusion.33), channel_id=1, source_target_pairs={{0,1},{1,0},{2,3},{3,2},{4,5},{5,4},{6,7},{7,6},{8,9},{9,8},{10,11... | collective-permute-start | bytes 786440 | tf_op jit(solution)/shard_map/ppermute | solution.py:34
  (80 other events, 1075.5 us)

commit v4 on v3

--- a/solution.py
+++ b/solution.py
@@ -358,7 +358,7 @@
         self.send_sems, self.recv_sems, self.local_sems = send_sems, recv_sems, local_sems
         self.sizes = sizes
         self.sent, self.local, self.open = [], [], []
-        self.locals_used = 0
+        self.locals_used, self.sends_used = 0, 0
         self.dp, self.wide, self.narrow = (lax.axis_index(a) for a in ("dp", "wide", "narrow"))
         self.y, self.core = self.narrow // 2, self.narrow % 2
         self.x, self.far = self.dp % 2, self.wide // 2
@@ -375,7 +375,8 @@
         pl.semaphore_wait(barrier, len(peers))
 
     def make(self, source, target, to):
-        i = len(self.sent)
+        i = self.sends_used
+        self.sends_used += 1
         copy = pltpu.make_async_remote_copy(
             src_ref=source, dst_ref=target, send_sem=self.send_sems.at[i], recv_sem=self.recv_sems.at[i],
             device_id=self.peer(*to), device_id_type=pl.DeviceIdType.MESH,
@@ -705,6 +706,367 @@
     )
 
 
+def spread_flow(net, rows_ref, out_ref):
+    rows, width = rows_ref.shape[0], out_ref.shape[1]
+    half = width // 2
+    base = pl.multiple_of(net.narrow * rows, rows)
+    for distance, to in ((3, CORNER), (2, Y), (1, CORE), (0, None)):
+        target = net.narrow if to is None else net.peer(*to)["narrow"]
+        at = (2 * (distance % 2) + target // 2) * width
+        for j in range(2):
+            sub = net.x if j == 0 else 1 - net.x
+            source = rows_ref.at[:, pl.ds(pl.multiple_of(at + j * half, half), half)]
+            goal = out_ref.at[pl.ds(base, rows), pl.ds(pl.multiple_of(sub * half, half), half)]
+            if to is None:
+                net.copy(source, goal)
+            else:
+                net.send(source, goal, to)
+
+
+class Gradient:
+    def __init__(self, net, axis, acc, from_core=None, from_x=None, from_far=None, out=None, result=None):
+        self.net, self.axis = net, axis
+        self.acc, self.from_core, self.from_x, self.from_far, self.out = acc, from_core, from_x, from_far, out
+        self.result = acc if result is None else result
+        self.step = (from_far if from_far is not None else acc).shape[axis] // 2
+        self.across = (from_far if from_far is not None else acc).shape[1 - axis]
+
+    def window(self, ref, at, start, count, length=None):
+        along, wide = pl.ds(at, self.step if length is None else length), pl.ds(start, count)
+        return (along, wide) if self.axis == 0 else (wide, along)
+
+    def view(self, ref, *place):
+        return ref.at[self.window(ref, *place)]
+
+    def add(self, to, other, ref, result=None):
+        (rows, cols), (rows_b, cols_b) = to, other
+
+        def body(at):
+            move = lambda r: pl.ds(pl.multiple_of(at.start + r.start, 16), at.size)
+            value = (self.acc[move(rows), cols].astype(F32) + ref[move(rows_b), cols_b].astype(F32)).astype(BF16)
+            if result is None:
+                self.acc[move(rows), cols] = value
+            else:
+                result[move(rows_b), cols_b] = value
+
+        by_rows(rows.size, body)
+
+    def start(self, g_ref):
+        count = 4 * self.step
+        own, other = (self.window(g_ref, i * count, 0, 2 * self.across, count) for i in range(2))
+        self.loaded = self.net.copy(g_ref.at[own], self.acc)
+        self.core = self.net.send(g_ref.at[other], self.from_core, CORE)
+
+    def after_core(self):
+        self.loaded.wait()
+        self.net.local = [copy for copy in self.net.local if copy is not self.loaded]
+        self.net.arrived(self.core)
+        self.x = []
+        for slot in range(2):
+            place = self.window(self.acc, (2 * slot + 1) * self.step, 0, 2 * self.across)
+            self.add(place, place, self.from_core)
+            self.x.append(
+                self.net.send(self.acc.at[place], self.view(self.from_x, slot * self.step, 0, 2 * self.across), X)
+            )
+        for slot in range(2):
+            place = self.window(self.acc, 2 * slot * self.step, 0, 2 * self.across)
+            self.add(place, place, self.from_core)
+
+    def after_x(self):
+        for slot in range(2):
+            self.net.arrived(self.x[slot])
+            to = self.window(self.acc, 2 * slot * self.step, 0, 2 * self.across)
+            self.add(to, self.window(self.from_x, slot * self.step, 0, 2 * self.across), self.from_x)
+
+    def send_far(self, stride=2):
+        self.stride = stride
+        self.far = []
+        for slot in range(2):
+            source = self.view(self.acc, stride * slot * self.step, self.across, self.across)
+            self.far.append(self.net.send(source, self.view(self.from_far, slot * self.step, 0, self.across), FAR))
+
+    def after_far(self):
+        for slot in range(2):
+            self.net.arrived(self.far[slot])
+            to = self.window(self.acc, self.stride * slot * self.step, 0, self.across)
+            result = None if self.result is self.acc else self.result
+            self.add(to, self.window(self.from_far, slot * self.step, 0, self.across), self.from_far, result)
+
+    def send_y(self, stride=2):
+        net, step, across = self.net, self.step, self.across
+        at = lambda slot: pl.multiple_of(stride * slot * step, step)
+        base, start = pl.multiple_of(net.x * step, step), pl.multiple_of(net.y * across, across)
+        goal = self.view(self.out, base, start, across)
+        mine = self.view(self.result, at(net.y), 0, across)
+        self.y = net.send(self.view(self.result, at(1 - net.y), 0, across), goal, Y)
+        net.copy(mine, goal)
+        net.send(mine, goal, X)
+
+    def after_y(self):
+        net, across = self.net, self.across
+        self.net.arrived(self.y)
+        start = pl.multiple_of((1 - net.y) * across, across)
+        place = self.view(self.out, pl.multiple_of(net.x * self.step, self.step), start, across)
+        net.send(place, place, X)
+
+
+def row_back(grad, values, gain):
+    inverse = lax.rsqrt(jnp.mean(values * values, axis=1, keepdims=True) + EPS)
+    hat = values * inverse
+    scaled = grad * gain
+    inner = jnp.mean(scaled * hat, axis=1, keepdims=True)
+    return jnp.sum(grad * hat, axis=0, keepdims=True), inverse * (scaled - hat * inner)
+
+
+def turn_kernel(
+    partial_ref, middle_ref, upstream_ref, gain_ref, down_ref, gate_ref, up_ref,
+    grad_ref, all_ref, term_ref, down_out, gate_out, up_out,
+    first, second, sums, last, total, low, *rest, sizes,
+):
+    buffers, (send, recv, local) = rest[:-3], rest[-3:]
+    net = Wires(send, recv, local, sizes)
+    net.greet([Y, CORE, NEAR, FAR, X])
+    scatter = scatter_flow(net, partial_ref, first, second, sums, last, total)
+    run(scatter)
+    down = Gradient(net, 1, *buffers[0:4])
+    gate = Gradient(net, 0, *buffers[4:8])
+    up = Gradient(net, 0, *buffers[8:12])
+    for flow, ref in ((down, down_ref), (gate, gate_ref), (up, up_ref)):
+        flow.start(ref)
+    down.after_core()
+    run(scatter)
+    gate.after_core()
+    run(scatter)
+    run(scatter)
+    term_ref[...] = jnp.zeros_like(term_ref)
+
+    def rows(at):
+        grad = total[at, :] + last[at, :].astype(F32)
+        term, change = row_back(grad, middle_ref[at, :], gain_ref[...])
+        term_ref[...] += term
+        value = upstream_ref[at, :].astype(F32) + change
+        grad_ref[at, :] = value
+        low[at, :] = value.astype(BF16)
+
+    by_rows(low.shape[0], rows)
+    gather = gather_flow(net, low, all_ref)
+    run(gather)
+    down.after_x()
+    down.send_far()
+    run(gather)
+    up.after_core()
+    run(gather)
+    gate.after_x()
+    gate.send_far()
+    down.after_far()
+    up.after_x()
+    gate.after_far()
+    for flow, ref, wide in ((down, down_out, 1), (gate, gate_out, 1), (up, up_out, 2)):
+        for slot in range(2):
+            source = flow.view(flow.acc, 2 * slot * flow.step, 0, wide * flow.across)
+            net.copy(source, flow.view(ref, slot * flow.step, 0, wide * flow.across))
+    net.finish()
+
+
+def gradient_buffers(size, across, axis, whole=True):
+    shape = lambda a, b: pltpu.VMEM((a, b) if axis == 0 else (b, a), BF16)
+    first = [shape(2 * size, 2 * across), shape(2 * size, 2 * across), shape(size, 2 * across)]
+    return first + [shape(size, across)] if whole else first[:1]
+
+
+def scatter_buffers(rows, width):
+    buffer = lambda kind: pltpu.VMEM((rows, width), kind)
+    return [buffer(BF16), buffer(BF16), buffer(BF16), buffer(BF16), buffer(F32)]
+
+
+def turn(partial, middle, upstream, gain, down, gate, up, sizes):
+    rows, width = middle.shape
+    size, across = width // sizes["narrow"], down.shape[0] // 2
+    return wire_call(
+        turn_kernel, "turn", 4, [VMEM] * 4 + [ANY] * 3, [VMEM, ANY, VMEM, ANY, ANY, ANY],
+        [
+            ((rows, width), F32), ((4 * rows, width), BF16), ((1, width), F32),
+            ((across, size), BF16), ((size, across), BF16), ((size, 2 * across), BF16),
+        ],
+        [
+            *scatter_buffers(rows, width), pltpu.VMEM((rows, width), BF16),
+            *gradient_buffers(size, across, 1), *gradient_buffers(size, across, 0), *gradient_buffers(size, across, 0), *sems(40, 16),
+        ],
+        sizes, 105, partial, middle, upstream, gain[None], down, gate, up,
+    )
+
+
+def owner_kernel(
+    dkv_ref, partial_ref, middle_ref, down_ref, gate_ref, up_ref,
+    mine_ref, layer_ref, down_out, gate_out, up_out,
+    prompt_core, rest_core, prompt, prompt_far, first, second, sums, last, total, rows_low, up_far, up_sums, send, recv, local, *, sizes,
+):
+    net = Wires(send, recv, local, sizes)
+    net.greet([Y, CORE, CORNER, NEAR, FAR, X])
+    count, width = prompt.shape
+    size = width // 4
+    region = lambda i: dkv_ref.at[pl.ds(i * count, count), :]
+    come = net.send(region(1), prompt_core, CORE)
+    rest = net.send(region(3), rest_core, CORE)
+    scatter = scatter_flow(net, partial_ref, first, second, sums, last, total)
+    run(scatter)
+    down, gate = Gradient(net, 1, down_ref, out=down_out), Gradient(net, 0, gate_ref, out=gate_out)
+    up = Gradient(net, 0, up_ref, from_far=up_far, out=up_out, result=up_sums)
+    net.arrived(come)
+
+    def add(at):
+        prompt[at, :] = (dkv_ref[at, :].astype(F32) + prompt_core[at, :].astype(F32)).astype(BF16)
+
+    by_rows(count, add)
+    cols = lambda ref, j: ref.at[:, pl.ds(j * size, size)]
+    far = [net.make(cols(prompt, j), cols(prompt_far, j ^ 1), FAR) for j in range(4)]
+
+    @pl.when(net.far == 1)
+    def _():
+        for copy in far:
+            copy.start()
+
+    up.send_far(1)
+    down.send_y(1)
+    run(scatter)
+    gate.send_y(1)
+    run(scatter)
+    run(scatter)
+
+    def rows(at):
+        rows_low[at, :] = (middle_ref[at, :] + total[at, :] + last[at, :].astype(F32)).astype(BF16)
+
+    by_rows(rows_low.shape[0], rows)
+    spread_flow(net, rows_low, layer_ref)
+    down.after_y()
+    gate.after_y()
+    net.arrived(rest)
+
+    @pl.when(net.far == 1)
+    def _():
+        def add(at):
+            move = pl.ds(pl.multiple_of(at.start + 2 * count, 16), at.size)
+            mine_ref[at, :] = dkv_ref[move, :].astype(F32) + rest_core[at, :].astype(F32)
+
+        by_rows(count, add)
+        for copy in far:
+            copy.wait_send()
+
+    @pl.when(net.far == 0)
+    def _():
+        for copy in far:
+            copy.wait_recv()
+
+        def add(at):
+            mine_ref[at, :] = dkv_ref[at, :].astype(F32) + prompt_core[at, :].astype(F32) + prompt_far[at, :].astype(F32)
+
+        by_rows(count, add)
+
+    net.sent = [copy for copy in net.sent if all(copy is not other for other in far)]
+    up.after_far()
+    up.send_y(1)
+    up.after_y()
+    net.finish()
+
+
+def to_owner(dkv, partial, middle, down, gate, up, sizes):
+    rows, width = middle.shape
+    size, across = width // sizes["narrow"], gate.shape[1]
+    count = dkv.shape[0] // 4
+    block = lambda: pltpu.VMEM((count, dkv.shape[1]), BF16)
+    return wire_call(
+        owner_kernel, "owner", 5, [VMEM] * 6, [VMEM, ANY, ANY, ANY, ANY],
+        [
+            ((count, dkv.shape[1]), F32), ((sizes["narrow"] * rows, size), BF16),
+            ((2 * across, size), BF16), ((size, 2 * across), BF16), ((size, 2 * across), BF16),
+        ],
+        [
+            block(), block(), block(), block(), *scatter_buffers(rows, width), pltpu.VMEM((rows, width), BF16),
+            pltpu.VMEM((size, across), BF16), pltpu.VMEM((size, across), BF16), *sems(40, 16),
+        ],
+        sizes, 80, dkv, partial, middle, down, gate, up,
+    )
+
+
+SUMS = [X, CORE, Y, NEAR, FAR]
+
+
+def end_kernel(
+    partial_ref, x_ref, gain_ref, grad_ref, two_ref, query_ref, key_ref, qkv_ref, out_ref,
+    tokens_ref, gains_ref, qkv_out, out_out,
+    first, second, sums, last, total, rows_low, vectors, *rest, sizes,
+):
+    buffers, (send, recv, local) = rest[:-3], rest[-3:]
+    net = Wires(send, recv, local, sizes)
+    net.greet([Y, CORE, CORNER, NEAR, FAR, X])
+    qkv = Gradient(net, 0, *buffers[0:4], out=qkv_out)
+    out = Gradient(net, 1, *buffers[4:8], out=out_out)
+    qkv.start(qkv_ref)
+    out.start(out_ref)
+    scatter = scatter_flow(net, partial_ref, first, second, sums, last, total)
+    run(scatter)
+    qkv.after_core()
+    out.after_core()
+    run(scatter)
+    run(scatter)
+    run(scatter)
+    width = x_ref.shape[1]
+    size = query_ref.shape[1]
+    block = width // sizes["narrow"]
+    half = block // 2
+    gains_ref[...] = jnp.zeros_like(gains_ref)
+
+    def rows(at):
+        grad = total[at, :] + last[at, :].astype(F32)
+        term, change = row_back(grad, x_ref[at, :].astype(F32), gain_ref[...])
+        gains_ref[:, :width] += term
+        rows_low[at, :] = (grad_ref[at, :] + change).astype(BF16)
+
+    by_rows(rows_low.shape[0], rows)
+    spread_flow(net, rows_low, tokens_ref)
+    for i, ref in enumerate((gains_ref, two_ref)):
+        for slot in range(4):
+            to = (2 * (slot % 2) + jnp.bitwise_xor(net.core, slot // 2)) * block + i * width
+            for j in range(2):
+                sub = net.x if j == 0 else 1 - net.x
+                at = slot * block + j * half
+                vectors[0, :, pl.ds(pl.multiple_of(to + sub * half, half), half)] = ref[:, at : at + half]
+    vectors[0, :, 2 * width : 2 * width + size] = query_ref[...]
+    vectors[0, :, 2 * width + size :] = key_ref[...]
+    qkv.after_x()
+    qkv.send_far()
+    out.after_x()
+    out.send_far()
+    for i, to in enumerate(SUMS):
+        copy = net.send(vectors.at[i], vectors.at[len(SUMS) + 1 + i], to)
+        net.arrived(copy)
+        vectors[i + 1] = vectors[i] + vectors[len(SUMS) + 1 + i]
+    gains_ref[...] = vectors[len(SUMS)]
+    qkv.after_far()
+    qkv.send_y()
+    out.after_far()
+    out.send_y()
+    qkv.after_y()
+    out.after_y()
+    net.finish()
+
+
+def end(partial, x, gain, grad, two, query, key, qkv, out, sizes):
+    rows, width = x.shape
+    size = width // sizes["narrow"]
+    wide, deep = qkv.shape[1], out.shape[0]
+    length = 2 * width + 2 * query.shape[1]
+    return wire_call(
+        end_kernel, "end", 6, [VMEM] * 7 + [ANY] * 2, [ANY, VMEM, ANY, ANY],
+        [((sizes["narrow"] * rows, size), BF16), ((1, length), F32), ((size, wide), BF16), ((deep, size), BF16)],
+        [
+            *scatter_buffers(rows, width), pltpu.VMEM((rows, width), BF16), pltpu.VMEM((2 * len(SUMS) + 1, 1, length), F32),
+            *gradient_buffers(size, wide // 2, 0), *gradient_buffers(size, deep // 2, 1), *sems(40, 16),
+        ],
+        sizes, 90, partial, x, gain[None], grad, two, query, key, qkv, out,
+    )
+
+
 def layout(lengths, group_rows):
     ends = jnp.cumsum(lengths)
     begins = ends - lengths
@@ -722,48 +1084,15 @@
     def over_y(values):
         return exchange(values, "narrow", 2, n_narrow)
 
-    def over_core(values):
-        return exchange(values, "narrow", 1, n_narrow)
-
-    def over_z(values):
-        return exchange(values, "wide", 1, n_wide)
-
     def over_far(values):
         return exchange(values, "wide", 2, n_wide)
 
-    def over_x(values):
-        return exchange(values, "dp", 1, n_dp)
-
-    def gather_rows(values):
-        half = values.shape[0] // 2
-        first, second = values[:half], values[half:]
-        first_y, second_z = over_y(first), over_z(second)
-        come = over_z(join([first, first_y]))
-        first_z, first_d = come[:half], come[half:]
-        come = over_y(join([second, second_z]))
-        second_y, second_d = come[:half], come[half:]
-        return join([first, second, first_y, second_y, first_z, second_z, first_d, second_d])
-
-    def scatter_rows(partial):
-        half = partial.shape[0] // 8
-        part = lambda i: partial[i * half : (i + 1) * half]
-        come = over_z(join([part(4), part(6)]))
-        first = part(0).astype(F32) + come[:half]
-        first_y = (part(2).astype(F32) + come[half:]).astype(BF16)
-        come = over_y(join([part(3), part(7)]))
-        second = part(1).astype(F32) + come[:half]
-        second_z = (part(5).astype(F32) + come[half:]).astype(BF16)
-        first = first + over_y(first_y).astype(F32)
-        second = second + over_z(second_z).astype(F32)
-        return join([first, second])
-
-    def all_sum(values):
-        for axis, size in (("dp", n_dp), ("narrow", n_narrow), ("wide", n_wide)):
-            distance = 1
-            while distance < size:
-                values = values + exchange(values, axis, distance, size)
-                distance *= 2
-        return values
+    def over_groups(values, kind):
+        distance = 2
+        while distance < n_dp:
+            values = values.astype(F32) + exchange(values.astype(kind), "dp", distance, n_dp).astype(F32)
+            distance *= 2
+        return values.astype(F32)
 
     def on_device(
         tokens, continuation_lengths, attention_gain, query_weight, key_weight, value_weight, head_gate, query_gain, key_gain,
@@ -794,81 +1123,12 @@
 
         owners = [2 * (i % 2) + (core ^ (i // 2)) for i in range(4)]
 
-        def from_local(values):
-            out = jnp.zeros((rows_wide, width_local), values.dtype)
-            for r in RELATIVE:
-                slot = 2 * (r % 2) + (y ^ (r // 2))
-                part = by_x(cut(values, slot * width_local, width_local, 1), 1)
-                if r:
-                    part = exchange(part, "narrow", r, n_narrow)
-                out = lax.dynamic_update_slice_in_dim(out, part, (narrow ^ r) * rows_local, 0)
-            return out
-
         def relative_vector(vector):
             return join([by_x(cut(vector, i * width_local, width_local, 0), 0) for i in owners])
-
-        def absolute_vector(vector):
-            out = jnp.zeros((width,), vector.dtype)
-            for at, i in enumerate(owners):
-                part = by_x(vector[at * width_local : (at + 1) * width_local], 0)
-                out = lax.dynamic_update_slice_in_dim(out, part, i * width_local, 0)
-            return out
-
-        def norm(values, gain):
-            inverse = lax.rsqrt(jnp.mean(values * values, axis=1, keepdims=True) + EPS)
-            hat = values * inverse
-            return inverse, hat, (hat * gain).astype(BF16)
-
-        def norm_back(grad, hat, inverse, gain):
-            scaled = grad * gain
-            inner = jnp.mean(scaled * hat, axis=1, keepdims=True)
-            return jnp.sum(grad * hat, axis=0), inverse * (scaled - hat * inner)
 
         def piece_of(weight, i, axis):
             half = weight.shape[1 - axis] // 2
             return cut(cut(weight, x * quarter, quarter, axis), i * half, half, 1 - axis)
-
-        def reduce_first(first, second, axis, *ready):
-            step = first.shape[axis] // 4
-            piece = lambda v, i: lax.slice_in_dim(v, i * step, (i + 1) * step, axis=axis)
-            total = first + over_core(second.astype(BF16)).astype(F32)
-            send = join([piece(total, 1), piece(total, 3)], axis).astype(BF16)
-            come = over_x(after(send, *ready) if ready else send)
-            total = join([piece(total, 0), piece(total, 2)], axis) + come.astype(F32)
-            distance = 2
-            while distance < n_dp:
-                total = total + exchange(total.astype(BF16), "dp", distance, n_dp).astype(F32)
-                distance *= 2
-            return total, come
-
-        def reduce_second(total, axis, *ready):
-            across = 1 - axis
-            count = total.shape[across] // 2
-            send = lax.slice_in_dim(total, count, 2 * count, axis=across).astype(BF16)
-            come = over_far(after(send, *ready) if ready else send)
-            return (lax.slice_in_dim(total, 0, count, axis=across) + come.astype(F32)).astype(BF16)
-
-        def reduce_third(total, axis, *ready):
-            step = total.shape[axis] // 2
-            piece = lambda i: cut(total, i * step, step, axis)
-            send = piece(1 - y)
-            ours = join([piece(y), over_y(after(send, *ready) if ready else send)], 1 - axis)
-            return ours, over_x(ours)
-
-        def reduce_last(ours, theirs, axis, widths):
-            across = 1 - axis
-            outs, at = [], 0
-            count = sum(widths)
-            for length in widths:
-                sides = []
-                for v in (ours, theirs):
-                    a = lax.slice_in_dim(v, at, at + length, axis=across)
-                    b = lax.slice_in_dim(v, count + at, count + at + length, axis=across)
-                    sides.append(join([jnp.where(y == 0, a, b), jnp.where(y == 0, b, a)], across))
-                a, b = sides
-                outs.append(join([jnp.where(x == 0, a, b), jnp.where(x == 0, b, a)], axis).astype(F32))
-                at += length
-            return outs
 
         gain_one, gain_two = relative_vector(attention_gain), relative_vector(feedforward_gain)
         lane_pad = ((0, 0), (0, LANES - heads // 2))
@@ -921,9 +1181,6 @@
         middle, normed_two_all, gate_up, down = to_middle(
             partial, inputs, gain_two, gate_weight, up_weight, down_weight, from_y + from_far, sizes
         )
-        inputs = inputs.astype(F32)
-        inverse_one, hat_one, _ = norm(inputs, gain_one)
-        inverse_two, hat_two, _ = norm(middle, gain_two)
         both = dot_rows(normed_two_all, gate_up)
         hidden_cols = gate_weight.shape[1]
         gate_pre, up_pre = both[:, :hidden_cols], both[:, hidden_cols:]
@@ -934,69 +1191,44 @@
         gate_grad = hidden_grad * up_pre * gate_sigmoid * (1.0 + gate_pre * (1.0 - gate_sigmoid))
         up_grad = hidden_grad * silu
         gate_up_low = join([gate_grad, up_grad], 1).astype(BF16)
-        normed_two_grad = scatter_rows(dot_trans(gate_up_low, gate_up).astype(BF16))
-        gain_two_term, change = norm_back(normed_two_grad, hat_two, inverse_two, gain_two)
-        middle_grad = upstream.astype(F32) + change
-        middle_low = middle_grad.astype(BF16)
-        middle_all = gather_rows(middle_low)
-        half = width // 2
-        down_total, down_x = reduce_first(
-            dot_inner(hidden, upstream_all[:, :half]), dot_inner(hidden, upstream_all[:, half:]), 1
-        )
+        partial = dot_trans(gate_up_low, gate_up).astype(BF16)
         gate_low, up_low = gate_up_low[:, :hidden_cols], gate_up_low[:, hidden_cols:]
-        gate_total, gate_x = reduce_first(
-            dot_inner(normed_two_all[:, :half], gate_low), dot_inner(normed_two_all[:, half:], gate_low), 0, down_x
-        )
-        up_total, up_x = reduce_first(
-            dot_inner(normed_two_all[:, :half], up_low), dot_inner(normed_two_all[:, half:], up_low), 0, gate_x
+        down_sums = dot_inner(hidden, upstream_all).astype(BF16)
+        gate_sums = dot_inner(normed_two_all, gate_low).astype(BF16)
+        up_sums = dot_inner(normed_two_all, up_low).astype(BF16)
+        middle_grad, middle_all, two_term, down_part, gate_part, up_part = turn(
+            partial, middle, upstream, gain_two, down_sums, gate_sums, up_sums, sizes
         )
         gated_grad = dot_trans(middle_all, out_weight)
         dq, dkv, logit_grad = attend_back(
             table, q, kv_all, my_index, my_start, raw, context, inverse_total, gated_grad, pairs, size
         )
-        down_total = reduce_second(down_total, 1)
-        gate_total = reduce_second(gate_total, 0, down_total)
-        mlp_term = scatter_rows(dot_rows(after(hidden, middle_all), down).astype(BF16))
-        layer_output = from_local((middle + mlp_term).astype(BF16))
-        out_total, _ = reduce_first(
-            dot_inner(gated, middle_all[:, :half]), dot_inner(gated, middle_all[:, half:]), 1, up_x
+        partial = dot_rows(hidden, down).astype(BF16)
+        dkv_mine, layer_output, down_gradient, gate_gradient, up_gradient = to_owner(
+            dkv, partial, middle, down_part, gate_part, up_part, sizes
         )
-
-        part = lambda i: dkv[i * rows_wide : (i + 1) * rows_wide]
-        come = over_core(join([part(1), part(3)]))
-        prompt = part(0).astype(F32) + come[:rows_wide].astype(F32)
-        rest = part(2).astype(F32) + come[rows_wide:].astype(F32)
-        far_grad = lax.ppermute(turn_pairs(prompt.astype(BF16)), "wide", [(i + 2, i) for i in near])
-        down_ours, down_theirs = reduce_third(down_total, 1, dkv)
-        gate_ours, gate_theirs = reduce_third(gate_total, 0, down_ours)
-        far_grad = after(far_grad, down_theirs, gate_theirs)
-        dkv_mine = jnp.where(z_far == 0, prompt + far_grad.astype(F32), rest)
-        low, query_gain_term, key_gain_term = project_back(
+        low, query_term, key_term = project_back(
             dq, dkv_mine, raw, cosine, sine, query_gain, key_gain, logit_grad, heads, pairs, size, scale, log_two
         )
-        up_total = reduce_second(up_total, 0, far_grad)
-        out_total = reduce_second(out_total, 1, far_grad)
-        normed_grad = scatter_rows(dot_trans(low, joined_weight).astype(BF16))
-        qkv_total, _ = reduce_first(
-            dot_inner(normed_all[:, :half], low), dot_inner(normed_all[:, half:], low), 0
+        partial = dot_trans(low, joined_weight).astype(BF16)
+        qkv_sums = dot_inner(normed_all, low).astype(BF16)
+        out_sums = dot_inner(gated, middle_all).astype(BF16)
+        tokens_gradient, gains, qkv_gradient, output_gradient = end(
+            partial, inputs, gain_one, middle_grad, two_term, query_term, key_term, qkv_sums, out_sums, sizes
         )
-        qkv_total = reduce_second(qkv_total, 0, up_total, out_total)
-        up_ours, up_theirs = reduce_third(up_total, 0, low)
-        out_ours, out_theirs = reduce_third(out_total, 1, low)
-        gain_one_term, change = norm_back(normed_grad, hat_one, inverse_one, gain_one)
-        tokens_gradient = from_local((middle_grad + change).astype(BF16)).astype(F32)
-        gains = all_sum(
-            join([absolute_vector(gain_one_term), absolute_vector(gain_two_term), query_gain_term[0], key_gain_term[0]])
+        tokens_gradient = tokens_gradient.astype(F32)
+        gains = over_groups(gains[0], F32)
+        qkv_gradient = over_groups(qkv_gradient, BF16)
+        down_gradient, gate_gradient, up_gradient, output_gradient = (
+            over_groups(v, BF16) for v in (down_gradient, gate_gradient, up_gradient, output_gradient)
         )
-        qkv_ours, qkv_theirs = reduce_third(qkv_total, 0)
-        query_gradient, key_gradient, value_gradient, gates_gradient = reduce_last(
-            qkv_ours, qkv_theirs, 0, [heads // 2 * size, pairs // 2 * size, pairs // 2 * size, LANES]
-        )
-        head_gate_gradient = join([gates_gradient[:, : heads // 2], gates_gradient[:, LANES : LANES + heads // 2]], 1)
-        down_gradient, = reduce_last(down_ours, down_theirs, 1, [hidden_cols // 2])
-        gate_gradient, = reduce_last(gate_ours, gate_theirs, 0, [hidden_cols // 2])
-        up_gradient, = reduce_last(up_ours, up_theirs, 0, [hidden_cols // 2])
-        output_gradient, = reduce_last(out_ours, out_theirs, 1, [output_weight.shape[0] // 2])
+        block = qkv_gradient.shape[1] // 2
+        query_cols, key_cols = heads // 2 * size, pairs // 2 * size
+        take = lambda at, count: join([qkv_gradient[:, at + i * block : at + i * block + count] for i in range(2)], 1)
+        query_gradient = take(0, query_cols)
+        key_gradient = take(query_cols, key_cols)
+        value_gradient = take(query_cols + key_cols, key_cols)
+        head_gate_gradient = take(query_cols + 2 * key_cols, heads // 2)
         return (
             layer_output,
             tokens_gradient,

time: 929 us -> 941 us (1.013)
  Pallas kernels: 307 us -> 679 us
  waiting for transfers between devices: 291 us -> 24.7 us
  starting transfers between devices: 89.1 us -> 17.9 us
  other arithmetic: 49.7 us -> 38.7 us
  local copies, waits for them, and re-layouts: 45.1 us -> 35.4 us
    pallas_call x3 -> x6, Pallas kernels: 247 us -> 620 us  [wire_call(): pl.pallas_call(functools.partial(kernel, sizes=sizes), in_specs=specs, ou...]
    ppermute x59 -> x6, waiting for transfers between devices: 288 us -> 24.7 us  [exchange(): return lax.ppermute(values, axis, [(i, i ^ distance) for i in range(size)])]
    ppermute x59 -> x6, starting transfers between devices: 87.8 us -> 17.9 us  [exchange(): return lax.ppermute(values, axis, [(i, i ^ distance) for i in range(size)])]
    unnamed x119 -> x78, local copies, waits for them, and re-layouts: 22.2 us -> 10.7 us
    dot_general x10 -> x5, matrix products: 45.4 us -> 40.2 us  [dot_inner(): lax.dot_general(left, right, (((0,), (0,)), ((), ())), preferred_element_...]
  transfers between devices with their start and end apart: 60 -> 6, of which waited for: 30 -> 3; matrix products, arithmetic and copies ran while one was open for 16% -> 6% of each run, Pallas kernels for 6% -> 3%
where the time goes in v4:
time: 941 us; the launch traced here: 930 us
  Pallas kernels  679 us (72%)
  matrix products  133 us (14%)
  other arithmetic  38.7 us (4%)
  local copies, waits for them, and re-layouts  35.4 us (4%)
  waiting for transfers between devices  24.7 us (3%)
  starting transfers between devices  17.9 us (2%)
    pallas_call x6, Pallas kernels, wire_call(): pl.pallas_call(functools.partial(kernel, sizes=sizes), in_specs=specs, ou...  620 us
    dot_general x4, matrix products, dot_trans(): lax.dot_general(left, right, (((1,), (1,)), ((), ())), preferred_element_...  49.1 us
    dot_general x4, matrix products, dot_rows(): return jnp.dot(left, right, preferred_element_type=F32)  43.4 us
    dot_general x5, matrix products, dot_inner(): lax.dot_general(left, right, (((0,), (0,)), ((), ())), preferred_element_...  40.2 us
    pallas_call x1, Pallas kernels, attend_back(): pl.pallas_call(functools.partial(backward_kernel, pairs=pairs, repeat=hea...  26 us
    ppermute x6, waiting for transfers between devices, exchange(): return lax.ppermute(values, axis, [(i, i ^ distance) for i in range(size)])  24.7 us
  transfers between devices with their start and end apart: 6, of which 3 were waited for; matrix products, arithmetic and copies ran while one was open for 6% of the time, Pallas kernels for 3%

profile of v4, /device:TPU:0, one launch (start us, length us, event | category | flops | bytes accessed | tf_op | source)
XLA Modules:
  0.0 930.3 jit_solution(11931782352735333336)
XLA Ops:
  10.5 69.8 %begin.1 = (bf16[256,2048]{1,0:T(8,128)(2,1)}, bf16[1024,2048]{1,0:T(8,128)(2,1)}, bf16[2048,1280]{1,0:T(8,128)(2,1)}, bf16[512,2048]{1,0:T(8,128)(2,1)}) custom-call(bf16[1024,512]{1,0:T(8,128)(2,1)} %tokens_ref.1, f32[1,2048]{1,0:T(1,128)} %bitcast.58, bf16[512,1280]{1,0:T(8,128)(2,1)} %copy-done.2, bf16[512,512]{1,0:T(8,128)(2,1)} %out_ref.1), custom_call_target="tpu_custom_call" | custom-call | bytes 165000000 | tf_op jit(solution)/shard_map/begin/pallas_call | solution.py:546
  112.2 2.6 fusion.8
  115.8 10.4 %fusion.22.raw_ref.own_ref.other_ref = f32[1024,1280]{1,0:T(8,128)} fusion(bf16[1024,2048]{1,0:T(8,128)(2,1)} %get-tuple-element.58, bf16[2048,1280]{1,0:T(8,128)(2,1)} %get-tuple-element.59), kind=kOutput, calls=%fused_computation.95 | convolution fusion | flops 5368709120 | bytes 14680064 | tf_op jit(solution)/shard_map/dot_general | solution.py:22
  129.8 6.3 post.1
  138.7 68.3 %keys.1 = (bf16[4096,512]{1,0:T(8,128)(2,1)}, bf16[256,2048]{1,0:T(8,128)(2,1)}, bf16[1024,2048]{1,0:T(8,128)(2,1)}) custom-call(bf16[1024,512]{1,0:T(8,128)(2,1)} %get-tuple-element.65.kv_ref, bf16[1024,512]{1,0:T(8,128)(2,1)} %cotangent_ref.1), custom_call_target="tpu_custom_call" | custom-call | bytes 165000000 | tf_op jit(solution)/shard_map/keys/pallas_call | solution.py:546
  208.8 12.4 %collective-permute-start.5 = (bf16[768,256]{1,0:T(8,128)(2,1)S(1)}, bf16[768,256]{1,0:T(8,128)(2,1)S(1)}, u32[]{:S(2)}, u32[]{:S(2)}) collective-permute-start(bf16[768,256]{1,0:T(8,128)(2,1)S(1)} %dynamic_slice.109), channel_id=1, source_target_pairs={{0,8},{4,12},{8,0},{12,4},{1,9},{5,13},{9,1},{13,5},{2,10},{6,14},... | collective-permute-start | bytes 1179656 | tf_op jit(solution)/shard_map/ppermute | solution.py:34
  221.3 2.8 collective-permute-start.3
  224.2 18.5 %attend.1 = (bf16[1024,512]{1,0:T(8,128)(2,1)}, f32[1024,512]{1,0:T(8,128)}, f32[1024,512]{1,0:T(8,128)}) custom-call(s32[4,5]{1,0:T(4,128)} %stack.15.table_ref, bf16[1024,512]{1,0:T(8,128)(2,1)} %get-tuple-element.60.q_ref, bf16[4096,512]{1,0:T(8,128)(2,1)} %get-tuple-element.66.kv_ref, s32[1024,1]{1,0:T(8,128)} %copy.57.row_ref, ...), custom_call_target="tpu_custom_call" | custom-call | flops 20000000000 | bytes 12000000 | tf_op jit(solution)/shard_map/attend/pallas_call | solution.py:240
  242.7 5.5 convolution_convert_fusion.6.partial_ref
  248.2 8.3 collective-permute-done.5.down_far_ref
  256.5 8.4 collective-permute-done.4.up_far_ref
  264.9 8.0 collective-permute-done.3.gate_far_ref
  273.6 109.3 %middle.1 = (f32[256,2048]{1,0:T(8,128)}, bf16[1024,2048]{1,0:T(8,128)(2,1)}, bf16[2048,3072]{1,0:T(8,128)(2,1)}, bf16[1536,2048]{1,0:T(8,128)(2,1)}) custom-call(bf16[1024,2048]{1,0:T(8,128)(2,1)} %convolution_convert_fusion.6.partial_ref, bf16[256,2048]{1,0:T(8,128)(2,1)} %get-tuple-element.72.x_ref, f32[1,2048]{1,0:T(1,128)} %bitcast.60, ...), custom_call_target="tpu_custom_call" | custom-call | bytes 240000000 | tf_op jit(solution)/shard_map/middle/pallas_call | solution.py:546
  382.9 19.3 %fusion.23 = f32[1024,3072]{1,0:T(8,128)} fusion(bf16[1024,2048]{1,0:T(8,128)(2,1)} %get-tuple-element.77, bf16[2048,3072]{1,0:T(8,128)(2,1)} %get-tuple-element.78), kind=kOutput, calls=%fused_computation.96 | convolution fusion | flops 12884901888 | bytes 29360128 | tf_op jit(solution)/shard_map/dot_general | solution.py:22
  402.2 14.7 %multiply_convert_fusion.2 = (bf16[1024,1536]{1,0:T(8,128)(2,1)}, bf16[1024,1536]{1,0:T(8,128)(2,1)}, bf16[1024,1536]{1,0:T(8,128)(2,1)S(1)}) fusion(f32[1024,3072]{1,0:T(8,128)} %fusion.23, bf16[1024,2048]{1,0:T(8,128)(2,1)} %get-tuple-element.69, bf16[1536,2048]{1,0:T(8,128)(2,1)S(1)} %copy-done.24), kind=kOutput, calls=%fused_computation.10 | convolution fusion | flops 6466043904 | bytes 32505856 | tf_op jit(solution)/shard_map/dot_general | solution.py:26
  416.9 8.2 convolution_convert_fusion.4.partial_ref
  425.1 8.9 convolution_convert_fusion.3.down_ref
  434.0 8.8 convolution_convert_fusion.2.gate_ref
  442.8 18.4 %fusion.5.partial_ref = bf16[1024,2048]{1,0:T(8,128)(2,1)} fusion(bf16[2048,3072]{1,0:T(8,128)(2,1)} %get-tuple-element.78, bf16[1024,1536]{1,0:T(8,128)(2,1)S(1)} %copy-done.32, bf16[1024,1536]{1,0:T(8,128)(2,1)} %get-tuple-element.133), kind=kOutput, calls=%fused_computation.14 | convolution fusion | flops 12899581952 | bytes 23068672 | tf_op jit(solution)/shard_map/dot_general | solution.py:26
  461.3 11.3 %convolution_convert_fusion.1.up_ref = bf16[2048,1536]{1,0:T(8,128)(2,1)} fusion(bf16[1024,2048]{1,0:T(8,128)(2,1)} %get-tuple-element.77, bf16[1024,1536]{1,0:T(8,128)(2,1)S(1)} %copy-done.32), kind=kOutput, calls=%fused_computation.1 | convolution fusion | flops 6445596672 | bytes 13631488 | tf_op jit(solution)/shard_map/dot_general | solution.py:30
  472.5 121.2 %turn.1 = (f32[256,2048]{1,0:T(8,128)}, bf16[1024,2048]{1,0:T(8,128)(2,1)}, f32[1,2048]{1,0:T(1,128)}, bf16[768,512]{1,0:T(8,128)(2,1)}, bf16[512,768]{1,0:T(8,128)(2,1)}, /*index=5*/bf16[512,1536]{1,0:T(8,128)(2,1)}) custom-call(bf16[1024,2048]{1,0:T(8,128)(2,1)} %fusion.5.partial_ref, f32[256,2048]{1,0:T(8,128)} %get-tuple-element.79.middle_ref, ...), custom_call_target="tpu_custom_call" | custom-call | bytes 315000000 | tf_op jit(solution)/shard_map/turn/pallas_call | solution.py:546
  593.7 5.9 fusion.24.grad_ref
  599.6 26.0 %attend_back.1 = (f32[1024,512]{1,0:T(8,128)}, bf16[4096,512]{1,0:T(8,128)(2,1)}, f32[1024,256]{1,0:T(8,128)}) custom-call(s32[4,5]{1,0:T(4,128)} %stack.15.table_ref, bf16[1024,512]{1,0:T(8,128)(2,1)} %get-tuple-element.60.q_ref, bf16[4096,512]{1,0:T(8,128)(2,1)} %get-tuple-element.66.kv_ref, s32[4,1,256]{2,1,0:T(1,128)} %pad_add_fusion.2.row_ref, ...), custom_call_target="tpu_custom_call" | custom-call | flops 49999998976 | bytes 20000000 | tf_op jit(solution)/shard_map/attend_back/pallas_call | solution.py:336
  625.6 129.9 %owner.1 = (f32[1024,512]{1,0:T(8,128)}, bf16[1024,512]{1,0:T(8,128)(2,1)}, bf16[1536,512]{1,0:T(8,128)(2,1)}, bf16[512,1536]{1,0:T(8,128)(2,1)}, bf16[512,1536]{1,0:T(8,128)(2,1)}) custom-call(bf16[4096,512]{1,0:T(8,128)(2,1)} %get-tuple-element.82.dkv_ref, bf16[1024,2048]{1,0:T(8,128)(2,1)} %convolution_convert_fusion.4.partial_ref, ...), custom_call_target="tpu_custom_call" | custom-call | bytes 240000000 | tf_op jit(solution)/shard_map/owner/pallas_call | solution.py:546
  755.5 8.5 project_back.1
  764.1 10.2 %convolution_convert_fusion.5.partial_ref = bf16[1024,2048]{1,0:T(8,128)(2,1)} fusion(bf16[1024,1280]{1,0:T(8,128)(2,1)} %get-tuple-element.90, bf16[2048,1280]{1,0:T(8,128)(2,1)} %get-tuple-element.59), kind=kOutput, calls=%fused_computation.15 | convolution fusion | flops 5370806272 | bytes 12058624 | tf_op jit(solution)/shard_map/dot_general | solution.py:26
  774.2 7.5 convolution_convert_fusion.qkv_ref
  781.7 3.7 convolution_convert_fusion.7.out_ref
  785.4 121.4 %end.1 = (bf16[1024,512]{1,0:T(8,128)(2,1)}, f32[1,4352]{1,0:T(1,128)}, bf16[512,1280]{1,0:T(8,128)(2,1)}, bf16[512,512]{1,0:T(8,128)(2,1)}) custom-call(bf16[1024,2048]{1,0:T(8,128)(2,1)} %convolution_convert_fusion.5.partial_ref, bf16[256,2048]{1,0:T(8,128)(2,1)} %get-tuple-element.72.x_ref, f32[1,2048]{1,0:T(1,128)} %bitcast.59, ...), custom_call_target="tpu_custom_call" | custom-call | bytes 270000000 | tf_op jit(solution)/shard_map/end/pallas_call | solution.py:546
  913.7 3.0 convert_element_type.71
  917.8 3.6 convert_element_type.74
  923.4 2.1 convert_element_type.76
  (153 shorter events, 65.6 us)
Async XLA Ops:
  0.6 81.5 %copy-start.1 = (bf16[512,1536]{1,0:T(8,128)(2,1)S(1)}, bf16[512,1536]{1,0:T(8,128)(2,1)}, u32[]{:S(2)}) copy-start(bf16[512,1536]{1,0:T(8,128)(2,1)} %up_ref.1) | copy-start | bytes 4718596
  0.7 84.0 %copy-start = (bf16[512,1536]{1,0:T(8,128)(2,1)S(1)}, bf16[512,1536]{1,0:T(8,128)(2,1)}, u32[]{:S(2)}) copy-start(bf16[512,1536]{1,0:T(8,128)(2,1)} %gate_ref.1) | copy-start | bytes 4718596
  3.2 6.2 copy-start.11
  81.6 57.1 %collective-permute-start.2 = (bf16[768,256]{1,0:T(8,128)(2,1)S(1)}, bf16[768,256]{1,0:T(8,128)(2,1)}, u32[]{:S(2)}, u32[]{:S(2)}) collective-permute-start(bf16[768,256]{1,0:T(8,128)(2,1)S(1)} %dynamic_slice.102), channel_id=1, source_target_pairs={{0,2},{1,3},{2,0},{3,1},{4,6},{5,7},{6,4},{7,5},{8,10},{9,11},{10,... | collective-permute-start | bytes 1179656 | tf_op jit(solution)/shard_map/ppermute | solution.py:34
  83.1 55.6 %collective-permute-start.1 = (bf16[256,768]{1,0:T(8,128)(2,1)}, bf16[256,768]{1,0:T(8,128)(2,1)}, u32[]{:S(2)}, u32[]{:S(2)}) collective-permute-start(bf16[256,768]{1,0:T(8,128)(2,1)} %dynamic_slice.101), channel_id=1, source_target_pairs={{0,2},{1,3},{2,0},{3,1},{4,6},{5,7},{6,4},{7,5},{8,10},{9,11},{10,... | collective-permute-start | bytes 1179656 | tf_op jit(solution)/shard_map/ppermute | solution.py:34
  85.6 53.1 %collective-permute-start = (bf16[256,768]{1,0:T(8,128)(2,1)}, bf16[256,768]{1,0:T(8,128)(2,1)}, u32[]{:S(2)}, u32[]{:S(2)}) collective-permute-start(bf16[256,768]{1,0:T(8,128)(2,1)} %dynamic_slice.100), channel_id=1, source_target_pairs={{0,2},{1,3},{2,0},{3,1},{4,6},{5,7},{6,4},{7,5},{8,10},{9,11},{10,... | collective-permute-start | bytes 1179656 | tf_op jit(solution)/shard_map/ppermute | solution.py:34
  115.8 11.4 %copy-start.14 = (s32[256]{0:T(256)S(1)}, s32[256]{0:T(256)}, u32[]{:S(2)}) copy-start(s32[256]{0:T(256)} %copy-done.13) | copy-start | bytes 3076
  115.8 11.4 %copy-start.16 = (s32[256]{0:T(256)S(1)}, s32[256]{0:T(256)}, u32[]{:S(2)}) copy-start(s32[256]{0:T(256)} %copy-done.15) | copy-start | bytes 3076
  115.8 11.4 %copy-start.18 = (s32[256]{0:T(256)S(1)}, s32[256]{0:T(256)}, u32[]{:S(2)}) copy-start(s32[256]{0:T(256)} %copy-done.17) | copy-start | bytes 3076
  115.8 11.4 %copy-start.20 = (s32[256]{0:T(256)S(1)}, s32[256]{0:T(256)}, u32[]{:S(2)}) copy-start(s32[256]{0:T(256)} %copy-done.19) | copy-start | bytes 3076
  115.8 12.0 %copy-start.22 = (s32[256]{0:T(256)S(1)}, s32[256]{0:T(256)}, u32[]{:S(2)}) copy-start(s32[256]{0:T(256)} %copy-done.21) | copy-start | bytes 3076
  126.2 9.9 %copy-start.12 = (f32[512]{0:T(512)S(1)}, f32[512]{0:T(512)}, u32[]{:S(2)}) copy-start(f32[512]{0:T(512)} %get-tuple-element.158) | copy-start | bytes 6148
  208.8 47.6 %collective-permute-start.5 = (bf16[768,256]{1,0:T(8,128)(2,1)S(1)}, bf16[768,256]{1,0:T(8,128)(2,1)S(1)}, u32[]{:S(2)}, u32[]{:S(2)}) collective-permute-start(bf16[768,256]{1,0:T(8,128)(2,1)S(1)} %dynamic_slice.109), channel_id=1, source_target_pairs={{0,8},{4,12},{8,0},{12,4},{1,9},{5,13},{9,1},{13,5},{2,10},{6,14},... | collective-permute-start | bytes 1179656 | tf_op jit(solution)/shard_map/ppermute | solution.py:34
  221.2 43.7 %collective-permute-start.4 = (bf16[256,768]{1,0:T(8,128)(2,1)S(1)}, bf16[256,768]{1,0:T(8,128)(2,1)S(1)}, u32[]{:S(2)}, u32[]{:S(2)}) collective-permute-start(bf16[256,768]{1,0:T(8,128)(2,1)S(1)} %dynamic_slice.108), channel_id=1, source_target_pairs={{0,8},{4,12},{8,0},{12,4},{1,9},{5,13},{9,1},{13,5},{2,10},{6,14},... | collective-permute-start | bytes 1179656 | tf_op jit(solution)/shard_map/ppermute | solution.py:34
  221.3 51.6 %collective-permute-start.3 = (bf16[256,768]{1,0:T(8,128)(2,1)S(1)}, bf16[256,768]{1,0:T(8,128)(2,1)S(1)}, u32[]{:S(2)}, u32[]{:S(2)}) collective-permute-start(bf16[256,768]{1,0:T(8,128)(2,1)S(1)} %dynamic_slice.107), channel_id=1, source_target_pairs={{0,8},{4,12},{8,0},{12,4},{1,9},{5,13},{9,1},{13,5},{2,10},{6,14},... | collective-permute-start | bytes 1179656 | tf_op jit(solution)/shard_map/ppermute | solution.py:34
  224.2 18.5 %copy-start.30 = (bf16[512,2048]{1,0:T(8,128)(2,1)S(1)}, bf16[512,2048]{1,0:T(8,128)(2,1)}, u32[]{:S(2)}) copy-start(bf16[512,2048]{1,0:T(8,128)(2,1)} %get-tuple-element.71) | copy-start | bytes 6291460
  256.5 16.4 %copy-start.8 = (bf16[768,256]{1,0:T(8,128)(2,1)}, bf16[768,256]{1,0:T(8,128)(2,1)S(1)}, u32[]{:S(2)}) copy-start(bf16[768,256]{1,0:T(8,128)(2,1)S(1)} %collective-permute-done.5.down_far_ref) | copy-start | bytes 1179652
  264.9 8.0 copy-start.9
  382.9 19.3 %copy-start.24 = (bf16[1536,2048]{1,0:T(8,128)(2,1)S(1)}, bf16[1536,2048]{1,0:T(8,128)(2,1)}, u32[]{:S(2)}) copy-start(bf16[1536,2048]{1,0:T(8,128)(2,1)} %get-tuple-element.76) | copy-start | bytes 18874372
  416.9 8.2 copy-start.26
  425.1 8.9 copy-start.28
  425.1 8.9 copy-start.33
  434.0 8.8 copy-start.32
  764.0 10.2 %copy-start.25 = (bf16[1024,2048]{1,0:T(8,128)(2,1)S(1)}, bf16[1024,2048]{1,0:T(8,128)(2,1)}, u32[]{:S(2)}) copy-start(bf16[1024,2048]{1,0:T(8,128)(2,1)} %get-tuple-element.58) | copy-start | bytes 12582916
  764.0 10.2 %copy-start.29 = (bf16[1024,1280]{1,0:T(8,128)(2,1)S(1)}, bf16[1024,1280]{1,0:T(8,128)(2,1)}, u32[]{:S(2)}) copy-start(bf16[1024,1280]{1,0:T(8,128)(2,1)} %get-tuple-element.90) | copy-start | bytes 7864324
  774.2 7.5 copy-start.27
  774.2 7.5 copy-start.31
  910.4 6.3 copy-start.7
  913.7 7.7 copy-start.4
  917.8 5.7 copy-start.3
  923.4 3.8 copy-start.6
  923.4 5.5 copy-start.5
  (8 other events, 5.2 us)

commit v5 on v4

--- a/solution.py
+++ b/solution.py
@@ -505,7 +505,10 @@
     lax.fori_loop(0, count // step, lambda i, _: (body(pl.ds(pl.multiple_of(i * step, step), step)), 0)[1], 0)
 
 
-def begin_kernel(tokens_ref, gain_ref, qkv_ref, out_ref, x_ref, all_ref, joined_ref, output_ref, here, normed, send, recv, local, *, sizes):
+def begin_kernel(
+    tokens_ref, cotangent_ref, gain_ref, qkv_ref, out_ref, x_ref, rows_ref, all_ref, joined_ref, output_ref,
+    here, normed, there, send, recv, local, *, sizes,
+):
     net = Wires(send, recv, local, sizes)
     net.greet([Y, CORE, CORNER, NEAR, FAR, X])
     rows = local_flow(net, tokens_ref, here)
@@ -529,8 +532,17 @@
     run(gather)
     across = out_ref.shape[0] // 2
     output = weight_flow(net, out_ref, output_ref, 1, 0, across, across)
-    for flow in (joined, output, gather, joined, gather, joined, output, joined, output, output, output):
+    for flow in (joined, gather, output, joined, gather):
         run(flow)
+    rows = local_flow(net, cotangent_ref, there)
+    for flow in (joined, output, joined, output, output, output):
+        run(flow)
+    for copy in rows[:2]:
+        copy.wait()
+    net.local = [copy for copy in net.local if all(copy is not other for other in rows[:2])]
+    for copy in rows[2:]:
+        net.arrived(copy)
+    net.copy(there, rows_ref)
     net.finish()
 
 
@@ -555,43 +567,36 @@
     )(*args)
 
 
-def begin(tokens, gain, qkv, out, sizes):
+def begin(tokens, cotangent, gain, qkv, out, sizes):
     rows, width = tokens.shape[0] // sizes["narrow"], gain.shape[0]
+    row = pltpu.VMEM((rows, width), BF16)
     return wire_call(
-        begin_kernel, "begin", 1, [ANY, VMEM, VMEM, VMEM], [VMEM, ANY, ANY, ANY],
-        [((rows, width), BF16), ((4 * rows, width), BF16), ((width, qkv.shape[1]), BF16), ((out.shape[0], width), BF16)],
-        [pltpu.VMEM((rows, width), BF16), pltpu.VMEM((rows, width), BF16), *sems(48, 8)], sizes, 55,
-        tokens, gain[None], qkv, out,
+        begin_kernel, "begin", 1, [ANY, ANY, VMEM, VMEM, VMEM], [VMEM, ANY, ANY, ANY, ANY],
+        [
+            ((rows, width), BF16), ((rows, width), BF16), ((4 * rows, width), BF16), ((width, qkv.shape[1]), BF16),
+            ((out.shape[0], width), BF16),
+        ],
+        [row, row, row, *sems(48, 16)], sizes, 55, tokens, cotangent, gain[None], qkv, out,
     )
 
 
-def keys_kernel(kv_ref, cotangent_ref, keys_ref, rows_ref, all_ref, here, send, recv, local, *, sizes):
+def keys_kernel(kv_ref, keys_ref, send, recv, local, *, sizes):
     net = Wires(send, recv, local, sizes)
-    net.greet([Y, CORE, CORNER, NEAR, FAR])
+    net.greet([CORE, FAR])
     count, width = kv_ref.shape
     size = width // 4
     part = lambda i, j: keys_ref.at[pl.ds(i, count), pl.ds(j * size, size)]
     base = pl.multiple_of(net.far * 2 * count, count)
     far = [net.make(kv_ref.at[:, pl.ds(j * size, size)], part(0, j ^ 1), FAR) for j in range(4)]
+    on = [net.make(part(0, j ^ 1), part(count, j ^ 1), CORE) for j in range(4)]
 
     @pl.when(net.far == 0)
     def _():
         for copy in far:
             copy.start()
 
-    rows = local_flow(net, cotangent_ref, here)
     net.copy(kv_ref, keys_ref.at[pl.ds(base, count), :])
     net.send(kv_ref, keys_ref.at[pl.ds(base + count, count), :], CORE)
-    rows[0].wait()
-    rows[1].wait()
-    net.local = net.local[2:]
-    for copy in rows[2:]:
-        net.arrived(copy)
-    net.copy(here, rows_ref)
-    gather = gather_flow(net, here, all_ref)
-    for _ in range(3):
-        run(gather)
-    on = [net.make(part(0, j ^ 1), part(count, j ^ 1), CORE) for j in range(4)]
 
     @pl.when(net.far == 1)
     def _():
@@ -610,13 +615,10 @@
     net.finish()
 
 
-def exchange_keys(kv, cotangent, width, sizes):
-    rows = cotangent.shape[0] // sizes["narrow"]
+def exchange_keys(kv, sizes):
     return wire_call(
-        keys_kernel, "keys", 2, [VMEM, ANY], [ANY, ANY, ANY],
-        [((4 * kv.shape[0], kv.shape[1]), BF16), ((rows, width), BF16), ((4 * rows, width), BF16)],
-        [pltpu.VMEM((rows, width), BF16), *sems(24, 8)], sizes, 55, kv, cotangent,
-    )
+        keys_kernel, "keys", 2, [VMEM], [ANY], [((4 * kv.shape[0], kv.shape[1]), BF16)], [*sems(16, 4)], sizes, 45, kv,
+    )[0]
 
 
 def scatter_flow(net, partial_ref, first_ref, second_ref, send_ref, last_ref, total_ref):
@@ -683,10 +685,10 @@
     gather = gather_flow(net, normed, all_ref)
     run(gather)
     run(flows[0])
+    run(flows[1])
     run(gather)
+    run(flows[2])
     run(gather)
-    run(flows[1])
-    run(flows[2])
     for flow in flows:
         run(flow)
     net.finish()
@@ -723,91 +725,87 @@
                 net.send(source, goal, to)
 
 
+def add_rows(target, terms):
+    ref, (rows, cols) = target
+
+    def body(at):
+        move = lambda r: pl.ds(pl.multiple_of(at.start + r.start, 16), at.size)
+        value = sum(term[move(r), c].astype(F32) for term, (r, c) in terms)
+        ref[move(rows), cols] = value.astype(BF16)
+
+    by_rows(rows.size, body)
+
+
 class Gradient:
-    def __init__(self, net, axis, acc, from_core=None, from_x=None, from_far=None, out=None, result=None):
-        self.net, self.axis = net, axis
-        self.acc, self.from_core, self.from_x, self.from_far, self.out = acc, from_core, from_x, from_far, out
-        self.result = acc if result is None else result
-        self.step = (from_far if from_far is not None else acc).shape[axis] // 2
-        self.across = (from_far if from_far is not None else acc).shape[1 - axis]
-
-    def window(self, ref, at, start, count, length=None):
-        along, wide = pl.ds(at, self.step if length is None else length), pl.ds(start, count)
+    def __init__(self, net, axis, step, across):
+        self.net, self.axis, self.step, self.across = net, axis, step, across
+        self.order = (1 - net.y, net.y)
+        self.x, self.far = [], []
+
+    def window(self, at, start, count, length=None):
+        step = self.step if length is None else length
+        hint = lambda v, unit: v if isinstance(v, int) else pl.multiple_of(v, unit)
+        along, wide = pl.ds(hint(at, self.step), step), pl.ds(hint(start, self.across), count)
         return (along, wide) if self.axis == 0 else (wide, along)
 
-    def view(self, ref, *place):
-        return ref.at[self.window(ref, *place)]
-
-    def add(self, to, other, ref, result=None):
-        (rows, cols), (rows_b, cols_b) = to, other
-
-        def body(at):
-            move = lambda r: pl.ds(pl.multiple_of(at.start + r.start, 16), at.size)
-            value = (self.acc[move(rows), cols].astype(F32) + ref[move(rows_b), cols_b].astype(F32)).astype(BF16)
-            if result is None:
-                self.acc[move(rows), cols] = value
-            else:
-                result[move(rows_b), cols_b] = value
-
-        by_rows(rows.size, body)
-
-    def start(self, g_ref):
+    def start(self, g_ref, acc, from_core):
+        self.acc, self.from_core = acc, from_core
         count = 4 * self.step
-        own, other = (self.window(g_ref, i * count, 0, 2 * self.across, count) for i in range(2))
-        self.loaded = self.net.copy(g_ref.at[own], self.acc)
-        self.core = self.net.send(g_ref.at[other], self.from_core, CORE)
-
-    def after_core(self):
+        own, other = (self.window(i * count, 0, 2 * self.across, count) for i in range(2))
+        self.loaded = self.net.copy(g_ref.at[own], acc)
+        self.core = self.net.send(g_ref.at[other], from_core, CORE)
+
+    def wait_core(self):
         self.loaded.wait()
         self.net.local = [copy for copy in self.net.local if copy is not self.loaded]
         self.net.arrived(self.core)
-        self.x = []
-        for slot in range(2):
-            place = self.window(self.acc, (2 * slot + 1) * self.step, 0, 2 * self.across)
-            self.add(place, place, self.from_core)
-            self.x.append(
-                self.net.send(self.acc.at[place], self.view(self.from_x, slot * self.step, 0, 2 * self.across), X)
-            )
-        for slot in range(2):
-            place = self.window(self.acc, 2 * slot * self.step, 0, 2 * self.across)
-            self.add(place, place, self.from_core)
-
-    def after_x(self):
-        for slot in range(2):
-            self.net.arrived(self.x[slot])
-            to = self.window(self.acc, 2 * slot * self.step, 0, 2 * self.across)
-            self.add(to, self.window(self.from_x, slot * self.step, 0, 2 * self.across), self.from_x)
-
-    def send_far(self, stride=2):
-        self.stride = stride
-        self.far = []
-        for slot in range(2):
-            source = self.view(self.acc, stride * slot * self.step, self.across, self.across)
-            self.far.append(self.net.send(source, self.view(self.from_far, slot * self.step, 0, self.across), FAR))
-
-    def after_far(self):
-        for slot in range(2):
-            self.net.arrived(self.far[slot])
-            to = self.window(self.acc, self.stride * slot * self.step, 0, self.across)
-            result = None if self.result is self.acc else self.result
-            self.add(to, self.window(self.from_far, slot * self.step, 0, self.across), self.from_far, result)
-
-    def send_y(self, stride=2):
-        net, step, across = self.net, self.step, self.across
-        at = lambda slot: pl.multiple_of(stride * slot * step, step)
-        base, start = pl.multiple_of(net.x * step, step), pl.multiple_of(net.y * across, across)
-        goal = self.view(self.out, base, start, across)
-        mine = self.view(self.result, at(net.y), 0, across)
-        self.y = net.send(self.view(self.result, at(1 - net.y), 0, across), goal, Y)
-        net.copy(mine, goal)
-        net.send(mine, goal, X)
+
+    def core_to_x(self, from_x):
+        self.wait_core()
+        self.from_x = from_x
+        for slot in self.order:
+            place = self.window((2 * slot + 1) * self.step, 0, 2 * self.across)
+            add_rows((self.acc, place), [(self.acc, place), (self.from_core, place)])
+            goal = from_x.at[self.window(slot * self.step, 0, 2 * self.across)]
+            self.x.append(self.net.send(self.acc.at[place], goal, X))
+
+    def x_end(self, k, from_far=None):
+        slot = self.order[k]
+        self.net.arrived(self.x[k])
+        for start in (self.across, 0):
+            place = self.window(2 * slot * self.step, start, self.across)
+            come = self.window(slot * self.step, start, self.across)
+            add_rows((self.acc, place), [(self.acc, place), (self.from_core, place), (self.from_x, come)])
+            if start and from_far is not None:
+                self.from_far = from_far
+                goal = from_far.at[self.window(slot * self.step, 0, self.across)]
+                self.far.append(self.net.send(self.acc.at[place], goal, FAR))
+
+    def far_end(self, k, result=None):
+        slot = self.order[k]
+        self.net.arrived(self.far[k])
+        place = self.window(2 * slot * self.step, 0, self.across)
+        come = self.window(slot * self.step, 0, self.across)
+        add_rows((self.acc, place), [(self.acc, place), (self.from_far, come)])
+
+    def to_owner(self, k, source, out):
+        net, across = self.net, self.across
+        goal = out.at[self.window(net.x * self.step, net.y * across, across)]
+        if k == 0:
+            self.out = out
+            self.y = net.send(source, goal, Y)
+        else:
+            net.copy(source, goal)
+            net.send(source, goal, X)
 
     def after_y(self):
         net, across = self.net, self.across
-        self.net.arrived(self.y)
-        start = pl.multiple_of((1 - net.y) * across, across)
-        place = self.view(self.out, pl.multiple_of(net.x * self.step, self.step), start, across)
+        net.arrived(self.y)
+        place = self.out.at[self.window(net.x * self.step, (1 - net.y) * across, across)]
         net.send(place, place, X)
+
+    def slot(self, k, stride, start, count):
+        return self.window(stride * self.order[k] * self.step, start, count)
 
 
 def row_back(grad, values, gain):
@@ -820,7 +818,7 @@
 
 def turn_kernel(
     partial_ref, middle_ref, upstream_ref, gain_ref, down_ref, gate_ref, up_ref,
-    grad_ref, all_ref, term_ref, down_out, gate_out, up_out,
+    grad_ref, all_ref, term_ref, down_out, gate_out, up_keep, up_send,
     first, second, sums, last, total, low, *rest, sizes,
 ):
     buffers, (send, recv, local) = rest[:-3], rest[-3:]
@@ -828,14 +826,15 @@
     net.greet([Y, CORE, NEAR, FAR, X])
     scatter = scatter_flow(net, partial_ref, first, second, sums, last, total)
     run(scatter)
-    down = Gradient(net, 1, *buffers[0:4])
-    gate = Gradient(net, 0, *buffers[4:8])
-    up = Gradient(net, 0, *buffers[8:12])
-    for flow, ref in ((down, down_ref), (gate, gate_ref), (up, up_ref)):
-        flow.start(ref)
-    down.after_core()
-    run(scatter)
-    gate.after_core()
+    step, across = low.shape[1] // sizes["narrow"] // 2, gate_ref.shape[1] // 2
+    down, gate, up = (Gradient(net, axis, step, across) for axis in (1, 0, 0))
+    down.start(down_ref, *buffers[0:2])
+    gate.start(gate_ref, *buffers[4:6])
+    up.start(up_ref, *buffers[7:9])
+    down.core_to_x(buffers[2])
+    gate.core_to_x(buffers[6])
+    run(scatter)
+    down.x_end(0, buffers[3])
     run(scatter)
     run(scatter)
     term_ref[...] = jnp.zeros_like(term_ref)
@@ -851,27 +850,28 @@
     by_rows(low.shape[0], rows)
     gather = gather_flow(net, low, all_ref)
     run(gather)
-    down.after_x()
-    down.send_far()
+    down.x_end(1, buffers[3])
     run(gather)
-    up.after_core()
     run(gather)
-    gate.after_x()
-    gate.send_far()
-    down.after_far()
-    up.after_x()
-    gate.after_far()
-    for flow, ref, wide in ((down, down_out, 1), (gate, gate_out, 1), (up, up_out, 2)):
-        for slot in range(2):
-            source = flow.view(flow.acc, 2 * slot * flow.step, 0, wide * flow.across)
-            net.copy(source, flow.view(ref, slot * flow.step, 0, wide * flow.across))
+    up.wait_core()
+    for slot in range(2):
+        for j, ref in ((1, up_send), (0, up_keep)):
+            place = up.window((2 * slot + j) * step, 0, 2 * across)
+            add_rows((up.acc, place), [(up.acc, place), (up.from_core, place)])
+            net.copy(up.acc.at[place], ref.at[up.window(slot * step, 0, 2 * across)])
+    for k in range(2):
+        gate.x_end(k)
+        net.copy(gate.acc.at[gate.slot(k, 2, 0, 2 * across)], gate_out.at[gate.slot(k, 1, 0, 2 * across)])
+    for k in range(2):
+        down.far_end(k)
+        net.copy(down.acc.at[down.slot(k, 2, 0, across)], down_out.at[down.slot(k, 1, 0, across)])
     net.finish()
 
 
-def gradient_buffers(size, across, axis, whole=True):
+def gradient_buffers(size, across, axis, count=4):
     shape = lambda a, b: pltpu.VMEM((a, b) if axis == 0 else (b, a), BF16)
-    first = [shape(2 * size, 2 * across), shape(2 * size, 2 * across), shape(size, 2 * across)]
-    return first + [shape(size, across)] if whole else first[:1]
+    every = [shape(2 * size, 2 * across), shape(2 * size, 2 * across), shape(size, 2 * across), shape(size, across)]
+    return every[:count]
 
 
 def scatter_buffers(rows, width):
@@ -883,23 +883,24 @@
     rows, width = middle.shape
     size, across = width // sizes["narrow"], down.shape[0] // 2
     return wire_call(
-        turn_kernel, "turn", 4, [VMEM] * 4 + [ANY] * 3, [VMEM, ANY, VMEM, ANY, ANY, ANY],
+        turn_kernel, "turn", 4, [VMEM] * 4 + [ANY] * 3, [VMEM, ANY, VMEM, ANY, ANY, ANY, ANY],
         [
             ((rows, width), F32), ((4 * rows, width), BF16), ((1, width), F32),
-            ((across, size), BF16), ((size, across), BF16), ((size, 2 * across), BF16),
+            ((across, size), BF16), ((size, 2 * across), BF16), ((size, 2 * across), BF16), ((size, 2 * across), BF16),
         ],
         [
             *scatter_buffers(rows, width), pltpu.VMEM((rows, width), BF16),
-            *gradient_buffers(size, across, 1), *gradient_buffers(size, across, 0), *gradient_buffers(size, across, 0), *sems(40, 16),
+            *gradient_buffers(size, across, 1), *gradient_buffers(size, across, 0, 3), *gradient_buffers(size, across, 0, 2), *sems(40, 16),
         ],
-        sizes, 105, partial, middle, upstream, gain[None], down, gate, up,
+        sizes, 80, partial, middle, upstream, gain[None], down, gate, up,
     )
 
 
 def owner_kernel(
-    dkv_ref, partial_ref, middle_ref, down_ref, gate_ref, up_ref,
+    dkv_ref, partial_ref, middle_ref, down_ref, gate_ref, gate_far_ref, up_ref, up_x_ref,
     mine_ref, layer_ref, down_out, gate_out, up_out,
-    prompt_core, rest_core, prompt, prompt_far, first, second, sums, last, total, rows_low, up_far, up_sums, send, recv, local, *, sizes,
+    prompt_core, rest_core, prompt, prompt_far, first, second, sums, last, total, rows_low, gate_sums, up_acc, up_far, up_sums,
+    send, recv, local, *, sizes,
 ):
     net = Wires(send, recv, local, sizes)
     net.greet([Y, CORE, CORNER, NEAR, FAR, X])
@@ -910,8 +911,10 @@
     rest = net.send(region(3), rest_core, CORE)
     scatter = scatter_flow(net, partial_ref, first, second, sums, last, total)
     run(scatter)
-    down, gate = Gradient(net, 1, down_ref, out=down_out), Gradient(net, 0, gate_ref, out=gate_out)
-    up = Gradient(net, 0, up_ref, from_far=up_far, out=up_out, result=up_sums)
+    step, across = down_ref.shape[1] // 2, down_ref.shape[0]
+    down, gate, up = (Gradient(net, axis, step, across) for axis in (1, 0, 0))
+    for k in range(2):
+        down.to_owner(k, down_ref.at[down.slot(k, 1, 0, across)], down_out)
     net.arrived(come)
 
     def add(at):
@@ -926,10 +929,17 @@
         for copy in far:
             copy.start()
 
-    up.send_far(1)
-    down.send_y(1)
-    run(scatter)
-    gate.send_y(1)
+    for k in range(2):
+        for start in (across, 0):
+            place = up.slot(k, 1, start, across)
+            add_rows((up_acc, place), [(up_ref, place), (up_x_ref, place)])
+            if start:
+                up.far.append(net.send(up_acc.at[place], up_far.at[up.slot(k, 1, 0, across)], FAR))
+    for k in range(2):
+        place = gate.slot(k, 1, 0, across)
+        add_rows((gate_sums, place), [(gate_ref, place), (gate_far_ref, place)])
+        gate.to_owner(k, gate_sums.at[place], gate_out)
+    run(scatter)
     run(scatter)
     run(scatter)
 
@@ -963,32 +973,36 @@
         by_rows(count, add)
 
     net.sent = [copy for copy in net.sent if all(copy is not other for other in far)]
-    up.after_far()
-    up.send_y(1)
+    for k in range(2):
+        net.arrived(up.far[k])
+        place = up.slot(k, 1, 0, across)
+        add_rows((up_sums, place), [(up_acc, place), (up_far, place)])
+        up.to_owner(k, up_sums.at[place], up_out)
     up.after_y()
     net.finish()
 
 
-def to_owner(dkv, partial, middle, down, gate, up, sizes):
+def to_owner(dkv, partial, middle, down, gate, gate_far, up, up_x, sizes):
     rows, width = middle.shape
-    size, across = width // sizes["narrow"], gate.shape[1]
+    size, across = width // sizes["narrow"], gate_far.shape[1]
     count = dkv.shape[0] // 4
     block = lambda: pltpu.VMEM((count, dkv.shape[1]), BF16)
+    part = lambda wide: pltpu.VMEM((size, wide), BF16)
     return wire_call(
-        owner_kernel, "owner", 5, [VMEM] * 6, [VMEM, ANY, ANY, ANY, ANY],
+        owner_kernel, "owner", 5, [VMEM] * 8, [VMEM, ANY, ANY, ANY, ANY],
         [
             ((count, dkv.shape[1]), F32), ((sizes["narrow"] * rows, size), BF16),
             ((2 * across, size), BF16), ((size, 2 * across), BF16), ((size, 2 * across), BF16),
         ],
         [
             block(), block(), block(), block(), *scatter_buffers(rows, width), pltpu.VMEM((rows, width), BF16),
-            pltpu.VMEM((size, across), BF16), pltpu.VMEM((size, across), BF16), *sems(40, 16),
+            part(across), part(2 * across), part(across), part(across), *sems(40, 16),
         ],
-        sizes, 80, dkv, partial, middle, down, gate, up,
+        sizes, 80, dkv, partial, middle, down, gate, gate_far, up, up_x,
     )
 
 
-SUMS = [X, CORE, Y, NEAR, FAR]
+SUMS = [CORE, Y, NEAR, X, FAR]
 
 
 def end_kernel(
@@ -999,16 +1013,19 @@
     buffers, (send, recv, local) = rest[:-3], rest[-3:]
     net = Wires(send, recv, local, sizes)
     net.greet([Y, CORE, CORNER, NEAR, FAR, X])
-    qkv = Gradient(net, 0, *buffers[0:4], out=qkv_out)
-    out = Gradient(net, 1, *buffers[4:8], out=out_out)
-    qkv.start(qkv_ref)
-    out.start(out_ref)
+    step = x_ref.shape[1] // sizes["narrow"] // 2
+    qkv = Gradient(net, 0, step, qkv_ref.shape[1] // 2)
+    out = Gradient(net, 1, step, out_ref.shape[0] // 2)
+    qkv.start(qkv_ref, *buffers[0:2])
+    out.start(out_ref, *buffers[4:6])
     scatter = scatter_flow(net, partial_ref, first, second, sums, last, total)
     run(scatter)
-    qkv.after_core()
-    out.after_core()
-    run(scatter)
-    run(scatter)
+    qkv.core_to_x(buffers[2])
+    out.core_to_x(buffers[6])
+    run(scatter)
+    qkv.x_end(0, buffers[3])
+    run(scatter)
+    qkv.x_end(1, buffers[3])
     run(scatter)
     width = x_ref.shape[1]
     size = query_ref.shape[1]
@@ -1023,7 +1040,6 @@
         rows_low[at, :] = (grad_ref[at, :] + change).astype(BF16)
 
     by_rows(rows_low.shape[0], rows)
-    spread_flow(net, rows_low, tokens_ref)
     for i, ref in enumerate((gains_ref, two_ref)):
         for slot in range(4):
             to = (2 * (slot % 2) + jnp.bitwise_xor(net.core, slot // 2)) * block + i * width
@@ -1033,21 +1049,36 @@
                 vectors[0, :, pl.ds(pl.multiple_of(to + sub * half, half), half)] = ref[:, at : at + half]
     vectors[0, :, 2 * width : 2 * width + size] = query_ref[...]
     vectors[0, :, 2 * width + size :] = key_ref[...]
-    qkv.after_x()
-    qkv.send_far()
-    out.after_x()
-    out.send_far()
-    for i, to in enumerate(SUMS):
-        copy = net.send(vectors.at[i], vectors.at[len(SUMS) + 1 + i], to)
-        net.arrived(copy)
-        vectors[i + 1] = vectors[i] + vectors[len(SUMS) + 1 + i]
-    gains_ref[...] = vectors[len(SUMS)]
-    qkv.after_far()
-    qkv.send_y()
-    out.after_far()
-    out.send_y()
+
+    def add_gains():
+        for i, to in enumerate(SUMS):
+            copy = net.send(vectors.at[i], vectors.at[len(SUMS) + 1 + i], to)
+            yield
+            net.arrived(copy)
+            vectors[i + 1] = vectors[i] + vectors[len(SUMS) + 1 + i]
+        gains_ref[...] = vectors[len(SUMS)]
+        yield
+
+    def own(flow, k, ref):
+        flow.far_end(k)
+        flow.to_owner(k, flow.acc.at[flow.slot(k, 2, 0, flow.across)], ref)
+
+    gains = add_gains()
+    run(gains)
+    out.x_end(0, buffers[7])
+    out.x_end(1, buffers[7])
+    run(gains)
+    own(qkv, 0, qkv_out)
+    run(gains)
+    spread_flow(net, rows_low, tokens_ref)
+    run(gains)
+    own(qkv, 1, qkv_out)
+    run(gains)
+    own(out, 0, out_out)
+    own(out, 1, out_out)
     qkv.after_y()
     out.after_y()
+    run(gains)
     net.finish()
 
 
@@ -1067,15 +1098,13 @@
     )
 
 
-def layout(lengths, group_rows):
-    ends = jnp.cumsum(lengths)
-    begins = ends - lengths
-    index = jnp.arange(group_rows, dtype=jnp.int32)
+def layout(lengths, index):
+    order = jnp.arange(lengths.shape[0])
+    ends = jnp.sum(jnp.where(order[None, :] <= order[:, None], lengths[None, :], 0), axis=1)[None, :]
+    begins = ends - lengths[None, :]
     offset = index - PROMPT
-    member = ((offset[:, None] >= begins[None, :]) & (offset[:, None] < ends[None, :])).astype(jnp.int32)
-    shift = jnp.sum(member * begins[None, :], axis=1)
-    start = jnp.where(offset >= 0, PROMPT + shift, 0)
-    return index, start, index - shift
+    shift = jnp.sum(jnp.where((offset >= begins) & (offset < ends), begins, 0), axis=1, keepdims=True)
+    return jnp.where(offset >= 0, PROMPT + shift, 0), index - shift
 
 
 def make(sizes):
@@ -1083,6 +1112,12 @@
 
     def over_y(values):
         return exchange(values, "narrow", 2, n_narrow)
+
+    def over_z(values):
+        return exchange(values, "wide", 1, n_wide)
+
+    def over_x(values):
+        return exchange(values, "dp", 1, n_dp)
 
     def over_far(values):
         return exchange(values, "wide", 2, n_wide)
@@ -1115,16 +1150,10 @@
         factor = scale * math.log2(math.e)
         log_two = math.log(2.0)
 
-        def by_x(values, axis):
-            half = values.shape[axis] // 2
-            low = lax.slice_in_dim(values, 0, half, axis=axis)
-            high = lax.slice_in_dim(values, half, 2 * half, axis=axis)
-            return join([jnp.where(x == 0, low, high), jnp.where(x == 0, high, low)], axis)
-
-        owners = [2 * (i % 2) + (core ^ (i // 2)) for i in range(4)]
-
         def relative_vector(vector):
-            return join([by_x(cut(vector, i * width_local, width_local, 0), 0) for i in owners])
+            values = jnp.transpose(vector.reshape(2, 2, 2, quarter), (1, 0, 2, 3))
+            values = jnp.where(core == 0, values, values[::-1])
+            return jnp.where(x == 0, values, values[:, :, ::-1]).reshape(width)
 
         def piece_of(weight, i, axis):
             half = weight.shape[1 - axis] // 2
@@ -1138,30 +1167,34 @@
                 halves(query_weight, i), halves(key_weight, i), halves(value_weight, i), jnp.pad(halves(head_gate, i), lane_pad)
             )], 1
         )
-        inputs, normed_all, joined_weight, out_weight = begin(tokens, gain_one, packed, output_weight, sizes)
-
-        index, start, position = layout(continuation_lengths[0], group_rows)
-        square = [(z ^ (i // 2), narrow ^ (2 * (i % 2))) for i in range(4)]
-        mine = lambda vector: join([cut(vector, (i * n_narrow + j) * rows_local, rows_local, 0) for i, j in square])
-        my_index, my_start, my_position = mine(index), mine(start), mine(position)
+        inputs, upstream, normed_all, joined_weight, out_weight = begin(tokens, cotangent, gain_one, packed, output_weight, sizes)
+
+        def indices(row):
+            part, at = row // rows_local, row % rows_local
+            return ((z ^ (part // 2)) * n_narrow + (narrow ^ (2 * (part % 2)))) * rows_local + at
+
+        my_index = indices(lax.broadcasted_iota(jnp.int32, (4 * rows_local, 1), 0))
+        my_start, my_position = layout(continuation_lengths[0], my_index)
         frequency = THETA ** (-2.0 * jnp.arange(size // 2, dtype=F32) / size)
-        angle = my_position.astype(F32)[:, None] * frequency[None, :]
+        angle = my_position.astype(F32) * frequency[None, :]
         cosine, sine = jnp.cos(angle), jnp.sin(angle)
         cosine = jnp.concatenate([cosine, cosine], axis=1)
         sine = jnp.concatenate([-sine, sine], axis=1)
-        block = my_index[::rows_local] // rows_local
-        first = my_start[::rows_local] // rows_local
+        heads_index = indices(lax.broadcasted_iota(jnp.int32, (4, 1), 0) * rows_local)
+        block = heads_index // rows_local
+        first = layout(continuation_lengths[0], heads_index)[0] // rows_local
         prompt_blocks = PROMPT // rows_local
         in_prompt = block < prompt_blocks
-        table = jnp.stack(
+        column = lax.broadcasted_iota(jnp.int32, (4, 5), 1)
+        pick = lambda values: functools.reduce(lambda acc, item: jnp.where(column == item[0], item[1], acc), enumerate(values), 0)
+        table = pick(
             [
                 jnp.where(in_prompt, block // 2, prompt_blocks // 2),
                 jnp.where(in_prompt, block // 2 * 2, first),
                 block,
-                jnp.full_like(block, 2 * z_near + y),
-                jnp.full_like(block, core),
-            ],
-            axis=1,
+                2 * z_near + y,
+                core,
+            ]
         ).astype(jnp.int32)
 
         raw = dot_rows(normed_all, joined_weight)
@@ -1169,13 +1202,19 @@
         send = after((gate_weight, up_weight, down_weight), normed_all)
         axes = (0, 0, 1)
         from_y = [over_y(piece_of(w, 1 - y, axis)) for w, axis in zip(send, axes)]
-        near = [i for i in range(n_wide) if i & 2 == 0]
-        kv_all, upstream, upstream_all = exchange_keys(after(kv, *from_y), cotangent, width, sizes)
+        part = rows_local // 2
+        upstream_y, upstream_z = over_y(upstream[:part]), over_z(upstream[part:])
+        kv_all = exchange_keys(after(kv, *from_y, upstream_y, upstream_z), sizes)
         send = after((gate_weight, up_weight, down_weight), kv_all)
         from_far = [over_far(piece_of(w, y, axis)) for w, axis in zip(send, axes)]
+        come_z = over_z(join([upstream[:part], after(upstream_y, kv_all)]))
+        come_y = over_y(join([upstream[part:], after(upstream_z, kv_all)]))
+        upstream_all = join(
+            [upstream, upstream_y, come_y[:part], come_z[:part], upstream_z, come_z[part:], come_y[part:]]
+        )
 
         gated, context, inverse_total = attend(
-            table, q, kv_all, my_index[:, None], my_start[:, None], raw, pairs, size
+            table, q, kv_all, my_index, my_start, raw, pairs, size
         )
         partial = dot_rows(gated, out_weight).astype(BF16)
         middle, normed_two_all, gate_up, down = to_middle(
@@ -1196,16 +1235,18 @@
         down_sums = dot_inner(hidden, upstream_all).astype(BF16)
         gate_sums = dot_inner(normed_two_all, gate_low).astype(BF16)
         up_sums = dot_inner(normed_two_all, up_low).astype(BF16)
-        middle_grad, middle_all, two_term, down_part, gate_part, up_part = turn(
+        middle_grad, middle_all, two_term, down_part, gate_part, up_keep, up_send = turn(
             partial, middle, upstream, gain_two, down_sums, gate_sums, up_sums, sizes
         )
+        gate_far = over_far(gate_part[:, hidden_cols // 2 :])
+        up_come = over_x(up_send)
         gated_grad = dot_trans(middle_all, out_weight)
         dq, dkv, logit_grad = attend_back(
             table, q, kv_all, my_index, my_start, raw, context, inverse_total, gated_grad, pairs, size
         )
         partial = dot_rows(hidden, down).astype(BF16)
         dkv_mine, layer_output, down_gradient, gate_gradient, up_gradient = to_owner(
-            dkv, partial, middle, down_part, gate_part, up_part, sizes
+            dkv, partial, middle, down_part, gate_part, gate_far, up_keep, up_come, sizes
         )
         low, query_term, key_term = project_back(
             dq, dkv_mine, raw, cosine, sine, query_gain, key_gain, logit_grad, heads, pairs, size, scale, log_two

time: 941 us -> 889 us (0.945)
  Pallas kernels: 679 us -> 608 us
  starting transfers between devices: 17.9 us -> 69.9 us
  waiting for transfers between devices: 24.7 us -> 0.03 us
  other arithmetic: 38.7 us -> 25.8 us
    pallas_call x6, Pallas kernels: 620 us -> 549 us  [wire_call(): pl.pallas_call(functools.partial(kernel, sizes=sizes), in_specs=specs, ou...]
    ppermute x6 -> x12, starting transfers between devices: 17.9 us -> 69.9 us  [exchange(): return lax.ppermute(values, axis, [(i, i ^ distance) for i in range(size)])]
    ppermute x6 -> x12, waiting for transfers between devices: 24.7 us -> 0.03 us  [exchange(): return lax.ppermute(values, axis, [(i, i ^ distance) for i in range(size)])]
    unnamed x16 -> x0, other arithmetic: 9.49 us -> none
  transfers between devices with their start and end apart: 6 -> 12, of which waited for: 3 -> 0; matrix products, arithmetic and copies ran while one was open for 6% -> 8% of each run, Pallas kernels for 3% -> 19%
where the time goes in v5:
time: 889 us; the launch traced here: 882 us
  Pallas kernels  608 us (68%)
  matrix products  142 us (16%)
  starting transfers between devices  69.9 us (8%)
  local copies, waits for them, and re-layouts  34.2 us (4%)
  other arithmetic  25.8 us (3%)
    pallas_call x6, Pallas kernels, wire_call(): pl.pallas_call(functools.partial(kernel, sizes=sizes), in_specs=specs, ou...  549 us
    ppermute x12, starting transfers between devices, exchange(): return lax.ppermute(values, axis, [(i, i ^ distance) for i in range(size)])  69.9 us
    dot_general x4, matrix products, dot_trans(): lax.dot_general(left, right, (((1,), (1,)), ((), ())), preferred_element_...  53.6 us
    dot_general x4, matrix products, dot_rows(): return jnp.dot(left, right, preferred_element_type=F32)  46.9 us
    dot_general x5, matrix products, dot_inner(): lax.dot_general(left, right, (((0,), (0,)), ((), ())), preferred_element_...  41.5 us
    pallas_call x1, Pallas kernels, attend_back(): pl.pallas_call(functools.partial(backward_kernel, pairs=pairs, repeat=hea...  26.2 us
    pallas_call x1, Pallas kernels, attend(): pl.pallas_call(functools.partial(forward_kernel, pairs=pairs, repeat=head...  18.2 us
  transfers between devices with their start and end apart: 12, of which 0 were waited for; matrix products, arithmetic and copies ran while one was open for 8% of the time, Pallas kernels for 19%

profile of v5, /device:TPU:0, one launch (start us, length us, event | category | flops | bytes accessed | tf_op | source)
XLA Modules:
  0.0 881.7 jit_solution(5787473048229023899)
XLA Ops:
  11.1 75.5 %begin.1 = (bf16[256,2048]{1,0:T(8,128)(2,1)}, bf16[256,2048]{1,0:T(8,128)(2,1)}, bf16[1024,2048]{1,0:T(8,128)(2,1)}, bf16[2048,1280]{1,0:T(8,128)(2,1)}, bf16[512,2048]{1,0:T(8,128)(2,1)}) custom-call(bf16[1024,512]{1,0:T(8,128)(2,1)} %tokens_ref.1, bf16[1024,512]{1,0:T(8,128)(2,1)} %cotangent_ref.1, f32[1,2048]{1,0:T(1,128)} %broadcast_in_dim_reshape.8.gain_ref, ...), custom_call_target="tpu_custom_call" | custom-call | bytes 165000000 | tf_op jit(solution)/shard_map/begin/pallas_call | solution.py:558
  93.6 2.3 fusion.65
  95.8 5.1 collective-permute-start.4
  106.0 10.4 %fusion.68.raw_ref.own_ref.other_ref = f32[1024,1280]{1,0:T(8,128)} fusion(bf16[1024,2048]{1,0:T(8,128)(2,1)} %get-tuple-element.59, bf16[2048,1280]{1,0:T(8,128)(2,1)} %get-tuple-element.60), kind=kOutput, calls=%fused_computation.180 | convolution fusion | flops 5368709120 | bytes 14680064 | tf_op jit(solution)/shard_map/dot_general | solution.py:22
  120.5 6.4 post.1
  128.8 25.4 %keys.1.kv_ref = bf16[4096,512]{1,0:T(8,128)(2,1)} custom-call(bf16[1024,512]{1,0:T(8,128)(2,1)} %get-tuple-element.67.kv_ref), custom_call_target="tpu_custom_call" | custom-call | bytes 135000000 | tf_op jit(solution)/shard_map/keys/pallas_call | solution.py:558
  158.3 5.1 collective-permute-start.9
  163.5 2.8 collective-permute-start.7
  168.7 49.1 %collective-permute-start.6 = (bf16[256,2048]{1,0:T(8,128)(2,1)S(1)}, bf16[256,2048]{1,0:T(8,128)(2,1)S(1)}, u32[]{:S(2)}, u32[]{:S(2)}) collective-permute-start(bf16[256,2048]{1,0:T(8,128)(2,1)S(1)} %pad_maximum_fusion.1), channel_id=1, source_target_pairs={{0,4},{4,0},{8,12},{12,8},{1,5},{5,1},{9,13},{13,9},{2,6},{6,2},{1... | collective-permute-start | bytes 3145736 | tf_op jit(solution)/shard_map/ppermute | solution.py:34
  217.8 18.2 %attend.1 = (bf16[1024,512]{1,0:T(8,128)(2,1)}, f32[1024,512]{1,0:T(8,128)}, f32[1024,512]{1,0:T(8,128)}) custom-call(s32[4,5]{1,0:T(4,128)} %select_select_fusion.table_ref, bf16[1024,512]{1,0:T(8,128)(2,1)} %get-tuple-element.61.q_ref, bf16[4096,512]{1,0:T(8,128)(2,1)} %keys.1.kv_ref, s32[1024,1]{1,0:T(8,128)} %get-tuple-element.159.row_ref, ...), custom_call_target="tpu_custom_call" | custom-call | flops 20000000000 | bytes 12000000 | tf_op jit(solution)/shard_map/attend/pallas_call | solution.py:240
  237.9 6.2 convolution_convert_fusion.6.partial_ref
  245.1 120.4 %middle.1 = (f32[256,2048]{1,0:T(8,128)}, bf16[1024,2048]{1,0:T(8,128)(2,1)}, bf16[2048,3072]{1,0:T(8,128)(2,1)}, bf16[1536,2048]{1,0:T(8,128)(2,1)}) custom-call(bf16[1024,2048]{1,0:T(8,128)(2,1)} %convolution_convert_fusion.6.partial_ref, bf16[256,2048]{1,0:T(8,128)(2,1)} %get-tuple-element.74.x_ref, f32[1,2048]{1,0:T(1,128)} %broadcast_in_dim_reshape.9.gain_ref, ...), custom_call_target="tpu_custom_call" | custom-call | bytes 240000000 | tf_op jit(solution)/shard_map/middle/pallas_call | solution.py:558
  365.6 19.1 %fusion.69 = f32[1024,3072]{1,0:T(8,128)} fusion(bf16[1024,2048]{1,0:T(8,128)(2,1)} %get-tuple-element.79, bf16[2048,3072]{1,0:T(8,128)(2,1)} %get-tuple-element.80), kind=kOutput, calls=%fused_computation.181 | convolution fusion | flops 12884901888 | bytes 29360128 | tf_op jit(solution)/shard_map/dot_general | solution.py:22
  385.0 18.0 %multiply_convert_fusion.2 = (bf16[1024,1536]{1,0:T(8,128)(2,1)}, bf16[1024,1536]{1,0:T(8,128)(2,1)}, bf16[1024,1536]{1,0:T(8,128)(2,1)}) fusion(f32[1024,3072]{1,0:T(8,128)} %fusion.69, bf16[1024,2048]{1,0:T(8,128)(2,1)S(1)} %slice_dynamic-update-slice_fusion, bf16[1536,2048]{1,0:T(8,128)(2,1)} %get-tuple-element.78), kind=kOutput, calls=%fused_computation.10 | convolution fusion | flops 6466043904 | bytes 32505856 | tf_op jit(solution)/shard_map/dot_general | solution.py:26
  402.9 10.6 %convolution_convert_fusion.2.gate_ref = bf16[2048,1536]{1,0:T(8,128)(2,1)} fusion(bf16[1024,2048]{1,0:T(8,128)(2,1)S(1)} %copy-done.24, bf16[1024,1536]{1,0:T(8,128)(2,1)} %get-tuple-element.135), kind=kOutput, calls=%fused_computation.2 | convolution fusion | flops 6445596672 | bytes 13631488 | tf_op jit(solution)/shard_map/dot_general | solution.py:30
  413.5 19.5 %fusion.5.partial_ref = bf16[1024,2048]{1,0:T(8,128)(2,1)} fusion(bf16[2048,3072]{1,0:T(8,128)(2,1)} %get-tuple-element.80, bf16[1024,1536]{1,0:T(8,128)(2,1)} %get-tuple-element.136, bf16[1024,1536]{1,0:T(8,128)(2,1)} %get-tuple-element.135), kind=kOutput, calls=%fused_computation.14 | convolution fusion | flops 12899581952 | bytes 23068672 | tf_op jit(solution)/shard_map/dot_general | solution.py:26
  433.1 10.8 %convolution_convert_fusion.1.up_ref = bf16[2048,1536]{1,0:T(8,128)(2,1)} fusion(bf16[1024,2048]{1,0:T(8,128)(2,1)S(1)} %copy-done.24, bf16[1024,1536]{1,0:T(8,128)(2,1)} %get-tuple-element.136), kind=kOutput, calls=%fused_computation.1 | convolution fusion | flops 6445596672 | bytes 13631488 | tf_op jit(solution)/shard_map/dot_general | solution.py:30
  443.8 8.8 convolution_convert_fusion.3.down_ref
  452.6 96.1 %turn.1 = (f32[256,2048]{1,0:T(8,128)}, bf16[1024,2048]{1,0:T(8,128)(2,1)}, f32[1,2048]{1,0:T(1,128)}, bf16[768,512]{1,0:T(8,128)(2,1)}, bf16[512,1536]{1,0:T(8,...) custom-call(bf16[1024,2048]{1,0:T(8,128)(2,1)} %fusion.5.partial_ref, ...), custom_call_target="tpu_custom_call" | custom-call | bytes 240000000 | tf_op jit(solution)/shard_map/turn/pallas_call | solution.py:558
  548.7 6.0 fusion.70.grad_ref
  554.8 3.3 collective-permute-start.10
  558.1 26.2 %attend_back.1 = (f32[1024,512]{1,0:T(8,128)}, bf16[4096,512]{1,0:T(8,128)(2,1)}, f32[1024,256]{1,0:T(8,128)}) custom-call(s32[4,5]{1,0:T(4,128)} %select_select_fusion.table_ref, bf16[1024,512]{1,0:T(8,128)(2,1)} %get-tuple-element.61.q_ref, bf16[4096,512]{1,0:T(8,128)(2,1)} %keys.1.kv_ref, s32[4,1,256]{2,1,0:T(1,128)} %get-tuple-element.162.row_ref, ...), custom_call_target="tpu_custom_call" | custom-call | flops 49999998976 | bytes 20000000 | tf_op jit(solution)/shard_map/attend_back/pallas_call | solution.py:336
  584.3 11.1 %convolution_convert_fusion.4.partial_ref = bf16[1024,2048]{1,0:T(8,128)(2,1)} fusion(bf16[1024,1536]{1,0:T(8,128)(2,1)S(1)} %copy-done.30, bf16[1536,2048]{1,0:T(8,128)(2,1)} %get-tuple-element.78), kind=kOutput, calls=%fused_computation.13 | convolution fusion | flops 6444548096 | bytes 13631488 | tf_op jit(solution)/shard_map/dot_general | solution.py:22
  595.5 3.8 convolution_convert_fusion.7.out_ref
  600.6 135.0 %owner.1 = (f32[1024,512]{1,0:T(8,128)}, bf16[1024,512]{1,0:T(8,128)(2,1)}, bf16[1536,512]{1,0:T(8,128)(2,1)}, bf16[512,1536]{1,0:T(8,128)(2,1)}, bf16[512,1536]{1,0:T(8,128)(2,1)}) custom-call(bf16[4096,512]{1,0:T(8,128)(2,1)} %get-tuple-element.83.dkv_ref, bf16[1024,2048]{1,0:T(8,128)(2,1)} %convolution_convert_fusion.4.partial_ref, ...), custom_call_target="tpu_custom_call" | custom-call | bytes 240000000 | tf_op jit(solution)/shard_map/owner/pallas_call | solution.py:558
  735.6 8.4 project_back.1
  744.0 10.2 %convolution_convert_fusion.5.partial_ref = bf16[1024,2048]{1,0:T(8,128)(2,1)} fusion(bf16[1024,1280]{1,0:T(8,128)(2,1)} %get-tuple-element.92, bf16[2048,1280]{1,0:T(8,128)(2,1)} %get-tuple-element.60), kind=kOutput, calls=%fused_computation.15 | convolution fusion | flops 5370806272 | bytes 12058624 | tf_op jit(solution)/shard_map/dot_general | solution.py:26
  754.2 7.6 convolution_convert_fusion.qkv_ref
  761.8 96.7 %end.1 = (bf16[1024,512]{1,0:T(8,128)(2,1)}, f32[1,4352]{1,0:T(1,128)}, bf16[512,1280]{1,0:T(8,128)(2,1)}, bf16[512,512]{1,0:T(8,128)(2,1)}) custom-call(bf16[1024,2048]{1,0:T(8,128)(2,1)} %convolution_convert_fusion.5.partial_ref, bf16[256,2048]{1,0:T(8,128)(2,1)} %get-tuple-element.74.x_ref, f32[1,2048]{1,0:T(1,128)} %broadcast_in_dim_reshape.8.gain_ref, ...), custom_call_target="tpu_custom_call" | custom-call | bytes 270000000 | tf_op jit(solution)/shard_map/end/pallas_call | solution.py:558
  865.5 3.0 convert_element_type.71
  868.5 2.1 convert_element_type.73
  874.8 2.1 convert_element_type.76
  (152 shorter events, 54.8 us)
Async XLA Ops:
  3.8 88.4 %copy-start.2 = (bf16[512,1536]{1,0:T(8,128)(2,1)S(1)}, bf16[512,1536]{1,0:T(8,128)(2,1)}, u32[]{:S(2)}) copy-start(bf16[512,1536]{1,0:T(8,128)(2,1)} %gate_ref.1) | copy-start | bytes 4718596
  86.6 15.9 %copy-start = (bf16[256,2048]{1,0:T(8,128)(2,1)S(1)}, bf16[256,2048]{1,0:T(8,128)(2,1)}, u32[]{:S(2)}) copy-start(bf16[256,2048]{1,0:T(8,128)(2,1)} %get-tuple-element.66.upstream_ref) | copy-start | bytes 3145732
  88.0 40.7 %collective-permute-start.2 = (bf16[768,256]{1,0:T(8,128)(2,1)S(1)}, bf16[768,256]{1,0:T(8,128)(2,1)}, u32[]{:S(2)}, u32[]{:S(2)}) collective-permute-start(bf16[768,256]{1,0:T(8,128)(2,1)S(1)} %dynamic_slice.26), channel_id=1, source_target_pairs={{0,2},{1,3},{2,0},{3,1},{4,6},{5,7},{6,4},{7,5},{8,10},{9,11},{10,... | collective-permute-start | bytes 1179656 | tf_op jit(solution)/shard_map/ppermute | solution.py:34
  90.6 38.2 %collective-permute-start.1 = (bf16[256,768]{1,0:T(8,128)(2,1)}, bf16[256,768]{1,0:T(8,128)(2,1)}, u32[]{:S(2)}, u32[]{:S(2)}) collective-permute-start(bf16[256,768]{1,0:T(8,128)(2,1)} %dynamic_slice.25), channel_id=1, source_target_pairs={{0,2},{1,3},{2,0},{3,1},{4,6},{5,7},{6,4},{7,5},{8,10},{9,11},{10,... | collective-permute-start | bytes 1179656 | tf_op jit(solution)/shard_map/ppermute | solution.py:34
  93.1 35.7 %collective-permute-start = (bf16[256,768]{1,0:T(8,128)(2,1)}, bf16[256,768]{1,0:T(8,128)(2,1)}, u32[]{:S(2)}, u32[]{:S(2)}) collective-permute-start(bf16[256,768]{1,0:T(8,128)(2,1)} %dynamic_slice.24), channel_id=1, source_target_pairs={{0,2},{1,3},{2,0},{3,1},{4,6},{5,7},{6,4},{7,5},{8,10},{9,11},{10,... | collective-permute-start | bytes 1179656 | tf_op jit(solution)/shard_map/ppermute | solution.py:34
  95.8 32.9 %collective-permute-start.4 = (bf16[128,2048]{1,0:T(8,128)(2,1)}, bf16[128,2048]{1,0:T(8,128)(2,1)S(1)}, u32[]{:S(2)}, u32[]{:S(2)}) collective-permute-start(bf16[128,2048]{1,0:T(8,128)(2,1)} %get-tuple-element.146), channel_id=1, source_target_pairs={{0,4},{4,0},{8,12},{12,8},{1,5},{5,1},{9,13},{13,9},{2,6},{6,2},{1... | collective-permute-start | bytes 1572872 | tf_op jit(solution)/shard_map/ppermute | solution.py:34
  101.0 27.8 %collective-permute-start.3 = (bf16[128,2048]{1,0:T(8,128)(2,1)}, bf16[128,2048]{1,0:T(8,128)(2,1)}, u32[]{:S(2)}, u32[]{:S(2)}) collective-permute-start(bf16[128,2048]{1,0:T(8,128)(2,1)} %get-tuple-element.147), channel_id=1, source_target_pairs={{0,2},{1,3},{2,0},{3,1},{4,6},{5,7},{6,4},{7,5},{8,10},{9,11},{10,... | collective-permute-start | bytes 1572872 | tf_op jit(solution)/shard_map/ppermute | solution.py:34
  118.3 8.6 copy-start.19
  118.3 8.6 copy-start.20
  118.3 8.5 copy-start.21
  158.3 85.8 %collective-permute-start.9 = (bf16[768,256]{1,0:T(8,128)(2,1)S(1)}, bf16[768,256]{1,0:T(8,128)(2,1)S(1)}, u32[]{:S(2)}, u32[]{:S(2)}) collective-permute-start(bf16[768,256]{1,0:T(8,128)(2,1)S(1)} %dynamic_slice.29), channel_id=1, source_target_pairs={{0,8},{4,12},{8,0},{12,4},{1,9},{5,13},{9,1},{13,5},{2,10},{6,14},... | collective-permute-start | bytes 1179656 | tf_op jit(solution)/shard_map/ppermute | solution.py:34
  163.4 80.7 %collective-permute-start.8 = (bf16[256,768]{1,0:T(8,128)(2,1)S(1)}, bf16[256,768]{1,0:T(8,128)(2,1)S(1)}, u32[]{:S(2)}, u32[]{:S(2)}) collective-permute-start(bf16[256,768]{1,0:T(8,128)(2,1)S(1)} %dynamic_slice.28), channel_id=1, source_target_pairs={{0,8},{4,12},{8,0},{12,4},{1,9},{5,13},{9,1},{13,5},{2,10},{6,14},... | collective-permute-start | bytes 1179656 | tf_op jit(solution)/shard_map/ppermute | solution.py:34
  163.5 80.6 %collective-permute-start.7 = (bf16[256,768]{1,0:T(8,128)(2,1)S(1)}, bf16[256,768]{1,0:T(8,128)(2,1)S(1)}, u32[]{:S(2)}, u32[]{:S(2)}) collective-permute-start(bf16[256,768]{1,0:T(8,128)(2,1)S(1)} %dynamic_slice.27), channel_id=1, source_target_pairs={{0,8},{4,12},{8,0},{12,4},{1,9},{5,13},{9,1},{13,5},{2,10},{6,14},... | collective-permute-start | bytes 1179656 | tf_op jit(solution)/shard_map/ppermute | solution.py:34
  167.5 217.2 %collective-permute-start.5 = (bf16[256,2048]{1,0:T(8,128)(2,1)S(1)}, bf16[256,2048]{1,0:T(8,128)(2,1)S(1)}, u32[]{:S(2)}, u32[]{:S(2)}) collective-permute-start(bf16[256,2048]{1,0:T(8,128)(2,1)S(1)} %pad_maximum_fusion), channel_id=1, source_target_pairs={{0,2},{1,3},{2,0},{3,1},{4,6},{5,7},{6,4},{7,5},{8,10},{9,11},{10,... | collective-permute-start | bytes 3145736 | tf_op jit(solution)/shard_map/ppermute | solution.py:34
  168.7 216.0 %collective-permute-start.6 = (bf16[256,2048]{1,0:T(8,128)(2,1)S(1)}, bf16[256,2048]{1,0:T(8,128)(2,1)S(1)}, u32[]{:S(2)}, u32[]{:S(2)}) collective-permute-start(bf16[256,2048]{1,0:T(8,128)(2,1)S(1)} %pad_maximum_fusion.1), channel_id=1, source_target_pairs={{0,4},{4,0},{8,12},{12,8},{1,5},{5,1},{9,13},{13,9},{2,6},{6,2},{1... | collective-permute-start | bytes 3145736 | tf_op jit(solution)/shard_map/ppermute | solution.py:34
  365.6 19.1 %copy-start.16 = (bf16[1024,2048]{1,0:T(8,128)(2,1)S(1)}, bf16[1024,2048]{1,0:T(8,128)(2,1)}, u32[]{:S(2)}) copy-start(bf16[1024,2048]{1,0:T(8,128)(2,1)} %constant_dynamic-update-slice_fusion.1) | copy-start | bytes 12582916
  384.9 18.0 %copy-start.17 = (bf16[1024,2048]{1,0:T(8,128)(2,1)}, bf16[1024,2048]{1,0:T(8,128)(2,1)S(1)}, u32[]{:S(2)}) copy-start(bf16[1024,2048]{1,0:T(8,128)(2,1)S(1)} %slice_dynamic-update-slice_fusion) | copy-start | bytes 12582916
  385.0 18.0 %copy-start.24 = (bf16[1024,2048]{1,0:T(8,128)(2,1)S(1)}, bf16[1024,2048]{1,0:T(8,128)(2,1)}, u32[]{:S(2)}) copy-start(bf16[1024,2048]{1,0:T(8,128)(2,1)} %get-tuple-element.79) | copy-start | bytes 12582916
  433.1 10.8 %copy-start.18 = (bf16[1024,2048]{1,0:T(8,128)(2,1)S(1)}, bf16[1024,2048]{1,0:T(8,128)(2,1)}, u32[]{:S(2)}) copy-start(bf16[1024,2048]{1,0:T(8,128)(2,1)} %copy-done.17) | copy-start | bytes 12582916
  433.1 10.8 %copy-start.29 = (bf16[1024,1536]{1,0:T(8,128)(2,1)S(1)}, bf16[1024,1536]{1,0:T(8,128)(2,1)}, u32[]{:S(2)}) copy-start(bf16[1024,1536]{1,0:T(8,128)(2,1)} %get-tuple-element.137) | copy-start | bytes 9437188
  452.6 96.1 %copy-start.26 = (bf16[512,2048]{1,0:T(8,128)(2,1)S(1)}, bf16[512,2048]{1,0:T(8,128)(2,1)}, u32[]{:S(2)}) copy-start(bf16[512,2048]{1,0:T(8,128)(2,1)} %get-tuple-element.73) | copy-start | bytes 6291460
  548.7 6.0 copy-start.1
  548.7 9.4 %copy-start.27 = (bf16[512,1536]{1,0:T(8,128)(2,1)S(1)}, bf16[512,1536]{1,0:T(8,128)(2,1)}, u32[]{:S(2)}) copy-start(bf16[512,1536]{1,0:T(8,128)(2,1)} %get-tuple-element.87) | copy-start | bytes 4718596
  554.8 44.4 %collective-permute-start.10 = (bf16[512,768]{1,0:T(8,128)(2,1)S(1)}, bf16[512,768]{1,0:T(8,128)(2,1)S(1)}, u32[]{:S(2)}, u32[]{:S(2)}) collective-permute-start(bf16[512,768]{1,0:T(8,128)(2,1)S(1)} %slice.125), channel_id=1, source_target_pairs={{0,8},{4,12},{8,0},{12,4},{1,9},{5,13},{9,1},{13,5},{2,10},{6,14},... | collective-permute-start | bytes 2359304 | tf_op jit(solution)/shard_map/ppermute | solution.py:34
  558.1 41.2 %collective-permute-start.11 = (bf16[512,1536]{1,0:T(8,128)(2,1)S(1)}, bf16[512,1536]{1,0:T(8,128)(2,1)S(1)}, u32[]{:S(2)}, u32[]{:S(2)}) collective-permute-start(bf16[512,1536]{1,0:T(8,128)(2,1)S(1)} %copy-done.27), channel_id=1, source_target_pairs={{0,16},{16,0},{1,17},{17,1},{2,18},{18,2},{3,19},{19,3},{4,20},{20... | collective-permute-start | bytes 4718600 | tf_op jit(solution)/shard_map/ppermute | solution.py:34
  558.1 26.2 %copy-start.30 = (bf16[1024,1536]{1,0:T(8,128)(2,1)S(1)}, bf16[1024,1536]{1,0:T(8,128)(2,1)}, u32[]{:S(2)}) copy-start(bf16[1024,1536]{1,0:T(8,128)(2,1)} %get-tuple-element.137) | copy-start | bytes 9437188
  584.3 11.1 %copy-start.23 = (bf16[1024,2048]{1,0:T(8,128)(2,1)S(1)}, bf16[1024,2048]{1,0:T(8,128)(2,1)}, u32[]{:S(2)}) copy-start(bf16[1024,2048]{1,0:T(8,128)(2,1)} %get-tuple-element.82) | copy-start | bytes 12582916
  584.3 11.1 %copy-start.28 = (bf16[1024,512]{1,0:T(8,128)(2,1)S(1)}, bf16[1024,512]{1,0:T(8,128)(2,1)}, u32[]{:S(2)}) copy-start(bf16[1024,512]{1,0:T(8,128)(2,1)} %get-tuple-element.72) | copy-start | bytes 3145732
  744.0 10.2 %copy-start.22 = (bf16[1024,2048]{1,0:T(8,128)(2,1)S(1)}, bf16[1024,2048]{1,0:T(8,128)(2,1)}, u32[]{:S(2)}) copy-start(bf16[1024,2048]{1,0:T(8,128)(2,1)} %get-tuple-element.59) | copy-start | bytes 12582916
  744.0 10.2 %copy-start.25 = (bf16[1024,1280]{1,0:T(8,128)(2,1)S(1)}, bf16[1024,1280]{1,0:T(8,128)(2,1)}, u32[]{:S(2)}) copy-start(bf16[1024,1280]{1,0:T(8,128)(2,1)} %get-tuple-element.92) | copy-start | bytes 7864324
  864.0 6.6 copy-start.7
  865.5 7.2 copy-start.6
  (11 other events, 28.0 us)

commit v6 on v5

--- a/solution.py
+++ b/solution.py
@@ -202,28 +202,32 @@
     starts = start_ref[...]
     rows = jnp.concatenate([rows] * repeat, axis=0)
     starts = jnp.concatenate([starts] * repeat, axis=0)
-    for k in range(pairs):
-        heads = [k * repeat + r for r in range(repeat)]
-        query = jnp.concatenate([q_ref[:, h * size : (h + 1) * size] for h in heads], axis=0)
-        key_cols = slice(k * size, (k + 1) * size)
-        value_cols = slice((pairs + k) * size, (pairs + k + 1) * size)
-
-        def seen(total, where, first):
-            keys = join([kv_ref[at, key_cols] for at in where])
-            weights = jnp.exp2(dot_trans(query, keys))
+    queries = [
+        jnp.concatenate([q_ref[:, h * size : (h + 1) * size] for h in range(k * repeat, (k + 1) * repeat)], axis=0)
+        for k in range(pairs)
+    ]
+
+    def seen(totals, where, first):
+        outs = []
+        for k in range(pairs):
+            keys = join([kv_ref[at, k * size : (k + 1) * size] for at in where])
+            weights = jnp.exp2(dot_trans(queries[k], keys))
             if first is not None:
                 index = first + lax.broadcasted_iota(jnp.int32, weights.shape, 1)
                 weights = jnp.where((index <= rows) & (index >= starts), weights, 0.0)
-            values = join([kv_ref[at, value_cols] for at in where])
+            values = join([kv_ref[at, (pairs + k) * size : (pairs + k + 1) * size] for at in where])
             values = jnp.concatenate([values, jnp.ones_like(values)], axis=1)
-            return total + dot_rows(weights.astype(BF16), values)
-
-        total = jnp.zeros((query.shape[0], 2 * size), F32)
-        total = lax.fori_loop(0, wide_blocks, lambda i, t: seen(t, pair(i), None), total)
-        total = lax.fori_loop(low, high + 1, lambda i, t: seen(t, single(i), i * step), total)
+            outs.append(totals[k] + dot_rows(weights.astype(BF16), values))
+        return tuple(outs)
+
+    totals = tuple(jnp.zeros((query.shape[0], 2 * size), F32) for query in queries)
+    totals = lax.fori_loop(0, wide_blocks, lambda i, t: seen(t, pair(i), None), totals)
+    totals = lax.fori_loop(low, high + 1, lambda i, t: seen(t, single(i), i * step), totals)
+    for k, total in enumerate(totals):
         inverse = 1.0 / total[:, size:]
         context = total[:, :size] * inverse
-        for r, h in enumerate(heads):
+        for r in range(repeat):
+            h = k * repeat + r
             part = context[r * step : (r + 1) * step]
             cols = slice(h * size, (h + 1) * size)
             gate = jax.nn.sigmoid(logit_of(h, pairs * repeat, own_ref, other_ref))
@@ -363,7 +367,10 @@
         self.y, self.core = self.narrow // 2, self.narrow % 2
         self.x, self.far = self.dp % 2, self.wide // 2
 
-    def peer(self, axis, distance):
+    def peer(self, *to):
+        if isinstance(to[0], tuple):
+            return {axis: at for part in to for axis, at in self.peer(*part).items()}
+        axis, distance = to
         at = {"dp": self.dp, "wide": self.wide, "narrow": self.narrow}[axis]
         bit = at // distance % 2
         return {axis: at + distance * (1 - 2 * bit) if distance < 3 else 3 - at}
@@ -447,7 +454,7 @@
     yield
 
 
-def weight_flow(net, source_ref, out_ref, axis, own, other, across, from_y=None, from_far=None):
+def weight_flow(net, source_ref, out_ref, axis, own, other, across, from_y=None, from_far=None, from_both=None):
     step = source_ref.shape[axis] // 2
     count = source_ref.shape[axis]
 
@@ -475,7 +482,10 @@
         yield
         net.arrived(come_y)
         from_y = place(1 - y, 0, own)
-    come_both = net.send(from_y, place(1 - y, 0, other), FAR)
+    if from_both is None:
+        come_both = net.send(from_y, place(1 - y, 0, other), FAR)
+    else:
+        net.copy(from_both, place(1 - y, 0, other))
     their_y = net.send(from_y, place(1 - y, 1, own), X)
     net.send(from_y, place(3 - y, 0, own), CORE)
     if from_far is None:
@@ -484,11 +494,12 @@
         from_far = place(y, 0, other)
     their_far = net.send(from_far, place(y, 1, other), X)
     net.send(from_far, place(2 + y, 0, other), CORE)
-    yield
-    net.arrived(come_both)
-    both = place(1 - y, 0, other)
-    their_both = net.send(both, place(1 - y, 1, other), X)
-    net.send(both, place(3 - y, 0, other), CORE)
+    if from_both is None:
+        yield
+        net.arrived(come_both)
+        from_both = place(1 - y, 0, other)
+    their_both = net.send(from_both, place(1 - y, 1, other), X)
+    net.send(from_both, place(3 - y, 0, other), CORE)
     yield
     for copy, slot, start in ((their_y, 1 - y, own), (their_far, y, other), (their_both, 1 - y, other)):
         net.arrived(copy)
@@ -580,9 +591,10 @@
     )
 
 
-def keys_kernel(kv_ref, keys_ref, send, recv, local, *, sizes):
+def keys_kernel(kv_ref, keys_ref, done, send, recv, local, *, sizes):
     net = Wires(send, recv, local, sizes)
-    net.greet([CORE, FAR])
+    across = [FAR, ("wide", 3), (FAR, CORE), (("wide", 3), CORE)]
+    net.greet([CORE] + across)
     count, width = kv_ref.shape
     size = width // 4
     part = lambda i, j: keys_ref.at[pl.ds(i, count), pl.ds(j * size, size)]
@@ -603,6 +615,8 @@
         for copy, forward in zip(far, on):
             copy.wait_recv()
             forward.start()
+        for to in across:
+            pl.semaphore_signal(done, inc=1, device_id=net.peer(*to), device_id_type=pl.DeviceIdType.MESH)
         for forward in on:
             forward.wait()
 
@@ -610,6 +624,7 @@
     def _():
         for copy in far:
             copy.wait_send()
+        pl.semaphore_wait(done, len(across))
 
     net.sent = [copy for copy in net.sent if all(copy is not other for other in far + on)]
     net.finish()
@@ -617,7 +632,8 @@
 
 def exchange_keys(kv, sizes):
     return wire_call(
-        keys_kernel, "keys", 2, [VMEM], [ANY], [((4 * kv.shape[0], kv.shape[1]), BF16)], [*sems(16, 4)], sizes, 45, kv,
+        keys_kernel, "keys", 2, [VMEM], [ANY], [((4 * kv.shape[0], kv.shape[1]), BF16)],
+        [pltpu.SemaphoreType.REGULAR, *sems(16, 4)], sizes, 45, kv,
     )[0]
 
 
@@ -656,7 +672,7 @@
 
 def middle_kernel(
     partial_ref, x_ref, gain_ref, gate_ref, up_ref, down_ref, gate_y_ref, up_y_ref, down_y_ref, gate_far_ref, up_far_ref, down_far_ref,
-    middle_ref, all_ref, both_ref, last_ref,
+    gate_both_ref, up_both_ref, down_both_ref, middle_ref, all_ref, both_ref, last_ref,
     first, second, sums, last, total, normed, send, recv, local, *, sizes,
 ):
     net = Wires(send, recv, local, sizes)
@@ -665,9 +681,9 @@
     run(scatter)
     across = gate_ref.shape[1] // 2
     flows = [
-        weight_flow(net, gate_ref, both_ref, 0, 0, across, across, gate_y_ref, gate_far_ref),
-        weight_flow(net, up_ref, both_ref, 0, 2 * across, 3 * across, across, up_y_ref, up_far_ref),
-        weight_flow(net, down_ref, last_ref, 1, 0, across, across, down_y_ref, down_far_ref),
+        weight_flow(net, gate_ref, both_ref, 0, 0, across, across, gate_y_ref, gate_far_ref, gate_both_ref),
+        weight_flow(net, up_ref, both_ref, 0, 2 * across, 3 * across, across, up_y_ref, up_far_ref, up_both_ref),
+        weight_flow(net, down_ref, last_ref, 1, 0, across, across, down_y_ref, down_far_ref, down_both_ref),
     ]
     for flow in flows:
         run(flow)
@@ -685,12 +701,10 @@
     gather = gather_flow(net, normed, all_ref)
     run(gather)
     run(flows[0])
+    run(gather)
+    run(gather)
     run(flows[1])
-    run(gather)
     run(flows[2])
-    run(gather)
-    for flow in flows:
-        run(flow)
     net.finish()
 
 
@@ -698,11 +712,11 @@
     rows, width = x.shape
     buffer = lambda n, kind: pltpu.VMEM((n, width), kind)
     return wire_call(
-        middle_kernel, "middle", 3, [VMEM] * 12, [VMEM, ANY, ANY, ANY],
+        middle_kernel, "middle", 3, [VMEM] * 15, [VMEM, ANY, ANY, ANY],
         [((rows, width), F32), ((4 * rows, width), BF16), ((width, 2 * gate.shape[1]), BF16), ((down.shape[0], width), BF16)],
         [
             buffer(rows, BF16), buffer(rows, BF16), buffer(rows, BF16), buffer(rows, BF16), buffer(rows, F32), buffer(rows, BF16),
-            *sems(64, 16),
+            *sems(64, 24),
         ],
         sizes, 80, partial, x, gain[None], gate, up, down, *pieces,
     )
@@ -829,12 +843,11 @@
     step, across = low.shape[1] // sizes["narrow"] // 2, gate_ref.shape[1] // 2
     down, gate, up = (Gradient(net, axis, step, across) for axis in (1, 0, 0))
     down.start(down_ref, *buffers[0:2])
-    gate.start(gate_ref, *buffers[4:6])
-    up.start(up_ref, *buffers[7:9])
+    gate.start(gate_ref, *buffers[3:5])
+    up.start(up_ref, *buffers[6:8])
     down.core_to_x(buffers[2])
-    gate.core_to_x(buffers[6])
-    run(scatter)
-    down.x_end(0, buffers[3])
+    gate.core_to_x(buffers[5])
+    run(scatter)
     run(scatter)
     run(scatter)
     term_ref[...] = jnp.zeros_like(term_ref)
@@ -850,7 +863,9 @@
     by_rows(low.shape[0], rows)
     gather = gather_flow(net, low, all_ref)
     run(gather)
-    down.x_end(1, buffers[3])
+    for k in range(2):
+        down.x_end(k)
+        net.copy(down.acc.at[down.slot(k, 2, 0, 2 * across)], down_out.at[down.slot(k, 1, 0, 2 * across)])
     run(gather)
     run(gather)
     up.wait_core()
@@ -862,9 +877,6 @@
     for k in range(2):
         gate.x_end(k)
         net.copy(gate.acc.at[gate.slot(k, 2, 0, 2 * across)], gate_out.at[gate.slot(k, 1, 0, 2 * across)])
-    for k in range(2):
-        down.far_end(k)
-        net.copy(down.acc.at[down.slot(k, 2, 0, across)], down_out.at[down.slot(k, 1, 0, across)])
     net.finish()
 
 
@@ -886,20 +898,20 @@
         turn_kernel, "turn", 4, [VMEM] * 4 + [ANY] * 3, [VMEM, ANY, VMEM, ANY, ANY, ANY, ANY],
         [
             ((rows, width), F32), ((4 * rows, width), BF16), ((1, width), F32),
-            ((across, size), BF16), ((size, 2 * across), BF16), ((size, 2 * across), BF16), ((size, 2 * across), BF16),
+            ((2 * across, size), BF16), ((size, 2 * across), BF16), ((size, 2 * across), BF16), ((size, 2 * across), BF16),
         ],
         [
             *scatter_buffers(rows, width), pltpu.VMEM((rows, width), BF16),
-            *gradient_buffers(size, across, 1), *gradient_buffers(size, across, 0, 3), *gradient_buffers(size, across, 0, 2), *sems(40, 16),
+            *gradient_buffers(size, across, 1, 3), *gradient_buffers(size, across, 0, 3), *gradient_buffers(size, across, 0, 2), *sems(40, 16),
         ],
         sizes, 80, partial, middle, upstream, gain[None], down, gate, up,
     )
 
 
 def owner_kernel(
-    dkv_ref, partial_ref, middle_ref, down_ref, gate_ref, gate_far_ref, up_ref, up_x_ref,
-    mine_ref, layer_ref, down_out, gate_out, up_out,
-    prompt_core, rest_core, prompt, prompt_far, first, second, sums, last, total, rows_low, gate_sums, up_acc, up_far, up_sums,
+    dkv_ref, partial_ref, middle_ref, down_ref, down_far_ref, gate_ref, gate_far_ref,
+    mine_ref, layer_ref, down_out, gate_out,
+    prompt_core, rest_core, prompt, prompt_far, first, second, sums, last, total, rows_low, down_sums, gate_sums,
     send, recv, local, *, sizes,
 ):
     net = Wires(send, recv, local, sizes)
@@ -911,10 +923,8 @@
     rest = net.send(region(3), rest_core, CORE)
     scatter = scatter_flow(net, partial_ref, first, second, sums, last, total)
     run(scatter)
-    step, across = down_ref.shape[1] // 2, down_ref.shape[0]
-    down, gate, up = (Gradient(net, axis, step, across) for axis in (1, 0, 0))
-    for k in range(2):
-        down.to_owner(k, down_ref.at[down.slot(k, 1, 0, across)], down_out)
+    step, across = down_far_ref.shape[1] // 2, down_far_ref.shape[0]
+    down, gate = (Gradient(net, axis, step, across) for axis in (1, 0))
     net.arrived(come)
 
     def add(at):
@@ -929,16 +939,12 @@
         for copy in far:
             copy.start()
 
-    for k in range(2):
-        for start in (across, 0):
-            place = up.slot(k, 1, start, across)
-            add_rows((up_acc, place), [(up_ref, place), (up_x_ref, place)])
-            if start:
-                up.far.append(net.send(up_acc.at[place], up_far.at[up.slot(k, 1, 0, across)], FAR))
-    for k in range(2):
-        place = gate.slot(k, 1, 0, across)
-        add_rows((gate_sums, place), [(gate_ref, place), (gate_far_ref, place)])
-        gate.to_owner(k, gate_sums.at[place], gate_out)
+    parts = ((down, down_sums, down_ref, down_far_ref, down_out), (gate, gate_sums, gate_ref, gate_far_ref, gate_out))
+    for flow, total_ref, ref, far_ref, goal in parts:
+        for k in range(2):
+            place = flow.slot(k, 1, 0, across)
+            add_rows((total_ref, place), [(ref, place), (far_ref, place)])
+            flow.to_owner(k, total_ref.at[place], goal)
     run(scatter)
     run(scatter)
     run(scatter)
@@ -973,32 +979,25 @@
         by_rows(count, add)
 
     net.sent = [copy for copy in net.sent if all(copy is not other for other in far)]
-    for k in range(2):
-        net.arrived(up.far[k])
-        place = up.slot(k, 1, 0, across)
-        add_rows((up_sums, place), [(up_acc, place), (up_far, place)])
-        up.to_owner(k, up_sums.at[place], up_out)
-    up.after_y()
     net.finish()
 
 
-def to_owner(dkv, partial, middle, down, gate, gate_far, up, up_x, sizes):
+def to_owner(dkv, partial, middle, down, down_far, gate, gate_far, sizes):
     rows, width = middle.shape
     size, across = width // sizes["narrow"], gate_far.shape[1]
     count = dkv.shape[0] // 4
     block = lambda: pltpu.VMEM((count, dkv.shape[1]), BF16)
-    part = lambda wide: pltpu.VMEM((size, wide), BF16)
     return wire_call(
-        owner_kernel, "owner", 5, [VMEM] * 8, [VMEM, ANY, ANY, ANY, ANY],
+        owner_kernel, "owner", 5, [VMEM] * 7, [VMEM, ANY, ANY, ANY],
         [
-            ((count, dkv.shape[1]), F32), ((sizes["narrow"] * rows, size), BF16),
-            ((2 * across, size), BF16), ((size, 2 * across), BF16), ((size, 2 * across), BF16),
+            ((count, dkv.shape[1]), F32), ((sizes["narrow"] * rows, size), BF16), ((2 * across, size), BF16),
+            ((size, 2 * across), BF16),
         ],
         [
             block(), block(), block(), block(), *scatter_buffers(rows, width), pltpu.VMEM((rows, width), BF16),
-            part(across), part(2 * across), part(across), part(across), *sems(40, 16),
+            pltpu.VMEM((across, size), BF16), pltpu.VMEM((size, across), BF16), *sems(40, 16),
         ],
-        sizes, 80, dkv, partial, middle, down, gate, gate_far, up, up_x,
+        sizes, 80, dkv, partial, middle, down, down_far, gate, gate_far,
     )
 
 
@@ -1006,9 +1005,9 @@
 
 
 def end_kernel(
-    partial_ref, x_ref, gain_ref, grad_ref, two_ref, query_ref, key_ref, qkv_ref, out_ref,
-    tokens_ref, gains_ref, qkv_out, out_out,
-    first, second, sums, last, total, rows_low, vectors, *rest, sizes,
+    partial_ref, x_ref, gain_ref, grad_ref, two_ref, query_ref, key_ref, up_ref, up_far_ref, qkv_ref, out_ref,
+    tokens_ref, gains_ref, qkv_out, out_out, up_out,
+    first, second, sums, last, total, rows_low, vectors, up_sums, *rest, sizes,
 ):
     buffers, (send, recv, local) = rest[:-3], rest[-3:]
     net = Wires(send, recv, local, sizes)
@@ -1020,8 +1019,13 @@
     out.start(out_ref, *buffers[4:6])
     scatter = scatter_flow(net, partial_ref, first, second, sums, last, total)
     run(scatter)
+    up = Gradient(net, 0, step, up_far_ref.shape[1])
     qkv.core_to_x(buffers[2])
     out.core_to_x(buffers[6])
+    for k in range(2):
+        place = up.slot(k, 1, 0, up.across)
+        add_rows((up_sums, place), [(up_ref, place), (up_far_ref, place)])
+        up.to_owner(k, up_sums.at[place], up_out)
     run(scatter)
     qkv.x_end(0, buffers[3])
     run(scatter)
@@ -1076,25 +1080,28 @@
     run(gains)
     own(out, 0, out_out)
     own(out, 1, out_out)
+    up.after_y()
     qkv.after_y()
     out.after_y()
     run(gains)
     net.finish()
 
 
-def end(partial, x, gain, grad, two, query, key, qkv, out, sizes):
+def end(partial, x, gain, grad, two, query, key, up, up_far, qkv, out, sizes):
     rows, width = x.shape
     size = width // sizes["narrow"]
     wide, deep = qkv.shape[1], out.shape[0]
     length = 2 * width + 2 * query.shape[1]
     return wire_call(
-        end_kernel, "end", 6, [VMEM] * 7 + [ANY] * 2, [ANY, VMEM, ANY, ANY],
-        [((sizes["narrow"] * rows, size), BF16), ((1, length), F32), ((size, wide), BF16), ((deep, size), BF16)],
+        end_kernel, "end", 6, [VMEM] * 9 + [ANY] * 2, [ANY, VMEM, ANY, ANY, ANY],
+        [((sizes["narrow"] * rows, size), BF16), ((1, length), F32), ((size, wide), BF16), ((deep, size), BF16),
+         ((size, 2 * up_far.shape[1]), BF16)],
         [
             *scatter_buffers(rows, width), pltpu.VMEM((rows, width), BF16), pltpu.VMEM((2 * len(SUMS) + 1, 1, length), F32),
+            pltpu.VMEM(up_far.shape, BF16),
             *gradient_buffers(size, wide // 2, 0), *gradient_buffers(size, deep // 2, 1), *sems(40, 16),
         ],
-        sizes, 90, partial, x, gain[None], grad, two, query, key, qkv, out,
+        sizes, 90, partial, x, gain[None], grad, two, query, key, up, up_far, qkv, out,
     )
 
 
@@ -1202,11 +1209,11 @@
         send = after((gate_weight, up_weight, down_weight), normed_all)
         axes = (0, 0, 1)
         from_y = [over_y(piece_of(w, 1 - y, axis)) for w, axis in zip(send, axes)]
+        from_far = [over_far(piece_of(w, y, axis)) for w, axis in zip(send, axes)]
         part = rows_local // 2
         upstream_y, upstream_z = over_y(upstream[:part]), over_z(upstream[part:])
-        kv_all = exchange_keys(after(kv, *from_y, upstream_y, upstream_z), sizes)
-        send = after((gate_weight, up_weight, down_weight), kv_all)
-        from_far = [over_far(piece_of(w, y, axis)) for w, axis in zip(send, axes)]
+        kv_all = exchange_keys(after(kv, *from_y, *from_far, upstream_y, upstream_z), sizes)
+        from_both = [over_far(after(v, kv_all)) for v in from_y]
         come_z = over_z(join([upstream[:part], after(upstream_y, kv_all)]))
         come_y = over_y(join([upstream[part:], after(upstream_z, kv_all)]))
         upstream_all = join(
@@ -1218,7 +1225,7 @@
         )
         partial = dot_rows(gated, out_weight).astype(BF16)
         middle, normed_two_all, gate_up, down = to_middle(
-            partial, inputs, gain_two, gate_weight, up_weight, down_weight, from_y + from_far, sizes
+            partial, inputs, gain_two, gate_weight, up_weight, down_weight, from_y + from_far + from_both, sizes
         )
         both = dot_rows(normed_two_all, gate_up)
         hidden_cols = gate_weight.shape[1]
@@ -1238,6 +1245,7 @@
         middle_grad, middle_all, two_term, down_part, gate_part, up_keep, up_send = turn(
             partial, middle, upstream, gain_two, down_sums, gate_sums, up_sums, sizes
         )
+        down_far = over_far(down_part[hidden_cols // 2 :])
         gate_far = over_far(gate_part[:, hidden_cols // 2 :])
         up_come = over_x(up_send)
         gated_grad = dot_trans(middle_all, out_weight)
@@ -1245,17 +1253,20 @@
             table, q, kv_all, my_index, my_start, raw, context, inverse_total, gated_grad, pairs, size
         )
         partial = dot_rows(hidden, down).astype(BF16)
-        dkv_mine, layer_output, down_gradient, gate_gradient, up_gradient = to_owner(
-            dkv, partial, middle, down_part, gate_part, gate_far, up_keep, up_come, sizes
+        up_part = (up_keep.astype(F32) + up_come.astype(F32)).astype(BF16)
+        dkv_mine, layer_output, down_gradient, gate_gradient = to_owner(
+            dkv, partial, middle, down_part, down_far, gate_part, gate_far, sizes
         )
+        up_far = over_far(after(up_part[:, hidden_cols // 2 :], dkv_mine))
         low, query_term, key_term = project_back(
             dq, dkv_mine, raw, cosine, sine, query_gain, key_gain, logit_grad, heads, pairs, size, scale, log_two
         )
         partial = dot_trans(low, joined_weight).astype(BF16)
         qkv_sums = dot_inner(normed_all, low).astype(BF16)
         out_sums = dot_inner(gated, middle_all).astype(BF16)
-        tokens_gradient, gains, qkv_gradient, output_gradient = end(
-            partial, inputs, gain_one, middle_grad, two_term, query_term, key_term, qkv_sums, out_sums, sizes
+        tokens_gradient, gains, qkv_gradient, output_gradient, up_gradient = end(
+            partial, inputs, gain_one, middle_grad, two_term, query_term, key_term, up_part[:, : hidden_cols // 2], up_far,
+            qkv_sums, out_sums, sizes
         )
         tokens_gradient = tokens_gradient.astype(F32)
         gains = over_groups(gains[0], F32)

time: 889 us -> 868 us (0.976)
  waiting for transfers between devices: 0.03 us -> 98.1 us
  Pallas kernels: 608 us -> 541 us
  starting transfers between devices: 69.9 us -> 22.6 us
    ppermute x12 -> x17, waiting for transfers between devices: 0.03 us -> 98.1 us  [exchange(): return lax.ppermute(values, axis, [(i, i ^ distance) for i in range(size)])]
    pallas_call x6, Pallas kernels: 549 us -> 485 us  [wire_call(): pl.pallas_call(functools.partial(kernel, sizes=sizes), in_specs=specs, ou...]
    ppermute x12 -> x17, starting transfers between devices: 69.9 us -> 22.6 us  [exchange(): return lax.ppermute(values, axis, [(i, i ^ distance) for i in range(size)])]
  transfers between devices with their start and end apart: 12 -> 17, of which waited for: 0 -> 8; matrix products, arithmetic and copies ran while one was open for 8% -> 9% of each run, Pallas kernels for 19% -> 27%
where the time goes in v6:
time: 868 us; the launch traced here: 860 us
  Pallas kernels  541 us (62%)
  matrix products  141 us (16%)
  waiting for transfers between devices  98.1 us (11%)
  local copies, waits for them, and re-layouts  32.1 us (4%)
  other arithmetic  23 us (3%)
  starting transfers between devices  22.6 us (3%)
    pallas_call x6, Pallas kernels, wire_call(): pl.pallas_call(functools.partial(kernel, sizes=sizes), in_specs=specs, ou...  485 us
    ppermute x17, waiting for transfers between devices, exchange(): return lax.ppermute(values, axis, [(i, i ^ distance) for i in range(size)])  98.1 us
    dot_general x4, matrix products, dot_trans(): lax.dot_general(left, right, (((1,), (1,)), ((), ())), preferred_element_...  53.4 us
    dot_general x4, matrix products, dot_rows(): return jnp.dot(left, right, preferred_element_type=F32)  46 us
    dot_general x5, matrix products, dot_inner(): lax.dot_general(left, right, (((0,), (0,)), ((), ())), preferred_element_...  41.7 us
    pallas_call x1, Pallas kernels, attend_back(): pl.pallas_call(functools.partial(backward_kernel, pairs=pairs, repeat=hea...  26.1 us
    ppermute x17, starting transfers between devices, exchange(): return lax.ppermute(values, axis, [(i, i ^ distance) for i in range(size)])  22.6 us
  transfers between devices with their start and end apart: 17, of which 8 were waited for; matrix products, arithmetic and copies ran while one was open for 9% of the time, Pallas kernels for 27%

profile of v6, /device:TPU:0, one launch (start us, length us, event | category | flops | bytes accessed | tf_op | source)
XLA Modules:
  0.0 859.7 jit_solution(3919635315787080743)
XLA Ops:
  11.2 75.5 %begin.1 = (bf16[256,2048]{1,0:T(8,128)(2,1)}, bf16[256,2048]{1,0:T(8,128)(2,1)}, bf16[1024,2048]{1,0:T(8,128)(2,1)}, bf16[2048,1280]{1,0:T(8,128)(2,1)}, bf16[512,2048]{1,0:T(8,128)(2,1)}) custom-call(bf16[1024,512]{1,0:T(8,128)(2,1)} %tokens_ref.1, bf16[1024,512]{1,0:T(8,128)(2,1)} %cotangent_ref.1, f32[1,2048]{1,0:T(1,128)} %broadcast_in_dim_reshape.8.gain_ref, ...), custom_call_target="tpu_custom_call" | custom-call | bytes 165000000 | tf_op jit(solution)/shard_map/begin/pallas_call | solution.py:569
  94.5 4.8 collective-permute-start.7
  103.4 10.4 %fusion.72.raw_ref.own_ref.other_ref = f32[1024,1280]{1,0:T(8,128)} fusion(bf16[1024,2048]{1,0:T(8,128)(2,1)} %get-tuple-element.60, bf16[2048,1280]{1,0:T(8,128)(2,1)} %get-tuple-element.61), kind=kOutput, calls=%fused_computation.185 | convolution fusion | flops 5368709120 | bytes 14680064 | tf_op jit(solution)/shard_map/dot_general | solution.py:22
  118.9 6.4 post.1
  129.3 8.2 collective-permute-done.1.up_y_ref
  137.5 8.5 collective-permute-done.5.down_far_ref
  146.8 51.1 %keys.1.kv_ref = bf16[4096,512]{1,0:T(8,128)(2,1)} custom-call(bf16[1024,512]{1,0:T(8,128)(2,1)} %get-tuple-element.68.kv_ref), custom_call_target="tpu_custom_call" | custom-call | bytes 135000000 | tf_op jit(solution)/shard_map/keys/pallas_call | solution.py:569
  203.9 15.3 %attend.1 = (bf16[1024,512]{1,0:T(8,128)(2,1)}, f32[1024,512]{1,0:T(8,128)}, f32[1024,512]{1,0:T(8,128)}) custom-call(s32[4,5]{1,0:T(4,128)} %select_select_fusion.table_ref, bf16[1024,512]{1,0:T(8,128)(2,1)} %get-tuple-element.62.q_ref, bf16[4096,512]{1,0:T(8,128)(2,1)} %keys.1.kv_ref, s32[1024,1]{1,0:T(8,128)} %get-tuple-element.169.row_ref, ...), custom_call_target="tpu_custom_call" | custom-call | flops 20000000000 | bytes 12000000 | tf_op jit(solution)/shard_map/attend/pallas_call | solution.py:244
  220.1 6.2 convolution_convert_fusion.6.partial_ref
  226.3 9.4 %collective-permute-done.10.gate_both_ref = bf16[256,768]{1,0:T(8,128)(2,1)S(1)} collective-permute-done((bf16[256,768]{1,0:T(8,128)(2,1)}, bf16[256,768]{1,0:T(8,128)(2,1)S(1)}, u32[]{:S(2)}, u32[]{:S(2)}) %collective-permute-start.10) | collective-permute-done | bytes 393248 | tf_op jit(solution)/shard_map/ppermute | solution.py:34
  235.7 8.4 collective-permute-done.11.up_both_ref
  244.1 8.3 collective-permute-done.12.down_both_ref
  253.2 87.8 %middle.1 = (f32[256,2048]{1,0:T(8,128)}, bf16[1024,2048]{1,0:T(8,128)(2,1)}, bf16[2048,3072]{1,0:T(8,128)(2,1)}, bf16[1536,2048]{1,0:T(8,128)(2,1)}) custom-call(bf16[1024,2048]{1,0:T(8,128)(2,1)} %convolution_convert_fusion.6.partial_ref, bf16[256,2048]{1,0:T(8,128)(2,1)} %get-tuple-element.75.x_ref, f32[1,2048]{1,0:T(1,128)} %broadcast_in_dim_reshape.9.gain_ref, ...), custom_call_target="tpu_custom_call" | custom-call | bytes 240000000 | tf_op jit(solution)/shard_map/middle/pallas_call | solution.py:569
  341.0 19.1 %fusion.73 = f32[1024,3072]{1,0:T(8,128)} fusion(bf16[1024,2048]{1,0:T(8,128)(2,1)} %get-tuple-element.80, bf16[2048,3072]{1,0:T(8,128)(2,1)} %get-tuple-element.81), kind=kOutput, calls=%fused_computation.186 | convolution fusion | flops 12884901888 | bytes 29360128 | tf_op jit(solution)/shard_map/dot_general | solution.py:22
  360.4 17.8 %multiply_convert_fusion.2 = (bf16[1024,1536]{1,0:T(8,128)(2,1)}, bf16[1024,1536]{1,0:T(8,128)(2,1)}, bf16[1024,1536]{1,0:T(8,128)(2,1)}) fusion(f32[1024,3072]{1,0:T(8,128)} %fusion.73, bf16[1024,2048]{1,0:T(8,128)(2,1)S(1)} %slice_dynamic-update-slice_fusion, bf16[1536,2048]{1,0:T(8,128)(2,1)} %get-tuple-element.79), kind=kOutput, calls=%fused_computation.10 | convolution fusion | flops 6466043904 | bytes 32505856 | tf_op jit(solution)/shard_map/dot_general | solution.py:26
  378.3 10.3 %convolution_convert_fusion.4.partial_ref = bf16[1024,2048]{1,0:T(8,128)(2,1)} fusion(bf16[1024,1536]{1,0:T(8,128)(2,1)} %get-tuple-element.139, bf16[1536,2048]{1,0:T(8,128)(2,1)S(1)} %bitcast.57), kind=kOutput, calls=%fused_computation.13 | convolution fusion | flops 6444548096 | bytes 13631488 | tf_op jit(solution)/shard_map/dot_general | solution.py:22
  388.6 8.8 %convolution_convert_fusion.3.down_ref = bf16[1536,2048]{1,0:T(8,128)(2,1)} fusion(bf16[1024,1536]{1,0:T(8,128)(2,1)S(1)} %copy-done.31, bf16[1024,2048]{1,0:T(8,128)(2,1)S(1)} %slice_dynamic-update-slice_fusion), kind=kOutput, calls=%fused_computation.3 | convolution fusion | flops 6445596672 | bytes 13631488 | tf_op jit(solution)/shard_map/dot_general | solution.py:30
  397.4 9.1 %convolution_convert_fusion.2.gate_ref = bf16[2048,1536]{1,0:T(8,128)(2,1)} fusion(bf16[1024,2048]{1,0:T(8,128)(2,1)S(1)} %copy-done.25, bf16[1024,1536]{1,0:T(8,128)(2,1)S(1)} %copy-done.32), kind=kOutput, calls=%fused_computation.2 | convolution fusion | flops 6445596672 | bytes 13631488 | tf_op jit(solution)/shard_map/dot_general | solution.py:30
  406.4 19.4 %fusion.5.partial_ref = bf16[1024,2048]{1,0:T(8,128)(2,1)} fusion(bf16[2048,3072]{1,0:T(8,128)(2,1)} %get-tuple-element.81, bf16[1024,1536]{1,0:T(8,128)(2,1)} %get-tuple-element.138, bf16[1024,1536]{1,0:T(8,128)(2,1)} %get-tuple-element.137), kind=kOutput, calls=%fused_computation.14 | convolution fusion | flops 12899581952 | bytes 23068672 | tf_op jit(solution)/shard_map/dot_general | solution.py:26
  425.8 10.6 %convolution_convert_fusion.1.up_ref = bf16[2048,1536]{1,0:T(8,128)(2,1)} fusion(bf16[1024,2048]{1,0:T(8,128)(2,1)S(1)} %copy-done.25, bf16[1024,1536]{1,0:T(8,128)(2,1)} %get-tuple-element.138), kind=kOutput, calls=%fused_computation.1 | convolution fusion | flops 6445596672 | bytes 13631488 | tf_op jit(solution)/shard_map/dot_general | solution.py:30
  436.4 84.7 %turn.1 = (f32[256,2048]{1,0:T(8,128)}, bf16[1024,2048]{1,0:T(8,128)(2,1)}, f32[1,2048]{1,0:T(1,128)}, bf16[1536,512]{1,0:T(8,128)(2,1)}, bf16[512,1536]{1,0:T(8...) custom-call(bf16[1024,2048]{1,0:T(8,128)(2,1)} %fusion.5.partial_ref, ...), custom_call_target="tpu_custom_call" | custom-call | bytes 240000000 | tf_op jit(solution)/shard_map/turn/pallas_call | solution.py:569
  521.2 6.0 fusion.74.grad_ref
  530.7 26.1 %attend_back.1 = (f32[1024,512]{1,0:T(8,128)}, bf16[4096,512]{1,0:T(8,128)(2,1)}, f32[1024,256]{1,0:T(8,128)}) custom-call(s32[4,5]{1,0:T(4,128)} %select_select_fusion.table_ref, bf16[1024,512]{1,0:T(8,128)(2,1)} %get-tuple-element.62.q_ref, bf16[4096,512]{1,0:T(8,128)(2,1)} %keys.1.kv_ref, s32[4,1,256]{2,1,0:T(1,128)} %get-tuple-element.172.row_ref, ...), custom_call_target="tpu_custom_call" | custom-call | flops 49999998976 | bytes 20000000 | tf_op jit(solution)/shard_map/attend_back/pallas_call | solution.py:340
  556.8 5.9 convolution_convert_fusion.7.out_ref
  562.7 17.9 %collective-permute-done.14.gate_far_ref = bf16[512,768]{1,0:T(8,128)(2,1)S(1)} collective-permute-done((bf16[512,768]{1,0:T(8,128)(2,1)S(1)}, bf16[512,768]{1,0:T(8,128)(2,1)S(1)}, u32[]{:S(2)}, u32[]{:S(2)}) %collective-permute-start.14) | collective-permute-done | bytes 786464 | tf_op jit(solution)/shard_map/ppermute | solution.py:34
  580.6 16.8 %collective-permute-done.13.down_far_ref = bf16[768,512]{1,0:T(8,128)(2,1)S(1)} collective-permute-done((bf16[768,512]{1,0:T(8,128)(2,1)S(1)}, bf16[768,512]{1,0:T(8,128)(2,1)S(1)}, u32[]{:S(2)}, u32[]{:S(2)}) %collective-permute-start.13) | collective-permute-done | bytes 786464 | tf_op jit(solution)/shard_map/ppermute | solution.py:34
  598.2 84.6 %owner.1 = (f32[1024,512]{1,0:T(8,128)}, bf16[1024,512]{1,0:T(8,128)(2,1)}, bf16[1536,512]{1,0:T(8,128)(2,1)}, bf16[512,1536]{1,0:T(8,128)(2,1)}) custom-call(bf16[4096,512]{1,0:T(8,128)(2,1)} %get-tuple-element.84.dkv_ref, bf16[1024,2048]{1,0:T(8,128)(2,1)} %convolution_convert_fusion.4.partial_ref, f32[256,2048]{1,0:T(8,128)} %get-tuple-element.82.middle_ref, ...), custom_call_target="tpu_custom_call" | custom-call | bytes 240000000 | tf_op jit(solution)/shard_map/owner/pallas_call | solution.py:569
  688.6 8.6 %project_back.1 = (bf16[1024,1280]{1,0:T(8,128)(2,1)}, f32[1,128]{1,0:T(1,128)}, f32[1,128]{1,0:T(1,128)}) custom-call(f32[1024,512]{1,0:T(8,128)} %get-tuple-element.88.dq_ref, f32[1024,512]{1,0:T(8,128)} %get-tuple-element.89.dkv_ref, f32[1024,1280]{1,0:T(8,128)} %fusion.72.raw_ref.own_ref.other_ref, f32[1024,128]{1,0:T(8,128)} %get-tuple-element.179.cos_ref, ...), custom_call_target="tpu_custom_call" | custom-call | flops 39321600 | bytes 15728640 | tf_op jit(solution)/shard_map/project_back/pallas_call | solution.py:150
  697.2 10.1 %convolution_convert_fusion.5.partial_ref = bf16[1024,2048]{1,0:T(8,128)(2,1)} fusion(bf16[1024,1280]{1,0:T(8,128)(2,1)} %get-tuple-element.91, bf16[2048,1280]{1,0:T(8,128)(2,1)} %get-tuple-element.61), kind=kOutput, calls=%fused_computation.15 | convolution fusion | flops 5370806272 | bytes 12058624 | tf_op jit(solution)/shard_map/dot_general | solution.py:26
  711.0 7.4 convolution_convert_fusion.qkv_ref
  718.4 20.6 %collective-permute-done.16.up_far_ref = bf16[512,768]{1,0:T(8,128)(2,1)S(1)} collective-permute-done((bf16[512,768]{1,0:T(8,128)(2,1)S(1)}, bf16[512,768]{1,0:T(8,128)(2,1)S(1)}, u32[]{:S(2)}, u32[]{:S(2)}) %collective-permute-start.16) | collective-permute-done | bytes 786464 | tf_op jit(solution)/shard_map/ppermute | solution.py:34
  739.8 101.0 %end.1 = (bf16[1024,512]{1,0:T(8,128)(2,1)}, f32[1,4352]{1,0:T(1,128)}, bf16[512,1280]{1,0:T(8,128)(2,1)}, bf16[512,512]{1,0:T(8,128)(2,1)}, bf16[512,1536]{1,0:T(8,128)(2,1)}) custom-call(bf16[1024,2048]{1,0:T(8,128)(2,1)} %convolution_convert_fusion.5.partial_ref, bf16[256,2048]{1,0:T(8,128)(2,1)} %get-tuple-element.75.x_ref, ...), custom_call_target="tpu_custom_call" | custom-call | bytes 270000000 | tf_op jit(solution)/shard_map/end/pallas_call | solution.py:569
  (171 shorter events, 73.0 us)
Async XLA Ops:
  0.6 86.1 %copy-start.3 = (bf16[512,1536]{1,0:T(8,128)(2,1)S(1)}, bf16[512,1536]{1,0:T(8,128)(2,1)}, u32[]{:S(2)}) copy-start(bf16[512,1536]{1,0:T(8,128)(2,1)} %gate_ref.1) | copy-start | bytes 4718596
  3.8 88.1 %copy-start.4 = (bf16[512,1536]{1,0:T(8,128)(2,1)S(1)}, bf16[512,1536]{1,0:T(8,128)(2,1)}, u32[]{:S(2)}) copy-start(bf16[512,1536]{1,0:T(8,128)(2,1)} %up_ref.1) | copy-start | bytes 4718596
  11.2 88.6 %copy-start.29 = (s32[1,8]{1,0:T(1,128)S(1)}, s32[1,8]{1,0:T(1,128)}, u32[]{:S(2)}) copy-start(s32[1,8]{1,0:T(1,128)} %param.16) | copy-start | bytes 100
  88.1 37.2 %collective-permute-start.3 = (bf16[256,768]{1,0:T(8,128)(2,1)}, bf16[256,768]{1,0:T(8,128)(2,1)S(1)}, u32[]{:S(2)}, u32[]{:S(2)}) collective-permute-start(bf16[256,768]{1,0:T(8,128)(2,1)} %get-tuple-element.146), channel_id=1, source_target_pairs={{0,8},{4,12},{8,0},{12,4},{1,9},{5,13},{9,1},{13,5},{2,10},{6,14},... | collective-permute-start | bytes 1179656 | tf_op jit(solution)/shard_map/ppermute | solution.py:34
  91.4 35.5 %collective-permute-start = (bf16[256,768]{1,0:T(8,128)(2,1)}, bf16[256,768]{1,0:T(8,128)(2,1)}, u32[]{:S(2)}, u32[]{:S(2)}) collective-permute-start(bf16[256,768]{1,0:T(8,128)(2,1)} %get-tuple-element.147), channel_id=1, source_target_pairs={{0,2},{1,3},{2,0},{3,1},{4,6},{5,7},{6,4},{7,5},{8,10},{9,11},{10,... | collective-permute-start | bytes 1179656 | tf_op jit(solution)/shard_map/ppermute | solution.py:34
  93.2 33.7 %collective-permute-start.4 = (bf16[256,768]{1,0:T(8,128)(2,1)}, bf16[256,768]{1,0:T(8,128)(2,1)S(1)}, u32[]{:S(2)}, u32[]{:S(2)}) collective-permute-start(bf16[256,768]{1,0:T(8,128)(2,1)} %get-tuple-element.144), channel_id=1, source_target_pairs={{0,8},{4,12},{8,0},{12,4},{1,9},{5,13},{9,1},{13,5},{2,10},{6,14},... | collective-permute-start | bytes 1179656 | tf_op jit(solution)/shard_map/ppermute | solution.py:34
  94.5 51.5 %collective-permute-start.7 = (bf16[128,2048]{1,0:T(8,128)(2,1)S(1)}, bf16[128,2048]{1,0:T(8,128)(2,1)S(1)}, u32[]{:S(2)}, u32[]{:S(2)}) collective-permute-start(bf16[128,2048]{1,0:T(8,128)(2,1)S(1)} %get-tuple-element.156), channel_id=1, source_target_pairs={{0,4},{4,0},{8,12},{12,8},{1,5},{5,1},{9,13},{13,9},{2,6},{6,2},{1... | collective-permute-start | bytes 1572872 | tf_op jit(solution)/shard_map/ppermute | solution.py:34
  99.3 46.7 %collective-permute-start.6 = (bf16[128,2048]{1,0:T(8,128)(2,1)S(1)}, bf16[128,2048]{1,0:T(8,128)(2,1)S(1)}, u32[]{:S(2)}, u32[]{:S(2)}) collective-permute-start(bf16[128,2048]{1,0:T(8,128)(2,1)S(1)} %get-tuple-element.157), channel_id=1, source_target_pairs={{0,2},{1,3},{2,0},{3,1},{4,6},{5,7},{6,4},{7,5},{8,10},{9,11},{10,... | collective-permute-start | bytes 1572872 | tf_op jit(solution)/shard_map/ppermute | solution.py:34
  125.2 72.7 %copy-start.16 = (bf16[256,768]{1,0:T(8,128)(2,1)}, bf16[256,768]{1,0:T(8,128)(2,1)S(1)}, u32[]{:S(2)}) copy-start(bf16[256,768]{1,0:T(8,128)(2,1)S(1)} %collective-permute-done.3.gate_far_ref) | copy-start | bytes 1179652
  125.3 12.3 %collective-permute-start.1 = (bf16[256,768]{1,0:T(8,128)(2,1)}, bf16[256,768]{1,0:T(8,128)(2,1)S(1)}, u32[]{:S(2)}, u32[]{:S(2)}) collective-permute-start(bf16[256,768]{1,0:T(8,128)(2,1)} %get-tuple-element.145), channel_id=1, source_target_pairs={{0,2},{1,3},{2,0},{3,1},{4,6},{5,7},{6,4},{7,5},{8,10},{9,11},{10,... | collective-permute-start | bytes 1179656 | tf_op jit(solution)/shard_map/ppermute | solution.py:34
  126.9 19.1 %collective-permute-start.5 = (bf16[768,256]{1,0:T(8,128)(2,1)}, bf16[768,256]{1,0:T(8,128)(2,1)S(1)}, u32[]{:S(2)}, u32[]{:S(2)}) collective-permute-start(bf16[768,256]{1,0:T(8,128)(2,1)} %get-tuple-element.142), channel_id=1, source_target_pairs={{0,8},{4,12},{8,0},{12,4},{1,9},{5,13},{9,1},{13,5},{2,10},{6,14},... | collective-permute-start | bytes 1179656 | tf_op jit(solution)/shard_map/ppermute | solution.py:34
  126.9 71.0 %copy-start.17 = (bf16[256,768]{1,0:T(8,128)(2,1)}, bf16[256,768]{1,0:T(8,128)(2,1)S(1)}, u32[]{:S(2)}) copy-start(bf16[256,768]{1,0:T(8,128)(2,1)S(1)} %collective-permute-done.4.up_far_ref) | copy-start | bytes 1179652
  127.0 19.1 %collective-permute-start.2 = (bf16[768,256]{1,0:T(8,128)(2,1)}, bf16[768,256]{1,0:T(8,128)(2,1)}, u32[]{:S(2)}, u32[]{:S(2)}) collective-permute-start(bf16[768,256]{1,0:T(8,128)(2,1)} %get-tuple-element.143), channel_id=1, source_target_pairs={{0,2},{1,3},{2,0},{3,1},{4,6},{5,7},{6,4},{7,5},{8,10},{9,11},{10,... | collective-permute-start | bytes 1179656 | tf_op jit(solution)/shard_map/ppermute | solution.py:34
  137.5 63.6 %copy-start.18 = (bf16[256,768]{1,0:T(8,128)(2,1)}, bf16[256,768]{1,0:T(8,128)(2,1)S(1)}, u32[]{:S(2)}) copy-start(bf16[256,768]{1,0:T(8,128)(2,1)S(1)} %collective-permute-done.1.up_y_ref) | copy-start | bytes 1179652
  198.0 37.7 %collective-permute-start.10 = (bf16[256,768]{1,0:T(8,128)(2,1)}, bf16[256,768]{1,0:T(8,128)(2,1)S(1)}, u32[]{:S(2)}, u32[]{:S(2)}) collective-permute-start(bf16[256,768]{1,0:T(8,128)(2,1)} %collective-permute-done.gate_y_ref), channel_id=1, source_target_pairs={{0,8},{4,12},{8,0},{12,4},{1,9},{5,13},{9,1},{13,5},{2,10},{6,14},... | collective-permute-start | bytes 1179656 | tf_op jit(solution)/shard_map/ppermute | solution.py:34
  198.1 46.0 %collective-permute-start.11 = (bf16[256,768]{1,0:T(8,128)(2,1)S(1)}, bf16[256,768]{1,0:T(8,128)(2,1)S(1)}, u32[]{:S(2)}, u32[]{:S(2)}) collective-permute-start(bf16[256,768]{1,0:T(8,128)(2,1)S(1)} %collective-permute-done.1.up_y_ref), channel_id=1, source_target_pairs={{0,8},{4,12},{8,0},{12,4},{1,9},{5,13},{9,1},{13,5},{2,10},{6,14},... | collective-permute-start | bytes 1179656 | tf_op jit(solution)/shard_map/ppermute | solution.py:34
  201.0 51.5 %collective-permute-start.12 = (bf16[768,256]{1,0:T(8,128)(2,1)}, bf16[768,256]{1,0:T(8,128)(2,1)S(1)}, u32[]{:S(2)}, u32[]{:S(2)}) collective-permute-start(bf16[768,256]{1,0:T(8,128)(2,1)} %collective-permute-done.2.down_y_ref), channel_id=1, source_target_pairs={{0,8},{4,12},{8,0},{12,4},{1,9},{5,13},{9,1},{13,5},{2,10},{6,14},... | collective-permute-start | bytes 1179656 | tf_op jit(solution)/shard_map/ppermute | solution.py:34
  201.1 159.0 %collective-permute-start.8 = (bf16[256,2048]{1,0:T(8,128)(2,1)S(1)}, bf16[256,2048]{1,0:T(8,128)(2,1)S(1)}, u32[]{:S(2)}, u32[]{:S(2)}) collective-permute-start(bf16[256,2048]{1,0:T(8,128)(2,1)S(1)} %pad_maximum_fusion), channel_id=1, source_target_pairs={{0,2},{1,3},{2,0},{3,1},{4,6},{5,7},{6,4},{7,5},{8,10},{9,11},{10,... | collective-permute-start | bytes 3145736 | tf_op jit(solution)/shard_map/ppermute | solution.py:34
  201.9 158.3 %collective-permute-start.9 = (bf16[256,2048]{1,0:T(8,128)(2,1)S(1)}, bf16[256,2048]{1,0:T(8,128)(2,1)S(1)}, u32[]{:S(2)}, u32[]{:S(2)}) collective-permute-start(bf16[256,2048]{1,0:T(8,128)(2,1)S(1)} %pad_maximum_fusion.1), channel_id=1, source_target_pairs={{0,4},{4,0},{8,12},{12,8},{1,5},{5,1},{9,13},{13,9},{2,6},{6,2},{1... | collective-permute-start | bytes 3145736 | tf_op jit(solution)/shard_map/ppermute | solution.py:34
  235.7 16.8 %copy-start.20 = (bf16[256,768]{1,0:T(8,128)(2,1)}, bf16[256,768]{1,0:T(8,128)(2,1)S(1)}, u32[]{:S(2)}) copy-start(bf16[256,768]{1,0:T(8,128)(2,1)S(1)} %collective-permute-done.10.gate_both_ref) | copy-start | bytes 1179652
  341.0 19.1 %copy-start.23 = (bf16[1024,2048]{1,0:T(8,128)(2,1)S(1)}, bf16[1024,2048]{1,0:T(8,128)(2,1)}, u32[]{:S(2)}) copy-start(bf16[1024,2048]{1,0:T(8,128)(2,1)} %constant_dynamic-update-slice_fusion.1) | copy-start | bytes 12582916
  360.3 18.0 %slice-start = ((s8[6291456]{0:T(1024)(128)(4,1)}), s8[2097152]{0:T(1024)(128)(4,1)S(1)}, s32[]{:S(2)}) async-start(s8[6291456]{0:T(1024)(128)(4,1)} %bitcast.56), calls=%async_computation | async-start | bytes 4194304
  360.4 17.9 %slice-start.1 = ((s8[6291456]{0:T(1024)(128)(4,1)}), s8[4194304]{0:T(1024)(128)(4,1)S(1)}, s32[]{:S(2)}) async-start(s8[6291456]{0:T(1024)(128)(4,1)} %bitcast.56), calls=%async_computation.1 | async-start | bytes 8388608
  378.3 10.3 %copy-start.31 = (bf16[1024,1536]{1,0:T(8,128)(2,1)S(1)}, bf16[1024,1536]{1,0:T(8,128)(2,1)}, u32[]{:S(2)}) copy-start(bf16[1024,1536]{1,0:T(8,128)(2,1)} %get-tuple-element.139) | copy-start | bytes 9437188
  436.4 84.7 %copy-start.27 = (bf16[512,2048]{1,0:T(8,128)(2,1)S(1)}, bf16[512,2048]{1,0:T(8,128)(2,1)}, u32[]{:S(2)}) copy-start(bf16[512,2048]{1,0:T(8,128)(2,1)} %get-tuple-element.74) | copy-start | bytes 6291460
  527.3 53.3 %collective-permute-start.14 = (bf16[512,768]{1,0:T(8,128)(2,1)S(1)}, bf16[512,768]{1,0:T(8,128)(2,1)S(1)}, u32[]{:S(2)}, u32[]{:S(2)}) collective-permute-start(bf16[512,768]{1,0:T(8,128)(2,1)S(1)} %slice.135), channel_id=1, source_target_pairs={{0,8},{4,12},{8,0},{12,4},{1,9},{5,13},{9,1},{13,5},{2,10},{6,14},... | collective-permute-start | bytes 2359304 | tf_op jit(solution)/shard_map/ppermute | solution.py:34
  528.1 69.2 %collective-permute-start.13 = (bf16[768,512]{1,0:T(8,128)(2,1)S(1)}, bf16[768,512]{1,0:T(8,128)(2,1)S(1)}, u32[]{:S(2)}, u32[]{:S(2)}) collective-permute-start(bf16[768,512]{1,0:T(8,128)(2,1)S(1)} %slice.134), channel_id=1, source_target_pairs={{0,8},{4,12},{8,0},{12,4},{1,9},{5,13},{9,1},{13,5},{2,10},{6,14},... | collective-permute-start | bytes 2359304 | tf_op jit(solution)/shard_map/ppermute | solution.py:34
  530.3 177.0 %collective-permute-start.15 = (bf16[512,1536]{1,0:T(8,128)(2,1)S(1)}, bf16[512,1536]{1,0:T(8,128)(2,1)S(1)}, u32[]{:S(2)}, u32[]{:S(2)}) collective-permute-start(bf16[512,1536]{1,0:T(8,128)(2,1)S(1)} %copy-done.28), channel_id=1, source_target_pairs={{0,16},{16,0},{1,17},{17,1},{2,18},{18,2},{3,19},{19,3},{4,20},{20... | collective-permute-start | bytes 4718600 | tf_op jit(solution)/shard_map/ppermute | solution.py:34
  530.7 26.1 %copy-start.30 = (bf16[1024,512]{1,0:T(8,128)(2,1)S(1)}, bf16[1024,512]{1,0:T(8,128)(2,1)}, u32[]{:S(2)}) copy-start(bf16[1024,512]{1,0:T(8,128)(2,1)} %get-tuple-element.73) | copy-start | bytes 3145732
  580.6 16.8 %copy-start.14 = (bf16[512,768]{1,0:T(8,128)(2,1)}, bf16[512,768]{1,0:T(8,128)(2,1)S(1)}, u32[]{:S(2)}) copy-start(bf16[512,768]{1,0:T(8,128)(2,1)S(1)} %collective-permute-done.14.gate_far_ref) | copy-start | bytes 2359300
  697.2 10.2 %copy-start.6 = (bf16[512,1536]{1,0:T(8,128)(2,1)S(1)}, bf16[512,1536]{1,0:T(8,128)(2,1)}, u32[]{:S(2)}) copy-start(bf16[512,1536]{1,0:T(8,128)(2,1)} %get-tuple-element.96) | copy-start | bytes 4718596
  708.7 30.2 %collective-permute-start.16 = (bf16[512,768]{1,0:T(8,128)(2,1)S(1)}, bf16[512,768]{1,0:T(8,128)(2,1)S(1)}, u32[]{:S(2)}, u32[]{:S(2)}) collective-permute-start(bf16[512,768]{1,0:T(8,128)(2,1)S(1)} %get-tuple-element.98), channel_id=1, source_target_pairs={{0,8},{4,12},{8,0},{12,4},{1,9},{5,13},{9,1},{13,5},{2,10},{6,14},... | collective-permute-start | bytes 2359304 | tf_op jit(solution)/shard_map/ppermute | solution.py:34
  (20 other events, 94.4 us)

commit v7 on v6

--- a/solution.py
+++ b/solution.py
@@ -283,9 +283,10 @@
     dlogit_ref[...] = jnp.zeros_like(dlogit_ref)
     rows = jnp.concatenate([row_ref[0]] * repeat, axis=1)
     starts = jnp.concatenate([start_ref[0]] * repeat, axis=1)
+    queries, all_grads, all_inners = [], [], []
     for k in range(pairs):
         heads = [k * repeat + r for r in range(repeat)]
-        query = jnp.concatenate([q_ref[:, h * size : (h + 1) * size] for h in heads], axis=0)
+        queries.append(jnp.concatenate([q_ref[:, h * size : (h + 1) * size] for h in heads], axis=0))
         grads, inners = [], []
         for h in heads:
             cols = slice(h * size, (h + 1) * size)
@@ -298,30 +299,35 @@
             inverse = inverse_ref[:, cols]
             grads.append((up * gate * inverse).astype(BF16))
             inners.append(product * gate * inverse)
-        grad = jnp.concatenate(grads, axis=0)
-        inner = jnp.transpose(jnp.concatenate(inners, axis=0))[0:1]
-        key_cols = slice(k * size, (k + 1) * size)
-        value_cols = slice((pairs + k) * size, (pairs + k + 1) * size)
-
-        def seen(total, where, first):
+        all_grads.append(jnp.concatenate(grads, axis=0))
+        all_inners.append(jnp.transpose(jnp.concatenate(inners, axis=0))[0:1])
+
+    def seen(totals, where, first):
+        outs = []
+        for k in range(pairs):
+            key_cols = slice(k * size, (k + 1) * size)
+            value_cols = slice((pairs + k) * size, (pairs + k + 1) * size)
             keys = join([kv_ref[at, key_cols] for at in where])
-            weights = jnp.exp2(dot_trans(keys, query))
+            weights = jnp.exp2(dot_trans(keys, queries[k]))
             if first is not None:
                 index = first + lax.broadcasted_iota(jnp.int32, weights.shape, 0)
                 weights = jnp.where((index <= rows) & (index >= starts), weights, 0.0)
-            changes = dot_trans(join([kv_ref[at, value_cols] for at in where]), grad)
-            changes = (weights * (changes - inner)).astype(BF16)
-            value_sums = dot_rows(weights.astype(BF16), grad)
-            key_sums = dot_rows(changes, query)
+            changes = dot_trans(join([kv_ref[at, value_cols] for at in where]), all_grads[k])
+            changes = (weights * (changes - all_inners[k])).astype(BF16)
+            value_sums = dot_rows(weights.astype(BF16), all_grads[k])
+            key_sums = dot_rows(changes, queries[k])
             for i, at in enumerate(where):
                 sums_ref[at, value_cols] += value_sums[i * step : (i + 1) * step]
                 sums_ref[at, key_cols] += key_sums[i * step : (i + 1) * step]
-            return total + dot_inner(changes, keys)
-
-        total = jnp.zeros((query.shape[0], size), F32)
-        total = lax.fori_loop(0, wide_blocks, lambda i, t: seen(t, pair(i), None), total)
-        total = lax.fori_loop(low, high + 1, lambda i, t: seen(t, single(i), i * step), total)
-        for r, h in enumerate(heads):
+            outs.append(totals[k] + dot_inner(changes, keys))
+        return tuple(outs)
+
+    totals = tuple(jnp.zeros((query.shape[0], size), F32) for query in queries)
+    totals = lax.fori_loop(0, wide_blocks, lambda i, t: seen(t, pair(i), None), totals)
+    totals = lax.fori_loop(low, high + 1, lambda i, t: seen(t, single(i), i * step), totals)
+    for k, total in enumerate(totals):
+        for r in range(repeat):
+            h = k * repeat + r
             dq_ref[:, h * size : (h + 1) * size] = total[r * step : (r + 1) * step]
 
     @pl.when(stripe == pl.num_programs(0) - 1)
@@ -454,7 +460,7 @@
     yield
 
 
-def weight_flow(net, source_ref, out_ref, axis, own, other, across, from_y=None, from_far=None, from_both=None):
+def weight_flow(net, source_ref, out_ref, axis, own, other, across, from_y=None, from_far=None, from_both=None, their_y=None, their_far=None):
     step = source_ref.shape[axis] // 2
     count = source_ref.shape[axis]
 
@@ -486,13 +492,20 @@
         come_both = net.send(from_y, place(1 - y, 0, other), FAR)
     else:
         net.copy(from_both, place(1 - y, 0, other))
-    their_y = net.send(from_y, place(1 - y, 1, own), X)
+    given = their_y is not None
+    if given:
+        for ref, slot, start in ((their_y, 1 - y, own), (their_far, y, other)):
+            net.copy(ref, place(slot, 1, start))
+            net.send(ref, place(slot + 2, 1, start), CORE)
+    else:
+        their_y = net.send(from_y, place(1 - y, 1, own), X)
     net.send(from_y, place(3 - y, 0, own), CORE)
     if from_far is None:
         yield
         net.arrived(come_far)
         from_far = place(y, 0, other)
-    their_far = net.send(from_far, place(y, 1, other), X)
+    if not given:
+        their_far = net.send(from_far, place(y, 1, other), X)
     net.send(from_far, place(2 + y, 0, other), CORE)
     if from_both is None:
         yield
@@ -501,7 +514,8 @@
     their_both = net.send(from_both, place(1 - y, 1, other), X)
     net.send(from_both, place(3 - y, 0, other), CORE)
     yield
-    for copy, slot, start in ((their_y, 1 - y, own), (their_far, y, other), (their_both, 1 - y, other)):
+    waiting = ((their_y, 1 - y, own), (their_far, y, other), (their_both, 1 - y, other))
+    for copy, slot, start in waiting[2 * given :]:
         net.arrived(copy)
         net.send(place(slot, 1, start), place(slot + 2, 1, start), CORE)
     yield
@@ -672,7 +686,7 @@
 
 def middle_kernel(
     partial_ref, x_ref, gain_ref, gate_ref, up_ref, down_ref, gate_y_ref, up_y_ref, down_y_ref, gate_far_ref, up_far_ref, down_far_ref,
-    gate_both_ref, up_both_ref, down_both_ref, middle_ref, all_ref, both_ref, last_ref,
+    gate_both_ref, up_both_ref, down_both_ref, wide_x_ref, down_x_ref, middle_ref, all_ref, both_ref, last_ref,
     first, second, sums, last, total, normed, send, recv, local, *, sizes,
 ):
     net = Wires(send, recv, local, sizes)
@@ -680,10 +694,12 @@
     scatter = scatter_flow(net, partial_ref, first, second, sums, last, total)
     run(scatter)
     across = gate_ref.shape[1] // 2
+    step = gate_ref.shape[0] // 2
+    their = [wide_x_ref.at[pl.ds(i * step, step), :] for i in range(4)] + [down_x_ref.at[:, pl.ds(i * step, step)] for i in range(2)]
     flows = [
-        weight_flow(net, gate_ref, both_ref, 0, 0, across, across, gate_y_ref, gate_far_ref, gate_both_ref),
-        weight_flow(net, up_ref, both_ref, 0, 2 * across, 3 * across, across, up_y_ref, up_far_ref, up_both_ref),
-        weight_flow(net, down_ref, last_ref, 1, 0, across, across, down_y_ref, down_far_ref, down_both_ref),
+        weight_flow(net, gate_ref, both_ref, 0, 0, across, across, gate_y_ref, gate_far_ref, gate_both_ref, their[0], their[2]),
+        weight_flow(net, up_ref, both_ref, 0, 2 * across, 3 * across, across, up_y_ref, up_far_ref, up_both_ref, their[1], their[3]),
+        weight_flow(net, down_ref, last_ref, 1, 0, across, across, down_y_ref, down_far_ref, down_both_ref, their[4], their[5]),
     ]
     for flow in flows:
         run(flow)
@@ -712,11 +728,11 @@
     rows, width = x.shape
     buffer = lambda n, kind: pltpu.VMEM((n, width), kind)
     return wire_call(
-        middle_kernel, "middle", 3, [VMEM] * 15, [VMEM, ANY, ANY, ANY],
+        middle_kernel, "middle", 3, [VMEM] * 17, [VMEM, ANY, ANY, ANY],
         [((rows, width), F32), ((4 * rows, width), BF16), ((width, 2 * gate.shape[1]), BF16), ((down.shape[0], width), BF16)],
         [
             buffer(rows, BF16), buffer(rows, BF16), buffer(rows, BF16), buffer(rows, BF16), buffer(rows, F32), buffer(rows, BF16),
-            *sems(64, 24),
+            *sems(64, 32),
         ],
         sizes, 80, partial, x, gain[None], gate, up, down, *pieces,
     )
@@ -762,17 +778,18 @@
         along, wide = pl.ds(hint(at, self.step), step), pl.ds(hint(start, self.across), count)
         return (along, wide) if self.axis == 0 else (wide, along)
 
-    def start(self, g_ref, acc, from_core):
+    def start(self, g_ref, acc, from_core, given=False):
         self.acc, self.from_core = acc, from_core
         count = 4 * self.step
         own, other = (self.window(i * count, 0, 2 * self.across, count) for i in range(2))
         self.loaded = self.net.copy(g_ref.at[own], acc)
-        self.core = self.net.send(g_ref.at[other], from_core, CORE)
+        self.core = None if given else self.net.send(g_ref.at[other], from_core, CORE)
 
     def wait_core(self):
         self.loaded.wait()
         self.net.local = [copy for copy in self.net.local if copy is not self.loaded]
-        self.net.arrived(self.core)
+        if self.core is not None:
+            self.net.arrived(self.core)
 
     def core_to_x(self, from_x):
         self.wait_core()
@@ -1005,7 +1022,7 @@
 
 
 def end_kernel(
-    partial_ref, x_ref, gain_ref, grad_ref, two_ref, query_ref, key_ref, up_ref, up_far_ref, qkv_ref, out_ref,
+    partial_ref, x_ref, gain_ref, grad_ref, two_ref, query_ref, key_ref, up_ref, up_far_ref, qkv_core_ref, qkv_ref, out_ref,
     tokens_ref, gains_ref, qkv_out, out_out, up_out,
     first, second, sums, last, total, rows_low, vectors, up_sums, *rest, sizes,
 ):
@@ -1015,21 +1032,21 @@
     step = x_ref.shape[1] // sizes["narrow"] // 2
     qkv = Gradient(net, 0, step, qkv_ref.shape[1] // 2)
     out = Gradient(net, 1, step, out_ref.shape[0] // 2)
-    qkv.start(qkv_ref, *buffers[0:2])
-    out.start(out_ref, *buffers[4:6])
+    qkv.start(qkv_ref, buffers[0], qkv_core_ref, True)
+    out.start(out_ref, *buffers[3:5])
     scatter = scatter_flow(net, partial_ref, first, second, sums, last, total)
     run(scatter)
     up = Gradient(net, 0, step, up_far_ref.shape[1])
-    qkv.core_to_x(buffers[2])
-    out.core_to_x(buffers[6])
+    qkv.core_to_x(buffers[1])
+    out.core_to_x(buffers[5])
     for k in range(2):
         place = up.slot(k, 1, 0, up.across)
         add_rows((up_sums, place), [(up_ref, place), (up_far_ref, place)])
         up.to_owner(k, up_sums.at[place], up_out)
     run(scatter)
-    qkv.x_end(0, buffers[3])
-    run(scatter)
-    qkv.x_end(1, buffers[3])
+    qkv.x_end(0, buffers[2])
+    run(scatter)
+    qkv.x_end(1, buffers[2])
     run(scatter)
     width = x_ref.shape[1]
     size = query_ref.shape[1]
@@ -1069,8 +1086,8 @@
 
     gains = add_gains()
     run(gains)
-    out.x_end(0, buffers[7])
-    out.x_end(1, buffers[7])
+    out.x_end(0, buffers[6])
+    out.x_end(1, buffers[6])
     run(gains)
     own(qkv, 0, qkv_out)
     run(gains)
@@ -1087,21 +1104,22 @@
     net.finish()
 
 
-def end(partial, x, gain, grad, two, query, key, up, up_far, qkv, out, sizes):
+def end(partial, x, gain, grad, two, query, key, up, up_far, qkv_core, qkv, out, sizes):
     rows, width = x.shape
     size = width // sizes["narrow"]
     wide, deep = qkv.shape[1], out.shape[0]
     length = 2 * width + 2 * query.shape[1]
     return wire_call(
-        end_kernel, "end", 6, [VMEM] * 9 + [ANY] * 2, [ANY, VMEM, ANY, ANY, ANY],
+        end_kernel, "end", 6, [VMEM] * 10 + [ANY] * 2, [ANY, VMEM, ANY, ANY, ANY],
         [((sizes["narrow"] * rows, size), BF16), ((1, length), F32), ((size, wide), BF16), ((deep, size), BF16),
          ((size, 2 * up_far.shape[1]), BF16)],
         [
             *scatter_buffers(rows, width), pltpu.VMEM((rows, width), BF16), pltpu.VMEM((2 * len(SUMS) + 1, 1, length), F32),
             pltpu.VMEM(up_far.shape, BF16),
-            *gradient_buffers(size, wide // 2, 0), *gradient_buffers(size, deep // 2, 1), *sems(40, 16),
+            *(v for i, v in enumerate(gradient_buffers(size, wide // 2, 0)) if i != 1), *gradient_buffers(size, deep // 2, 1),
+            *sems(40, 16),
         ],
-        sizes, 90, partial, x, gain[None], grad, two, query, key, up, up_far, qkv, out,
+        sizes, 90, partial, x, gain[None], grad, two, query, key, up, up_far, qkv_core, qkv, out,
     )
 
 
@@ -1125,6 +1143,9 @@
 
     def over_x(values):
         return exchange(values, "dp", 1, n_dp)
+
+    def over_core(values):
+        return exchange(values, "narrow", 1, n_narrow)
 
     def over_far(values):
         return exchange(values, "wide", 2, n_wide)
@@ -1211,21 +1232,25 @@
         from_y = [over_y(piece_of(w, 1 - y, axis)) for w, axis in zip(send, axes)]
         from_far = [over_far(piece_of(w, y, axis)) for w, axis in zip(send, axes)]
         part = rows_local // 2
-        upstream_y, upstream_z = over_y(upstream[:part]), over_z(upstream[part:])
-        kv_all = exchange_keys(after(kv, *from_y, *from_far, upstream_y, upstream_z), sizes)
+        kv_all = exchange_keys(after(kv, *from_y, *from_far), sizes)
+        upstream_y, upstream_z = over_y(after(upstream[:part], kv_all)), over_z(after(upstream[part:], kv_all))
         from_both = [over_far(after(v, kv_all)) for v in from_y]
-        come_z = over_z(join([upstream[:part], after(upstream_y, kv_all)]))
-        come_y = over_y(join([upstream[part:], after(upstream_z, kv_all)]))
-        upstream_all = join(
-            [upstream, upstream_y, come_y[:part], come_z[:part], upstream_z, come_z[part:], come_y[part:]]
-        )
+        their_parts = [
+            over_x(after(join(from_y[:2] + from_far[:2]), kv_all)),
+            over_x(after(join([from_y[2], from_far[2]], 1), kv_all)),
+        ]
 
         gated, context, inverse_total = attend(
             table, q, kv_all, my_index, my_start, raw, pairs, size
         )
-        partial = dot_rows(gated, out_weight).astype(BF16)
+        partial = dot_rows(after(gated, their_parts[0], upstream_y, upstream_z), out_weight).astype(BF16)
         middle, normed_two_all, gate_up, down = to_middle(
-            partial, inputs, gain_two, gate_weight, up_weight, down_weight, from_y + from_far + from_both, sizes
+            partial, inputs, gain_two, gate_weight, up_weight, down_weight, from_y + from_far + from_both + their_parts, sizes
+        )
+        come_z = over_z(join([upstream[:part], after(upstream_y, normed_two_all)]))
+        come_y = over_y(join([upstream[part:], after(upstream_z, normed_two_all)]))
+        upstream_all = join(
+            [upstream, upstream_y, come_y[:part], come_z[:part], upstream_z, come_z[part:], come_y[part:]]
         )
         both = dot_rows(normed_two_all, gate_up)
         hidden_cols = gate_weight.shape[1]
@@ -1246,27 +1271,33 @@
             partial, middle, upstream, gain_two, down_sums, gate_sums, up_sums, sizes
         )
         down_far = over_far(down_part[hidden_cols // 2 :])
-        gate_far = over_far(gate_part[:, hidden_cols // 2 :])
+        far_part = gate_part[:, hidden_cols // 2 :]
+        gate_far = [over_far(far_part[i * quarter : (i + 1) * quarter]) for i in range(2)]
         up_come = over_x(up_send)
         gated_grad = dot_trans(middle_all, out_weight)
+        mlp_partial = dot_rows(after(hidden, gated_grad), down).astype(BF16)
+        gated_grad = after(gated_grad, gate_far[0], mlp_partial)
         dq, dkv, logit_grad = attend_back(
             table, q, kv_all, my_index, my_start, raw, context, inverse_total, gated_grad, pairs, size
         )
-        partial = dot_rows(hidden, down).astype(BF16)
         up_part = (up_keep.astype(F32) + up_come.astype(F32)).astype(BF16)
         dkv_mine, layer_output, down_gradient, gate_gradient = to_owner(
-            dkv, partial, middle, down_part, down_far, gate_part, gate_far, sizes
+            dkv, mlp_partial, middle, down_part, down_far, gate_part, join(gate_far), sizes
         )
-        up_far = over_far(after(up_part[:, hidden_cols // 2 :], dkv_mine))
+        far_part = after(up_part[:, hidden_cols // 2 :], dkv_mine)
+        up_far = [over_far(far_part[i * quarter : (i + 1) * quarter]) for i in range(2)]
         low, query_term, key_term = project_back(
             dq, dkv_mine, raw, cosine, sine, query_gain, key_gain, logit_grad, heads, pairs, size, scale, log_two
         )
-        partial = dot_trans(low, joined_weight).astype(BF16)
+        half = width // 2
+        low = after(low, up_far[0])
         qkv_sums = dot_inner(normed_all, low).astype(BF16)
-        out_sums = dot_inner(gated, middle_all).astype(BF16)
+        qkv_core = over_core(qkv_sums[half:])
+        partial = dot_trans(after(low, qkv_sums), joined_weight).astype(BF16)
+        out_sums = dot_inner(after(gated, dkv_mine), middle_all).astype(BF16)
         tokens_gradient, gains, qkv_gradient, output_gradient, up_gradient = end(
-            partial, inputs, gain_one, middle_grad, two_term, query_term, key_term, up_part[:, : hidden_cols // 2], up_far,
-            qkv_sums, out_sums, sizes
+            partial, inputs, gain_one, middle_grad, two_term, query_term, key_term, up_part[:, : hidden_cols // 2], join(up_far),
+            qkv_core, qkv_sums, out_sums, sizes
         )
         tokens_gradient = tokens_gradient.astype(F32)
         gains = over_groups(gains[0], F32)

time: 868 us -> 890 us (1.025)
  Pallas kernels: 541 us -> 555 us
  starting transfers between devices: 22.6 us -> 33.7 us
    pallas_call x6, Pallas kernels: 485 us -> 500 us  [wire_call(): pl.pallas_call(functools.partial(kernel, sizes=sizes), in_specs=specs, ou...]
    ppermute x17 -> x22, starting transfers between devices: 22.6 us -> 33.7 us  [exchange(): return lax.ppermute(values, axis, [(i, i ^ distance) for i in range(size)])]
    ppermute x17 -> x22, waiting for transfers between devices: 98.1 us -> 92.4 us  [exchange(): return lax.ppermute(values, axis, [(i, i ^ distance) for i in range(size)])]
    unnamed x86 -> x110, local copies, waits for them, and re-layouts: 13.6 us -> 18 us
  transfers between devices with their start and end apart: 17 -> 22, of which waited for: 8 -> 9; matrix products, arithmetic and copies ran while one was open for 9% -> 9% of each run, Pallas kernels for 27% -> 18%
where the time goes in v7:
time: 890 us; the launch traced here: 882 us
  Pallas kernels  555 us (62%)
  matrix products  139 us (16%)
  waiting for transfers between devices  92.4 us (10%)
  starting transfers between devices  33.7 us (4%)
  local copies, waits for them, and re-layouts  33.3 us (4%)
  other arithmetic  27.2 us (3%)
    pallas_call x6, Pallas kernels, wire_call(): pl.pallas_call(functools.partial(kernel, sizes=sizes), in_specs=specs, ou...  500 us
    ppermute x22, waiting for transfers between devices, exchange(): return lax.ppermute(values, axis, [(i, i ^ distance) for i in range(size)])  92.4 us
    dot_general x4, matrix products, dot_trans(): lax.dot_general(left, right, (((1,), (1,)), ((), ())), preferred_element_...  49 us
    dot_general x4, matrix products, dot_rows(): return jnp.dot(left, right, preferred_element_type=F32)  46.5 us
    dot_general x5, matrix products, dot_inner(): lax.dot_general(left, right, (((0,), (0,)), ((), ())), preferred_element_...  43 us
    ppermute x22, starting transfers between devices, exchange(): return lax.ppermute(values, axis, [(i, i ^ distance) for i in range(size)])  33.7 us
    pallas_call x1, Pallas kernels, attend_back(): pl.pallas_call(functools.partial(backward_kernel, pairs=pairs, repeat=hea...  24.2 us
    unnamed x110, local copies, waits for them, and re-layouts  18 us
  transfers between devices with their start and end apart: 22, of which 9 were waited for; matrix products, arithmetic and copies ran while one was open for 9% of the time, Pallas kernels for 18%

profile of v7, /device:TPU:0, one launch (start us, length us, event | category | flops | bytes accessed | tf_op | source)
XLA Modules:
  0.0 881.6 jit_solution(8747844585885088697)
XLA Ops:
  11.3 75.6 %begin.1 = (bf16[256,2048]{1,0:T(8,128)(2,1)}, bf16[256,2048]{1,0:T(8,128)(2,1)}, bf16[1024,2048]{1,0:T(8,128)(2,1)}, bf16[2048,1280]{1,0:T(8,128)(2,1)}, bf16[512,2048]{1,0:T(8,128)(2,1)}) custom-call(bf16[1024,512]{1,0:T(8,128)(2,1)} %tokens_ref.1, bf16[1024,512]{1,0:T(8,128)(2,1)} %cotangent_ref.1, f32[1,2048]{1,0:T(1,128)} %broadcast_in_dim_reshape.8.gain_ref, ...), custom_call_target="tpu_custom_call" | custom-call | bytes 165000000 | tf_op jit(solution)/shard_map/begin/pallas_call | solution.py:583
  104.9 10.4 %fusion.74.raw_ref.own_ref.other_ref = f32[1024,1280]{1,0:T(8,128)} fusion(bf16[1024,2048]{1,0:T(8,128)(2,1)} %get-tuple-element.70, bf16[2048,1280]{1,0:T(8,128)(2,1)} %get-tuple-element.71), kind=kOutput, calls=%fused_computation.191 | convolution fusion | flops 5368709120 | bytes 14680064 | tf_op jit(solution)/shard_map/dot_general | solution.py:22
  119.0 6.4 post.1
  128.6 6.9 collective-permute-done.4.up_far_ref
  135.5 8.0 collective-permute-done.5.down_far_ref
  143.5 54.2 %keys.1.kv_ref = bf16[4096,512]{1,0:T(8,128)(2,1)} custom-call(bf16[1024,512]{1,0:T(8,128)(2,1)} %get-tuple-element.77.kv_ref), custom_call_target="tpu_custom_call" | custom-call | bytes 135000000 | tf_op jit(solution)/shard_map/keys/pallas_call | solution.py:583
  203.6 15.3 %attend.1 = (bf16[1024,512]{1,0:T(8,128)(2,1)}, f32[1024,512]{1,0:T(8,128)}, f32[1024,512]{1,0:T(8,128)}) custom-call(s32[4,5]{1,0:T(4,128)} %select_select_fusion.table_ref, bf16[1024,512]{1,0:T(8,128)(2,1)} %get-tuple-element.72.q_ref, bf16[4096,512]{1,0:T(8,128)(2,1)} %keys.1.kv_ref, s32[1024,1]{1,0:T(8,128)} %get-tuple-element.193.row_ref, ...), custom_call_target="tpu_custom_call" | custom-call | flops 20000000000 | bytes 12000000 | tf_op jit(solution)/shard_map/attend/pallas_call | solution.py:244
  218.9 12.7 %collective-permute-start.10 = (bf16[256,768]{1,0:T(8,128)(2,1)S(1)}, bf16[256,768]{1,0:T(8,128)(2,1)S(1)}, u32[]{:S(2)}, u32[]{:S(2)}) collective-permute-start(bf16[256,768]{1,0:T(8,128)(2,1)S(1)} %collective-permute-done.1.up_y_ref), channel_id=1, source_target_pairs={{0,8},{4,12},{8,0},{12,4},{1,9},{5,13},{9,1},{13,5},{2,10},{6,14},... | collective-permute-start | bytes 1179656 | tf_op jit(solution)/shard_map/ppermute | solution.py:34
  232.5 22.0 %collective-permute-done.8.wide_x_ref = bf16[1024,768]{1,0:T(8,128)(2,1)S(1)} collective-permute-done((bf16[1024,768]{1,0:T(8,128)(2,1)S(1)}, bf16[1024,768]{1,0:T(8,128)(2,1)S(1)}, u32[]{:S(2)}, u32[]{:S(2)}) %collective-permute-start.8) | collective-permute-done | bytes 1572896 | tf_op jit(solution)/shard_map/ppermute | solution.py:34
  254.5 6.8 convolution_convert_fusion.6.partial_ref
  261.3 4.9 collective-permute-done.11.down_both_ref
  267.8 83.8 %middle.1 = (f32[256,2048]{1,0:T(8,128)}, bf16[1024,2048]{1,0:T(8,128)(2,1)}, bf16[2048,3072]{1,0:T(8,128)(2,1)}, bf16[1536,2048]{1,0:T(8,128)(2,1)}) custom-call(bf16[1024,2048]{1,0:T(8,128)(2,1)} %convolution_convert_fusion.6.partial_ref, bf16[256,2048]{1,0:T(8,128)(2,1)} %get-tuple-element.87.x_ref, f32[1,2048]{1,0:T(1,128)} %broadcast_in_dim_reshape.9.gain_ref, ...), custom_call_target="tpu_custom_call" | custom-call | bytes 240000000 | tf_op jit(solution)/shard_map/middle/pallas_call | solution.py:583
  353.9 18.0 %fusion.75 = f32[1024,3072]{1,0:T(8,128)} fusion(bf16[1024,2048]{1,0:T(8,128)(2,1)S(1)} %copy-done.37, bf16[2048,3072]{1,0:T(8,128)(2,1)} %get-tuple-element.96), kind=kOutput, calls=%fused_computation.192 | convolution fusion | flops 12884901888 | bytes 29360128 | tf_op jit(solution)/shard_map/dot_general | solution.py:22
  371.9 3.6 collective-permute-done.13
  376.2 16.3 %multiply_convert_fusion.2 = (bf16[1024,1536]{1,0:T(8,128)(2,1)}, bf16[1024,1536]{1,0:T(8,128)(2,1)}, bf16[1024,1536]{1,0:T(8,128)(2,1)}) fusion(f32[1024,3072]{1,0:T(8,128)} %fusion.75, bf16[1024,2048]{1,0:T(8,128)(2,1)S(1)} %slice_dynamic-update-slice_fusion, bf16[1536,2048]{1,0:T(8,128)(2,1)} %get-tuple-element.95), kind=kOutput, calls=%fused_computation.10 | convolution fusion | flops 6466043904 | bytes 32505856 | tf_op jit(solution)/shard_map/dot_general | solution.py:26
  392.4 10.5 %convolution_convert_fusion.2.gate_ref = bf16[2048,1536]{1,0:T(8,128)(2,1)} fusion(bf16[1024,2048]{1,0:T(8,128)(2,1)S(1)} %copy-done.37, bf16[1024,1536]{1,0:T(8,128)(2,1)} %get-tuple-element.157), kind=kOutput, calls=%fused_computation.2 | convolution fusion | flops 6445596672 | bytes 13631488 | tf_op jit(solution)/shard_map/dot_general | solution.py:30
  402.9 19.5 %fusion.5.partial_ref = bf16[1024,2048]{1,0:T(8,128)(2,1)} fusion(bf16[2048,3072]{1,0:T(8,128)(2,1)} %get-tuple-element.96, bf16[1024,1536]{1,0:T(8,128)(2,1)} %get-tuple-element.158, bf16[1024,1536]{1,0:T(8,128)(2,1)} %get-tuple-element.157), kind=kOutput, calls=%fused_computation.14 | convolution fusion | flops 12899581952 | bytes 23068672 | tf_op jit(solution)/shard_map/dot_general | solution.py:26
  422.4 11.7 %convolution_convert_fusion.1.up_ref = bf16[2048,1536]{1,0:T(8,128)(2,1)} fusion(bf16[1024,2048]{1,0:T(8,128)(2,1)} %get-tuple-element.92, bf16[1024,1536]{1,0:T(8,128)(2,1)} %get-tuple-element.158), kind=kOutput, calls=%fused_computation.1 | convolution fusion | flops 6445596672 | bytes 13631488 | tf_op jit(solution)/shard_map/dot_general | solution.py:30
  434.1 8.8 convolution_convert_fusion.3.down_ref
  442.9 83.2 %turn.1 = (f32[256,2048]{1,0:T(8,128)}, bf16[1024,2048]{1,0:T(8,128)(2,1)}, f32[1,2048]{1,0:T(1,128)}, bf16[1536,512]{1,0:T(8,128)(2,1)}, bf16[512,1536]{1,0:T(8...) custom-call(bf16[1024,2048]{1,0:T(8,128)(2,1)} %fusion.5.partial_ref, ...), custom_call_target="tpu_custom_call" | custom-call | bytes 240000000 | tf_op jit(solution)/shard_map/turn/pallas_call | solution.py:583
  526.1 6.0 fusion.76.grad_ref
  532.3 11.3 %convolution_convert_fusion.4.partial_ref = bf16[1024,2048]{1,0:T(8,128)(2,1)} fusion(bf16[1024,1536]{1,0:T(8,128)(2,1)S(1)} %copy-done.44, bf16[1536,2048]{1,0:T(8,128)(2,1)} %get-tuple-element.95), kind=kOutput, calls=%fused_computation.13 | convolution fusion | flops 6444548096 | bytes 13631488 | tf_op jit(solution)/shard_map/dot_general | solution.py:22
  548.1 30.1 %collective-permute-done.15 = bf16[256,768]{1,0:T(8,128)(2,1)S(1)} collective-permute-done((bf16[256,768]{1,0:T(8,128)(2,1)S(1)}, bf16[256,768]{1,0:T(8,128)(2,1)S(1)}, u32[]{:S(2)}, u32[]{:S(2)}) %collective-permute-start.15) | collective-permute-done | bytes 393248 | tf_op jit(solution)/shard_map/ppermute | solution.py:34
  578.1 24.2 %attend_back.1 = (f32[1024,512]{1,0:T(8,128)}, bf16[4096,512]{1,0:T(8,128)(2,1)}, f32[1024,256]{1,0:T(8,128)}) custom-call(s32[4,5]{1,0:T(4,128)} %select_select_fusion.table_ref, bf16[1024,512]{1,0:T(8,128)(2,1)} %get-tuple-element.72.q_ref, bf16[4096,512]{1,0:T(8,128)(2,1)} %keys.1.kv_ref, s32[4,1,256]{2,1,0:T(1,128)} %get-tuple-element.196.row_ref, ...), custom_call_target="tpu_custom_call" | custom-call | flops 49999998976 | bytes 20000000 | tf_op jit(solution)/shard_map/attend_back/pallas_call | solution.py:346
  604.2 106.4 %owner.1 = (f32[1024,512]{1,0:T(8,128)}, bf16[1024,512]{1,0:T(8,128)(2,1)}, bf16[1536,512]{1,0:T(8,128)(2,1)}, bf16[512,1536]{1,0:T(8,128)(2,1)}) custom-call(bf16[4096,512]{1,0:T(8,128)(2,1)} %get-tuple-element.102.dkv_ref, bf16[1024,2048]{1,0:T(8,128)(2,1)} %convolution_convert_fusion.4.partial_ref, f32[256,2048]{1,0:T(8,128)} %get-tuple-element.97.middle_ref, ...), custom_call_target="tpu_custom_call" | custom-call | bytes 240000000 | tf_op jit(solution)/shard_map/owner/pallas_call | solution.py:583
  712.7 8.6 project_back.1
  721.4 5.1 collective-permute-done.19
  726.5 8.3 convolution_convert_fusion.qkv_ref
  742.7 3.8 convolution_convert_fusion.7.out_ref
  746.5 11.4 %collective-permute-done.20 = bf16[256,768]{1,0:T(8,128)(2,1)S(1)} collective-permute-done((bf16[256,768]{1,0:T(8,128)(2,1)S(1)}, bf16[256,768]{1,0:T(8,128)(2,1)S(1)}, u32[]{:S(2)}, u32[]{:S(2)}) %collective-permute-start.20) | collective-permute-done | bytes 393248 | tf_op jit(solution)/shard_map/ppermute | solution.py:34
  758.9 7.2 convolution_convert_fusion.5.partial_ref
  767.6 97.1 %end.1 = (bf16[1024,512]{1,0:T(8,128)(2,1)}, f32[1,4352]{1,0:T(1,128)}, bf16[512,1280]{1,0:T(8,128)(2,1)}, bf16[512,512]{1,0:T(8,128)(2,1)}, bf16[512,1536]{1,0:T(8,128)(2,1)}) custom-call(bf16[1024,2048]{1,0:T(8,128)(2,1)} %convolution_convert_fusion.5.partial_ref, bf16[256,2048]{1,0:T(8,128)(2,1)} %get-tuple-element.87.x_ref, ...), custom_call_target="tpu_custom_call" | custom-call | bytes 270000000 | tf_op jit(solution)/shard_map/end/pallas_call | solution.py:583
  (211 shorter events, 82.0 us)
Async XLA Ops:
  5.1 81.8 %copy-start.3 = (bf16[512,1536]{1,0:T(8,128)(2,1)S(1)}, bf16[512,1536]{1,0:T(8,128)(2,1)}, u32[]{:S(2)}) copy-start(bf16[512,1536]{1,0:T(8,128)(2,1)} %gate_ref.1) | copy-start | bytes 4718596
  8.2 84.0 %copy-start.4 = (bf16[512,1536]{1,0:T(8,128)(2,1)S(1)}, bf16[512,1536]{1,0:T(8,128)(2,1)}, u32[]{:S(2)}) copy-start(bf16[512,1536]{1,0:T(8,128)(2,1)} %up_ref.1) | copy-start | bytes 4718596
  11.3 83.7 %copy-start.5 = (bf16[1536,512]{1,0:T(8,128)(2,1)S(1)}, bf16[1536,512]{1,0:T(8,128)(2,1)}, u32[]{:S(2)}) copy-start(bf16[1536,512]{1,0:T(8,128)(2,1)} %down_ref.1) | copy-start | bytes 4718596
  88.3 39.7 %collective-permute-start.3 = (bf16[256,768]{1,0:T(8,128)(2,1)}, bf16[256,768]{1,0:T(8,128)(2,1)S(1)}, u32[]{:S(2)}, u32[]{:S(2)}) collective-permute-start(bf16[256,768]{1,0:T(8,128)(2,1)} %get-tuple-element.168), channel_id=1, source_target_pairs={{0,8},{4,12},{8,0},{12,4},{1,9},{5,13},{9,1},{13,5},{2,10},{6,14},... | collective-permute-start | bytes 1179656 | tf_op jit(solution)/shard_map/ppermute | solution.py:34
  91.6 37.0 %collective-permute-start = (bf16[256,768]{1,0:T(8,128)(2,1)}, bf16[256,768]{1,0:T(8,128)(2,1)S(1)}, u32[]{:S(2)}, u32[]{:S(2)}) collective-permute-start(bf16[256,768]{1,0:T(8,128)(2,1)} %get-tuple-element.169), channel_id=1, source_target_pairs={{0,2},{1,3},{2,0},{3,1},{4,6},{5,7},{6,4},{7,5},{8,10},{9,11},{10,... | collective-permute-start | bytes 1179656 | tf_op jit(solution)/shard_map/ppermute | solution.py:34
  93.5 42.0 %collective-permute-start.4 = (bf16[256,768]{1,0:T(8,128)(2,1)}, bf16[256,768]{1,0:T(8,128)(2,1)S(1)}, u32[]{:S(2)}, u32[]{:S(2)}) collective-permute-start(bf16[256,768]{1,0:T(8,128)(2,1)} %get-tuple-element.166), channel_id=1, source_target_pairs={{0,8},{4,12},{8,0},{12,4},{1,9},{5,13},{9,1},{13,5},{2,10},{6,14},... | collective-permute-start | bytes 1179656 | tf_op jit(solution)/shard_map/ppermute | solution.py:34
  93.5 42.0 %collective-permute-start.1 = (bf16[256,768]{1,0:T(8,128)(2,1)}, bf16[256,768]{1,0:T(8,128)(2,1)S(1)}, u32[]{:S(2)}, u32[]{:S(2)}) collective-permute-start(bf16[256,768]{1,0:T(8,128)(2,1)} %get-tuple-element.167), channel_id=1, source_target_pairs={{0,2},{1,3},{2,0},{3,1},{4,6},{5,7},{6,4},{7,5},{8,10},{9,11},{10,... | collective-permute-start | bytes 1179656 | tf_op jit(solution)/shard_map/ppermute | solution.py:34
  96.3 47.1 %collective-permute-start.5 = (bf16[768,256]{1,0:T(8,128)(2,1)}, bf16[768,256]{1,0:T(8,128)(2,1)S(1)}, u32[]{:S(2)}, u32[]{:S(2)}) collective-permute-start(bf16[768,256]{1,0:T(8,128)(2,1)} %get-tuple-element.164), channel_id=1, source_target_pairs={{0,8},{4,12},{8,0},{12,4},{1,9},{5,13},{9,1},{13,5},{2,10},{6,14},... | collective-permute-start | bytes 1179656 | tf_op jit(solution)/shard_map/ppermute | solution.py:34
  128.0 70.6 %copy-start.15 = (bf16[256,768]{1,0:T(8,128)(2,1)}, bf16[256,768]{1,0:T(8,128)(2,1)S(1)}, u32[]{:S(2)}) copy-start(bf16[256,768]{1,0:T(8,128)(2,1)S(1)} %collective-permute-done.3.gate_far_ref) | copy-start | bytes 1179652
  128.0 15.5 %collective-permute-start.2 = (bf16[768,256]{1,0:T(8,128)(2,1)}, bf16[768,256]{1,0:T(8,128)(2,1)S(1)}, u32[]{:S(2)}, u32[]{:S(2)}) collective-permute-start(bf16[768,256]{1,0:T(8,128)(2,1)} %get-tuple-element.165), channel_id=1, source_target_pairs={{0,2},{1,3},{2,0},{3,1},{4,6},{5,7},{6,4},{7,5},{8,10},{9,11},{10,... | collective-permute-start | bytes 1179656 | tf_op jit(solution)/shard_map/ppermute | solution.py:34
  128.6 70.1 %copy-start.16 = (bf16[256,768]{1,0:T(8,128)(2,1)}, bf16[256,768]{1,0:T(8,128)(2,1)S(1)}, u32[]{:S(2)}) copy-start(bf16[256,768]{1,0:T(8,128)(2,1)S(1)} %collective-permute-done.gate_y_ref) | copy-start | bytes 1179652
  135.5 63.1 %copy-start.17 = (bf16[256,768]{1,0:T(8,128)(2,1)}, bf16[256,768]{1,0:T(8,128)(2,1)S(1)}, u32[]{:S(2)}) copy-start(bf16[256,768]{1,0:T(8,128)(2,1)S(1)} %collective-permute-done.4.up_far_ref) | copy-start | bytes 1179652
  135.5 83.4 %copy-start.18 = (bf16[256,768]{1,0:T(8,128)(2,1)}, bf16[256,768]{1,0:T(8,128)(2,1)S(1)}, u32[]{:S(2)}) copy-start(bf16[256,768]{1,0:T(8,128)(2,1)S(1)} %collective-permute-done.1.up_y_ref) | copy-start | bytes 1179652
  143.5 89.0 %copy-start.20 = (bf16[768,256]{1,0:T(8,128)(2,1)}, bf16[768,256]{1,0:T(8,128)(2,1)S(1)}, u32[]{:S(2)}) copy-start(bf16[768,256]{1,0:T(8,128)(2,1)S(1)} %collective-permute-done.2.down_y_ref) | copy-start | bytes 1179652
  198.7 62.5 %collective-permute-start.9 = (bf16[256,768]{1,0:T(8,128)(2,1)S(1)}, bf16[256,768]{1,0:T(8,128)(2,1)S(1)}, u32[]{:S(2)}, u32[]{:S(2)}) collective-permute-start(bf16[256,768]{1,0:T(8,128)(2,1)S(1)} %collective-permute-done.gate_y_ref), channel_id=1, source_target_pairs={{0,8},{4,12},{8,0},{12,4},{1,9},{5,13},{9,1},{13,5},{2,10},{6,14},... | collective-permute-start | bytes 1179656 | tf_op jit(solution)/shard_map/ppermute | solution.py:34
  198.8 20.1 %collective-permute-start.6 = (bf16[128,2048]{1,0:T(8,128)(2,1)S(1)}, bf16[128,2048]{1,0:T(8,128)(2,1)S(1)}, u32[]{:S(2)}, u32[]{:S(2)}) collective-permute-start(bf16[128,2048]{1,0:T(8,128)(2,1)S(1)} %get-tuple-element.81), channel_id=1, source_target_pairs={{0,2},{1,3},{2,0},{3,1},{4,6},{5,7},{6,4},{7,5},{8,10},{9,11},{10,... | collective-permute-start | bytes 1572872 | tf_op jit(solution)/shard_map/ppermute | solution.py:34
  199.6 32.9 %collective-permute-start.7 = (bf16[128,2048]{1,0:T(8,128)(2,1)S(1)}, bf16[128,2048]{1,0:T(8,128)(2,1)S(1)}, u32[]{:S(2)}, u32[]{:S(2)}) collective-permute-start(bf16[128,2048]{1,0:T(8,128)(2,1)S(1)} %get-tuple-element.82), channel_id=1, source_target_pairs={{0,4},{4,0},{8,12},{12,8},{1,5},{5,1},{9,13},{13,9},{2,6},{6,2},{1... | collective-permute-start | bytes 1572872 | tf_op jit(solution)/shard_map/ppermute | solution.py:34
  201.6 64.6 %collective-permute-start.12 = (bf16[768,512]{1,0:T(8,128)(2,1)}, bf16[768,512]{1,0:T(8,128)(2,1)S(1)}, u32[]{:S(2)}, u32[]{:S(2)}) collective-permute-start(bf16[768,512]{1,0:T(8,128)(2,1)} %pad_maximum_fusion.4), channel_id=1, source_target_pairs={{0,16},{16,0},{1,17},{17,1},{2,18},{18,2},{3,19},{19,3},{4,20},{20... | collective-permute-start | bytes 2359304 | tf_op jit(solution)/shard_map/ppermute | solution.py:34
  202.7 51.8 %collective-permute-start.8 = (bf16[1024,768]{1,0:T(8,128)(2,1)S(1)}, bf16[1024,768]{1,0:T(8,128)(2,1)S(1)}, u32[]{:S(2)}, u32[]{:S(2)}) collective-permute-start(bf16[1024,768]{1,0:T(8,128)(2,1)S(1)} %pad_maximum_fusion), channel_id=1, source_target_pairs={{0,16},{16,0},{1,17},{17,1},{2,18},{18,2},{3,19},{19,3},{4,20},{20... | collective-permute-start | bytes 4718600 | tf_op jit(solution)/shard_map/ppermute | solution.py:34
  218.9 42.3 %collective-permute-start.10 = (bf16[256,768]{1,0:T(8,128)(2,1)S(1)}, bf16[256,768]{1,0:T(8,128)(2,1)S(1)}, u32[]{:S(2)}, u32[]{:S(2)}) collective-permute-start(bf16[256,768]{1,0:T(8,128)(2,1)S(1)} %collective-permute-done.1.up_y_ref), channel_id=1, source_target_pairs={{0,8},{4,12},{8,0},{12,4},{1,9},{5,13},{9,1},{13,5},{2,10},{6,14},... | collective-permute-start | bytes 1179656 | tf_op jit(solution)/shard_map/ppermute | solution.py:34
  232.5 33.7 %collective-permute-start.11 = (bf16[768,256]{1,0:T(8,128)(2,1)S(1)}, bf16[768,256]{1,0:T(8,128)(2,1)S(1)}, u32[]{:S(2)}, u32[]{:S(2)}) collective-permute-start(bf16[768,256]{1,0:T(8,128)(2,1)S(1)} %collective-permute-done.2.down_y_ref), channel_id=1, source_target_pairs={{0,8},{4,12},{8,0},{12,4},{1,9},{5,13},{9,1},{13,5},{2,10},{6,14},... | collective-permute-start | bytes 1179656 | tf_op jit(solution)/shard_map/ppermute | solution.py:34
  351.8 23.7 %collective-permute-start.13 = (bf16[256,2048]{1,0:T(8,128)(2,1)S(1)}, bf16[256,2048]{1,0:T(8,128)(2,1)S(1)}, u32[]{:S(2)}, u32[]{:S(2)}) collective-permute-start(bf16[256,2048]{1,0:T(8,128)(2,1)S(1)} %pad_maximum_fusion.1), channel_id=1, source_target_pairs={{0,2},{1,3},{2,0},{3,1},{4,6},{5,7},{6,4},{7,5},{8,10},{9,11},{10,... | collective-permute-start | bytes 3145736 | tf_op jit(solution)/shard_map/ppermute | solution.py:34
  352.6 23.4 %collective-permute-start.14 = (bf16[256,2048]{1,0:T(8,128)(2,1)S(1)}, bf16[256,2048]{1,0:T(8,128)(2,1)S(1)}, u32[]{:S(2)}, u32[]{:S(2)}) collective-permute-start(bf16[256,2048]{1,0:T(8,128)(2,1)S(1)} %pad_maximum_fusion.2), channel_id=1, source_target_pairs={{0,4},{4,0},{8,12},{12,8},{1,5},{5,1},{9,13},{13,9},{2,6},{6,2},{1... | collective-permute-start | bytes 3145736 | tf_op jit(solution)/shard_map/ppermute | solution.py:34
  442.9 83.2 %copy-start.39 = (bf16[512,2048]{1,0:T(8,128)(2,1)S(1)}, bf16[512,2048]{1,0:T(8,128)(2,1)}, u32[]{:S(2)}) copy-start(bf16[512,2048]{1,0:T(8,128)(2,1)} %get-tuple-element.86) | copy-start | bytes 6291460
  532.2 45.9 %collective-permute-start.15 = (bf16[256,768]{1,0:T(8,128)(2,1)S(1)}, bf16[256,768]{1,0:T(8,128)(2,1)S(1)}, u32[]{:S(2)}, u32[]{:S(2)}) collective-permute-start(bf16[256,768]{1,0:T(8,128)(2,1)S(1)} %get-tuple-element.163), channel_id=1, source_target_pairs={{0,8},{4,12},{8,0},{12,4},{1,9},{5,13},{9,1},{13,5},{2,10},{6,14},... | collective-permute-start | bytes 1179656 | tf_op jit(solution)/shard_map/ppermute | solution.py:34
  543.7 58.6 %collective-permute-start.17 = (bf16[256,768]{1,0:T(8,128)(2,1)S(1)}, bf16[256,768]{1,0:T(8,128)(2,1)S(1)}, u32[]{:S(2)}, u32[]{:S(2)}) collective-permute-start(bf16[256,768]{1,0:T(8,128)(2,1)S(1)} %get-tuple-element.162), channel_id=1, source_target_pairs={{0,8},{4,12},{8,0},{12,4},{1,9},{5,13},{9,1},{13,5},{2,10},{6,14},... | collective-permute-start | bytes 1179656 | tf_op jit(solution)/shard_map/ppermute | solution.py:34
  546.5 56.8 %collective-permute-start.16 = (bf16[768,512]{1,0:T(8,128)(2,1)S(1)}, bf16[768,512]{1,0:T(8,128)(2,1)S(1)}, u32[]{:S(2)}, u32[]{:S(2)}) collective-permute-start(bf16[768,512]{1,0:T(8,128)(2,1)S(1)} %slice.150), channel_id=1, source_target_pairs={{0,8},{4,12},{8,0},{12,4},{1,9},{5,13},{9,1},{13,5},{2,10},{6,14},... | collective-permute-start | bytes 2359304 | tf_op jit(solution)/shard_map/ppermute | solution.py:34
  546.7 163.9 %collective-permute-start.18 = (bf16[512,1536]{1,0:T(8,128)(2,1)S(1)}, bf16[512,1536]{1,0:T(8,128)(2,1)S(1)}, u32[]{:S(2)}, u32[]{:S(2)}) collective-permute-start(bf16[512,1536]{1,0:T(8,128)(2,1)S(1)} %copy-done.40), channel_id=1, source_target_pairs={{0,16},{16,0},{1,17},{17,1},{2,18},{18,2},{3,19},{19,3},{4,20},{20... | collective-permute-start | bytes 4718600 | tf_op jit(solution)/shard_map/ppermute | solution.py:34
  604.2 106.4 %copy-start.11 = (bf16[512,1536]{1,0:T(8,128)(2,1)S(1)}, bf16[512,1536]{1,0:T(8,128)(2,1)}, u32[]{:S(2)}) copy-start(bf16[512,1536]{1,0:T(8,128)(2,1)} %get-tuple-element.109) | copy-start | bytes 4718596
  712.0 14.4 %collective-permute-start.19 = (bf16[256,768]{1,0:T(8,128)(2,1)S(1)}, bf16[256,768]{1,0:T(8,128)(2,1)S(1)}, u32[]{:S(2)}, u32[]{:S(2)}) collective-permute-start(bf16[256,768]{1,0:T(8,128)(2,1)S(1)} %get-tuple-element.181), channel_id=1, source_target_pairs={{0,8},{4,12},{8,0},{12,4},{1,9},{5,13},{9,1},{13,5},{2,10},{6,14},... | collective-permute-start | bytes 1179656 | tf_op jit(solution)/shard_map/ppermute | solution.py:34
  734.9 31.1 %collective-permute-start.21 = (bf16[1024,1280]{1,0:T(8,128)(2,1)S(1)}, bf16[1024,1280]{1,0:T(8,128)(2,1)S(1)}, u32[]{:S(2)}, u32[]{:S(2)}) collective-permute-start(bf16[1024,1280]{1,0:T(8,128)(2,1)S(1)} %slice.181), channel_id=1, source_target_pairs={{0,1},{1,0},{2,3},{3,2},{4,5},{5,4},{6,7},{7,6},{8,9},{9,8},{10,11... | collective-permute-start | bytes 7864328 | tf_op jit(solution)/shard_map/ppermute | solution.py:34
  741.5 16.4 %collective-permute-start.20 = (bf16[256,768]{1,0:T(8,128)(2,1)S(1)}, bf16[256,768]{1,0:T(8,128)(2,1)S(1)}, u32[]{:S(2)}, u32[]{:S(2)}) collective-permute-start(bf16[256,768]{1,0:T(8,128)(2,1)S(1)} %get-tuple-element.180), channel_id=1, source_target_pairs={{0,8},{4,12},{8,0},{12,4},{1,9},{5,13},{9,1},{13,5},{2,10},{6,14},... | collective-permute-start | bytes 1179656 | tf_op jit(solution)/shard_map/ppermute | solution.py:34
  (37 other events, 317.5 us)

commit v8 on v7

--- a/solution.py
+++ b/solution.py
@@ -686,7 +686,7 @@
 
 def middle_kernel(
     partial_ref, x_ref, gain_ref, gate_ref, up_ref, down_ref, gate_y_ref, up_y_ref, down_y_ref, gate_far_ref, up_far_ref, down_far_ref,
-    gate_both_ref, up_both_ref, down_both_ref, wide_x_ref, down_x_ref, middle_ref, all_ref, both_ref, last_ref,
+    gate_both_ref, up_both_ref, down_both_ref, middle_ref, all_ref, both_ref, last_ref,
     first, second, sums, last, total, normed, send, recv, local, *, sizes,
 ):
     net = Wires(send, recv, local, sizes)
@@ -694,12 +694,10 @@
     scatter = scatter_flow(net, partial_ref, first, second, sums, last, total)
     run(scatter)
     across = gate_ref.shape[1] // 2
-    step = gate_ref.shape[0] // 2
-    their = [wide_x_ref.at[pl.ds(i * step, step), :] for i in range(4)] + [down_x_ref.at[:, pl.ds(i * step, step)] for i in range(2)]
     flows = [
-        weight_flow(net, gate_ref, both_ref, 0, 0, across, across, gate_y_ref, gate_far_ref, gate_both_ref, their[0], their[2]),
-        weight_flow(net, up_ref, both_ref, 0, 2 * across, 3 * across, across, up_y_ref, up_far_ref, up_both_ref, their[1], their[3]),
-        weight_flow(net, down_ref, last_ref, 1, 0, across, across, down_y_ref, down_far_ref, down_both_ref, their[4], their[5]),
+        weight_flow(net, gate_ref, both_ref, 0, 0, across, across, gate_y_ref, gate_far_ref, gate_both_ref),
+        weight_flow(net, up_ref, both_ref, 0, 2 * across, 3 * across, across, up_y_ref, up_far_ref, up_both_ref),
+        weight_flow(net, down_ref, last_ref, 1, 0, across, across, down_y_ref, down_far_ref, down_both_ref),
     ]
     for flow in flows:
         run(flow)
@@ -728,7 +726,7 @@
     rows, width = x.shape
     buffer = lambda n, kind: pltpu.VMEM((n, width), kind)
     return wire_call(
-        middle_kernel, "middle", 3, [VMEM] * 17, [VMEM, ANY, ANY, ANY],
+        middle_kernel, "middle", 3, [VMEM] * 15, [VMEM, ANY, ANY, ANY],
         [((rows, width), F32), ((4 * rows, width), BF16), ((width, 2 * gate.shape[1]), BF16), ((down.shape[0], width), BF16)],
         [
             buffer(rows, BF16), buffer(rows, BF16), buffer(rows, BF16), buffer(rows, BF16), buffer(rows, F32), buffer(rows, BF16),
@@ -1022,9 +1020,9 @@
 
 
 def end_kernel(
-    partial_ref, x_ref, gain_ref, grad_ref, two_ref, query_ref, key_ref, up_ref, up_far_ref, qkv_core_ref, qkv_ref, out_ref,
+    partial_ref, x_ref, gain_ref, grad_ref, two_ref, query_ref, key_ref, up_ref, up_x_ref, qkv_core_ref, qkv_ref, out_ref,
     tokens_ref, gains_ref, qkv_out, out_out, up_out,
-    first, second, sums, last, total, rows_low, vectors, up_sums, *rest, sizes,
+    first, second, sums, last, total, rows_low, vectors, up_sums, up_far, *rest, sizes,
 ):
     buffers, (send, recv, local) = rest[:-3], rest[-3:]
     net = Wires(send, recv, local, sizes)
@@ -1036,17 +1034,23 @@
     out.start(out_ref, *buffers[3:5])
     scatter = scatter_flow(net, partial_ref, first, second, sums, last, total)
     run(scatter)
-    up = Gradient(net, 0, step, up_far_ref.shape[1])
+    up = Gradient(net, 0, step, up_ref.shape[1] // 2)
     qkv.core_to_x(buffers[1])
     out.core_to_x(buffers[5])
-    for k in range(2):
-        place = up.slot(k, 1, 0, up.across)
-        add_rows((up_sums, place), [(up_ref, place), (up_far_ref, place)])
-        up.to_owner(k, up_sums.at[place], up_out)
+
+    def up_to_far(k):
+        for start in (up.across, 0):
+            place = up.slot(k, 1, start, up.across)
+            add_rows((up_sums, place), [(up_ref, place), (up_x_ref, place)])
+            if start:
+                up.far.append(net.send(up_sums.at[place], up_far.at[up.slot(k, 1, 0, up.across)], FAR))
+
     run(scatter)
     qkv.x_end(0, buffers[2])
+    up_to_far(0)
     run(scatter)
     qkv.x_end(1, buffers[2])
+    up_to_far(1)
     run(scatter)
     width = x_ref.shape[1]
     size = query_ref.shape[1]
@@ -1084,16 +1088,24 @@
         flow.far_end(k)
         flow.to_owner(k, flow.acc.at[flow.slot(k, 2, 0, flow.across)], ref)
 
+    def own_up(k):
+        net.arrived(up.far[k])
+        place = up.slot(k, 1, 0, up.across)
+        add_rows((up_sums, place), [(up_sums, place), (up_far, place)])
+        up.to_owner(k, up_sums.at[place], up_out)
+
     gains = add_gains()
     run(gains)
     out.x_end(0, buffers[6])
     out.x_end(1, buffers[6])
     run(gains)
     own(qkv, 0, qkv_out)
+    own_up(0)
     run(gains)
     spread_flow(net, rows_low, tokens_ref)
     run(gains)
     own(qkv, 1, qkv_out)
+    own_up(1)
     run(gains)
     own(out, 0, out_out)
     own(out, 1, out_out)
@@ -1104,7 +1116,7 @@
     net.finish()
 
 
-def end(partial, x, gain, grad, two, query, key, up, up_far, qkv_core, qkv, out, sizes):
+def end(partial, x, gain, grad, two, query, key, up, up_x, qkv_core, qkv, out, sizes):
     rows, width = x.shape
     size = width // sizes["narrow"]
     wide, deep = qkv.shape[1], out.shape[0]
@@ -1112,14 +1124,14 @@
     return wire_call(
         end_kernel, "end", 6, [VMEM] * 10 + [ANY] * 2, [ANY, VMEM, ANY, ANY, ANY],
         [((sizes["narrow"] * rows, size), BF16), ((1, length), F32), ((size, wide), BF16), ((deep, size), BF16),
-         ((size, 2 * up_far.shape[1]), BF16)],
+         (up.shape, BF16)],
         [
             *scatter_buffers(rows, width), pltpu.VMEM((rows, width), BF16), pltpu.VMEM((2 * len(SUMS) + 1, 1, length), F32),
-            pltpu.VMEM(up_far.shape, BF16),
+            pltpu.VMEM(up.shape, BF16), pltpu.VMEM((size, up.shape[1] // 2), BF16),
             *(v for i, v in enumerate(gradient_buffers(size, wide // 2, 0)) if i != 1), *gradient_buffers(size, deep // 2, 1),
             *sems(40, 16),
         ],
-        sizes, 90, partial, x, gain[None], grad, two, query, key, up, up_far, qkv_core, qkv, out,
+        sizes, 90, partial, x, gain[None], grad, two, query, key, up, up_x, qkv_core, qkv, out,
     )
 
 
@@ -1235,17 +1247,13 @@
         kv_all = exchange_keys(after(kv, *from_y, *from_far), sizes)
         upstream_y, upstream_z = over_y(after(upstream[:part], kv_all)), over_z(after(upstream[part:], kv_all))
         from_both = [over_far(after(v, kv_all)) for v in from_y]
-        their_parts = [
-            over_x(after(join(from_y[:2] + from_far[:2]), kv_all)),
-            over_x(after(join([from_y[2], from_far[2]], 1), kv_all)),
-        ]
 
         gated, context, inverse_total = attend(
             table, q, kv_all, my_index, my_start, raw, pairs, size
         )
-        partial = dot_rows(after(gated, their_parts[0], upstream_y, upstream_z), out_weight).astype(BF16)
+        partial = dot_rows(after(gated, upstream_y, upstream_z), out_weight).astype(BF16)
         middle, normed_two_all, gate_up, down = to_middle(
-            partial, inputs, gain_two, gate_weight, up_weight, down_weight, from_y + from_far + from_both + their_parts, sizes
+            partial, inputs, gain_two, gate_weight, up_weight, down_weight, from_y + from_far + from_both, sizes
         )
         come_z = over_z(join([upstream[:part], after(upstream_y, normed_two_all)]))
         come_y = over_y(join([upstream[part:], after(upstream_z, normed_two_all)]))
@@ -1267,36 +1275,31 @@
         down_sums = dot_inner(hidden, upstream_all).astype(BF16)
         gate_sums = dot_inner(normed_two_all, gate_low).astype(BF16)
         up_sums = dot_inner(normed_two_all, up_low).astype(BF16)
+        mlp_partial = dot_rows(hidden, down).astype(BF16)
+        partial = after(partial, mlp_partial)
         middle_grad, middle_all, two_term, down_part, gate_part, up_keep, up_send = turn(
             partial, middle, upstream, gain_two, down_sums, gate_sums, up_sums, sizes
         )
         down_far = over_far(down_part[hidden_cols // 2 :])
-        far_part = gate_part[:, hidden_cols // 2 :]
-        gate_far = [over_far(far_part[i * quarter : (i + 1) * quarter]) for i in range(2)]
+        gate_far = over_far(gate_part[:, hidden_cols // 2 :])
         up_come = over_x(up_send)
         gated_grad = dot_trans(middle_all, out_weight)
-        mlp_partial = dot_rows(after(hidden, gated_grad), down).astype(BF16)
-        gated_grad = after(gated_grad, gate_far[0], mlp_partial)
         dq, dkv, logit_grad = attend_back(
             table, q, kv_all, my_index, my_start, raw, context, inverse_total, gated_grad, pairs, size
         )
-        up_part = (up_keep.astype(F32) + up_come.astype(F32)).astype(BF16)
+        out_sums = dot_inner(gated, middle_all).astype(BF16)
         dkv_mine, layer_output, down_gradient, gate_gradient = to_owner(
-            dkv, mlp_partial, middle, down_part, down_far, gate_part, join(gate_far), sizes
+            after(dkv, up_come, out_sums), mlp_partial, middle, down_part, down_far, gate_part, gate_far, sizes
         )
-        far_part = after(up_part[:, hidden_cols // 2 :], dkv_mine)
-        up_far = [over_far(far_part[i * quarter : (i + 1) * quarter]) for i in range(2)]
         low, query_term, key_term = project_back(
             dq, dkv_mine, raw, cosine, sine, query_gain, key_gain, logit_grad, heads, pairs, size, scale, log_two
         )
         half = width // 2
-        low = after(low, up_far[0])
         qkv_sums = dot_inner(normed_all, low).astype(BF16)
         qkv_core = over_core(qkv_sums[half:])
         partial = dot_trans(after(low, qkv_sums), joined_weight).astype(BF16)
-        out_sums = dot_inner(after(gated, dkv_mine), middle_all).astype(BF16)
         tokens_gradient, gains, qkv_gradient, output_gradient, up_gradient = end(
-            partial, inputs, gain_one, middle_grad, two_term, query_term, key_term, up_part[:, : hidden_cols // 2], join(up_far),
+            partial, inputs, gain_one, middle_grad, two_term, query_term, key_term, up_keep, up_come,
             qkv_core, qkv_sums, out_sums, sizes
         )
         tokens_gradient = tokens_gradient.astype(F32)

time: 890 us -> 876 us (0.984)
  starting transfers between devices: 33.7 us -> 20.6 us
  Pallas kernels: 555 us -> 565 us
    ppermute x22 -> x17, starting transfers between devices: 33.7 us -> 20.6 us  [exchange(): return lax.ppermute(values, axis, [(i, i ^ distance) for i in range(size)])]
    pallas_call x6, Pallas kernels: 500 us -> 511 us  [wire_call(): pl.pallas_call(functools.partial(kernel, sizes=sizes), in_specs=specs, ou...]
    ppermute x22 -> x17, waiting for transfers between devices: 92.4 us -> 88.3 us  [exchange(): return lax.ppermute(values, axis, [(i, i ^ distance) for i in range(size)])]
    unnamed x110 -> x92, local copies, waits for them, and re-layouts: 18 us -> 16.8 us
  transfers between devices with their start and end apart: 22 -> 17, of which waited for: 9 -> 11; matrix products, arithmetic and copies ran while one was open for 9% -> 7% of each run, Pallas kernels for 18% -> 5%
where the time goes in v8:
time: 876 us; the launch traced here: 868 us
  Pallas kernels  565 us (64%)
  matrix products  137 us (16%)
  waiting for transfers between devices  88.3 us (10%)
  local copies, waits for them, and re-layouts  33.3 us (4%)
  other arithmetic  21.1 us (2%)
  starting transfers between devices  20.6 us (2%)
    pallas_call x6, Pallas kernels, wire_call(): pl.pallas_call(functools.partial(kernel, sizes=sizes), in_specs=specs, ou...  511 us
    ppermute x17, waiting for transfers between devices, exchange(): return lax.ppermute(values, axis, [(i, i ^ distance) for i in range(size)])  88.3 us
    dot_general x4, matrix products, dot_trans(): lax.dot_general(left, right, (((1,), (1,)), ((), ())), preferred_element_...  50.5 us
    dot_general x4, matrix products, dot_rows(): return jnp.dot(left, right, preferred_element_type=F32)  44.1 us
    dot_general x5, matrix products, dot_inner(): lax.dot_general(left, right, (((0,), (0,)), ((), ())), preferred_element_...  42.6 us
    pallas_call x1, Pallas kernels, attend_back(): pl.pallas_call(functools.partial(backward_kernel, pairs=pairs, repeat=hea...  24.3 us
    ppermute x17, starting transfers between devices, exchange(): return lax.ppermute(values, axis, [(i, i ^ distance) for i in range(size)])  20.6 us
  transfers between devices with their start and end apart: 17, of which 11 were waited for; matrix products, arithmetic and copies ran while one was open for 7% of the time, Pallas kernels for 5%

profile of v8, /device:TPU:0, one launch (start us, length us, event | category | flops | bytes accessed | tf_op | source)
XLA Modules:
  0.0 867.5 jit_solution(18119185447952925935)
XLA Ops:
  11.2 75.5 %begin.1 = (bf16[256,2048]{1,0:T(8,128)(2,1)}, bf16[256,2048]{1,0:T(8,128)(2,1)}, bf16[1024,2048]{1,0:T(8,128)(2,1)}, bf16[2048,1280]{1,0:T(8,128)(2,1)}, bf16[512,2048]{1,0:T(8,128)(2,1)}) custom-call(bf16[1024,512]{1,0:T(8,128)(2,1)} %tokens_ref.1, bf16[1024,512]{1,0:T(8,128)(2,1)} %cotangent_ref.1, f32[1,2048]{1,0:T(1,128)} %broadcast_in_dim_reshape.8.gain_ref, ...), custom_call_target="tpu_custom_call" | custom-call | bytes 165000000 | tf_op jit(solution)/shard_map/begin/pallas_call | solution.py:583
  88.1 3.3 collective-permute-start.3
  103.4 10.4 %fusion.71.raw_ref.own_ref.other_ref = f32[1024,1280]{1,0:T(8,128)} fusion(bf16[1024,2048]{1,0:T(8,128)(2,1)} %get-tuple-element.65, bf16[2048,1280]{1,0:T(8,128)(2,1)} %get-tuple-element.66), kind=kOutput, calls=%fused_computation.183 | convolution fusion | flops 5368709120 | bytes 14680064 | tf_op jit(solution)/shard_map/dot_general | solution.py:22
  117.0 6.4 post.1
  127.5 7.9 collective-permute-done.4.up_far_ref
  135.4 8.0 collective-permute-done.5.down_far_ref
  143.4 54.0 %keys.1.kv_ref = bf16[4096,512]{1,0:T(8,128)(2,1)} custom-call(bf16[1024,512]{1,0:T(8,128)(2,1)} %get-tuple-element.72.kv_ref), custom_call_target="tpu_custom_call" | custom-call | bytes 135000000 | tf_op jit(solution)/shard_map/keys/pallas_call | solution.py:583
  203.2 15.4 %attend.1 = (bf16[1024,512]{1,0:T(8,128)(2,1)}, f32[1024,512]{1,0:T(8,128)}, f32[1024,512]{1,0:T(8,128)}) custom-call(s32[4,5]{1,0:T(4,128)} %select_select_fusion.table_ref, bf16[1024,512]{1,0:T(8,128)(2,1)} %get-tuple-element.67.q_ref, bf16[4096,512]{1,0:T(8,128)(2,1)} %keys.1.kv_ref, s32[1024,1]{1,0:T(8,128)} %get-tuple-element.177.row_ref, ...), custom_call_target="tpu_custom_call" | custom-call | flops 20000000000 | bytes 12000000 | tf_op jit(solution)/shard_map/attend/pallas_call | solution.py:244
  218.7 15.9 %collective-permute-done.7 = bf16[128,2048]{1,0:T(8,128)(2,1)S(1)} collective-permute-done((bf16[128,2048]{1,0:T(8,128)(2,1)S(1)}, bf16[128,2048]{1,0:T(8,128)(2,1)S(1)}, u32[]{:S(2)}, u32[]{:S(2)}) %collective-permute-start.7) | collective-permute-done | bytes 524320 | tf_op jit(solution)/shard_map/ppermute | solution.py:34
  234.6 5.5 convolution_convert_fusion.6.partial_ref
  243.3 8.3 collective-permute-done.10.down_both_ref
  252.4 88.0 %middle.1 = (f32[256,2048]{1,0:T(8,128)}, bf16[1024,2048]{1,0:T(8,128)(2,1)}, bf16[2048,3072]{1,0:T(8,128)(2,1)}, bf16[1536,2048]{1,0:T(8,128)(2,1)}) custom-call(bf16[1024,2048]{1,0:T(8,128)(2,1)} %convolution_convert_fusion.6.partial_ref, bf16[256,2048]{1,0:T(8,128)(2,1)} %get-tuple-element.81.x_ref, f32[1,2048]{1,0:T(1,128)} %broadcast_in_dim_reshape.9.gain_ref, ...), custom_call_target="tpu_custom_call" | custom-call | bytes 240000000 | tf_op jit(solution)/shard_map/middle/pallas_call | solution.py:583
  342.6 17.9 %fusion.72 = f32[1024,3072]{1,0:T(8,128)} fusion(bf16[1024,2048]{1,0:T(8,128)(2,1)S(1)} %copy-done.26, bf16[2048,3072]{1,0:T(8,128)(2,1)} %get-tuple-element.89), kind=kOutput, calls=%fused_computation.184 | convolution fusion | flops 12884901888 | bytes 29360128 | tf_op jit(solution)/shard_map/dot_general | solution.py:22
  360.6 5.7 collective-permute-done.11
  366.8 17.8 %multiply_convert_fusion.2 = (bf16[1024,1536]{1,0:T(8,128)(2,1)}, bf16[1024,1536]{1,0:T(8,128)(2,1)}, bf16[1024,1536]{1,0:T(8,128)(2,1)}) fusion(f32[1024,3072]{1,0:T(8,128)} %fusion.72, bf16[1024,2048]{1,0:T(8,128)(2,1)S(1)} %slice_dynamic-update-slice_fusion, bf16[1536,2048]{1,0:T(8,128)(2,1)} %get-tuple-element.88), kind=kOutput, calls=%fused_computation.10 | convolution fusion | flops 6466043904 | bytes 32505856 | tf_op jit(solution)/shard_map/dot_general | solution.py:26
  384.7 10.3 %convolution_convert_fusion.4.partial_ref = bf16[1024,2048]{1,0:T(8,128)(2,1)} fusion(bf16[1024,1536]{1,0:T(8,128)(2,1)} %get-tuple-element.149, bf16[1536,2048]{1,0:T(8,128)(2,1)S(1)} %bitcast.57), kind=kOutput, calls=%fused_computation.13 | convolution fusion | flops 6444548096 | bytes 13631488 | tf_op jit(solution)/shard_map/dot_general | solution.py:22
  395.0 8.8 %convolution_convert_fusion.3.down_ref = bf16[1536,2048]{1,0:T(8,128)(2,1)} fusion(bf16[1024,1536]{1,0:T(8,128)(2,1)S(1)} %copy-done.32, bf16[1024,2048]{1,0:T(8,128)(2,1)S(1)} %slice_dynamic-update-slice_fusion), kind=kOutput, calls=%fused_computation.3 | convolution fusion | flops 6445596672 | bytes 13631488 | tf_op jit(solution)/shard_map/dot_general | solution.py:30
  403.8 9.1 %convolution_convert_fusion.2.gate_ref = bf16[2048,1536]{1,0:T(8,128)(2,1)} fusion(bf16[1024,2048]{1,0:T(8,128)(2,1)S(1)} %copy-done.27, bf16[1024,1536]{1,0:T(8,128)(2,1)S(1)} %copy-done.33), kind=kOutput, calls=%fused_computation.2 | convolution fusion | flops 6445596672 | bytes 13631488 | tf_op jit(solution)/shard_map/dot_general | solution.py:30
  412.8 19.4 %fusion.5.partial_ref = bf16[1024,2048]{1,0:T(8,128)(2,1)} fusion(bf16[2048,3072]{1,0:T(8,128)(2,1)} %get-tuple-element.89, bf16[1024,1536]{1,0:T(8,128)(2,1)} %get-tuple-element.148, bf16[1024,1536]{1,0:T(8,128)(2,1)} %get-tuple-element.147), kind=kOutput, calls=%fused_computation.14 | convolution fusion | flops 12899581952 | bytes 23068672 | tf_op jit(solution)/shard_map/dot_general | solution.py:26
  432.2 10.6 %convolution_convert_fusion.1.up_ref = bf16[2048,1536]{1,0:T(8,128)(2,1)} fusion(bf16[1024,2048]{1,0:T(8,128)(2,1)S(1)} %copy-done.27, bf16[1024,1536]{1,0:T(8,128)(2,1)} %get-tuple-element.148), kind=kOutput, calls=%fused_computation.1 | convolution fusion | flops 6445596672 | bytes 13631488 | tf_op jit(solution)/shard_map/dot_general | solution.py:30
  442.8 83.0 %turn.1 = (f32[256,2048]{1,0:T(8,128)}, bf16[1024,2048]{1,0:T(8,128)(2,1)}, f32[1,2048]{1,0:T(1,128)}, bf16[1536,512]{1,0:T(8,128)(2,1)}, bf16[512,1536]{1,0:T(8...) custom-call(bf16[1024,2048]{1,0:T(8,128)(2,1)} %fusion.5.partial_ref, ...), custom_call_target="tpu_custom_call" | custom-call | bytes 240000000 | tf_op jit(solution)/shard_map/turn/pallas_call | solution.py:583
  525.8 6.0 fusion.73.grad_ref
  536.1 24.3 %attend_back.1 = (f32[1024,512]{1,0:T(8,128)}, bf16[4096,512]{1,0:T(8,128)(2,1)}, f32[1024,256]{1,0:T(8,128)}) custom-call(s32[4,5]{1,0:T(4,128)} %select_select_fusion.table_ref, bf16[1024,512]{1,0:T(8,128)(2,1)} %get-tuple-element.67.q_ref, bf16[4096,512]{1,0:T(8,128)(2,1)} %keys.1.kv_ref, s32[4,1,256]{2,1,0:T(1,128)} %get-tuple-element.180.row_ref, ...), custom_call_target="tpu_custom_call" | custom-call | flops 49999998976 | bytes 20000000 | tf_op jit(solution)/shard_map/attend_back/pallas_call | solution.py:346
  560.4 5.9 convolution_convert_fusion.7.out_ref
  566.3 5.2 collective-permute-done.13.up_x_ref
  571.5 15.3 %collective-permute-done.15.gate_far_ref = bf16[512,768]{1,0:T(8,128)(2,1)S(1)} collective-permute-done((bf16[512,768]{1,0:T(8,128)(2,1)S(1)}, bf16[512,768]{1,0:T(8,128)(2,1)S(1)}, u32[]{:S(2)}, u32[]{:S(2)}) %collective-permute-start.15) | collective-permute-done | bytes 786464 | tf_op jit(solution)/shard_map/ppermute | solution.py:34
  586.8 16.7 %collective-permute-done.14.down_far_ref = bf16[768,512]{1,0:T(8,128)(2,1)S(1)} collective-permute-done((bf16[768,512]{1,0:T(8,128)(2,1)S(1)}, bf16[768,512]{1,0:T(8,128)(2,1)S(1)}, u32[]{:S(2)}, u32[]{:S(2)}) %collective-permute-start.14) | collective-permute-done | bytes 786464 | tf_op jit(solution)/shard_map/ppermute | solution.py:34
  604.4 84.9 %owner.1 = (f32[1024,512]{1,0:T(8,128)}, bf16[1024,512]{1,0:T(8,128)(2,1)}, bf16[1536,512]{1,0:T(8,128)(2,1)}, bf16[512,1536]{1,0:T(8,128)(2,1)}) custom-call(bf16[4096,512]{1,0:T(8,128)(2,1)} %get-tuple-element.95.dkv_ref, bf16[1024,2048]{1,0:T(8,128)(2,1)} %convolution_convert_fusion.4.partial_ref, f32[256,2048]{1,0:T(8,128)} %get-tuple-element.91.middle_ref, ...), custom_call_target="tpu_custom_call" | custom-call | bytes 240000000 | tf_op jit(solution)/shard_map/owner/pallas_call | solution.py:583
  689.4 8.7 project_back.1
  698.0 8.3 convolution_convert_fusion.qkv_ref
  714.7 7.2 convolution_convert_fusion.5.partial_ref
  723.5 125.2 %end.1 = (bf16[1024,512]{1,0:T(8,128)(2,1)}, f32[1,4352]{1,0:T(1,128)}, bf16[512,1280]{1,0:T(8,128)(2,1)}, bf16[512,512]{1,0:T(8,128)(2,1)}, bf16[512,1536]{1,0:T(8,128)(2,1)}) custom-call(bf16[1024,2048]{1,0:T(8,128)(2,1)} %convolution_convert_fusion.5.partial_ref, bf16[256,2048]{1,0:T(8,128)(2,1)} %get-tuple-element.81.x_ref, ...), custom_call_target="tpu_custom_call" | custom-call | bytes 270000000 | tf_op jit(solution)/shard_map/end/pallas_call | solution.py:583
  (177 shorter events, 76.9 us)
Async XLA Ops:
  0.6 86.1 %copy-start.4 = (bf16[512,1536]{1,0:T(8,128)(2,1)S(1)}, bf16[512,1536]{1,0:T(8,128)(2,1)}, u32[]{:S(2)}) copy-start(bf16[512,1536]{1,0:T(8,128)(2,1)} %gate_ref.1) | copy-start | bytes 4718596
  7.1 88.8 %copy-start.5 = (bf16[1536,512]{1,0:T(8,128)(2,1)S(1)}, bf16[1536,512]{1,0:T(8,128)(2,1)}, u32[]{:S(2)}) copy-start(bf16[1536,512]{1,0:T(8,128)(2,1)} %down_ref.1) | copy-start | bytes 4718596
  11.2 89.1 %copy-start.30 = (s32[1,8]{1,0:T(1,128)S(1)}, s32[1,8]{1,0:T(1,128)}, u32[]{:S(2)}) copy-start(s32[1,8]{1,0:T(1,128)} %param.16) | copy-start | bytes 100
  86.8 15.5 %copy-start.1 = (bf16[256,2048]{1,0:T(8,128)(2,1)S(1)}, bf16[256,2048]{1,0:T(8,128)(2,1)}, u32[]{:S(2)}) copy-start(bf16[256,2048]{1,0:T(8,128)(2,1)} %get-tuple-element.75.upstream_ref) | copy-start | bytes 3145732
  88.1 38.8 %collective-permute-start.3 = (bf16[256,768]{1,0:T(8,128)(2,1)}, bf16[256,768]{1,0:T(8,128)(2,1)S(1)}, u32[]{:S(2)}, u32[]{:S(2)}) collective-permute-start(bf16[256,768]{1,0:T(8,128)(2,1)} %get-tuple-element.154), channel_id=1, source_target_pairs={{0,8},{4,12},{8,0},{12,4},{1,9},{5,13},{9,1},{13,5},{2,10},{6,14},... | collective-permute-start | bytes 1179656 | tf_op jit(solution)/shard_map/ppermute | solution.py:34
  91.5 36.1 %collective-permute-start = (bf16[256,768]{1,0:T(8,128)(2,1)}, bf16[256,768]{1,0:T(8,128)(2,1)S(1)}, u32[]{:S(2)}, u32[]{:S(2)}) collective-permute-start(bf16[256,768]{1,0:T(8,128)(2,1)} %get-tuple-element.155), channel_id=1, source_target_pairs={{0,2},{1,3},{2,0},{3,1},{4,6},{5,7},{6,4},{7,5},{8,10},{9,11},{10,... | collective-permute-start | bytes 1179656 | tf_op jit(solution)/shard_map/ppermute | solution.py:34
  94.4 41.0 %collective-permute-start.4 = (bf16[256,768]{1,0:T(8,128)(2,1)}, bf16[256,768]{1,0:T(8,128)(2,1)}, u32[]{:S(2)}, u32[]{:S(2)}) collective-permute-start(bf16[256,768]{1,0:T(8,128)(2,1)} %get-tuple-element.152), channel_id=1, source_target_pairs={{0,8},{4,12},{8,0},{12,4},{1,9},{5,13},{9,1},{13,5},{2,10},{6,14},... | collective-permute-start | bytes 1179656 | tf_op jit(solution)/shard_map/ppermute | solution.py:34
  94.4 41.0 %collective-permute-start.1 = (bf16[256,768]{1,0:T(8,128)(2,1)}, bf16[256,768]{1,0:T(8,128)(2,1)}, u32[]{:S(2)}, u32[]{:S(2)}) collective-permute-start(bf16[256,768]{1,0:T(8,128)(2,1)} %get-tuple-element.153), channel_id=1, source_target_pairs={{0,2},{1,3},{2,0},{3,1},{4,6},{5,7},{6,4},{7,5},{8,10},{9,11},{10,... | collective-permute-start | bytes 1179656 | tf_op jit(solution)/shard_map/ppermute | solution.py:34
  97.3 46.1 %collective-permute-start.5 = (bf16[768,256]{1,0:T(8,128)(2,1)}, bf16[768,256]{1,0:T(8,128)(2,1)}, u32[]{:S(2)}, u32[]{:S(2)}) collective-permute-start(bf16[768,256]{1,0:T(8,128)(2,1)} %get-tuple-element.150), channel_id=1, source_target_pairs={{0,8},{4,12},{8,0},{12,4},{1,9},{5,13},{9,1},{13,5},{2,10},{6,14},... | collective-permute-start | bytes 1179656 | tf_op jit(solution)/shard_map/ppermute | solution.py:34
  126.9 91.7 %copy-start.18 = (bf16[256,768]{1,0:T(8,128)(2,1)}, bf16[256,768]{1,0:T(8,128)(2,1)S(1)}, u32[]{:S(2)}) copy-start(bf16[256,768]{1,0:T(8,128)(2,1)S(1)} %collective-permute-done.3.gate_far_ref) | copy-start | bytes 1179652
  126.9 16.5 %collective-permute-start.2 = (bf16[768,256]{1,0:T(8,128)(2,1)S(1)}, bf16[768,256]{1,0:T(8,128)(2,1)S(1)}, u32[]{:S(2)}, u32[]{:S(2)}) collective-permute-start(bf16[768,256]{1,0:T(8,128)(2,1)S(1)} %copy-done.24), channel_id=1, source_target_pairs={{0,2},{1,3},{2,0},{3,1},{4,6},{5,7},{6,4},{7,5},{8,10},{9,11},{10,... | collective-permute-start | bytes 1179656 | tf_op jit(solution)/shard_map/ppermute | solution.py:34
  127.5 91.1 %copy-start.19 = (bf16[256,768]{1,0:T(8,128)(2,1)}, bf16[256,768]{1,0:T(8,128)(2,1)S(1)}, u32[]{:S(2)}) copy-start(bf16[256,768]{1,0:T(8,128)(2,1)S(1)} %collective-permute-done.gate_y_ref) | copy-start | bytes 1179652
  143.4 75.2 %copy-start.20 = (bf16[768,256]{1,0:T(8,128)(2,1)}, bf16[768,256]{1,0:T(8,128)(2,1)S(1)}, u32[]{:S(2)}) copy-start(bf16[768,256]{1,0:T(8,128)(2,1)S(1)} %collective-permute-done.2.down_y_ref) | copy-start | bytes 1179652
  197.4 42.7 %collective-permute-start.8 = (bf16[256,768]{1,0:T(8,128)(2,1)S(1)}, bf16[256,768]{1,0:T(8,128)(2,1)S(1)}, u32[]{:S(2)}, u32[]{:S(2)}) collective-permute-start(bf16[256,768]{1,0:T(8,128)(2,1)S(1)} %collective-permute-done.gate_y_ref), channel_id=1, source_target_pairs={{0,8},{4,12},{8,0},{12,4},{1,9},{5,13},{9,1},{13,5},{2,10},{6,14},... | collective-permute-start | bytes 1179656 | tf_op jit(solution)/shard_map/ppermute | solution.py:34
  197.5 45.8 %collective-permute-start.9 = (bf16[256,768]{1,0:T(8,128)(2,1)}, bf16[256,768]{1,0:T(8,128)(2,1)S(1)}, u32[]{:S(2)}, u32[]{:S(2)}) collective-permute-start(bf16[256,768]{1,0:T(8,128)(2,1)} %collective-permute-done.1.up_y_ref), channel_id=1, source_target_pairs={{0,8},{4,12},{8,0},{12,4},{1,9},{5,13},{9,1},{13,5},{2,10},{6,14},... | collective-permute-start | bytes 1179656 | tf_op jit(solution)/shard_map/ppermute | solution.py:34
  200.4 51.2 %collective-permute-start.10 = (bf16[768,256]{1,0:T(8,128)(2,1)S(1)}, bf16[768,256]{1,0:T(8,128)(2,1)S(1)}, u32[]{:S(2)}, u32[]{:S(2)}) collective-permute-start(bf16[768,256]{1,0:T(8,128)(2,1)S(1)} %collective-permute-done.2.down_y_ref), channel_id=1, source_target_pairs={{0,8},{4,12},{8,0},{12,4},{1,9},{5,13},{9,1},{13,5},{2,10},{6,14},... | collective-permute-start | bytes 1179656 | tf_op jit(solution)/shard_map/ppermute | solution.py:34
  200.5 18.2 %collective-permute-start.6 = (bf16[128,2048]{1,0:T(8,128)(2,1)S(1)}, bf16[128,2048]{1,0:T(8,128)(2,1)S(1)}, u32[]{:S(2)}, u32[]{:S(2)}) collective-permute-start(bf16[128,2048]{1,0:T(8,128)(2,1)S(1)} %get-tuple-element.76), channel_id=1, source_target_pairs={{0,2},{1,3},{2,0},{3,1},{4,6},{5,7},{6,4},{7,5},{8,10},{9,11},{10,... | collective-permute-start | bytes 1572872 | tf_op jit(solution)/shard_map/ppermute | solution.py:34
  201.2 33.4 %collective-permute-start.7 = (bf16[128,2048]{1,0:T(8,128)(2,1)S(1)}, bf16[128,2048]{1,0:T(8,128)(2,1)S(1)}, u32[]{:S(2)}, u32[]{:S(2)}) collective-permute-start(bf16[128,2048]{1,0:T(8,128)(2,1)S(1)} %get-tuple-element.77), channel_id=1, source_target_pairs={{0,4},{4,0},{8,12},{12,8},{1,5},{5,1},{9,13},{13,9},{2,6},{6,2},{1... | collective-permute-start | bytes 1572872 | tf_op jit(solution)/shard_map/ppermute | solution.py:34
  203.2 31.4 %copy-start.29 = (bf16[512,2048]{1,0:T(8,128)(2,1)S(1)}, bf16[512,2048]{1,0:T(8,128)(2,1)}, u32[]{:S(2)}) copy-start(bf16[512,2048]{1,0:T(8,128)(2,1)} %get-tuple-element.80) | copy-start | bytes 6291460
  240.1 11.6 %copy-start.21 = (bf16[256,768]{1,0:T(8,128)(2,1)}, bf16[256,768]{1,0:T(8,128)(2,1)S(1)}, u32[]{:S(2)}) copy-start(bf16[256,768]{1,0:T(8,128)(2,1)S(1)} %collective-permute-done.8.gate_both_ref) | copy-start | bytes 1179652
  340.6 25.6 %collective-permute-start.11 = (bf16[256,2048]{1,0:T(8,128)(2,1)S(1)}, bf16[256,2048]{1,0:T(8,128)(2,1)S(1)}, u32[]{:S(2)}, u32[]{:S(2)}) collective-permute-start(bf16[256,2048]{1,0:T(8,128)(2,1)S(1)} %pad_maximum_fusion), channel_id=1, source_target_pairs={{0,2},{1,3},{2,0},{3,1},{4,6},{5,7},{6,4},{7,5},{8,10},{9,11},{10,... | collective-permute-start | bytes 3145736 | tf_op jit(solution)/shard_map/ppermute | solution.py:34
  341.4 25.2 %collective-permute-start.12 = (bf16[256,2048]{1,0:T(8,128)(2,1)S(1)}, bf16[256,2048]{1,0:T(8,128)(2,1)S(1)}, u32[]{:S(2)}, u32[]{:S(2)}) collective-permute-start(bf16[256,2048]{1,0:T(8,128)(2,1)S(1)} %pad_maximum_fusion.1), channel_id=1, source_target_pairs={{0,4},{4,0},{8,12},{12,8},{1,5},{5,1},{9,13},{13,9},{2,6},{6,2},{1... | collective-permute-start | bytes 3145736 | tf_op jit(solution)/shard_map/ppermute | solution.py:34
  342.6 17.9 %copy-start.25 = (bf16[1024,2048]{1,0:T(8,128)(2,1)S(1)}, bf16[1024,2048]{1,0:T(8,128)(2,1)}, u32[]{:S(2)}) copy-start(bf16[1024,2048]{1,0:T(8,128)(2,1)} %constant_dynamic-update-slice_fusion.2) | copy-start | bytes 12582916
  366.7 17.9 %slice-start = ((s8[6291456]{0:T(1024)(128)(4,1)}), s8[2097152]{0:T(1024)(128)(4,1)S(1)}, s32[]{:S(2)}) async-start(s8[6291456]{0:T(1024)(128)(4,1)} %bitcast.56), calls=%async_computation | async-start | bytes 4194304
  366.8 17.8 %slice-start.1 = ((s8[6291456]{0:T(1024)(128)(4,1)}), s8[4194304]{0:T(1024)(128)(4,1)S(1)}, s32[]{:S(2)}) async-start(s8[6291456]{0:T(1024)(128)(4,1)} %bitcast.56), calls=%async_computation.1 | async-start | bytes 8388608
  532.0 54.9 %collective-permute-start.15 = (bf16[512,768]{1,0:T(8,128)(2,1)S(1)}, bf16[512,768]{1,0:T(8,128)(2,1)S(1)}, u32[]{:S(2)}, u32[]{:S(2)}) collective-permute-start(bf16[512,768]{1,0:T(8,128)(2,1)S(1)} %slice.132), channel_id=1, source_target_pairs={{0,8},{4,12},{8,0},{12,4},{1,9},{5,13},{9,1},{13,5},{2,10},{6,14},... | collective-permute-start | bytes 2359304 | tf_op jit(solution)/shard_map/ppermute | solution.py:34
  533.7 69.9 %collective-permute-start.14 = (bf16[768,512]{1,0:T(8,128)(2,1)S(1)}, bf16[768,512]{1,0:T(8,128)(2,1)S(1)}, u32[]{:S(2)}, u32[]{:S(2)}) collective-permute-start(bf16[768,512]{1,0:T(8,128)(2,1)S(1)} %slice.131), channel_id=1, source_target_pairs={{0,8},{4,12},{8,0},{12,4},{1,9},{5,13},{9,1},{13,5},{2,10},{6,14},... | collective-permute-start | bytes 2359304 | tf_op jit(solution)/shard_map/ppermute | solution.py:34
  535.0 36.6 %collective-permute-start.13 = (bf16[512,1536]{1,0:T(8,128)(2,1)}, bf16[512,1536]{1,0:T(8,128)(2,1)S(1)}, u32[]{:S(2)}, u32[]{:S(2)}) collective-permute-start(bf16[512,1536]{1,0:T(8,128)(2,1)} %get-tuple-element.94), channel_id=1, source_target_pairs={{0,16},{16,0},{1,17},{17,1},{2,18},{18,2},{3,19},{19,3},{4,20},{20... | collective-permute-start | bytes 4718600 | tf_op jit(solution)/shard_map/ppermute | solution.py:34
  536.1 24.3 %copy-start.31 = (bf16[1024,512]{1,0:T(8,128)(2,1)S(1)}, bf16[1024,512]{1,0:T(8,128)(2,1)}, u32[]{:S(2)}) copy-start(bf16[1024,512]{1,0:T(8,128)(2,1)} %get-tuple-element.79) | copy-start | bytes 3145732
  571.5 117.8 %copy-start.8 = (bf16[512,1536]{1,0:T(8,128)(2,1)}, bf16[512,1536]{1,0:T(8,128)(2,1)S(1)}, u32[]{:S(2)}) copy-start(bf16[512,1536]{1,0:T(8,128)(2,1)S(1)} %collective-permute-done.13.up_x_ref) | copy-start | bytes 4718596
  586.8 16.7 %copy-start.16 = (bf16[512,768]{1,0:T(8,128)(2,1)}, bf16[512,768]{1,0:T(8,128)(2,1)S(1)}, u32[]{:S(2)}) copy-start(bf16[512,768]{1,0:T(8,128)(2,1)S(1)} %collective-permute-done.15.gate_far_ref) | copy-start | bytes 2359300
  706.5 15.4 %collective-permute-start.16 = (bf16[1024,1280]{1,0:T(8,128)(2,1)S(1)}, bf16[1024,1280]{1,0:T(8,128)(2,1)S(1)}, u32[]{:S(2)}, u32[]{:S(2)}) collective-permute-start(bf16[1024,1280]{1,0:T(8,128)(2,1)S(1)} %slice.156), channel_id=1, source_target_pairs={{0,1},{1,0},{2,3},{3,2},{4,5},{5,4},{6,7},{7,6},{8,9},{9,8},{10,11... | collective-permute-start | bytes 7864328 | tf_op jit(solution)/shard_map/ppermute | solution.py:34
  (23 other events, 122.4 us)

commit v9 on v8

--- a/solution.py
+++ b/solution.py
@@ -531,13 +531,22 @@
 
 
 def begin_kernel(
-    tokens_ref, cotangent_ref, gain_ref, qkv_ref, out_ref, x_ref, rows_ref, all_ref, joined_ref, output_ref,
-    here, normed, there, send, recv, local, *, sizes,
+    tokens_ref, cotangent_ref, gain_ref, query_ref, key_ref, value_ref, gates_ref, out_ref,
+    x_ref, rows_ref, all_ref, joined_ref, output_ref, here, normed, there, qkv_ref, send, recv, local, *, sizes,
 ):
     net = Wires(send, recv, local, sizes)
     net.greet([Y, CORE, CORNER, NEAR, FAR, X])
     rows = local_flow(net, tokens_ref, here)
     across = qkv_ref.shape[1] // 2
+    packed, at = [], 0
+    for ref in (query_ref, key_ref, value_ref, gates_ref):
+        wide = ref.shape[1] // 2
+        for i in range(2):
+            packed.append(net.copy(ref.at[:, pl.ds(i * wide, wide)], qkv_ref.at[:, pl.ds(i * across + at, wide)]))
+        at += wide
+    for copy in packed:
+        copy.wait()
+    net.local = [copy for copy in net.local if all(copy is not other for other in packed)]
     joined = weight_flow(net, qkv_ref, joined_ref, 0, 0, across, across)
     run(joined)
     rows[0].wait()
@@ -592,16 +601,18 @@
     )(*args)
 
 
-def begin(tokens, cotangent, gain, qkv, out, sizes):
+def begin(tokens, cotangent, gain, weights, out, sizes):
     rows, width = tokens.shape[0] // sizes["narrow"], gain.shape[0]
+    wide = sum(w.shape[1] for w in weights)
     row = pltpu.VMEM((rows, width), BF16)
     return wire_call(
-        begin_kernel, "begin", 1, [ANY, ANY, VMEM, VMEM, VMEM], [VMEM, ANY, ANY, ANY, ANY],
+        begin_kernel, "begin", 1, [ANY, ANY, VMEM] + [ANY] * 4 + [VMEM], [VMEM, ANY, ANY, ANY, ANY],
         [
-            ((rows, width), BF16), ((rows, width), BF16), ((4 * rows, width), BF16), ((width, qkv.shape[1]), BF16),
+            ((rows, width), BF16), ((rows, width), BF16), ((4 * rows, width), BF16), ((width, wide), BF16),
             ((out.shape[0], width), BF16),
         ],
-        [row, row, row, *sems(48, 16)], sizes, 55, tokens, cotangent, gain[None], qkv, out,
+        [row, row, row, pltpu.VMEM((weights[0].shape[0], wide), BF16), *sems(48, 24)],
+        sizes, 55, tokens, cotangent, gain[None], *weights, out,
     )
 
 
@@ -784,8 +795,9 @@
         self.core = None if given else self.net.send(g_ref.at[other], from_core, CORE)
 
     def wait_core(self):
-        self.loaded.wait()
-        self.net.local = [copy for copy in self.net.local if copy is not self.loaded]
+        if self.loaded is not None:
+            self.loaded.wait()
+            self.net.local = [copy for copy in self.net.local if copy is not self.loaded]
         if self.core is not None:
             self.net.arrived(self.core)
 
@@ -846,11 +858,11 @@
 
 
 def turn_kernel(
-    partial_ref, middle_ref, upstream_ref, gain_ref, down_ref, gate_ref, up_ref,
+    partial_ref, middle_ref, upstream_ref, gain_ref, down_ref, gate_ref, inputs_ref, grads_ref,
     grad_ref, all_ref, term_ref, down_out, gate_out, up_keep, up_send,
     first, second, sums, last, total, low, *rest, sizes,
 ):
-    buffers, (send, recv, local) = rest[:-3], rest[-3:]
+    buffers, (rows_two, up_grads, up_other), (send, recv, local) = rest[:-6], rest[-6:-3], rest[-3:]
     net = Wires(send, recv, local, sizes)
     net.greet([Y, CORE, NEAR, FAR, X])
     scatter = scatter_flow(net, partial_ref, first, second, sums, last, total)
@@ -859,7 +871,8 @@
     down, gate, up = (Gradient(net, axis, step, across) for axis in (1, 0, 0))
     down.start(down_ref, *buffers[0:2])
     gate.start(gate_ref, *buffers[3:5])
-    up.start(up_ref, *buffers[6:8])
+    up.acc, up.from_core = buffers[6:8]
+    loads = [net.copy(inputs_ref, rows_two), net.copy(grads_ref.at[:, pl.ds(2 * across, 2 * across)], up_grads)]
     down.core_to_x(buffers[2])
     gate.core_to_x(buffers[5])
     run(scatter)
@@ -878,11 +891,28 @@
     by_rows(low.shape[0], rows)
     gather = gather_flow(net, low, all_ref)
     run(gather)
+    for copy in loads:
+        copy.wait()
+    net.local = [copy for copy in net.local if all(copy is not other for other in loads)]
+    half = rows_two.shape[1] // 2
+
+    def up_dots(base, target):
+        def body(i, _):
+            at = pl.multiple_of(i * step, step)
+            part = dot_inner(rows_two[:, pl.ds(pl.multiple_of(base + at, step), step)], up_grads[...])
+            target[pl.ds(at, step), :] = part.astype(BF16)
+            return 0
+
+        lax.fori_loop(0, half // step, body, 0)
+
+    up_dots(half, up_other)
+    up.loaded, up.core = None, net.send(up_other, up.from_core, CORE)
     for k in range(2):
         down.x_end(k)
         net.copy(down.acc.at[down.slot(k, 2, 0, 2 * across)], down_out.at[down.slot(k, 1, 0, 2 * across)])
     run(gather)
     run(gather)
+    up_dots(0, up.acc)
     up.wait_core()
     for slot in range(2):
         for j, ref in ((1, up_send), (0, up_keep)):
@@ -906,20 +936,22 @@
     return [buffer(BF16), buffer(BF16), buffer(BF16), buffer(BF16), buffer(F32)]
 
 
-def turn(partial, middle, upstream, gain, down, gate, up, sizes):
+def turn(partial, middle, upstream, gain, down, gate, inputs, grads, sizes):
     rows, width = middle.shape
     size, across = width // sizes["narrow"], down.shape[0] // 2
     return wire_call(
-        turn_kernel, "turn", 4, [VMEM] * 4 + [ANY] * 3, [VMEM, ANY, VMEM, ANY, ANY, ANY, ANY],
+        turn_kernel, "turn", 4, [VMEM] * 4 + [ANY] * 4, [VMEM, ANY, VMEM, ANY, ANY, ANY, ANY],
         [
             ((rows, width), F32), ((4 * rows, width), BF16), ((1, width), F32),
             ((2 * across, size), BF16), ((size, 2 * across), BF16), ((size, 2 * across), BF16), ((size, 2 * across), BF16),
         ],
         [
             *scatter_buffers(rows, width), pltpu.VMEM((rows, width), BF16),
-            *gradient_buffers(size, across, 1, 3), *gradient_buffers(size, across, 0, 3), *gradient_buffers(size, across, 0, 2), *sems(40, 16),
+            *gradient_buffers(size, across, 1, 3), *gradient_buffers(size, across, 0, 3), *gradient_buffers(size, across, 0, 2),
+            pltpu.VMEM(inputs.shape, BF16), pltpu.VMEM((inputs.shape[0], 2 * across), BF16), pltpu.VMEM((2 * size, 2 * across), BF16),
+            *sems(40, 24),
         ],
-        sizes, 80, partial, middle, upstream, gain[None], down, gate, up,
+        sizes, 80, partial, middle, upstream, gain[None], down, gate, inputs, grads,
     )
 
 
@@ -1202,11 +1234,8 @@
         gain_one, gain_two = relative_vector(attention_gain), relative_vector(feedforward_gain)
         lane_pad = ((0, 0), (0, LANES - heads // 2))
         halves = lambda w, i: w[:, i * (w.shape[1] // 2) : (i + 1) * (w.shape[1] // 2)]
-        packed = join(
-            [v for i in range(2) for v in (
-                halves(query_weight, i), halves(key_weight, i), halves(value_weight, i), jnp.pad(halves(head_gate, i), lane_pad)
-            )], 1
-        )
+        gates = join([jnp.pad(halves(head_gate, i), lane_pad) for i in range(2)], 1)
+        packed = (query_weight, key_weight, value_weight, gates)
         inputs, upstream, normed_all, joined_weight, out_weight = begin(tokens, cotangent, gain_one, packed, output_weight, sizes)
 
         def indices(row):
@@ -1244,21 +1273,22 @@
         from_y = [over_y(piece_of(w, 1 - y, axis)) for w, axis in zip(send, axes)]
         from_far = [over_far(piece_of(w, y, axis)) for w, axis in zip(send, axes)]
         part = rows_local // 2
-        kv_all = exchange_keys(after(kv, *from_y, *from_far), sizes)
-        upstream_y, upstream_z = over_y(after(upstream[:part], kv_all)), over_z(after(upstream[part:], kv_all))
+        upstream_y, upstream_z = over_y(upstream[:part]), over_z(upstream[part:])
+        kv_all = exchange_keys(after(kv, *from_y, *from_far, upstream_y, upstream_z), sizes)
         from_both = [over_far(after(v, kv_all)) for v in from_y]
+
+        come_z = over_z(join([upstream[:part], after(upstream_y, kv_all)]))
+        come_y = over_y(join([upstream[part:], after(upstream_z, kv_all)]))
+        upstream_all = join(
+            [upstream, upstream_y, come_y[:part], come_z[:part], upstream_z, come_z[part:], come_y[part:]]
+        )
 
         gated, context, inverse_total = attend(
             table, q, kv_all, my_index, my_start, raw, pairs, size
         )
-        partial = dot_rows(after(gated, upstream_y, upstream_z), out_weight).astype(BF16)
+        partial = dot_rows(gated, out_weight).astype(BF16)
         middle, normed_two_all, gate_up, down = to_middle(
             partial, inputs, gain_two, gate_weight, up_weight, down_weight, from_y + from_far + from_both, sizes
-        )
-        come_z = over_z(join([upstream[:part], after(upstream_y, normed_two_all)]))
-        come_y = over_y(join([upstream[part:], after(upstream_z, normed_two_all)]))
-        upstream_all = join(
-            [upstream, upstream_y, come_y[:part], come_z[:part], upstream_z, come_z[part:], come_y[part:]]
         )
         both = dot_rows(normed_two_all, gate_up)
         hidden_cols = gate_weight.shape[1]
@@ -1271,14 +1301,12 @@
         up_grad = hidden_grad * silu
         gate_up_low = join([gate_grad, up_grad], 1).astype(BF16)
         partial = dot_trans(gate_up_low, gate_up).astype(BF16)
-        gate_low, up_low = gate_up_low[:, :hidden_cols], gate_up_low[:, hidden_cols:]
         down_sums = dot_inner(hidden, upstream_all).astype(BF16)
-        gate_sums = dot_inner(normed_two_all, gate_low).astype(BF16)
-        up_sums = dot_inner(normed_two_all, up_low).astype(BF16)
+        gate_sums = dot_inner(normed_two_all, gate_up_low[:, :hidden_cols]).astype(BF16)
         mlp_partial = dot_rows(hidden, down).astype(BF16)
         partial = after(partial, mlp_partial)
         middle_grad, middle_all, two_term, down_part, gate_part, up_keep, up_send = turn(
-            partial, middle, upstream, gain_two, down_sums, gate_sums, up_sums, sizes
+            partial, middle, upstream, gain_two, down_sums, gate_sums, normed_two_all, gate_up_low, sizes
         )
         down_far = over_far(down_part[hidden_cols // 2 :])
         gate_far = over_far(gate_part[:, hidden_cols // 2 :])

time: 876 us -> 852 us (0.973)
  matrix products: 137 us -> 125 us
  waiting for transfers between devices: 88.3 us -> 79.1 us
    dot_general x5 -> x4, matrix products: 42.6 us -> 31.6 us  [dot_inner(): lax.dot_general(left, right, (((0,), (0,)), ((), ())), preferred_element_...]
    ppermute x17, waiting for transfers between devices: 88.3 us -> 79.1 us  [exchange(): return lax.ppermute(values, axis, [(i, i ^ distance) for i in range(size)])]
  transfers between devices with their start and end apart: 17 -> 17, of which waited for: 11 -> 8; matrix products, arithmetic and copies ran while one was open for 7% -> 8% of each run, Pallas kernels for 5% -> 16%
where the time goes in v9:
time: 852 us; the launch traced here: 844 us
  Pallas kernels  564 us (66%)
  matrix products  125 us (15%)
  waiting for transfers between devices  79.1 us (9%)
  local copies, waits for them, and re-layouts  29.1 us (3%)
  other arithmetic  25.5 us (3%)
  starting transfers between devices  20.5 us (2%)
    pallas_call x6, Pallas kernels, wire_call(): pl.pallas_call(functools.partial(kernel, sizes=sizes), in_specs=specs, ou...  509 us
    ppermute x17, waiting for transfers between devices, exchange(): return lax.ppermute(values, axis, [(i, i ^ distance) for i in range(size)])  79.1 us
    dot_general x4, matrix products, dot_rows(): return jnp.dot(left, right, preferred_element_type=F32)  46.9 us
    dot_general x4, matrix products, dot_trans(): lax.dot_general(left, right, (((1,), (1,)), ((), ())), preferred_element_...  46.1 us
    dot_general x4, matrix products, dot_inner(): lax.dot_general(left, right, (((0,), (0,)), ((), ())), preferred_element_...  31.6 us
    pallas_call x1, Pallas kernels, attend_back(): pl.pallas_call(functools.partial(backward_kernel, pairs=pairs, repeat=hea...  24.3 us
    ppermute x17, starting transfers between devices, exchange(): return lax.ppermute(values, axis, [(i, i ^ distance) for i in range(size)])  20.5 us
  transfers between devices with their start and end apart: 17, of which 8 were waited for; matrix products, arithmetic and copies ran while one was open for 8% of the time, Pallas kernels for 16%

profile of v9, /device:TPU:0, one launch (start us, length us, event | category | flops | bytes accessed | tf_op | source)
XLA Modules:
  0.0 844.1 jit_solution(5791085916902470548)
XLA Ops:
  5.1 75.2 %begin.1 = (bf16[256,2048]{1,0:T(8,128)(2,1)}, bf16[256,2048]{1,0:T(8,128)(2,1)}, bf16[1024,2048]{1,0:T(8,128)(2,1)}, bf16[2048,1280]{1,0:T(8,128)(2,1)}, bf16[512,2048]{1,0:T(8,128)(2,1)}) custom-call(bf16[1024,512]{1,0:T(8,128)(2,1)} %tokens_ref.1, bf16[1024,512]{1,0:T(8,128)(2,1)} %cotangent_ref.1, f32[1,2048]{1,0:T(1,128)} %broadcast_in_dim_reshape.8.gain_ref, ...), custom_call_target="tpu_custom_call" | custom-call | bytes 165000000 | tf_op jit(solution)/shard_map/begin/pallas_call | solution.py:592
  88.1 4.8 collective-permute-start.7
  97.0 10.4 %fusion.66.raw_ref.own_ref.other_ref = f32[1024,1280]{1,0:T(8,128)} fusion(bf16[1024,2048]{1,0:T(8,128)(2,1)} %get-tuple-element.62, bf16[2048,1280]{1,0:T(8,128)(2,1)} %get-tuple-element.63), kind=kOutput, calls=%fused_computation.175 | convolution fusion | flops 5368709120 | bytes 14680064 | tf_op jit(solution)/shard_map/dot_general | solution.py:22
  112.5 6.4 post.1
  122.9 8.2 collective-permute-done.1.up_y_ref
  131.1 8.5 %collective-permute-done.5.down_far_ref = bf16[768,256]{1,0:T(8,128)(2,1)S(1)} collective-permute-done((bf16[768,256]{1,0:T(8,128)(2,1)}, bf16[768,256]{1,0:T(8,128)(2,1)S(1)}, u32[]{:S(2)}, u32[]{:S(2)}) %collective-permute-start.5) | collective-permute-done | bytes 393248 | tf_op jit(solution)/shard_map/ppermute | solution.py:34
  140.4 51.1 %keys.1.kv_ref = bf16[4096,512]{1,0:T(8,128)(2,1)} custom-call(bf16[1024,512]{1,0:T(8,128)(2,1)} %get-tuple-element.70.kv_ref), custom_call_target="tpu_custom_call" | custom-call | bytes 135000000 | tf_op jit(solution)/shard_map/keys/pallas_call | solution.py:592
  197.5 15.3 %attend.1 = (bf16[1024,512]{1,0:T(8,128)(2,1)}, f32[1024,512]{1,0:T(8,128)}, f32[1024,512]{1,0:T(8,128)}) custom-call(s32[4,5]{1,0:T(4,128)} %select_select_fusion.table_ref, bf16[1024,512]{1,0:T(8,128)(2,1)} %get-tuple-element.64.q_ref, bf16[4096,512]{1,0:T(8,128)(2,1)} %keys.1.kv_ref, s32[1024,1]{1,0:T(8,128)} %get-tuple-element.171.row_ref, ...), custom_call_target="tpu_custom_call" | custom-call | flops 20000000000 | bytes 12000000 | tf_op jit(solution)/shard_map/attend/pallas_call | solution.py:244
  213.7 6.2 convolution_convert_fusion.6.partial_ref
  219.9 9.2 %collective-permute-done.10.gate_both_ref = bf16[256,768]{1,0:T(8,128)(2,1)S(1)} collective-permute-done((bf16[256,768]{1,0:T(8,128)(2,1)S(1)}, bf16[256,768]{1,0:T(8,128)(2,1)S(1)}, u32[]{:S(2)}, u32[]{:S(2)}) %collective-permute-start.10) | collective-permute-done | bytes 393248 | tf_op jit(solution)/shard_map/ppermute | solution.py:34
  229.0 8.4 collective-permute-done.11.up_both_ref
  237.5 8.3 collective-permute-done.12.down_both_ref
  246.6 88.0 %middle.1 = (f32[256,2048]{1,0:T(8,128)}, bf16[1024,2048]{1,0:T(8,128)(2,1)}, bf16[2048,3072]{1,0:T(8,128)(2,1)}, bf16[1536,2048]{1,0:T(8,128)(2,1)}) custom-call(bf16[1024,2048]{1,0:T(8,128)(2,1)} %convolution_convert_fusion.6.partial_ref, bf16[256,2048]{1,0:T(8,128)(2,1)} %get-tuple-element.77.x_ref, f32[1,2048]{1,0:T(1,128)} %broadcast_in_dim_reshape.9.gain_ref, ...), custom_call_target="tpu_custom_call" | custom-call | bytes 240000000 | tf_op jit(solution)/shard_map/middle/pallas_call | solution.py:592
  334.5 19.1 %fusion.67 = f32[1024,3072]{1,0:T(8,128)} fusion(bf16[1024,2048]{1,0:T(8,128)(2,1)} %get-tuple-element.82.inputs_ref, bf16[2048,3072]{1,0:T(8,128)(2,1)} %get-tuple-element.83), kind=kOutput, calls=%fused_computation.176 | convolution fusion | flops 12884901888 | bytes 29360128 | tf_op jit(solution)/shard_map/dot_general | solution.py:22
  353.9 15.2 %multiply_convert_fusion.2 = (bf16[1024,1536]{1,0:T(8,128)(2,1)S(1)}, bf16[1024,1536]{1,0:T(8,128)(2,1)S(1)}, bf16[1024,1536]{1,0:T(8,128)(2,1)}) fusion(f32[1024,3072]{1,0:T(8,128)} %fusion.67, bf16[1024,2048]{1,0:T(8,128)(2,1)S(1)} %slice_dynamic-update-slice_fusion, bf16[1536,2048]{1,0:T(8,128)(2,1)} %get-tuple-element.81), kind=kOutput, calls=%fused_computation.6 | convolution fusion | flops 6466043904 | bytes 32505856 | tf_op jit(solution)/shard_map/dot_general | solution.py:26
  369.1 11.2 %convolution_convert_fusion.4.partial_ref = bf16[1024,2048]{1,0:T(8,128)(2,1)} fusion(bf16[1024,1536]{1,0:T(8,128)(2,1)} %get-tuple-element.143, bf16[1536,2048]{1,0:T(8,128)(2,1)} %get-tuple-element.81), kind=kOutput, calls=%fused_computation.10 | convolution fusion | flops 6444548096 | bytes 13631488 | tf_op jit(solution)/shard_map/dot_general | solution.py:22
  380.3 8.8 %convolution_convert_fusion.2.down_ref = bf16[1536,2048]{1,0:T(8,128)(2,1)} fusion(bf16[1024,1536]{1,0:T(8,128)(2,1)S(1)} %copy-done.31, bf16[1024,2048]{1,0:T(8,128)(2,1)S(1)} %slice_dynamic-update-slice_fusion), kind=kOutput, calls=%fused_computation.2 | convolution fusion | flops 6445596672 | bytes 13631488 | tf_op jit(solution)/shard_map/dot_general | solution.py:30
  389.1 17.6 %convolution_convert_fusion.3.partial_ref = bf16[1024,2048]{1,0:T(8,128)(2,1)} fusion(bf16[2048,3072]{1,0:T(8,128)(2,1)} %get-tuple-element.83, bf16[1024,1536]{1,0:T(8,128)(2,1)S(1)} %get-tuple-element.142, bf16[1024,1536]{1,0:T(8,128)(2,1)S(1)} %get-tuple-element.141), kind=kOutput, calls=%fused_computation.9 | convolution fusion | flops 12899581952 | bytes 23068672 | tf_op jit(solution)/shard_map/dot_general | solution.py:26
  406.7 3.7 pad_maximum_fusion.grads_ref
  410.4 8.6 %convolution_convert_fusion.1.gate_ref = bf16[2048,1536]{1,0:T(8,128)(2,1)} fusion(bf16[1024,2048]{1,0:T(8,128)(2,1)S(1)} %copy-done.2, bf16[1024,1536]{1,0:T(8,128)(2,1)S(1)} %get-tuple-element.141), kind=kOutput, calls=%fused_computation.1 | convolution fusion | flops 6445596672 | bytes 13631488 | tf_op jit(solution)/shard_map/dot_general | solution.py:30
  419.0 84.9 %turn.1 = (f32[256,2048]{1,0:T(8,128)}, bf16[1024,2048]{1,0:T(8,128)(2,1)}, f32[1,2048]{1,0:T(1,128)}, bf16[1536,512]{1,0:T(8,128)(2,1)}, bf16[512,1536]{1,0:T(8...) custom-call(bf16[1024,2048]{1,0:T(8,128)(2,1)} %convolution_convert_fusion.3.partial_ref, ...), custom_call_target="tpu_custom_call" | custom-call | bytes 240000000 | tf_op jit(solution)/shard_map/turn/pallas_call | solution.py:592
  504.0 6.0 fusion.68.grad_ref
  513.5 24.3 %attend_back.1 = (f32[1024,512]{1,0:T(8,128)}, bf16[4096,512]{1,0:T(8,128)(2,1)}, f32[1024,256]{1,0:T(8,128)}) custom-call(s32[4,5]{1,0:T(4,128)} %select_select_fusion.table_ref, bf16[1024,512]{1,0:T(8,128)(2,1)} %get-tuple-element.64.q_ref, bf16[4096,512]{1,0:T(8,128)(2,1)} %keys.1.kv_ref, s32[4,1,256]{2,1,0:T(1,128)} %get-tuple-element.174.row_ref, ...), custom_call_target="tpu_custom_call" | custom-call | flops 49999998976 | bytes 20000000 | tf_op jit(solution)/shard_map/attend_back/pallas_call | solution.py:346
  537.9 5.9 convolution_convert_fusion.7.out_ref
  543.7 4.9 collective-permute-done.13.up_x_ref
  548.6 14.8 %collective-permute-done.15.gate_far_ref = bf16[512,768]{1,0:T(8,128)(2,1)S(1)} collective-permute-done((bf16[512,768]{1,0:T(8,128)(2,1)S(1)}, bf16[512,768]{1,0:T(8,128)(2,1)S(1)}, u32[]{:S(2)}, u32[]{:S(2)}) %collective-permute-start.15) | collective-permute-done | bytes 786464 | tf_op jit(solution)/shard_map/ppermute | solution.py:34
  563.4 16.8 %collective-permute-done.14.down_far_ref = bf16[768,512]{1,0:T(8,128)(2,1)S(1)} collective-permute-done((bf16[768,512]{1,0:T(8,128)(2,1)S(1)}, bf16[768,512]{1,0:T(8,128)(2,1)S(1)}, u32[]{:S(2)}, u32[]{:S(2)}) %collective-permute-start.14) | collective-permute-done | bytes 786464 | tf_op jit(solution)/shard_map/ppermute | solution.py:34
  581.0 84.8 %owner.1 = (f32[1024,512]{1,0:T(8,128)}, bf16[1024,512]{1,0:T(8,128)(2,1)}, bf16[1536,512]{1,0:T(8,128)(2,1)}, bf16[512,1536]{1,0:T(8,128)(2,1)}) custom-call(bf16[4096,512]{1,0:T(8,128)(2,1)} %get-tuple-element.89.dkv_ref, bf16[1024,2048]{1,0:T(8,128)(2,1)} %convolution_convert_fusion.4.partial_ref, f32[256,2048]{1,0:T(8,128)} %get-tuple-element.85.middle_ref, ...), custom_call_target="tpu_custom_call" | custom-call | bytes 240000000 | tf_op jit(solution)/shard_map/owner/pallas_call | solution.py:592
  665.8 8.7 %project_back.1 = (bf16[1024,1280]{1,0:T(8,128)(2,1)}, f32[1,128]{1,0:T(1,128)}, f32[1,128]{1,0:T(1,128)}) custom-call(f32[1024,512]{1,0:T(8,128)} %get-tuple-element.93.dq_ref, f32[1024,512]{1,0:T(8,128)} %get-tuple-element.94.dkv_ref, f32[1024,1280]{1,0:T(8,128)} %fusion.66.raw_ref.own_ref.other_ref, f32[1024,128]{1,0:T(8,128)} %get-tuple-element.181.cos_ref, ...), custom_call_target="tpu_custom_call" | custom-call | flops 39321600 | bytes 15728640 | tf_op jit(solution)/shard_map/project_back/pallas_call | solution.py:150
  674.5 8.3 convolution_convert_fusion.qkv_ref
  691.2 7.2 convolution_convert_fusion.5.partial_ref
  699.9 125.2 %end.1 = (bf16[1024,512]{1,0:T(8,128)(2,1)}, f32[1,4352]{1,0:T(1,128)}, bf16[512,1280]{1,0:T(8,128)(2,1)}, bf16[512,512]{1,0:T(8,128)(2,1)}, bf16[512,1536]{1,0:T(8,128)(2,1)}) custom-call(bf16[1024,2048]{1,0:T(8,128)(2,1)} %convolution_convert_fusion.5.partial_ref, bf16[256,2048]{1,0:T(8,128)(2,1)} %get-tuple-element.77.x_ref, ...), custom_call_target="tpu_custom_call" | custom-call | bytes 270000000 | tf_op jit(solution)/shard_map/end/pallas_call | solution.py:592
  (161 shorter events, 66.7 us)
Async XLA Ops:
  0.6 84.8 %copy-start.6 = (bf16[512,1536]{1,0:T(8,128)(2,1)S(1)}, bf16[512,1536]{1,0:T(8,128)(2,1)}, u32[]{:S(2)}) copy-start(bf16[512,1536]{1,0:T(8,128)(2,1)} %up_ref.1) | copy-start | bytes 4718596
  0.7 79.6 %copy-start.5 = (bf16[512,1536]{1,0:T(8,128)(2,1)S(1)}, bf16[512,1536]{1,0:T(8,128)(2,1)}, u32[]{:S(2)}) copy-start(bf16[512,1536]{1,0:T(8,128)(2,1)} %gate_ref.1) | copy-start | bytes 4718596
  5.1 88.2 %copy-start.29 = (s32[1,8]{1,0:T(1,128)S(1)}, s32[1,8]{1,0:T(1,128)}, u32[]{:S(2)}) copy-start(s32[1,8]{1,0:T(1,128)} %param.16) | copy-start | bytes 100
  81.6 37.2 %collective-permute-start.3 = (bf16[256,768]{1,0:T(8,128)(2,1)}, bf16[256,768]{1,0:T(8,128)(2,1)S(1)}, u32[]{:S(2)}, u32[]{:S(2)}) collective-permute-start(bf16[256,768]{1,0:T(8,128)(2,1)} %get-tuple-element.148), channel_id=1, source_target_pairs={{0,8},{4,12},{8,0},{12,4},{1,9},{5,13},{9,1},{13,5},{2,10},{6,14},... | collective-permute-start | bytes 1179656 | tf_op jit(solution)/shard_map/ppermute | solution.py:34
  85.0 35.5 %collective-permute-start = (bf16[256,768]{1,0:T(8,128)(2,1)}, bf16[256,768]{1,0:T(8,128)(2,1)S(1)}, u32[]{:S(2)}, u32[]{:S(2)}) collective-permute-start(bf16[256,768]{1,0:T(8,128)(2,1)} %get-tuple-element.149), channel_id=1, source_target_pairs={{0,2},{1,3},{2,0},{3,1},{4,6},{5,7},{6,4},{7,5},{8,10},{9,11},{10,... | collective-permute-start | bytes 1179656 | tf_op jit(solution)/shard_map/ppermute | solution.py:34
  86.8 33.7 %collective-permute-start.4 = (bf16[256,768]{1,0:T(8,128)(2,1)}, bf16[256,768]{1,0:T(8,128)(2,1)}, u32[]{:S(2)}, u32[]{:S(2)}) collective-permute-start(bf16[256,768]{1,0:T(8,128)(2,1)} %get-tuple-element.146), channel_id=1, source_target_pairs={{0,8},{4,12},{8,0},{12,4},{1,9},{5,13},{9,1},{13,5},{2,10},{6,14},... | collective-permute-start | bytes 1179656 | tf_op jit(solution)/shard_map/ppermute | solution.py:34
  88.1 51.5 %collective-permute-start.7 = (bf16[128,2048]{1,0:T(8,128)(2,1)S(1)}, bf16[128,2048]{1,0:T(8,128)(2,1)S(1)}, u32[]{:S(2)}, u32[]{:S(2)}) collective-permute-start(bf16[128,2048]{1,0:T(8,128)(2,1)S(1)} %get-tuple-element.158), channel_id=1, source_target_pairs={{0,4},{4,0},{8,12},{12,8},{1,5},{5,1},{9,13},{13,9},{2,6},{6,2},{1... | collective-permute-start | bytes 1572872 | tf_op jit(solution)/shard_map/ppermute | solution.py:34
  92.8 46.8 %collective-permute-start.6 = (bf16[128,2048]{1,0:T(8,128)(2,1)S(1)}, bf16[128,2048]{1,0:T(8,128)(2,1)S(1)}, u32[]{:S(2)}, u32[]{:S(2)}) collective-permute-start(bf16[128,2048]{1,0:T(8,128)(2,1)S(1)} %get-tuple-element.159), channel_id=1, source_target_pairs={{0,2},{1,3},{2,0},{3,1},{4,6},{5,7},{6,4},{7,5},{8,10},{9,11},{10,... | collective-permute-start | bytes 1572872 | tf_op jit(solution)/shard_map/ppermute | solution.py:34
  118.8 72.7 %copy-start.18 = (bf16[256,768]{1,0:T(8,128)(2,1)}, bf16[256,768]{1,0:T(8,128)(2,1)S(1)}, u32[]{:S(2)}) copy-start(bf16[256,768]{1,0:T(8,128)(2,1)S(1)} %collective-permute-done.3.gate_far_ref) | copy-start | bytes 1179652
  118.8 12.3 %collective-permute-start.1 = (bf16[256,768]{1,0:T(8,128)(2,1)}, bf16[256,768]{1,0:T(8,128)(2,1)S(1)}, u32[]{:S(2)}, u32[]{:S(2)}) collective-permute-start(bf16[256,768]{1,0:T(8,128)(2,1)} %get-tuple-element.147), channel_id=1, source_target_pairs={{0,2},{1,3},{2,0},{3,1},{4,6},{5,7},{6,4},{7,5},{8,10},{9,11},{10,... | collective-permute-start | bytes 1179656 | tf_op jit(solution)/shard_map/ppermute | solution.py:34
  120.5 71.0 %copy-start.19 = (bf16[256,768]{1,0:T(8,128)(2,1)}, bf16[256,768]{1,0:T(8,128)(2,1)S(1)}, u32[]{:S(2)}) copy-start(bf16[256,768]{1,0:T(8,128)(2,1)S(1)} %collective-permute-done.gate_y_ref) | copy-start | bytes 1179652
  120.5 19.1 %collective-permute-start.5 = (bf16[768,256]{1,0:T(8,128)(2,1)}, bf16[768,256]{1,0:T(8,128)(2,1)S(1)}, u32[]{:S(2)}, u32[]{:S(2)}) collective-permute-start(bf16[768,256]{1,0:T(8,128)(2,1)} %get-tuple-element.144), channel_id=1, source_target_pairs={{0,8},{4,12},{8,0},{12,4},{1,9},{5,13},{9,1},{13,5},{2,10},{6,14},... | collective-permute-start | bytes 1179656 | tf_op jit(solution)/shard_map/ppermute | solution.py:34
  120.5 19.1 %collective-permute-start.2 = (bf16[768,256]{1,0:T(8,128)(2,1)}, bf16[768,256]{1,0:T(8,128)(2,1)}, u32[]{:S(2)}, u32[]{:S(2)}) collective-permute-start(bf16[768,256]{1,0:T(8,128)(2,1)} %get-tuple-element.145), channel_id=1, source_target_pairs={{0,2},{1,3},{2,0},{3,1},{4,6},{5,7},{6,4},{7,5},{8,10},{9,11},{10,... | collective-permute-start | bytes 1179656 | tf_op jit(solution)/shard_map/ppermute | solution.py:34
  131.1 63.6 %copy-start.20 = (bf16[256,768]{1,0:T(8,128)(2,1)}, bf16[256,768]{1,0:T(8,128)(2,1)S(1)}, u32[]{:S(2)}) copy-start(bf16[256,768]{1,0:T(8,128)(2,1)S(1)} %collective-permute-done.1.up_y_ref) | copy-start | bytes 1179652
  191.6 37.5 %collective-permute-start.10 = (bf16[256,768]{1,0:T(8,128)(2,1)S(1)}, bf16[256,768]{1,0:T(8,128)(2,1)S(1)}, u32[]{:S(2)}, u32[]{:S(2)}) collective-permute-start(bf16[256,768]{1,0:T(8,128)(2,1)S(1)} %collective-permute-done.gate_y_ref), channel_id=1, source_target_pairs={{0,8},{4,12},{8,0},{12,4},{1,9},{5,13},{9,1},{13,5},{2,10},{6,14},... | collective-permute-start | bytes 1179656 | tf_op jit(solution)/shard_map/ppermute | solution.py:34
  191.6 45.8 %collective-permute-start.11 = (bf16[256,768]{1,0:T(8,128)(2,1)S(1)}, bf16[256,768]{1,0:T(8,128)(2,1)S(1)}, u32[]{:S(2)}, u32[]{:S(2)}) collective-permute-start(bf16[256,768]{1,0:T(8,128)(2,1)S(1)} %collective-permute-done.1.up_y_ref), channel_id=1, source_target_pairs={{0,8},{4,12},{8,0},{12,4},{1,9},{5,13},{9,1},{13,5},{2,10},{6,14},... | collective-permute-start | bytes 1179656 | tf_op jit(solution)/shard_map/ppermute | solution.py:34
  194.6 51.2 %collective-permute-start.12 = (bf16[768,256]{1,0:T(8,128)(2,1)}, bf16[768,256]{1,0:T(8,128)(2,1)S(1)}, u32[]{:S(2)}, u32[]{:S(2)}) collective-permute-start(bf16[768,256]{1,0:T(8,128)(2,1)} %collective-permute-done.2.down_y_ref), channel_id=1, source_target_pairs={{0,8},{4,12},{8,0},{12,4},{1,9},{5,13},{9,1},{13,5},{2,10},{6,14},... | collective-permute-start | bytes 1179656 | tf_op jit(solution)/shard_map/ppermute | solution.py:34
  194.7 158.9 %collective-permute-start.8 = (bf16[256,2048]{1,0:T(8,128)(2,1)S(1)}, bf16[256,2048]{1,0:T(8,128)(2,1)S(1)}, u32[]{:S(2)}, u32[]{:S(2)}) collective-permute-start(bf16[256,2048]{1,0:T(8,128)(2,1)S(1)} %pad_maximum_fusion.1), channel_id=1, source_target_pairs={{0,2},{1,3},{2,0},{3,1},{4,6},{5,7},{6,4},{7,5},{8,10},{9,11},{10,... | collective-permute-start | bytes 3145736 | tf_op jit(solution)/shard_map/ppermute | solution.py:34
  195.5 158.2 %collective-permute-start.9 = (bf16[256,2048]{1,0:T(8,128)(2,1)S(1)}, bf16[256,2048]{1,0:T(8,128)(2,1)S(1)}, u32[]{:S(2)}, u32[]{:S(2)}) collective-permute-start(bf16[256,2048]{1,0:T(8,128)(2,1)S(1)} %pad_maximum_fusion.2), channel_id=1, source_target_pairs={{0,4},{4,0},{8,12},{12,8},{1,5},{5,1},{9,13},{13,9},{2,6},{6,2},{1... | collective-permute-start | bytes 3145736 | tf_op jit(solution)/shard_map/ppermute | solution.py:34
  229.0 16.8 %copy-start.22 = (bf16[256,768]{1,0:T(8,128)(2,1)}, bf16[256,768]{1,0:T(8,128)(2,1)S(1)}, u32[]{:S(2)}) copy-start(bf16[256,768]{1,0:T(8,128)(2,1)S(1)} %collective-permute-done.10.gate_both_ref) | copy-start | bytes 1179652
  237.5 8.4 copy-start.23
  334.5 19.1 %copy-start.25 = (bf16[1024,2048]{1,0:T(8,128)(2,1)S(1)}, bf16[1024,2048]{1,0:T(8,128)(2,1)}, u32[]{:S(2)}) copy-start(bf16[1024,2048]{1,0:T(8,128)(2,1)} %constant_dynamic-update-slice_fusion.1) | copy-start | bytes 12582916
  369.1 11.2 %copy-start.31 = (bf16[1024,1536]{1,0:T(8,128)(2,1)S(1)}, bf16[1024,1536]{1,0:T(8,128)(2,1)}, u32[]{:S(2)}) copy-start(bf16[1024,1536]{1,0:T(8,128)(2,1)} %get-tuple-element.143) | copy-start | bytes 9437188
  419.0 84.9 %copy-start.27 = (bf16[512,2048]{1,0:T(8,128)(2,1)S(1)}, bf16[512,2048]{1,0:T(8,128)(2,1)}, u32[]{:S(2)}) copy-start(bf16[512,2048]{1,0:T(8,128)(2,1)} %get-tuple-element.76) | copy-start | bytes 6291460
  503.9 9.2 %copy-start.28 = (bf16[512,1536]{1,0:T(8,128)(2,1)S(1)}, bf16[512,1536]{1,0:T(8,128)(2,1)}, u32[]{:S(2)}) copy-start(bf16[512,1536]{1,0:T(8,128)(2,1)} %get-tuple-element.88) | copy-start | bytes 4718596
  510.1 53.3 %collective-permute-start.15 = (bf16[512,768]{1,0:T(8,128)(2,1)S(1)}, bf16[512,768]{1,0:T(8,128)(2,1)S(1)}, u32[]{:S(2)}, u32[]{:S(2)}) collective-permute-start(bf16[512,768]{1,0:T(8,128)(2,1)S(1)} %slice.104), channel_id=1, source_target_pairs={{0,8},{4,12},{8,0},{12,4},{1,9},{5,13},{9,1},{13,5},{2,10},{6,14},... | collective-permute-start | bytes 2359304 | tf_op jit(solution)/shard_map/ppermute | solution.py:34
  510.9 69.2 %collective-permute-start.14 = (bf16[768,512]{1,0:T(8,128)(2,1)S(1)}, bf16[768,512]{1,0:T(8,128)(2,1)S(1)}, u32[]{:S(2)}, u32[]{:S(2)}) collective-permute-start(bf16[768,512]{1,0:T(8,128)(2,1)S(1)} %slice.103), channel_id=1, source_target_pairs={{0,8},{4,12},{8,0},{12,4},{1,9},{5,13},{9,1},{13,5},{2,10},{6,14},... | collective-permute-start | bytes 2359304 | tf_op jit(solution)/shard_map/ppermute | solution.py:34
  513.1 35.5 %collective-permute-start.13 = (bf16[512,1536]{1,0:T(8,128)(2,1)S(1)}, bf16[512,1536]{1,0:T(8,128)(2,1)S(1)}, u32[]{:S(2)}, u32[]{:S(2)}) collective-permute-start(bf16[512,1536]{1,0:T(8,128)(2,1)S(1)} %copy-done.28), channel_id=1, source_target_pairs={{0,16},{16,0},{1,17},{17,1},{2,18},{18,2},{3,19},{19,3},{4,20},{20... | collective-permute-start | bytes 4718600 | tf_op jit(solution)/shard_map/ppermute | solution.py:34
  513.5 24.3 %copy-start.30 = (bf16[1024,512]{1,0:T(8,128)(2,1)S(1)}, bf16[1024,512]{1,0:T(8,128)(2,1)}, u32[]{:S(2)}) copy-start(bf16[1024,512]{1,0:T(8,128)(2,1)} %get-tuple-element.75) | copy-start | bytes 3145732
  548.6 117.2 %copy-start.8 = (bf16[512,1536]{1,0:T(8,128)(2,1)}, bf16[512,1536]{1,0:T(8,128)(2,1)S(1)}, u32[]{:S(2)}) copy-start(bf16[512,1536]{1,0:T(8,128)(2,1)S(1)} %collective-permute-done.13.up_x_ref) | copy-start | bytes 4718596
  563.4 16.8 %copy-start.16 = (bf16[512,768]{1,0:T(8,128)(2,1)}, bf16[512,768]{1,0:T(8,128)(2,1)S(1)}, u32[]{:S(2)}) copy-start(bf16[512,768]{1,0:T(8,128)(2,1)S(1)} %collective-permute-done.15.gate_far_ref) | copy-start | bytes 2359300
  683.0 15.4 %collective-permute-start.16 = (bf16[1024,1280]{1,0:T(8,128)(2,1)S(1)}, bf16[1024,1280]{1,0:T(8,128)(2,1)S(1)}, u32[]{:S(2)}, u32[]{:S(2)}) collective-permute-start(bf16[1024,1280]{1,0:T(8,128)(2,1)S(1)} %slice.128), channel_id=1, source_target_pairs={{0,1},{1,0},{2,3},{3,2},{4,5},{5,4},{6,7},{7,6},{8,9},{9,8},{10,11... | collective-permute-start | bytes 7864328 | tf_op jit(solution)/shard_map/ppermute | solution.py:34
  (19 other events, 80.6 us)

commit v10 on v9

--- a/solution.py
+++ b/solution.py
@@ -858,11 +858,11 @@
 
 
 def turn_kernel(
-    partial_ref, middle_ref, upstream_ref, gain_ref, down_ref, gate_ref, inputs_ref, grads_ref,
+    partial_ref, middle_ref, upstream_ref, gain_ref, down_ref, inputs_ref, gate_ref, up_ref,
     grad_ref, all_ref, term_ref, down_out, gate_out, up_keep, up_send,
     first, second, sums, last, total, low, *rest, sizes,
 ):
-    buffers, (rows_two, up_grads, up_other), (send, recv, local) = rest[:-6], rest[-6:-3], rest[-3:]
+    buffers, (rows_two, gate_grads, up_grads, gate_other, up_other), (send, recv, local) = rest[:-8], rest[-8:-3], rest[-3:]
     net = Wires(send, recv, local, sizes)
     net.greet([Y, CORE, NEAR, FAR, X])
     scatter = scatter_flow(net, partial_ref, first, second, sums, last, total)
@@ -870,10 +870,27 @@
     step, across = low.shape[1] // sizes["narrow"] // 2, gate_ref.shape[1] // 2
     down, gate, up = (Gradient(net, axis, step, across) for axis in (1, 0, 0))
     down.start(down_ref, *buffers[0:2])
-    gate.start(gate_ref, *buffers[3:5])
+    gate.acc, gate.from_core = buffers[3:5]
     up.acc, up.from_core = buffers[6:8]
-    loads = [net.copy(inputs_ref, rows_two), net.copy(grads_ref.at[:, pl.ds(2 * across, 2 * across)], up_grads)]
+    loads = [net.copy(inputs_ref, rows_two), net.copy(gate_ref, gate_grads), net.copy(up_ref, up_grads)]
+    for copy in loads:
+        copy.wait()
+    net.local = [copy for copy in net.local if all(copy is not other for other in loads)]
+    half = rows_two.shape[1] // 2
+
+    def dots(base, grads, target):
+        def body(i, _):
+            at = pl.multiple_of(i * step, step)
+            part = dot_inner(rows_two[:, pl.ds(pl.multiple_of(base + at, step), step)], grads[...])
+            target[pl.ds(at, step), :] = part.astype(BF16)
+            return 0
+
+        lax.fori_loop(0, half // step, body, 0)
+
+    dots(half, gate_grads, gate_other)
+    gate.loaded, gate.core = None, net.send(gate_other, gate.from_core, CORE)
     down.core_to_x(buffers[2])
+    dots(0, gate_grads, gate.acc)
     gate.core_to_x(buffers[5])
     run(scatter)
     run(scatter)
@@ -891,28 +908,14 @@
     by_rows(low.shape[0], rows)
     gather = gather_flow(net, low, all_ref)
     run(gather)
-    for copy in loads:
-        copy.wait()
-    net.local = [copy for copy in net.local if all(copy is not other for other in loads)]
-    half = rows_two.shape[1] // 2
-
-    def up_dots(base, target):
-        def body(i, _):
-            at = pl.multiple_of(i * step, step)
-            part = dot_inner(rows_two[:, pl.ds(pl.multiple_of(base + at, step), step)], up_grads[...])
-            target[pl.ds(at, step), :] = part.astype(BF16)
-            return 0
-
-        lax.fori_loop(0, half // step, body, 0)
-
-    up_dots(half, up_other)
+    dots(half, up_grads, up_other)
     up.loaded, up.core = None, net.send(up_other, up.from_core, CORE)
     for k in range(2):
         down.x_end(k)
         net.copy(down.acc.at[down.slot(k, 2, 0, 2 * across)], down_out.at[down.slot(k, 1, 0, 2 * across)])
     run(gather)
     run(gather)
-    up_dots(0, up.acc)
+    dots(0, up_grads, up.acc)
     up.wait_core()
     for slot in range(2):
         for j, ref in ((1, up_send), (0, up_keep)):
@@ -936,7 +939,7 @@
     return [buffer(BF16), buffer(BF16), buffer(BF16), buffer(BF16), buffer(F32)]
 
 
-def turn(partial, middle, upstream, gain, down, gate, inputs, grads, sizes):
+def turn(partial, middle, upstream, gain, down, inputs, gate, up, sizes):
     rows, width = middle.shape
     size, across = width // sizes["narrow"], down.shape[0] // 2
     return wire_call(
@@ -948,10 +951,10 @@
         [
             *scatter_buffers(rows, width), pltpu.VMEM((rows, width), BF16),
             *gradient_buffers(size, across, 1, 3), *gradient_buffers(size, across, 0, 3), *gradient_buffers(size, across, 0, 2),
-            pltpu.VMEM(inputs.shape, BF16), pltpu.VMEM((inputs.shape[0], 2 * across), BF16), pltpu.VMEM((2 * size, 2 * across), BF16),
+            pltpu.VMEM(inputs.shape, BF16), *(pltpu.VMEM((n, 2 * across), BF16) for n in (gate.shape[0],) * 2 + (2 * size,) * 2),
             *sems(40, 24),
         ],
-        sizes, 80, partial, middle, upstream, gain[None], down, gate, inputs, grads,
+        sizes, 80, partial, middle, upstream, gain[None], down, inputs, gate, up,
     )
 
 
@@ -1048,7 +1051,7 @@
     )
 
 
-SUMS = [CORE, Y, NEAR, X, FAR]
+SUMS = [CORE, Y, X, NEAR, FAR]
 
 
 def end_kernel(
@@ -1131,10 +1134,9 @@
     out.x_end(0, buffers[6])
     out.x_end(1, buffers[6])
     run(gains)
+    spread_flow(net, rows_low, tokens_ref)
     own(qkv, 0, qkv_out)
     own_up(0)
-    run(gains)
-    spread_flow(net, rows_low, tokens_ref)
     run(gains)
     own(qkv, 1, qkv_out)
     own_up(1)
@@ -1144,6 +1146,7 @@
     up.after_y()
     qkv.after_y()
     out.after_y()
+    run(gains)
     run(gains)
     net.finish()
 
@@ -1299,14 +1302,14 @@
         hidden_grad = dot_trans(upstream_all, down)
         gate_grad = hidden_grad * up_pre * gate_sigmoid * (1.0 + gate_pre * (1.0 - gate_sigmoid))
         up_grad = hidden_grad * silu
-        gate_up_low = join([gate_grad, up_grad], 1).astype(BF16)
+        gate_low, up_low = gate_grad.astype(BF16), up_grad.astype(BF16)
+        gate_up_low = join([gate_low, up_low], 1)
         partial = dot_trans(gate_up_low, gate_up).astype(BF16)
         down_sums = dot_inner(hidden, upstream_all).astype(BF16)
-        gate_sums = dot_inner(normed_two_all, gate_up_low[:, :hidden_cols]).astype(BF16)
         mlp_partial = dot_rows(hidden, down).astype(BF16)
         partial = after(partial, mlp_partial)
         middle_grad, middle_all, two_term, down_part, gate_part, up_keep, up_send = turn(
-            partial, middle, upstream, gain_two, down_sums, gate_sums, normed_two_all, gate_up_low, sizes
+            partial, middle, upstream, gain_two, down_sums, normed_two_all, gate_low, up_low, sizes
         )
         down_far = over_far(down_part[hidden_cols // 2 :])
         gate_far = over_far(gate_part[:, hidden_cols // 2 :])

time: 852 us -> 881 us (1.034)
  waiting for transfers between devices: 79.1 us -> 108 us
    ppermute x17, waiting for transfers between devices: 79.1 us -> 108 us  [exchange(): return lax.ppermute(values, axis, [(i, i ^ distance) for i in range(size)])]
    dot_general x4 -> x3, matrix products: 31.6 us -> 27 us  [dot_inner(): lax.dot_general(left, right, (((0,), (0,)), ((), ())), preferred_element_...]
  transfers between devices with their start and end apart: 17 -> 17, of which waited for: 8 -> 10; matrix products, arithmetic and copies ran while one was open for 8% -> 8% of each run, Pallas kernels for 16% -> 15%
where the time goes in v10:
time: 881 us; the launch traced here: 873 us
  Pallas kernels  567 us (64%)
  matrix products  120 us (14%)
  waiting for transfers between devices  108 us (12%)
  local copies, waits for them, and re-layouts  29.8 us (3%)
  starting transfers between devices  24.1 us (3%)
  other arithmetic  21.9 us (2%)
    pallas_call x6, Pallas kernels, wire_call(): pl.pallas_call(functools.partial(kernel, sizes=sizes), in_specs=specs, ou...  512 us
    ppermute x17, waiting for transfers between devices, exchange(): return lax.ppermute(values, axis, [(i, i ^ distance) for i in range(size)])  108 us
    dot_general x4, matrix products, dot_rows(): return jnp.dot(left, right, preferred_element_type=F32)  47.1 us
    dot_general x4, matrix products, dot_trans(): lax.dot_general(left, right, (((1,), (1,)), ((), ())), preferred_element_...  46.1 us
    dot_general x3, matrix products, dot_inner(): lax.dot_general(left, right, (((0,), (0,)), ((), ())), preferred_element_...  27 us
    pallas_call x1, Pallas kernels, attend_back(): pl.pallas_call(functools.partial(backward_kernel, pairs=pairs, repeat=hea...  24.5 us
    ppermute x17, starting transfers between devices, exchange(): return lax.ppermute(values, axis, [(i, i ^ distance) for i in range(size)])  24.1 us
  transfers between devices with their start and end apart: 17, of which 10 were waited for; matrix products, arithmetic and copies ran while one was open for 8% of the time, Pallas kernels for 15%

profile of v10, /device:TPU:0, one launch (start us, length us, event | category | flops | bytes accessed | tf_op | source)
XLA Modules:
  0.0 872.8 jit_solution(2189005142653674139)
XLA Ops:
  5.0 75.2 %begin.1 = (bf16[256,2048]{1,0:T(8,128)(2,1)}, bf16[256,2048]{1,0:T(8,128)(2,1)}, bf16[1024,2048]{1,0:T(8,128)(2,1)}, bf16[2048,1280]{1,0:T(8,128)(2,1)}, bf16[512,2048]{1,0:T(8,128)(2,1)}) custom-call(bf16[1024,512]{1,0:T(8,128)(2,1)} %tokens_ref.1, bf16[1024,512]{1,0:T(8,128)(2,1)} %cotangent_ref.1, f32[1,2048]{1,0:T(1,128)} %broadcast_in_dim_reshape.8.gain_ref, ...), custom_call_target="tpu_custom_call" | custom-call | bytes 165000000 | tf_op jit(solution)/shard_map/begin/pallas_call | solution.py:592
  83.0 5.1 collective-permute-start.7
  95.5 10.4 %fusion.74.raw_ref.own_ref.other_ref = f32[1024,1280]{1,0:T(8,128)} fusion(bf16[1024,2048]{1,0:T(8,128)(2,1)} %get-tuple-element.62, bf16[2048,1280]{1,0:T(8,128)(2,1)} %get-tuple-element.63), kind=kOutput, calls=%fused_computation.178 | convolution fusion | flops 5368709120 | bytes 14680064 | tf_op jit(solution)/shard_map/dot_general | solution.py:22
  112.2 6.3 post.1
  118.6 2.9 collective-permute-start.4
  122.7 2.5 collective-permute-start.5
  127.1 27.5 %collective-permute-done.3.gate_far_ref = bf16[256,768]{1,0:T(8,128)(2,1)S(1)} collective-permute-done((bf16[256,768]{1,0:T(8,128)(2,1)S(1)}, bf16[256,768]{1,0:T(8,128)(2,1)S(1)}, u32[]{:S(2)}, u32[]{:S(2)}) %collective-permute-start.3) | collective-permute-done | bytes 393248 | tf_op jit(solution)/shard_map/ppermute | solution.py:34
  154.6 8.4 collective-permute-done.4.up_far_ref
  163.0 8.3 collective-permute-done.5.down_far_ref
  171.4 51.6 %keys.1.kv_ref = bf16[4096,512]{1,0:T(8,128)(2,1)} custom-call(bf16[1024,512]{1,0:T(8,128)(2,1)} %get-tuple-element.70.kv_ref), custom_call_target="tpu_custom_call" | custom-call | bytes 135000000 | tf_op jit(solution)/shard_map/keys/pallas_call | solution.py:592
  231.9 15.3 %attend.1 = (bf16[1024,512]{1,0:T(8,128)(2,1)}, f32[1024,512]{1,0:T(8,128)}, f32[1024,512]{1,0:T(8,128)}) custom-call(s32[4,5]{1,0:T(4,128)} %select_select_fusion.table_ref, bf16[1024,512]{1,0:T(8,128)(2,1)} %get-tuple-element.64.q_ref, bf16[4096,512]{1,0:T(8,128)(2,1)} %keys.1.kv_ref, s32[1024,1]{1,0:T(8,128)} %get-tuple-element.171.row_ref, ...), custom_call_target="tpu_custom_call" | custom-call | flops 20000000000 | bytes 12000000 | tf_op jit(solution)/shard_map/attend/pallas_call | solution.py:244
  249.1 6.2 convolution_convert_fusion.4.partial_ref
  255.4 4.1 collective-permute-done.12.down_both_ref
  259.5 8.4 collective-permute-done.11.up_both_ref
  267.9 13.2 %collective-permute-done.10.gate_both_ref = bf16[256,768]{1,0:T(8,128)(2,1)S(1)} collective-permute-done((bf16[256,768]{1,0:T(8,128)(2,1)S(1)}, bf16[256,768]{1,0:T(8,128)(2,1)S(1)}, u32[]{:S(2)}, u32[]{:S(2)}) %collective-permute-start.10) | collective-permute-done | bytes 393248 | tf_op jit(solution)/shard_map/ppermute | solution.py:34
  281.9 87.0 %middle.1 = (f32[256,2048]{1,0:T(8,128)}, bf16[1024,2048]{1,0:T(8,128)(2,1)}, bf16[2048,3072]{1,0:T(8,128)(2,1)}, bf16[1536,2048]{1,0:T(8,128)(2,1)}) custom-call(bf16[1024,2048]{1,0:T(8,128)(2,1)} %convolution_convert_fusion.4.partial_ref, bf16[256,2048]{1,0:T(8,128)(2,1)} %get-tuple-element.77.x_ref, f32[1,2048]{1,0:T(1,128)} %broadcast_in_dim_reshape.9.gain_ref, ...), custom_call_target="tpu_custom_call" | custom-call | bytes 240000000 | tf_op jit(solution)/shard_map/middle/pallas_call | solution.py:592
  368.9 19.3 %fusion.75 = f32[1024,3072]{1,0:T(8,128)} fusion(bf16[1024,2048]{1,0:T(8,128)(2,1)} %get-tuple-element.82.inputs_ref, bf16[2048,3072]{1,0:T(8,128)(2,1)} %get-tuple-element.83), kind=kOutput, calls=%fused_computation.179 | convolution fusion | flops 12884901888 | bytes 29360128 | tf_op jit(solution)/shard_map/dot_general | solution.py:22
  389.5 15.2 %multiply_convert_fusion.2 = (bf16[1024,1536]{1,0:T(8,128)(2,1)S(1)}, bf16[1024,1536]{1,0:T(8,128)(2,1)S(1)}, bf16[1024,1536]{1,0:T(8,128)(2,1)}) fusion(f32[1024,3072]{1,0:T(8,128)} %fusion.75, bf16[1024,2048]{1,0:T(8,128)(2,1)S(1)} %slice_dynamic-update-slice_fusion, bf16[1536,2048]{1,0:T(8,128)(2,1)} %get-tuple-element.81), kind=kOutput, calls=%fused_computation.8 | convolution fusion | flops 6466043904 | bytes 32505856 | tf_op jit(solution)/shard_map/dot_general | solution.py:26
  404.7 12.9 %convolution_convert_fusion.1.down_ref = bf16[1536,2048]{1,0:T(8,128)(2,1)} fusion(bf16[1024,1536]{1,0:T(8,128)(2,1)} %get-tuple-element.143, bf16[1024,2048]{1,0:T(8,128)(2,1)S(1)} %slice_dynamic-update-slice_fusion), kind=kOutput, calls=%fused_computation.1 | convolution fusion | flops 6445596672 | bytes 13631488 | tf_op jit(solution)/shard_map/dot_general | solution.py:30
  417.5 11.2 %convolution_convert_fusion.2.partial_ref = bf16[1024,2048]{1,0:T(8,128)(2,1)} fusion(bf16[1024,1536]{1,0:T(8,128)(2,1)S(1)} %copy-done.38, bf16[1536,2048]{1,0:T(8,128)(2,1)} %get-tuple-element.81), kind=kOutput, calls=%fused_computation.11 | convolution fusion | flops 6444548096 | bytes 13631488 | tf_op jit(solution)/shard_map/dot_general | solution.py:22
  428.7 17.7 %fusion.5.partial_ref = bf16[1024,2048]{1,0:T(8,128)(2,1)} fusion(bf16[2048,3072]{1,0:T(8,128)(2,1)} %get-tuple-element.83, bf16[1024,1536]{1,0:T(8,128)(2,1)S(1)} %get-tuple-element.142.up_ref, bf16[1024,1536]{1,0:T(8,128)(2,1)S(1)} %get-tuple-element.141.gate_ref), kind=kOutput, calls=%fused_computation.12 | convolution fusion | flops 12899581952 | bytes 23068672 | tf_op jit(solution)/shard_map/dot_general | solution.py:26
  446.4 87.7 %turn.1 = (f32[256,2048]{1,0:T(8,128)}, bf16[1024,2048]{1,0:T(8,128)(2,1)}, f32[1,2048]{1,0:T(1,128)}, bf16[1536,512]{1,0:T(8,128)(2,1)}, bf16[512,1536]{1,0:T(8...) custom-call(bf16[1024,2048]{1,0:T(8,128)(2,1)} %fusion.5.partial_ref, ...), custom_call_target="tpu_custom_call" | custom-call | bytes 240000000 | tf_op jit(solution)/shard_map/turn/pallas_call | solution.py:592
  534.2 6.0 fusion.76.grad_ref
  544.5 24.5 %attend_back.1 = (f32[1024,512]{1,0:T(8,128)}, bf16[4096,512]{1,0:T(8,128)(2,1)}, f32[1024,256]{1,0:T(8,128)}) custom-call(s32[4,5]{1,0:T(4,128)} %select_select_fusion.table_ref, bf16[1024,512]{1,0:T(8,128)(2,1)} %get-tuple-element.64.q_ref, bf16[4096,512]{1,0:T(8,128)(2,1)} %keys.1.kv_ref, s32[4,1,256]{2,1,0:T(1,128)} %get-tuple-element.174.row_ref, ...), custom_call_target="tpu_custom_call" | custom-call | flops 49999998976 | bytes 20000000 | tf_op jit(solution)/shard_map/attend_back/pallas_call | solution.py:346
  569.0 5.9 convolution_convert_fusion.5.out_ref
  576.1 18.8 %collective-permute-done.14.down_far_ref = bf16[768,512]{1,0:T(8,128)(2,1)S(1)} collective-permute-done((bf16[768,512]{1,0:T(8,128)(2,1)S(1)}, bf16[768,512]{1,0:T(8,128)(2,1)S(1)}, u32[]{:S(2)}, u32[]{:S(2)}) %collective-permute-start.14) | collective-permute-done | bytes 786464 | tf_op jit(solution)/shard_map/ppermute | solution.py:34
  594.9 16.7 %collective-permute-done.15.gate_far_ref = bf16[512,768]{1,0:T(8,128)(2,1)S(1)} collective-permute-done((bf16[512,768]{1,0:T(8,128)(2,1)S(1)}, bf16[512,768]{1,0:T(8,128)(2,1)S(1)}, u32[]{:S(2)}, u32[]{:S(2)}) %collective-permute-start.15) | collective-permute-done | bytes 786464 | tf_op jit(solution)/shard_map/ppermute | solution.py:34
  612.5 83.7 %owner.1 = (f32[1024,512]{1,0:T(8,128)}, bf16[1024,512]{1,0:T(8,128)(2,1)}, bf16[1536,512]{1,0:T(8,128)(2,1)}, bf16[512,1536]{1,0:T(8,128)(2,1)}) custom-call(bf16[4096,512]{1,0:T(8,128)(2,1)} %get-tuple-element.89.dkv_ref, bf16[1024,2048]{1,0:T(8,128)(2,1)} %convolution_convert_fusion.2.partial_ref, f32[256,2048]{1,0:T(8,128)} %get-tuple-element.85.middle_ref, ...), custom_call_target="tpu_custom_call" | custom-call | bytes 240000000 | tf_op jit(solution)/shard_map/owner/pallas_call | solution.py:592
  696.2 8.7 project_back.1
  704.9 8.3 convolution_convert_fusion.qkv_ref
  721.6 7.2 convolution_convert_fusion.3.partial_ref
  730.3 127.2 %end.1 = (bf16[1024,512]{1,0:T(8,128)(2,1)}, f32[1,4352]{1,0:T(1,128)}, bf16[512,1280]{1,0:T(8,128)(2,1)}, bf16[512,512]{1,0:T(8,128)(2,1)}, bf16[512,1536]{1,0:T(8,128)(2,1)}) custom-call(bf16[1024,2048]{1,0:T(8,128)(2,1)} %convolution_convert_fusion.3.partial_ref, bf16[256,2048]{1,0:T(8,128)(2,1)} %get-tuple-element.77.x_ref, ...), custom_call_target="tpu_custom_call" | custom-call | bytes 270000000 | tf_op jit(solution)/shard_map/end/pallas_call | solution.py:592
  (173 shorter events, 67.6 us)
Async XLA Ops:
  0.6 87.5 %copy-start.4 = (bf16[512,1536]{1,0:T(8,128)(2,1)S(1)}, bf16[512,1536]{1,0:T(8,128)(2,1)}, u32[]{:S(2)}) copy-start(bf16[512,1536]{1,0:T(8,128)(2,1)} %gate_ref.1) | copy-start | bytes 4718596
  4.1 85.6 %copy-start.5 = (bf16[512,1536]{1,0:T(8,128)(2,1)S(1)}, bf16[512,1536]{1,0:T(8,128)(2,1)}, u32[]{:S(2)}) copy-start(bf16[512,1536]{1,0:T(8,128)(2,1)} %up_ref.1) | copy-start | bytes 4718596
  82.5 88.9 %collective-permute-start.6 = (bf16[128,2048]{1,0:T(8,128)(2,1)}, bf16[128,2048]{1,0:T(8,128)(2,1)}, u32[]{:S(2)}, u32[]{:S(2)}) collective-permute-start(bf16[128,2048]{1,0:T(8,128)(2,1)} %get-tuple-element.159), channel_id=1, source_target_pairs={{0,2},{1,3},{2,0},{3,1},{4,6},{5,7},{6,4},{7,5},{8,10},{9,11},{10,... | collective-permute-start | bytes 1572872 | tf_op jit(solution)/shard_map/ppermute | solution.py:34
  83.0 88.4 %collective-permute-start.7 = (bf16[128,2048]{1,0:T(8,128)(2,1)}, bf16[128,2048]{1,0:T(8,128)(2,1)}, u32[]{:S(2)}, u32[]{:S(2)}) collective-permute-start(bf16[128,2048]{1,0:T(8,128)(2,1)} %get-tuple-element.158), channel_id=1, source_target_pairs={{0,4},{4,0},{8,12},{12,8},{1,5},{5,1},{9,13},{13,9},{2,6},{6,2},{1... | collective-permute-start | bytes 1572872 | tf_op jit(solution)/shard_map/ppermute | solution.py:34
  89.3 29.3 %collective-permute-start = (bf16[256,768]{1,0:T(8,128)(2,1)}, bf16[256,768]{1,0:T(8,128)(2,1)S(1)}, u32[]{:S(2)}, u32[]{:S(2)}) collective-permute-start(bf16[256,768]{1,0:T(8,128)(2,1)} %get-tuple-element.149), channel_id=1, source_target_pairs={{0,2},{1,3},{2,0},{3,1},{4,6},{5,7},{6,4},{7,5},{8,10},{9,11},{10,... | collective-permute-start | bytes 1179656 | tf_op jit(solution)/shard_map/ppermute | solution.py:34
  91.0 27.6 %collective-permute-start.1 = (bf16[256,768]{1,0:T(8,128)(2,1)}, bf16[256,768]{1,0:T(8,128)(2,1)S(1)}, u32[]{:S(2)}, u32[]{:S(2)}) collective-permute-start(bf16[256,768]{1,0:T(8,128)(2,1)} %get-tuple-element.147), channel_id=1, source_target_pairs={{0,2},{1,3},{2,0},{3,1},{4,6},{5,7},{6,4},{7,5},{8,10},{9,11},{10,... | collective-permute-start | bytes 1179656 | tf_op jit(solution)/shard_map/ppermute | solution.py:34
  95.1 27.7 %collective-permute-start.2 = (bf16[768,256]{1,0:T(8,128)(2,1)S(1)}, bf16[768,256]{1,0:T(8,128)(2,1)S(1)}, u32[]{:S(2)}, u32[]{:S(2)}) collective-permute-start(bf16[768,256]{1,0:T(8,128)(2,1)S(1)} %get-tuple-element.145), channel_id=1, source_target_pairs={{0,2},{1,3},{2,0},{3,1},{4,6},{5,7},{6,4},{7,5},{8,10},{9,11},{10,... | collective-permute-start | bytes 1179656 | tf_op jit(solution)/shard_map/ppermute | solution.py:34
  118.5 111.9 %copy-start.21 = (bf16[256,768]{1,0:T(8,128)(2,1)}, bf16[256,768]{1,0:T(8,128)(2,1)S(1)}, u32[]{:S(2)}) copy-start(bf16[256,768]{1,0:T(8,128)(2,1)S(1)} %collective-permute-done.gate_y_ref) | copy-start | bytes 1179652
  118.5 36.1 %collective-permute-start.3 = (bf16[256,768]{1,0:T(8,128)(2,1)S(1)}, bf16[256,768]{1,0:T(8,128)(2,1)S(1)}, u32[]{:S(2)}, u32[]{:S(2)}) collective-permute-start(bf16[256,768]{1,0:T(8,128)(2,1)S(1)} %get-tuple-element.148), channel_id=1, source_target_pairs={{0,8},{4,12},{8,0},{12,4},{1,9},{5,13},{9,1},{13,5},{2,10},{6,14},... | collective-permute-start | bytes 1179656 | tf_op jit(solution)/shard_map/ppermute | solution.py:34
  118.6 110.3 %copy-start.22 = (bf16[256,768]{1,0:T(8,128)(2,1)}, bf16[256,768]{1,0:T(8,128)(2,1)S(1)}, u32[]{:S(2)}) copy-start(bf16[256,768]{1,0:T(8,128)(2,1)S(1)} %collective-permute-done.1.up_y_ref) | copy-start | bytes 1179652
  118.6 44.4 %collective-permute-start.4 = (bf16[256,768]{1,0:T(8,128)(2,1)S(1)}, bf16[256,768]{1,0:T(8,128)(2,1)S(1)}, u32[]{:S(2)}, u32[]{:S(2)}) collective-permute-start(bf16[256,768]{1,0:T(8,128)(2,1)S(1)} %copy-done.30), channel_id=1, source_target_pairs={{0,8},{4,12},{8,0},{12,4},{1,9},{5,13},{9,1},{13,5},{2,10},{6,14},... | collective-permute-start | bytes 1179656 | tf_op jit(solution)/shard_map/ppermute | solution.py:34
  122.7 104.7 %copy-start.23 = (bf16[768,256]{1,0:T(8,128)(2,1)}, bf16[768,256]{1,0:T(8,128)(2,1)S(1)}, u32[]{:S(2)}) copy-start(bf16[768,256]{1,0:T(8,128)(2,1)S(1)} %collective-permute-done.2.down_y_ref) | copy-start | bytes 1179652
  122.7 48.6 %collective-permute-start.5 = (bf16[768,256]{1,0:T(8,128)(2,1)}, bf16[768,256]{1,0:T(8,128)(2,1)S(1)}, u32[]{:S(2)}, u32[]{:S(2)}) collective-permute-start(bf16[768,256]{1,0:T(8,128)(2,1)} %get-tuple-element.144), channel_id=1, source_target_pairs={{0,8},{4,12},{8,0},{12,4},{1,9},{5,13},{9,1},{13,5},{2,10},{6,14},... | collective-permute-start | bytes 1179656 | tf_op jit(solution)/shard_map/ppermute | solution.py:34
  154.6 72.2 %copy-start.24 = (bf16[256,768]{1,0:T(8,128)(2,1)}, bf16[256,768]{1,0:T(8,128)(2,1)S(1)}, u32[]{:S(2)}) copy-start(bf16[256,768]{1,0:T(8,128)(2,1)S(1)} %collective-permute-done.3.gate_far_ref) | copy-start | bytes 1179652
  163.0 63.8 %copy-start.25 = (bf16[256,768]{1,0:T(8,128)(2,1)}, bf16[256,768]{1,0:T(8,128)(2,1)S(1)}, u32[]{:S(2)}) copy-start(bf16[256,768]{1,0:T(8,128)(2,1)S(1)} %collective-permute-done.4.up_far_ref) | copy-start | bytes 1179652
  171.4 55.5 %copy-start.26 = (bf16[768,256]{1,0:T(8,128)(2,1)}, bf16[768,256]{1,0:T(8,128)(2,1)S(1)}, u32[]{:S(2)}) copy-start(bf16[768,256]{1,0:T(8,128)(2,1)S(1)} %collective-permute-done.5.down_far_ref) | copy-start | bytes 1179652
  224.3 163.9 %collective-permute-start.8 = (bf16[256,2048]{1,0:T(8,128)(2,1)S(1)}, bf16[256,2048]{1,0:T(8,128)(2,1)S(1)}, u32[]{:S(2)}, u32[]{:S(2)}) collective-permute-start(bf16[256,2048]{1,0:T(8,128)(2,1)S(1)} %pad_maximum_fusion), channel_id=1, source_target_pairs={{0,2},{1,3},{2,0},{3,1},{4,6},{5,7},{6,4},{7,5},{8,10},{9,11},{10,... | collective-permute-start | bytes 3145736 | tf_op jit(solution)/shard_map/ppermute | solution.py:34
  226.8 161.4 %collective-permute-start.9 = (bf16[256,2048]{1,0:T(8,128)(2,1)S(1)}, bf16[256,2048]{1,0:T(8,128)(2,1)S(1)}, u32[]{:S(2)}, u32[]{:S(2)}) collective-permute-start(bf16[256,2048]{1,0:T(8,128)(2,1)S(1)} %pad_maximum_fusion.1), channel_id=1, source_target_pairs={{0,4},{4,0},{8,12},{12,8},{1,5},{5,1},{9,13},{13,9},{2,6},{6,2},{1... | collective-permute-start | bytes 3145736 | tf_op jit(solution)/shard_map/ppermute | solution.py:34
  227.5 32.0 %collective-permute-start.12 = (bf16[768,256]{1,0:T(8,128)(2,1)S(1)}, bf16[768,256]{1,0:T(8,128)(2,1)S(1)}, u32[]{:S(2)}, u32[]{:S(2)}) collective-permute-start(bf16[768,256]{1,0:T(8,128)(2,1)S(1)} %collective-permute-done.2.down_y_ref), channel_id=1, source_target_pairs={{0,8},{4,12},{8,0},{12,4},{1,9},{5,13},{9,1},{13,5},{2,10},{6,14},... | collective-permute-start | bytes 1179656 | tf_op jit(solution)/shard_map/ppermute | solution.py:34
  229.0 38.9 %collective-permute-start.11 = (bf16[256,768]{1,0:T(8,128)(2,1)S(1)}, bf16[256,768]{1,0:T(8,128)(2,1)S(1)}, u32[]{:S(2)}, u32[]{:S(2)}) collective-permute-start(bf16[256,768]{1,0:T(8,128)(2,1)S(1)} %collective-permute-done.1.up_y_ref), channel_id=1, source_target_pairs={{0,8},{4,12},{8,0},{12,4},{1,9},{5,13},{9,1},{13,5},{2,10},{6,14},... | collective-permute-start | bytes 1179656 | tf_op jit(solution)/shard_map/ppermute | solution.py:34
  230.4 50.7 %collective-permute-start.10 = (bf16[256,768]{1,0:T(8,128)(2,1)S(1)}, bf16[256,768]{1,0:T(8,128)(2,1)S(1)}, u32[]{:S(2)}, u32[]{:S(2)}) collective-permute-start(bf16[256,768]{1,0:T(8,128)(2,1)S(1)} %collective-permute-done.gate_y_ref), channel_id=1, source_target_pairs={{0,8},{4,12},{8,0},{12,4},{1,9},{5,13},{9,1},{13,5},{2,10},{6,14},... | collective-permute-start | bytes 1179656 | tf_op jit(solution)/shard_map/ppermute | solution.py:34
  259.5 21.6 %copy-start.27 = (bf16[768,256]{1,0:T(8,128)(2,1)}, bf16[768,256]{1,0:T(8,128)(2,1)S(1)}, u32[]{:S(2)}) copy-start(bf16[768,256]{1,0:T(8,128)(2,1)S(1)} %collective-permute-done.12.down_both_ref) | copy-start | bytes 1179652
  368.9 19.3 %copy-start.31 = (bf16[1024,2048]{1,0:T(8,128)(2,1)S(1)}, bf16[1024,2048]{1,0:T(8,128)(2,1)}, u32[]{:S(2)}) copy-start(bf16[1024,2048]{1,0:T(8,128)(2,1)} %constant_dynamic-update-slice_fusion.1) | copy-start | bytes 12582916
  404.7 24.0 %copy-start.6 = (bf16[1024,1536]{1,0:T(8,128)(2,1)}, bf16[1024,1536]{1,0:T(8,128)(2,1)S(1)}, u32[]{:S(2)}) copy-start(bf16[1024,1536]{1,0:T(8,128)(2,1)S(1)} %get-tuple-element.141.gate_ref) | copy-start | bytes 9437188
  404.7 24.0 %copy-start.7 = (bf16[1024,1536]{1,0:T(8,128)(2,1)}, bf16[1024,1536]{1,0:T(8,128)(2,1)S(1)}, u32[]{:S(2)}) copy-start(bf16[1024,1536]{1,0:T(8,128)(2,1)S(1)} %get-tuple-element.142.up_ref) | copy-start | bytes 9437188
  446.4 87.7 %copy-start.34 = (bf16[512,2048]{1,0:T(8,128)(2,1)S(1)}, bf16[512,2048]{1,0:T(8,128)(2,1)}, u32[]{:S(2)}) copy-start(bf16[512,2048]{1,0:T(8,128)(2,1)} %get-tuple-element.76) | copy-start | bytes 6291460
  540.2 35.9 %collective-permute-start.13 = (bf16[512,1536]{1,0:T(8,128)(2,1)S(1)}, bf16[512,1536]{1,0:T(8,128)(2,1)S(1)}, u32[]{:S(2)}, u32[]{:S(2)}) collective-permute-start(bf16[512,1536]{1,0:T(8,128)(2,1)S(1)} %copy-done.35), channel_id=1, source_target_pairs={{0,16},{16,0},{1,17},{17,1},{2,18},{18,2},{3,19},{19,3},{4,20},{20... | collective-permute-start | bytes 4718600 | tf_op jit(solution)/shard_map/ppermute | solution.py:34
  541.4 53.5 %collective-permute-start.14 = (bf16[768,512]{1,0:T(8,128)(2,1)S(1)}, bf16[768,512]{1,0:T(8,128)(2,1)S(1)}, u32[]{:S(2)}, u32[]{:S(2)}) collective-permute-start(bf16[768,512]{1,0:T(8,128)(2,1)S(1)} %slice.99), channel_id=1, source_target_pairs={{0,8},{4,12},{8,0},{12,4},{1,9},{5,13},{9,1},{13,5},{2,10},{6,14},... | collective-permute-start | bytes 2359304 | tf_op jit(solution)/shard_map/ppermute | solution.py:34
  542.8 68.9 %collective-permute-start.15 = (bf16[512,768]{1,0:T(8,128)(2,1)S(1)}, bf16[512,768]{1,0:T(8,128)(2,1)S(1)}, u32[]{:S(2)}, u32[]{:S(2)}) collective-permute-start(bf16[512,768]{1,0:T(8,128)(2,1)S(1)} %slice.100), channel_id=1, source_target_pairs={{0,8},{4,12},{8,0},{12,4},{1,9},{5,13},{9,1},{13,5},{2,10},{6,14},... | collective-permute-start | bytes 2359304 | tf_op jit(solution)/shard_map/ppermute | solution.py:34
  544.5 24.5 %copy-start.37 = (bf16[1024,512]{1,0:T(8,128)(2,1)S(1)}, bf16[1024,512]{1,0:T(8,128)(2,1)}, u32[]{:S(2)}) copy-start(bf16[1024,512]{1,0:T(8,128)(2,1)} %get-tuple-element.75) | copy-start | bytes 3145732
  576.1 120.2 %copy-start.9 = (bf16[512,1536]{1,0:T(8,128)(2,1)}, bf16[512,1536]{1,0:T(8,128)(2,1)S(1)}, u32[]{:S(2)}) copy-start(bf16[512,1536]{1,0:T(8,128)(2,1)S(1)} %collective-permute-done.13.up_x_ref) | copy-start | bytes 4718596
  713.4 15.4 %collective-permute-start.16 = (bf16[1024,1280]{1,0:T(8,128)(2,1)S(1)}, bf16[1024,1280]{1,0:T(8,128)(2,1)S(1)}, u32[]{:S(2)}, u32[]{:S(2)}) collective-permute-start(bf16[1024,1280]{1,0:T(8,128)(2,1)S(1)} %slice.124), channel_id=1, source_target_pairs={{0,1},{1,0},{2,3},{3,2},{4,5},{5,4},{6,7},{7,6},{8,9},{9,8},{10,11... | collective-permute-start | bytes 7864328 | tf_op jit(solution)/shard_map/ppermute | solution.py:34
  (26 other events, 159.0 us)

commit v11 on v10

--- a/solution.py
+++ b/solution.py
@@ -1270,13 +1270,15 @@
         ).astype(jnp.int32)
 
         raw = dot_rows(normed_all, joined_weight)
-        q, kv = post(raw, cosine, sine, query_gain, key_gain, heads, pairs, size, factor)
         send = after((gate_weight, up_weight, down_weight), normed_all)
         axes = (0, 0, 1)
-        from_y = [over_y(piece_of(w, 1 - y, axis)) for w, axis in zip(send, axes)]
         from_far = [over_far(piece_of(w, y, axis)) for w, axis in zip(send, axes)]
+        from_y = [over_y(piece_of(w, 1 - y, axis)) for w, axis in zip(after(send, raw), axes)]
+        raw = after(raw, from_far[0], from_far[1])
+        q, kv = post(raw, cosine, sine, query_gain, key_gain, heads, pairs, size, factor)
         part = rows_local // 2
-        upstream_y, upstream_z = over_y(upstream[:part]), over_z(upstream[part:])
+        early = after(upstream, raw)
+        upstream_y, upstream_z = over_y(early[:part]), over_z(early[part:])
         kv_all = exchange_keys(after(kv, *from_y, *from_far, upstream_y, upstream_z), sizes)
         from_both = [over_far(after(v, kv_all)) for v in from_y]
 

time: 881 us -> 854 us (0.969)
  waiting for transfers between devices: 108 us -> 83.6 us
    ppermute x17, waiting for transfers between devices: 108 us -> 83.6 us  [exchange(): return lax.ppermute(values, axis, [(i, i ^ distance) for i in range(size)])]
  transfers between devices with their start and end apart: 17 -> 17, of which waited for: 10 -> 9; matrix products, arithmetic and copies ran while one was open for 8% -> 9% of each run, Pallas kernels for 15% -> 16%
where the time goes in v11:
time: 854 us; the launch traced here: 846 us
  Pallas kernels  569 us (67%)
  matrix products  120 us (14%)
  waiting for transfers between devices  83.6 us (10%)
  local copies, waits for them, and re-layouts  31.6 us (4%)
  starting transfers between devices  20.8 us (2%)
  other arithmetic  19.5 us (2%)
    pallas_call x6, Pallas kernels, wire_call(): pl.pallas_call(functools.partial(kernel, sizes=sizes), in_specs=specs, ou...  514 us
    ppermute x17, waiting for transfers between devices, exchange(): return lax.ppermute(values, axis, [(i, i ^ distance) for i in range(size)])  83.6 us
    dot_general x4, matrix products, dot_rows(): return jnp.dot(left, right, preferred_element_type=F32)  47 us
    dot_general x4, matrix products, dot_trans(): lax.dot_general(left, right, (((1,), (1,)), ((), ())), preferred_element_...  46.1 us
    dot_general x3, matrix products, dot_inner(): lax.dot_general(left, right, (((0,), (0,)), ((), ())), preferred_element_...  27 us
    pallas_call x1, Pallas kernels, attend_back(): pl.pallas_call(functools.partial(backward_kernel, pairs=pairs, repeat=hea...  24.5 us
    ppermute x17, starting transfers between devices, exchange(): return lax.ppermute(values, axis, [(i, i ^ distance) for i in range(size)])  20.8 us
  transfers between devices with their start and end apart: 17, of which 9 were waited for; matrix products, arithmetic and copies ran while one was open for 9% of the time, Pallas kernels for 16%

profile of v11, /device:TPU:0, one launch (start us, length us, event | category | flops | bytes accessed | tf_op | source)
XLA Modules:
  0.0 846.1 jit_solution(894425970343032465)
XLA Ops:
  5.0 75.2 %begin.1 = (bf16[256,2048]{1,0:T(8,128)(2,1)}, bf16[256,2048]{1,0:T(8,128)(2,1)}, bf16[1024,2048]{1,0:T(8,128)(2,1)}, bf16[2048,1280]{1,0:T(8,128)(2,1)}, bf16[512,2048]{1,0:T(8,128)(2,1)}) custom-call(bf16[1024,512]{1,0:T(8,128)(2,1)} %tokens_ref.1, bf16[1024,512]{1,0:T(8,128)(2,1)} %cotangent_ref.1, f32[1,2048]{1,0:T(1,128)} %broadcast_in_dim_reshape.8.gain_ref, ...), custom_call_target="tpu_custom_call" | custom-call | bytes 165000000 | tf_op jit(solution)/shard_map/begin/pallas_call | solution.py:592
  81.2 3.4 collective-permute-start
  86.6 10.5 %fusion.72.raw_ref.own_ref.other_ref = f32[1024,1280]{1,0:T(8,128)} fusion(bf16[1024,2048]{1,0:T(8,128)(2,1)} %get-tuple-element.67, bf16[2048,1280]{1,0:T(8,128)(2,1)} %get-tuple-element.68), kind=kOutput, calls=%fused_computation.176 | convolution fusion | flops 5368709120 | bytes 14680064 | tf_op jit(solution)/shard_map/dot_general | solution.py:22
  111.6 7.9 collective-permute-done.1.up_far_ref
  125.8 3.3 collective-permute-start.5
  129.2 6.4 post.1
  135.6 11.1 %collective-permute-done.5.down_far_ref = bf16[768,256]{1,0:T(8,128)(2,1)} collective-permute-done((bf16[768,256]{1,0:T(8,128)(2,1)}, bf16[768,256]{1,0:T(8,128)(2,1)}, u32[]{:S(2)}, u32[]{:S(2)}) %collective-permute-start.5) | collective-permute-done | bytes 393248 | tf_op jit(solution)/shard_map/ppermute | solution.py:34
  146.7 53.0 %keys.1.kv_ref = bf16[4096,512]{1,0:T(8,128)(2,1)} custom-call(bf16[1024,512]{1,0:T(8,128)(2,1)} %get-tuple-element.80.kv_ref), custom_call_target="tpu_custom_call" | custom-call | bytes 135000000 | tf_op jit(solution)/shard_map/keys/pallas_call | solution.py:592
  206.1 15.3 %attend.1 = (bf16[1024,512]{1,0:T(8,128)(2,1)}, f32[1024,512]{1,0:T(8,128)}, f32[1024,512]{1,0:T(8,128)}) custom-call(s32[4,5]{1,0:T(4,128)} %select_select_fusion.table_ref, bf16[1024,512]{1,0:T(8,128)(2,1)} %get-tuple-element.72.q_ref, bf16[4096,512]{1,0:T(8,128)(2,1)} %keys.1.kv_ref, s32[1024,1]{1,0:T(8,128)} %get-tuple-element.177.row_ref, ...), custom_call_target="tpu_custom_call" | custom-call | flops 20000000000 | bytes 12000000 | tf_op jit(solution)/shard_map/attend/pallas_call | solution.py:244
  222.3 6.2 convolution_convert_fusion.4.partial_ref
  228.5 5.3 collective-permute-done.12.down_both_ref
  233.8 8.4 collective-permute-done.11.up_both_ref
  242.3 13.3 %collective-permute-done.10.gate_both_ref = bf16[256,768]{1,0:T(8,128)(2,1)S(1)} collective-permute-done((bf16[256,768]{1,0:T(8,128)(2,1)}, bf16[256,768]{1,0:T(8,128)(2,1)S(1)}, u32[]{:S(2)}, u32[]{:S(2)}) %collective-permute-start.10) | collective-permute-done | bytes 393248 | tf_op jit(solution)/shard_map/ppermute | solution.py:34
  256.3 86.9 %middle.1 = (f32[256,2048]{1,0:T(8,128)}, bf16[1024,2048]{1,0:T(8,128)(2,1)}, bf16[2048,3072]{1,0:T(8,128)(2,1)}, bf16[1536,2048]{1,0:T(8,128)(2,1)}) custom-call(bf16[1024,2048]{1,0:T(8,128)(2,1)} %convolution_convert_fusion.4.partial_ref, bf16[256,2048]{1,0:T(8,128)(2,1)} %get-tuple-element.87.x_ref, f32[1,2048]{1,0:T(1,128)} %broadcast_in_dim_reshape.9.gain_ref, ...), custom_call_target="tpu_custom_call" | custom-call | bytes 240000000 | tf_op jit(solution)/shard_map/middle/pallas_call | solution.py:592
  343.2 19.2 %fusion.73 = f32[1024,3072]{1,0:T(8,128)} fusion(bf16[1024,2048]{1,0:T(8,128)(2,1)} %get-tuple-element.92.inputs_ref, bf16[2048,3072]{1,0:T(8,128)(2,1)} %get-tuple-element.93), kind=kOutput, calls=%fused_computation.177 | convolution fusion | flops 12884901888 | bytes 29360128 | tf_op jit(solution)/shard_map/dot_general | solution.py:22
  362.7 15.2 %multiply_convert_fusion.2 = (bf16[1024,1536]{1,0:T(8,128)(2,1)S(1)}, bf16[1024,1536]{1,0:T(8,128)(2,1)S(1)}, bf16[1024,1536]{1,0:T(8,128)(2,1)}) fusion(f32[1024,3072]{1,0:T(8,128)} %fusion.73, bf16[1024,2048]{1,0:T(8,128)(2,1)S(1)} %slice_dynamic-update-slice_fusion, bf16[1536,2048]{1,0:T(8,128)(2,1)} %get-tuple-element.91), kind=kOutput, calls=%fused_computation.8 | convolution fusion | flops 6466043904 | bytes 32505856 | tf_op jit(solution)/shard_map/dot_general | solution.py:26
  377.9 12.9 %convolution_convert_fusion.1.down_ref = bf16[1536,2048]{1,0:T(8,128)(2,1)} fusion(bf16[1024,1536]{1,0:T(8,128)(2,1)} %get-tuple-element.153, bf16[1024,2048]{1,0:T(8,128)(2,1)S(1)} %slice_dynamic-update-slice_fusion), kind=kOutput, calls=%fused_computation.1 | convolution fusion | flops 6445596672 | bytes 13631488 | tf_op jit(solution)/shard_map/dot_general | solution.py:30
  390.7 11.2 %convolution_convert_fusion.2.partial_ref = bf16[1024,2048]{1,0:T(8,128)(2,1)} fusion(bf16[1024,1536]{1,0:T(8,128)(2,1)S(1)} %copy-done.32, bf16[1536,2048]{1,0:T(8,128)(2,1)} %get-tuple-element.91), kind=kOutput, calls=%fused_computation.11 | convolution fusion | flops 6444548096 | bytes 13631488 | tf_op jit(solution)/shard_map/dot_general | solution.py:22
  401.9 17.7 %fusion.5.partial_ref = bf16[1024,2048]{1,0:T(8,128)(2,1)} fusion(bf16[2048,3072]{1,0:T(8,128)(2,1)} %get-tuple-element.93, bf16[1024,1536]{1,0:T(8,128)(2,1)S(1)} %get-tuple-element.152.up_ref, bf16[1024,1536]{1,0:T(8,128)(2,1)S(1)} %get-tuple-element.151.gate_ref), kind=kOutput, calls=%fused_computation.12 | convolution fusion | flops 12899581952 | bytes 23068672 | tf_op jit(solution)/shard_map/dot_general | solution.py:26
  419.6 87.9 %turn.1 = (f32[256,2048]{1,0:T(8,128)}, bf16[1024,2048]{1,0:T(8,128)(2,1)}, f32[1,2048]{1,0:T(1,128)}, bf16[1536,512]{1,0:T(8,128)(2,1)}, bf16[512,1536]{1,0:T(8...) custom-call(bf16[1024,2048]{1,0:T(8,128)(2,1)} %fusion.5.partial_ref, ...), custom_call_target="tpu_custom_call" | custom-call | bytes 240000000 | tf_op jit(solution)/shard_map/turn/pallas_call | solution.py:592
  507.5 6.0 fusion.74.grad_ref
  517.8 24.5 %attend_back.1 = (f32[1024,512]{1,0:T(8,128)}, bf16[4096,512]{1,0:T(8,128)(2,1)}, f32[1024,256]{1,0:T(8,128)}) custom-call(s32[4,5]{1,0:T(4,128)} %select_select_fusion.table_ref, bf16[1024,512]{1,0:T(8,128)(2,1)} %get-tuple-element.72.q_ref, bf16[4096,512]{1,0:T(8,128)(2,1)} %keys.1.kv_ref, s32[4,1,256]{2,1,0:T(1,128)} %get-tuple-element.180.row_ref, ...), custom_call_target="tpu_custom_call" | custom-call | flops 49999998976 | bytes 20000000 | tf_op jit(solution)/shard_map/attend_back/pallas_call | solution.py:346
  542.4 5.9 convolution_convert_fusion.5.out_ref
  549.5 18.8 %collective-permute-done.14.down_far_ref = bf16[768,512]{1,0:T(8,128)(2,1)S(1)} collective-permute-done((bf16[768,512]{1,0:T(8,128)(2,1)S(1)}, bf16[768,512]{1,0:T(8,128)(2,1)S(1)}, u32[]{:S(2)}, u32[]{:S(2)}) %collective-permute-start.14) | collective-permute-done | bytes 786464 | tf_op jit(solution)/shard_map/ppermute | solution.py:34
  568.2 16.7 %collective-permute-done.15.gate_far_ref = bf16[512,768]{1,0:T(8,128)(2,1)S(1)} collective-permute-done((bf16[512,768]{1,0:T(8,128)(2,1)S(1)}, bf16[512,768]{1,0:T(8,128)(2,1)S(1)}, u32[]{:S(2)}, u32[]{:S(2)}) %collective-permute-start.15) | collective-permute-done | bytes 786464 | tf_op jit(solution)/shard_map/ppermute | solution.py:34
  585.9 83.6 %owner.1 = (f32[1024,512]{1,0:T(8,128)}, bf16[1024,512]{1,0:T(8,128)(2,1)}, bf16[1536,512]{1,0:T(8,128)(2,1)}, bf16[512,1536]{1,0:T(8,128)(2,1)}) custom-call(bf16[4096,512]{1,0:T(8,128)(2,1)} %get-tuple-element.99.dkv_ref, bf16[1024,2048]{1,0:T(8,128)(2,1)} %convolution_convert_fusion.2.partial_ref, f32[256,2048]{1,0:T(8,128)} %get-tuple-element.95.middle_ref, ...), custom_call_target="tpu_custom_call" | custom-call | bytes 240000000 | tf_op jit(solution)/shard_map/owner/pallas_call | solution.py:592
  669.4 8.7 %project_back.1 = (bf16[1024,1280]{1,0:T(8,128)(2,1)}, f32[1,128]{1,0:T(1,128)}, f32[1,128]{1,0:T(1,128)}) custom-call(f32[1024,512]{1,0:T(8,128)} %get-tuple-element.103.dq_ref, f32[1024,512]{1,0:T(8,128)} %get-tuple-element.104.dkv_ref, f32[1024,1280]{1,0:T(8,128)} %fusion.72.raw_ref.own_ref.other_ref, f32[1024,128]{1,0:T(8,128)} %get-tuple-element.187.cos_ref, ...), custom_call_target="tpu_custom_call" | custom-call | flops 39321600 | bytes 15728640 | tf_op jit(solution)/shard_map/project_back/pallas_call | solution.py:150
  678.1 8.3 convolution_convert_fusion.qkv_ref
  686.7 2.3 copy-done.11
  691.1 2.1 convert_element_type.75
  694.8 7.2 convolution_convert_fusion.3.partial_ref
  703.5 127.3 %end.1 = (bf16[1024,512]{1,0:T(8,128)(2,1)}, f32[1,4352]{1,0:T(1,128)}, bf16[512,1280]{1,0:T(8,128)(2,1)}, bf16[512,512]{1,0:T(8,128)(2,1)}, bf16[512,1536]{1,0:T(8,128)(2,1)}) custom-call(bf16[1024,2048]{1,0:T(8,128)(2,1)} %convolution_convert_fusion.3.partial_ref, bf16[256,2048]{1,0:T(8,128)(2,1)} %get-tuple-element.87.x_ref, ...), custom_call_target="tpu_custom_call" | custom-call | bytes 270000000 | tf_op jit(solution)/shard_map/end/pallas_call | solution.py:592
  (165 shorter events, 62.9 us)
Async XLA Ops:
  0.6 79.6 %copy-start.4 = (bf16[512,1536]{1,0:T(8,128)(2,1)S(1)}, bf16[512,1536]{1,0:T(8,128)(2,1)}, u32[]{:S(2)}) copy-start(bf16[512,1536]{1,0:T(8,128)(2,1)} %gate_ref.1) | copy-start | bytes 4718596
  81.2 30.4 %collective-permute-start = (bf16[256,768]{1,0:T(8,128)(2,1)}, bf16[256,768]{1,0:T(8,128)(2,1)S(1)}, u32[]{:S(2)}, u32[]{:S(2)}) collective-permute-start(bf16[256,768]{1,0:T(8,128)(2,1)} %dynamic_slice.24), channel_id=1, source_target_pairs={{0,8},{4,12},{8,0},{12,4},{1,9},{5,13},{9,1},{13,5},{2,10},{6,14},... | collective-permute-start | bytes 1179656 | tf_op jit(solution)/shard_map/ppermute | solution.py:34
  86.6 33.0 %collective-permute-start.1 = (bf16[256,768]{1,0:T(8,128)(2,1)}, bf16[256,768]{1,0:T(8,128)(2,1)S(1)}, u32[]{:S(2)}, u32[]{:S(2)}) collective-permute-start(bf16[256,768]{1,0:T(8,128)(2,1)} %dynamic_slice.25), channel_id=1, source_target_pairs={{0,8},{4,12},{8,0},{12,4},{1,9},{5,13},{9,1},{13,5},{2,10},{6,14},... | collective-permute-start | bytes 1179656 | tf_op jit(solution)/shard_map/ppermute | solution.py:34
  86.6 18.1 %copy-start.30 = (s32[1,8]{1,0:T(1,128)S(1)}, s32[1,8]{1,0:T(1,128)}, u32[]{:S(2)}) copy-start(s32[1,8]{1,0:T(1,128)} %param.16) | copy-start | bytes 100
  86.6 18.3 %copy-start = (bf16[256,2048]{1,0:T(8,128)(2,1)S(1)}, bf16[256,2048]{1,0:T(8,128)(2,1)}, u32[]{:S(2)}) copy-start(bf16[256,2048]{1,0:T(8,128)(2,1)} %get-tuple-element.79.upstream_ref) | copy-start | bytes 3145732
  99.0 26.8 %collective-permute-start.3 = (bf16[256,768]{1,0:T(8,128)(2,1)}, bf16[256,768]{1,0:T(8,128)(2,1)}, u32[]{:S(2)}, u32[]{:S(2)}) collective-permute-start(bf16[256,768]{1,0:T(8,128)(2,1)} %dynamic_slice.27), channel_id=1, source_target_pairs={{0,2},{1,3},{2,0},{3,1},{4,6},{5,7},{6,4},{7,5},{8,10},{9,11},{10,... | collective-permute-start | bytes 1179656 | tf_op jit(solution)/shard_map/ppermute | solution.py:34
  101.6 34.0 %collective-permute-start.4 = (bf16[768,256]{1,0:T(8,128)(2,1)}, bf16[768,256]{1,0:T(8,128)(2,1)}, u32[]{:S(2)}, u32[]{:S(2)}) collective-permute-start(bf16[768,256]{1,0:T(8,128)(2,1)} %dynamic_slice.28), channel_id=1, source_target_pairs={{0,2},{1,3},{2,0},{3,1},{4,6},{5,7},{6,4},{7,5},{8,10},{9,11},{10,... | collective-permute-start | bytes 1179656 | tf_op jit(solution)/shard_map/ppermute | solution.py:34
  104.0 31.5 %collective-permute-start.2 = (bf16[256,768]{1,0:T(8,128)(2,1)}, bf16[256,768]{1,0:T(8,128)(2,1)}, u32[]{:S(2)}, u32[]{:S(2)}) collective-permute-start(bf16[256,768]{1,0:T(8,128)(2,1)} %dynamic_slice.26), channel_id=1, source_target_pairs={{0,2},{1,3},{2,0},{3,1},{4,6},{5,7},{6,4},{7,5},{8,10},{9,11},{10,... | collective-permute-start | bytes 1179656 | tf_op jit(solution)/shard_map/ppermute | solution.py:34
  111.6 24.0 %copy-start.20 = (bf16[256,768]{1,0:T(8,128)(2,1)}, bf16[256,768]{1,0:T(8,128)(2,1)S(1)}, u32[]{:S(2)}) copy-start(bf16[256,768]{1,0:T(8,128)(2,1)S(1)} %collective-permute-done.gate_far_ref) | copy-start | bytes 1179652
  120.7 26.0 %collective-permute-start.6 = (bf16[128,2048]{1,0:T(8,128)(2,1)}, bf16[128,2048]{1,0:T(8,128)(2,1)S(1)}, u32[]{:S(2)}, u32[]{:S(2)}) collective-permute-start(bf16[128,2048]{1,0:T(8,128)(2,1)} %get-tuple-element.165), channel_id=1, source_target_pairs={{0,2},{1,3},{2,0},{3,1},{4,6},{5,7},{6,4},{7,5},{8,10},{9,11},{10,... | collective-permute-start | bytes 1572872 | tf_op jit(solution)/shard_map/ppermute | solution.py:34
  121.2 25.5 %collective-permute-start.7 = (bf16[128,2048]{1,0:T(8,128)(2,1)}, bf16[128,2048]{1,0:T(8,128)(2,1)S(1)}, u32[]{:S(2)}, u32[]{:S(2)}) collective-permute-start(bf16[128,2048]{1,0:T(8,128)(2,1)} %get-tuple-element.164), channel_id=1, source_target_pairs={{0,4},{4,0},{8,12},{12,8},{1,5},{5,1},{9,13},{13,9},{2,6},{6,2},{1... | collective-permute-start | bytes 1572872 | tf_op jit(solution)/shard_map/ppermute | solution.py:34
  125.8 20.9 %collective-permute-start.5 = (bf16[768,256]{1,0:T(8,128)(2,1)}, bf16[768,256]{1,0:T(8,128)(2,1)}, u32[]{:S(2)}, u32[]{:S(2)}) collective-permute-start(bf16[768,256]{1,0:T(8,128)(2,1)} %dynamic_slice.29), channel_id=1, source_target_pairs={{0,8},{4,12},{8,0},{12,4},{1,9},{5,13},{9,1},{13,5},{2,10},{6,14},... | collective-permute-start | bytes 1179656 | tf_op jit(solution)/shard_map/ppermute | solution.py:34
  199.9 162.5 %collective-permute-start.8 = (bf16[256,2048]{1,0:T(8,128)(2,1)S(1)}, bf16[256,2048]{1,0:T(8,128)(2,1)S(1)}, u32[]{:S(2)}, u32[]{:S(2)}) collective-permute-start(bf16[256,2048]{1,0:T(8,128)(2,1)S(1)} %pad_maximum_fusion), channel_id=1, source_target_pairs={{0,2},{1,3},{2,0},{3,1},{4,6},{5,7},{6,4},{7,5},{8,10},{9,11},{10,... | collective-permute-start | bytes 3145736 | tf_op jit(solution)/shard_map/ppermute | solution.py:34
  201.1 161.4 %collective-permute-start.9 = (bf16[256,2048]{1,0:T(8,128)(2,1)S(1)}, bf16[256,2048]{1,0:T(8,128)(2,1)S(1)}, u32[]{:S(2)}, u32[]{:S(2)}) collective-permute-start(bf16[256,2048]{1,0:T(8,128)(2,1)S(1)} %pad_maximum_fusion.1), channel_id=1, source_target_pairs={{0,4},{4,0},{8,12},{12,8},{1,5},{5,1},{9,13},{13,9},{2,6},{6,2},{1... | collective-permute-start | bytes 3145736 | tf_op jit(solution)/shard_map/ppermute | solution.py:34
  201.7 32.1 %collective-permute-start.12 = (bf16[768,256]{1,0:T(8,128)(2,1)}, bf16[768,256]{1,0:T(8,128)(2,1)S(1)}, u32[]{:S(2)}, u32[]{:S(2)}) collective-permute-start(bf16[768,256]{1,0:T(8,128)(2,1)} %collective-permute-done.4.down_y_ref), channel_id=1, source_target_pairs={{0,8},{4,12},{8,0},{12,4},{1,9},{5,13},{9,1},{13,5},{2,10},{6,14},... | collective-permute-start | bytes 1179656 | tf_op jit(solution)/shard_map/ppermute | solution.py:34
  203.2 39.0 %collective-permute-start.11 = (bf16[256,768]{1,0:T(8,128)(2,1)}, bf16[256,768]{1,0:T(8,128)(2,1)S(1)}, u32[]{:S(2)}, u32[]{:S(2)}) collective-permute-start(bf16[256,768]{1,0:T(8,128)(2,1)} %collective-permute-done.3.up_y_ref), channel_id=1, source_target_pairs={{0,8},{4,12},{8,0},{12,4},{1,9},{5,13},{9,1},{13,5},{2,10},{6,14},... | collective-permute-start | bytes 1179656 | tf_op jit(solution)/shard_map/ppermute | solution.py:34
  204.6 50.9 %collective-permute-start.10 = (bf16[256,768]{1,0:T(8,128)(2,1)}, bf16[256,768]{1,0:T(8,128)(2,1)S(1)}, u32[]{:S(2)}, u32[]{:S(2)}) collective-permute-start(bf16[256,768]{1,0:T(8,128)(2,1)} %collective-permute-done.2.gate_y_ref), channel_id=1, source_target_pairs={{0,8},{4,12},{8,0},{12,4},{1,9},{5,13},{9,1},{13,5},{2,10},{6,14},... | collective-permute-start | bytes 1179656 | tf_op jit(solution)/shard_map/ppermute | solution.py:34
  233.8 21.7 %copy-start.22 = (bf16[768,256]{1,0:T(8,128)(2,1)}, bf16[768,256]{1,0:T(8,128)(2,1)S(1)}, u32[]{:S(2)}) copy-start(bf16[768,256]{1,0:T(8,128)(2,1)S(1)} %collective-permute-done.12.down_both_ref) | copy-start | bytes 1179652
  242.3 13.3 %copy-start.23 = (bf16[256,768]{1,0:T(8,128)(2,1)}, bf16[256,768]{1,0:T(8,128)(2,1)S(1)}, u32[]{:S(2)}) copy-start(bf16[256,768]{1,0:T(8,128)(2,1)S(1)} %collective-permute-done.11.up_both_ref) | copy-start | bytes 1179652
  343.2 19.2 %copy-start.25 = (bf16[1024,2048]{1,0:T(8,128)(2,1)S(1)}, bf16[1024,2048]{1,0:T(8,128)(2,1)}, u32[]{:S(2)}) copy-start(bf16[1024,2048]{1,0:T(8,128)(2,1)} %constant_dynamic-update-slice_fusion.1) | copy-start | bytes 12582916
  377.8 24.0 %copy-start.5 = (bf16[1024,1536]{1,0:T(8,128)(2,1)}, bf16[1024,1536]{1,0:T(8,128)(2,1)S(1)}, u32[]{:S(2)}) copy-start(bf16[1024,1536]{1,0:T(8,128)(2,1)S(1)} %get-tuple-element.151.gate_ref) | copy-start | bytes 9437188
  377.9 24.0 %copy-start.6 = (bf16[1024,1536]{1,0:T(8,128)(2,1)}, bf16[1024,1536]{1,0:T(8,128)(2,1)S(1)}, u32[]{:S(2)}) copy-start(bf16[1024,1536]{1,0:T(8,128)(2,1)S(1)} %get-tuple-element.152.up_ref) | copy-start | bytes 9437188
  377.9 12.9 %copy-start.32 = (bf16[1024,1536]{1,0:T(8,128)(2,1)S(1)}, bf16[1024,1536]{1,0:T(8,128)(2,1)}, u32[]{:S(2)}) copy-start(bf16[1024,1536]{1,0:T(8,128)(2,1)} %get-tuple-element.153) | copy-start | bytes 9437188
  419.6 87.9 %copy-start.28 = (bf16[512,2048]{1,0:T(8,128)(2,1)S(1)}, bf16[512,2048]{1,0:T(8,128)(2,1)}, u32[]{:S(2)}) copy-start(bf16[512,2048]{1,0:T(8,128)(2,1)} %get-tuple-element.86) | copy-start | bytes 6291460
  507.5 8.3 copy-start.3
  513.6 35.9 %collective-permute-start.13 = (bf16[512,1536]{1,0:T(8,128)(2,1)S(1)}, bf16[512,1536]{1,0:T(8,128)(2,1)S(1)}, u32[]{:S(2)}, u32[]{:S(2)}) collective-permute-start(bf16[512,1536]{1,0:T(8,128)(2,1)S(1)} %copy-done.29), channel_id=1, source_target_pairs={{0,16},{16,0},{1,17},{17,1},{2,18},{18,2},{3,19},{19,3},{4,20},{20... | collective-permute-start | bytes 4718600 | tf_op jit(solution)/shard_map/ppermute | solution.py:34
  514.7 53.5 %collective-permute-start.14 = (bf16[768,512]{1,0:T(8,128)(2,1)S(1)}, bf16[768,512]{1,0:T(8,128)(2,1)S(1)}, u32[]{:S(2)}, u32[]{:S(2)}) collective-permute-start(bf16[768,512]{1,0:T(8,128)(2,1)S(1)} %slice.105), channel_id=1, source_target_pairs={{0,8},{4,12},{8,0},{12,4},{1,9},{5,13},{9,1},{13,5},{2,10},{6,14},... | collective-permute-start | bytes 2359304 | tf_op jit(solution)/shard_map/ppermute | solution.py:34
  515.9 69.0 %collective-permute-start.15 = (bf16[512,768]{1,0:T(8,128)(2,1)S(1)}, bf16[512,768]{1,0:T(8,128)(2,1)S(1)}, u32[]{:S(2)}, u32[]{:S(2)}) collective-permute-start(bf16[512,768]{1,0:T(8,128)(2,1)S(1)} %slice.106), channel_id=1, source_target_pairs={{0,8},{4,12},{8,0},{12,4},{1,9},{5,13},{9,1},{13,5},{2,10},{6,14},... | collective-permute-start | bytes 2359304 | tf_op jit(solution)/shard_map/ppermute | solution.py:34
  517.8 24.5 %copy-start.31 = (bf16[1024,512]{1,0:T(8,128)(2,1)S(1)}, bf16[1024,512]{1,0:T(8,128)(2,1)}, u32[]{:S(2)}) copy-start(bf16[1024,512]{1,0:T(8,128)(2,1)} %get-tuple-element.85) | copy-start | bytes 3145732
  549.5 120.0 %copy-start.8 = (bf16[512,1536]{1,0:T(8,128)(2,1)}, bf16[512,1536]{1,0:T(8,128)(2,1)S(1)}, u32[]{:S(2)}) copy-start(bf16[512,1536]{1,0:T(8,128)(2,1)S(1)} %collective-permute-done.13.up_x_ref) | copy-start | bytes 4718596
  568.2 16.7 %copy-start.17 = (bf16[768,512]{1,0:T(8,128)(2,1)}, bf16[768,512]{1,0:T(8,128)(2,1)S(1)}, u32[]{:S(2)}) copy-start(bf16[768,512]{1,0:T(8,128)(2,1)S(1)} %collective-permute-done.14.down_far_ref) | copy-start | bytes 2359300
  686.6 15.4 %collective-permute-start.16 = (bf16[1024,1280]{1,0:T(8,128)(2,1)S(1)}, bf16[1024,1280]{1,0:T(8,128)(2,1)S(1)}, u32[]{:S(2)}, u32[]{:S(2)}) collective-permute-start(bf16[1024,1280]{1,0:T(8,128)(2,1)S(1)} %slice.130), channel_id=1, source_target_pairs={{0,1},{1,0},{2,3},{3,2},{4,5},{5,4},{6,7},{7,6},{8,9},{9,8},{10,11... | collective-permute-start | bytes 7864328 | tf_op jit(solution)/shard_map/ppermute | solution.py:34
  (20 other events, 90.7 us)

commit v12 on v11

--- a/solution.py
+++ b/solution.py
@@ -1274,7 +1274,7 @@
         axes = (0, 0, 1)
         from_far = [over_far(piece_of(w, y, axis)) for w, axis in zip(send, axes)]
         from_y = [over_y(piece_of(w, 1 - y, axis)) for w, axis in zip(after(send, raw), axes)]
-        raw = after(raw, from_far[0], from_far[1])
+        raw = after(raw, *from_far)
         q, kv = post(raw, cosine, sine, query_gain, key_gain, heads, pairs, size, factor)
         part = rows_local // 2
         early = after(upstream, raw)

time: 854 us -> 860 us (level)
  transfers between devices with their start and end apart: 17 -> 17, of which waited for: 9 -> 11; matrix products, arithmetic and copies ran while one was open for 9% -> 8% of each run, Pallas kernels for 16% -> 16%
where the time goes in v12:
time: 860 us; the launch traced here: 852 us
  Pallas kernels  570 us (66%)
  matrix products  120 us (14%)
  waiting for transfers between devices  88.9 us (10%)
  local copies, waits for them, and re-layouts  31.5 us (4%)
  starting transfers between devices  20.4 us (2%)
  other arithmetic  19.5 us (2%)
    pallas_call x6, Pallas kernels, wire_call(): pl.pallas_call(functools.partial(kernel, sizes=sizes), in_specs=specs, ou...  515 us
    ppermute x17, waiting for transfers between devices, exchange(): return lax.ppermute(values, axis, [(i, i ^ distance) for i in range(size)])  88.9 us
    dot_general x4, matrix products, dot_rows(): return jnp.dot(left, right, preferred_element_type=F32)  47 us
    dot_general x4, matrix products, dot_trans(): lax.dot_general(left, right, (((1,), (1,)), ((), ())), preferred_element_...  46.1 us
    dot_general x3, matrix products, dot_inner(): lax.dot_general(left, right, (((0,), (0,)), ((), ())), preferred_element_...  27 us
    pallas_call x1, Pallas kernels, attend_back(): pl.pallas_call(functools.partial(backward_kernel, pairs=pairs, repeat=hea...  24.5 us
    ppermute x17, starting transfers between devices, exchange(): return lax.ppermute(values, axis, [(i, i ^ distance) for i in range(size)])  20.4 us
  transfers between devices with their start and end apart: 17, of which 11 were waited for; matrix products, arithmetic and copies ran while one was open for 8% of the time, Pallas kernels for 16%

profile of v12, /device:TPU:0, one launch (start us, length us, event | category | flops | bytes accessed | tf_op | source)
XLA Modules:
  0.0 852.4 jit_solution(15420031123587934714)
XLA Ops:
  5.0 75.2 %begin.1 = (bf16[256,2048]{1,0:T(8,128)(2,1)}, bf16[256,2048]{1,0:T(8,128)(2,1)}, bf16[1024,2048]{1,0:T(8,128)(2,1)}, bf16[2048,1280]{1,0:T(8,128)(2,1)}, bf16[512,2048]{1,0:T(8,128)(2,1)}) custom-call(bf16[1024,512]{1,0:T(8,128)(2,1)} %tokens_ref.1, bf16[1024,512]{1,0:T(8,128)(2,1)} %cotangent_ref.1, f32[1,2048]{1,0:T(1,128)} %broadcast_in_dim_reshape.8.gain_ref, ...), custom_call_target="tpu_custom_call" | custom-call | bytes 165000000 | tf_op jit(solution)/shard_map/begin/pallas_call | solution.py:592
  81.2 3.4 collective-permute-start
  88.6 2.9 collective-permute-start.2
  91.5 10.4 %fusion.72.raw_ref.own_ref.other_ref = f32[1024,1280]{1,0:T(8,128)} fusion(bf16[1024,2048]{1,0:T(8,128)(2,1)} %get-tuple-element.67, bf16[2048,1280]{1,0:T(8,128)(2,1)} %get-tuple-element.68), kind=kOutput, calls=%fused_computation.176 | convolution fusion | flops 5368709120 | bytes 14680064 | tf_op jit(solution)/shard_map/dot_general | solution.py:22
  115.3 4.8 collective-permute-done.gate_far_ref
  120.5 7.9 collective-permute-done.1.up_far_ref
  128.5 8.1 collective-permute-done.2.down_far_ref
  140.7 6.4 post.1
  147.1 4.1 collective-permute-done.6
  151.5 54.5 %keys.1.kv_ref = bf16[4096,512]{1,0:T(8,128)(2,1)} custom-call(bf16[1024,512]{1,0:T(8,128)(2,1)} %get-tuple-element.80.kv_ref), custom_call_target="tpu_custom_call" | custom-call | bytes 135000000 | tf_op jit(solution)/shard_map/keys/pallas_call | solution.py:592
  212.4 15.3 %attend.1 = (bf16[1024,512]{1,0:T(8,128)(2,1)}, f32[1024,512]{1,0:T(8,128)}, f32[1024,512]{1,0:T(8,128)}) custom-call(s32[4,5]{1,0:T(4,128)} %select_select_fusion.table_ref, bf16[1024,512]{1,0:T(8,128)(2,1)} %get-tuple-element.73.q_ref, bf16[4096,512]{1,0:T(8,128)(2,1)} %keys.1.kv_ref, s32[1024,1]{1,0:T(8,128)} %get-tuple-element.177.row_ref, ...), custom_call_target="tpu_custom_call" | custom-call | flops 20000000000 | bytes 12000000 | tf_op jit(solution)/shard_map/attend/pallas_call | solution.py:244
  228.6 6.2 convolution_convert_fusion.4.partial_ref
  234.8 5.3 collective-permute-done.12.down_both_ref
  240.1 8.4 collective-permute-done.11.up_both_ref
  248.5 13.3 %collective-permute-done.10.gate_both_ref = bf16[256,768]{1,0:T(8,128)(2,1)S(1)} collective-permute-done((bf16[256,768]{1,0:T(8,128)(2,1)}, bf16[256,768]{1,0:T(8,128)(2,1)S(1)}, u32[]{:S(2)}, u32[]{:S(2)}) %collective-permute-start.10) | collective-permute-done | bytes 393248 | tf_op jit(solution)/shard_map/ppermute | solution.py:34
  262.6 86.9 %middle.1 = (f32[256,2048]{1,0:T(8,128)}, bf16[1024,2048]{1,0:T(8,128)(2,1)}, bf16[2048,3072]{1,0:T(8,128)(2,1)}, bf16[1536,2048]{1,0:T(8,128)(2,1)}) custom-call(bf16[1024,2048]{1,0:T(8,128)(2,1)} %convolution_convert_fusion.4.partial_ref, bf16[256,2048]{1,0:T(8,128)(2,1)} %get-tuple-element.87.x_ref, f32[1,2048]{1,0:T(1,128)} %broadcast_in_dim_reshape.9.gain_ref, ...), custom_call_target="tpu_custom_call" | custom-call | bytes 240000000 | tf_op jit(solution)/shard_map/middle/pallas_call | solution.py:592
  349.5 19.2 %fusion.73 = f32[1024,3072]{1,0:T(8,128)} fusion(bf16[1024,2048]{1,0:T(8,128)(2,1)} %get-tuple-element.92.inputs_ref, bf16[2048,3072]{1,0:T(8,128)(2,1)} %get-tuple-element.93), kind=kOutput, calls=%fused_computation.177 | convolution fusion | flops 12884901888 | bytes 29360128 | tf_op jit(solution)/shard_map/dot_general | solution.py:22
  369.0 15.2 %multiply_convert_fusion.2 = (bf16[1024,1536]{1,0:T(8,128)(2,1)S(1)}, bf16[1024,1536]{1,0:T(8,128)(2,1)S(1)}, bf16[1024,1536]{1,0:T(8,128)(2,1)}) fusion(f32[1024,3072]{1,0:T(8,128)} %fusion.73, bf16[1024,2048]{1,0:T(8,128)(2,1)S(1)} %slice_dynamic-update-slice_fusion, bf16[1536,2048]{1,0:T(8,128)(2,1)} %get-tuple-element.91), kind=kOutput, calls=%fused_computation.8 | convolution fusion | flops 6466043904 | bytes 32505856 | tf_op jit(solution)/shard_map/dot_general | solution.py:26
  384.2 12.9 %convolution_convert_fusion.1.down_ref = bf16[1536,2048]{1,0:T(8,128)(2,1)} fusion(bf16[1024,1536]{1,0:T(8,128)(2,1)} %get-tuple-element.153, bf16[1024,2048]{1,0:T(8,128)(2,1)S(1)} %slice_dynamic-update-slice_fusion), kind=kOutput, calls=%fused_computation.1 | convolution fusion | flops 6445596672 | bytes 13631488 | tf_op jit(solution)/shard_map/dot_general | solution.py:30
  397.0 11.2 %convolution_convert_fusion.2.partial_ref = bf16[1024,2048]{1,0:T(8,128)(2,1)} fusion(bf16[1024,1536]{1,0:T(8,128)(2,1)S(1)} %copy-done.32, bf16[1536,2048]{1,0:T(8,128)(2,1)} %get-tuple-element.91), kind=kOutput, calls=%fused_computation.11 | convolution fusion | flops 6444548096 | bytes 13631488 | tf_op jit(solution)/shard_map/dot_general | solution.py:22
  408.2 17.7 %fusion.5.partial_ref = bf16[1024,2048]{1,0:T(8,128)(2,1)} fusion(bf16[2048,3072]{1,0:T(8,128)(2,1)} %get-tuple-element.93, bf16[1024,1536]{1,0:T(8,128)(2,1)S(1)} %get-tuple-element.152.up_ref, bf16[1024,1536]{1,0:T(8,128)(2,1)S(1)} %get-tuple-element.151.gate_ref), kind=kOutput, calls=%fused_computation.12 | convolution fusion | flops 12899581952 | bytes 23068672 | tf_op jit(solution)/shard_map/dot_general | solution.py:26
  425.9 87.8 %turn.1 = (f32[256,2048]{1,0:T(8,128)}, bf16[1024,2048]{1,0:T(8,128)(2,1)}, f32[1,2048]{1,0:T(1,128)}, bf16[1536,512]{1,0:T(8,128)(2,1)}, bf16[512,1536]{1,0:T(8...) custom-call(bf16[1024,2048]{1,0:T(8,128)(2,1)} %fusion.5.partial_ref, ...), custom_call_target="tpu_custom_call" | custom-call | bytes 240000000 | tf_op jit(solution)/shard_map/turn/pallas_call | solution.py:592
  513.8 6.0 fusion.74.grad_ref
  524.1 24.5 %attend_back.1 = (f32[1024,512]{1,0:T(8,128)}, bf16[4096,512]{1,0:T(8,128)(2,1)}, f32[1024,256]{1,0:T(8,128)}) custom-call(s32[4,5]{1,0:T(4,128)} %select_select_fusion.table_ref, bf16[1024,512]{1,0:T(8,128)(2,1)} %get-tuple-element.73.q_ref, bf16[4096,512]{1,0:T(8,128)(2,1)} %keys.1.kv_ref, s32[4,1,256]{2,1,0:T(1,128)} %get-tuple-element.180.row_ref, ...), custom_call_target="tpu_custom_call" | custom-call | flops 49999998976 | bytes 20000000 | tf_op jit(solution)/shard_map/attend_back/pallas_call | solution.py:346
  548.6 5.9 convolution_convert_fusion.5.out_ref
  555.7 18.8 %collective-permute-done.14.down_far_ref = bf16[768,512]{1,0:T(8,128)(2,1)S(1)} collective-permute-done((bf16[768,512]{1,0:T(8,128)(2,1)S(1)}, bf16[768,512]{1,0:T(8,128)(2,1)S(1)}, u32[]{:S(2)}, u32[]{:S(2)}) %collective-permute-start.14) | collective-permute-done | bytes 786464 | tf_op jit(solution)/shard_map/ppermute | solution.py:34
  574.5 16.8 %collective-permute-done.15.gate_far_ref = bf16[512,768]{1,0:T(8,128)(2,1)S(1)} collective-permute-done((bf16[512,768]{1,0:T(8,128)(2,1)S(1)}, bf16[512,768]{1,0:T(8,128)(2,1)S(1)}, u32[]{:S(2)}, u32[]{:S(2)}) %collective-permute-start.15) | collective-permute-done | bytes 786464 | tf_op jit(solution)/shard_map/ppermute | solution.py:34
  592.1 83.7 %owner.1 = (f32[1024,512]{1,0:T(8,128)}, bf16[1024,512]{1,0:T(8,128)(2,1)}, bf16[1536,512]{1,0:T(8,128)(2,1)}, bf16[512,1536]{1,0:T(8,128)(2,1)}) custom-call(bf16[4096,512]{1,0:T(8,128)(2,1)} %get-tuple-element.99.dkv_ref, bf16[1024,2048]{1,0:T(8,128)(2,1)} %convolution_convert_fusion.2.partial_ref, f32[256,2048]{1,0:T(8,128)} %get-tuple-element.95.middle_ref, ...), custom_call_target="tpu_custom_call" | custom-call | bytes 240000000 | tf_op jit(solution)/shard_map/owner/pallas_call | solution.py:592
  675.8 8.7 %project_back.1 = (bf16[1024,1280]{1,0:T(8,128)(2,1)}, f32[1,128]{1,0:T(1,128)}, f32[1,128]{1,0:T(1,128)}) custom-call(f32[1024,512]{1,0:T(8,128)} %get-tuple-element.103.dq_ref, f32[1024,512]{1,0:T(8,128)} %get-tuple-element.104.dkv_ref, f32[1024,1280]{1,0:T(8,128)} %fusion.72.raw_ref.own_ref.other_ref, f32[1024,128]{1,0:T(8,128)} %get-tuple-element.187.cos_ref, ...), custom_call_target="tpu_custom_call" | custom-call | flops 39321600 | bytes 15728640 | tf_op jit(solution)/shard_map/project_back/pallas_call | solution.py:150
  684.5 8.3 convolution_convert_fusion.qkv_ref
  701.2 7.2 convolution_convert_fusion.3.partial_ref
  709.9 127.2 %end.1 = (bf16[1024,512]{1,0:T(8,128)(2,1)}, f32[1,4352]{1,0:T(1,128)}, bf16[512,1280]{1,0:T(8,128)(2,1)}, bf16[512,512]{1,0:T(8,128)(2,1)}, bf16[512,1536]{1,0:T(8,128)(2,1)}) custom-call(bf16[1024,2048]{1,0:T(8,128)(2,1)} %convolution_convert_fusion.3.partial_ref, bf16[256,2048]{1,0:T(8,128)(2,1)} %get-tuple-element.87.x_ref, ...), custom_call_target="tpu_custom_call" | custom-call | bytes 270000000 | tf_op jit(solution)/shard_map/end/pallas_call | solution.py:592
  (165 shorter events, 66.6 us)
Async XLA Ops:
  0.6 79.6 %copy-start.4 = (bf16[512,1536]{1,0:T(8,128)(2,1)S(1)}, bf16[512,1536]{1,0:T(8,128)(2,1)}, u32[]{:S(2)}) copy-start(bf16[512,1536]{1,0:T(8,128)(2,1)} %gate_ref.1) | copy-start | bytes 4718596
  81.2 38.8 %collective-permute-start = (bf16[256,768]{1,0:T(8,128)(2,1)}, bf16[256,768]{1,0:T(8,128)(2,1)S(1)}, u32[]{:S(2)}, u32[]{:S(2)}) collective-permute-start(bf16[256,768]{1,0:T(8,128)(2,1)} %dynamic_slice.24), channel_id=1, source_target_pairs={{0,8},{4,12},{8,0},{12,4},{1,9},{5,13},{9,1},{13,5},{2,10},{6,14},... | collective-permute-start | bytes 1179656 | tf_op jit(solution)/shard_map/ppermute | solution.py:34
  86.6 41.9 %collective-permute-start.1 = (bf16[256,768]{1,0:T(8,128)(2,1)}, bf16[256,768]{1,0:T(8,128)(2,1)S(1)}, u32[]{:S(2)}, u32[]{:S(2)}) collective-permute-start(bf16[256,768]{1,0:T(8,128)(2,1)} %dynamic_slice.25), channel_id=1, source_target_pairs={{0,8},{4,12},{8,0},{12,4},{1,9},{5,13},{9,1},{13,5},{2,10},{6,14},... | collective-permute-start | bytes 1179656 | tf_op jit(solution)/shard_map/ppermute | solution.py:34
  88.6 47.9 %collective-permute-start.2 = (bf16[768,256]{1,0:T(8,128)(2,1)}, bf16[768,256]{1,0:T(8,128)(2,1)}, u32[]{:S(2)}, u32[]{:S(2)}) collective-permute-start(bf16[768,256]{1,0:T(8,128)(2,1)} %dynamic_slice.26), channel_id=1, source_target_pairs={{0,8},{4,12},{8,0},{12,4},{1,9},{5,13},{9,1},{13,5},{2,10},{6,14},... | collective-permute-start | bytes 1179656 | tf_op jit(solution)/shard_map/ppermute | solution.py:34
  91.5 17.6 %copy-start.30 = (s32[1,8]{1,0:T(1,128)S(1)}, s32[1,8]{1,0:T(1,128)}, u32[]{:S(2)}) copy-start(s32[1,8]{1,0:T(1,128)} %param.16) | copy-start | bytes 100
  91.5 17.8 %copy-start = (bf16[256,2048]{1,0:T(8,128)(2,1)S(1)}, bf16[256,2048]{1,0:T(8,128)(2,1)}, u32[]{:S(2)}) copy-start(bf16[256,2048]{1,0:T(8,128)(2,1)} %get-tuple-element.79.upstream_ref) | copy-start | bytes 3145732
  104.0 43.1 %collective-permute-start.4 = (bf16[256,768]{1,0:T(8,128)(2,1)}, bf16[256,768]{1,0:T(8,128)(2,1)}, u32[]{:S(2)}, u32[]{:S(2)}) collective-permute-start(bf16[256,768]{1,0:T(8,128)(2,1)} %dynamic_slice.28), channel_id=1, source_target_pairs={{0,2},{1,3},{2,0},{3,1},{4,6},{5,7},{6,4},{7,5},{8,10},{9,11},{10,... | collective-permute-start | bytes 1179656 | tf_op jit(solution)/shard_map/ppermute | solution.py:34
  106.5 40.6 %collective-permute-start.5 = (bf16[768,256]{1,0:T(8,128)(2,1)}, bf16[768,256]{1,0:T(8,128)(2,1)}, u32[]{:S(2)}, u32[]{:S(2)}) collective-permute-start(bf16[768,256]{1,0:T(8,128)(2,1)} %dynamic_slice.29), channel_id=1, source_target_pairs={{0,2},{1,3},{2,0},{3,1},{4,6},{5,7},{6,4},{7,5},{8,10},{9,11},{10,... | collective-permute-start | bytes 1179656 | tf_op jit(solution)/shard_map/ppermute | solution.py:34
  120.0 27.0 %copy-start.20 = (bf16[256,768]{1,0:T(8,128)(2,1)}, bf16[256,768]{1,0:T(8,128)(2,1)S(1)}, u32[]{:S(2)}) copy-start(bf16[256,768]{1,0:T(8,128)(2,1)S(1)} %collective-permute-done.gate_far_ref) | copy-start | bytes 1179652
  120.0 27.0 %collective-permute-start.3 = (bf16[256,768]{1,0:T(8,128)(2,1)}, bf16[256,768]{1,0:T(8,128)(2,1)}, u32[]{:S(2)}, u32[]{:S(2)}) collective-permute-start(bf16[256,768]{1,0:T(8,128)(2,1)} %dynamic_slice.27), channel_id=1, source_target_pairs={{0,2},{1,3},{2,0},{3,1},{4,6},{5,7},{6,4},{7,5},{8,10},{9,11},{10,... | collective-permute-start | bytes 1179656 | tf_op jit(solution)/shard_map/ppermute | solution.py:34
  128.5 11.5 %copy-start.21 = (bf16[256,768]{1,0:T(8,128)(2,1)}, bf16[256,768]{1,0:T(8,128)(2,1)S(1)}, u32[]{:S(2)}) copy-start(bf16[256,768]{1,0:T(8,128)(2,1)S(1)} %collective-permute-done.1.up_far_ref) | copy-start | bytes 1179652
  137.6 13.7 %collective-permute-start.6 = (bf16[128,2048]{1,0:T(8,128)(2,1)}, bf16[128,2048]{1,0:T(8,128)(2,1)S(1)}, u32[]{:S(2)}, u32[]{:S(2)}) collective-permute-start(bf16[128,2048]{1,0:T(8,128)(2,1)} %get-tuple-element.165), channel_id=1, source_target_pairs={{0,2},{1,3},{2,0},{3,1},{4,6},{5,7},{6,4},{7,5},{8,10},{9,11},{10,... | collective-permute-start | bytes 1572872 | tf_op jit(solution)/shard_map/ppermute | solution.py:34
  138.1 13.4 %collective-permute-start.7 = (bf16[128,2048]{1,0:T(8,128)(2,1)}, bf16[128,2048]{1,0:T(8,128)(2,1)S(1)}, u32[]{:S(2)}, u32[]{:S(2)}) collective-permute-start(bf16[128,2048]{1,0:T(8,128)(2,1)} %get-tuple-element.164), channel_id=1, source_target_pairs={{0,4},{4,0},{8,12},{12,8},{1,5},{5,1},{9,13},{13,9},{2,6},{6,2},{1... | collective-permute-start | bytes 1572872 | tf_op jit(solution)/shard_map/ppermute | solution.py:34
  206.1 162.6 %collective-permute-start.8 = (bf16[256,2048]{1,0:T(8,128)(2,1)S(1)}, bf16[256,2048]{1,0:T(8,128)(2,1)S(1)}, u32[]{:S(2)}, u32[]{:S(2)}) collective-permute-start(bf16[256,2048]{1,0:T(8,128)(2,1)S(1)} %pad_maximum_fusion), channel_id=1, source_target_pairs={{0,2},{1,3},{2,0},{3,1},{4,6},{5,7},{6,4},{7,5},{8,10},{9,11},{10,... | collective-permute-start | bytes 3145736 | tf_op jit(solution)/shard_map/ppermute | solution.py:34
  207.3 161.5 %collective-permute-start.9 = (bf16[256,2048]{1,0:T(8,128)(2,1)S(1)}, bf16[256,2048]{1,0:T(8,128)(2,1)S(1)}, u32[]{:S(2)}, u32[]{:S(2)}) collective-permute-start(bf16[256,2048]{1,0:T(8,128)(2,1)S(1)} %pad_maximum_fusion.1), channel_id=1, source_target_pairs={{0,4},{4,0},{8,12},{12,8},{1,5},{5,1},{9,13},{13,9},{2,6},{6,2},{1... | collective-permute-start | bytes 3145736 | tf_op jit(solution)/shard_map/ppermute | solution.py:34
  207.9 32.1 %collective-permute-start.12 = (bf16[768,256]{1,0:T(8,128)(2,1)}, bf16[768,256]{1,0:T(8,128)(2,1)S(1)}, u32[]{:S(2)}, u32[]{:S(2)}) collective-permute-start(bf16[768,256]{1,0:T(8,128)(2,1)} %collective-permute-done.5.down_y_ref), channel_id=1, source_target_pairs={{0,8},{4,12},{8,0},{12,4},{1,9},{5,13},{9,1},{13,5},{2,10},{6,14},... | collective-permute-start | bytes 1179656 | tf_op jit(solution)/shard_map/ppermute | solution.py:34
  209.5 39.0 %collective-permute-start.11 = (bf16[256,768]{1,0:T(8,128)(2,1)}, bf16[256,768]{1,0:T(8,128)(2,1)S(1)}, u32[]{:S(2)}, u32[]{:S(2)}) collective-permute-start(bf16[256,768]{1,0:T(8,128)(2,1)} %collective-permute-done.4.up_y_ref), channel_id=1, source_target_pairs={{0,8},{4,12},{8,0},{12,4},{1,9},{5,13},{9,1},{13,5},{2,10},{6,14},... | collective-permute-start | bytes 1179656 | tf_op jit(solution)/shard_map/ppermute | solution.py:34
  210.9 50.9 %collective-permute-start.10 = (bf16[256,768]{1,0:T(8,128)(2,1)}, bf16[256,768]{1,0:T(8,128)(2,1)S(1)}, u32[]{:S(2)}, u32[]{:S(2)}) collective-permute-start(bf16[256,768]{1,0:T(8,128)(2,1)} %collective-permute-done.3.gate_y_ref), channel_id=1, source_target_pairs={{0,8},{4,12},{8,0},{12,4},{1,9},{5,13},{9,1},{13,5},{2,10},{6,14},... | collective-permute-start | bytes 1179656 | tf_op jit(solution)/shard_map/ppermute | solution.py:34
  240.1 21.7 %copy-start.22 = (bf16[768,256]{1,0:T(8,128)(2,1)}, bf16[768,256]{1,0:T(8,128)(2,1)S(1)}, u32[]{:S(2)}) copy-start(bf16[768,256]{1,0:T(8,128)(2,1)S(1)} %collective-permute-done.12.down_both_ref) | copy-start | bytes 1179652
  248.5 13.3 %copy-start.23 = (bf16[256,768]{1,0:T(8,128)(2,1)}, bf16[256,768]{1,0:T(8,128)(2,1)S(1)}, u32[]{:S(2)}) copy-start(bf16[256,768]{1,0:T(8,128)(2,1)S(1)} %collective-permute-done.11.up_both_ref) | copy-start | bytes 1179652
  349.5 19.2 %copy-start.25 = (bf16[1024,2048]{1,0:T(8,128)(2,1)S(1)}, bf16[1024,2048]{1,0:T(8,128)(2,1)}, u32[]{:S(2)}) copy-start(bf16[1024,2048]{1,0:T(8,128)(2,1)} %constant_dynamic-update-slice_fusion.1) | copy-start | bytes 12582916
  384.2 24.0 %copy-start.5 = (bf16[1024,1536]{1,0:T(8,128)(2,1)}, bf16[1024,1536]{1,0:T(8,128)(2,1)S(1)}, u32[]{:S(2)}) copy-start(bf16[1024,1536]{1,0:T(8,128)(2,1)S(1)} %get-tuple-element.151.gate_ref) | copy-start | bytes 9437188
  384.2 24.0 %copy-start.6 = (bf16[1024,1536]{1,0:T(8,128)(2,1)}, bf16[1024,1536]{1,0:T(8,128)(2,1)S(1)}, u32[]{:S(2)}) copy-start(bf16[1024,1536]{1,0:T(8,128)(2,1)S(1)} %get-tuple-element.152.up_ref) | copy-start | bytes 9437188
  384.2 12.9 %copy-start.32 = (bf16[1024,1536]{1,0:T(8,128)(2,1)S(1)}, bf16[1024,1536]{1,0:T(8,128)(2,1)}, u32[]{:S(2)}) copy-start(bf16[1024,1536]{1,0:T(8,128)(2,1)} %get-tuple-element.153) | copy-start | bytes 9437188
  425.9 87.9 %copy-start.28 = (bf16[512,2048]{1,0:T(8,128)(2,1)S(1)}, bf16[512,2048]{1,0:T(8,128)(2,1)}, u32[]{:S(2)}) copy-start(bf16[512,2048]{1,0:T(8,128)(2,1)} %get-tuple-element.86) | copy-start | bytes 6291460
  519.8 35.9 %collective-permute-start.13 = (bf16[512,1536]{1,0:T(8,128)(2,1)S(1)}, bf16[512,1536]{1,0:T(8,128)(2,1)S(1)}, u32[]{:S(2)}, u32[]{:S(2)}) collective-permute-start(bf16[512,1536]{1,0:T(8,128)(2,1)S(1)} %copy-done.29), channel_id=1, source_target_pairs={{0,16},{16,0},{1,17},{17,1},{2,18},{18,2},{3,19},{19,3},{4,20},{20... | collective-permute-start | bytes 4718600 | tf_op jit(solution)/shard_map/ppermute | solution.py:34
  521.0 53.5 %collective-permute-start.14 = (bf16[768,512]{1,0:T(8,128)(2,1)S(1)}, bf16[768,512]{1,0:T(8,128)(2,1)S(1)}, u32[]{:S(2)}, u32[]{:S(2)}) collective-permute-start(bf16[768,512]{1,0:T(8,128)(2,1)S(1)} %slice.105), channel_id=1, source_target_pairs={{0,8},{4,12},{8,0},{12,4},{1,9},{5,13},{9,1},{13,5},{2,10},{6,14},... | collective-permute-start | bytes 2359304 | tf_op jit(solution)/shard_map/ppermute | solution.py:34
  522.3 69.0 %collective-permute-start.15 = (bf16[512,768]{1,0:T(8,128)(2,1)S(1)}, bf16[512,768]{1,0:T(8,128)(2,1)S(1)}, u32[]{:S(2)}, u32[]{:S(2)}) collective-permute-start(bf16[512,768]{1,0:T(8,128)(2,1)S(1)} %slice.106), channel_id=1, source_target_pairs={{0,8},{4,12},{8,0},{12,4},{1,9},{5,13},{9,1},{13,5},{2,10},{6,14},... | collective-permute-start | bytes 2359304 | tf_op jit(solution)/shard_map/ppermute | solution.py:34
  524.1 24.5 %copy-start.31 = (bf16[1024,512]{1,0:T(8,128)(2,1)S(1)}, bf16[1024,512]{1,0:T(8,128)(2,1)}, u32[]{:S(2)}) copy-start(bf16[1024,512]{1,0:T(8,128)(2,1)} %get-tuple-element.85) | copy-start | bytes 3145732
  555.7 120.1 %copy-start.8 = (bf16[512,1536]{1,0:T(8,128)(2,1)}, bf16[512,1536]{1,0:T(8,128)(2,1)S(1)}, u32[]{:S(2)}) copy-start(bf16[512,1536]{1,0:T(8,128)(2,1)S(1)} %collective-permute-done.13.up_x_ref) | copy-start | bytes 4718596
  574.5 16.8 %copy-start.17 = (bf16[768,512]{1,0:T(8,128)(2,1)}, bf16[768,512]{1,0:T(8,128)(2,1)S(1)}, u32[]{:S(2)}) copy-start(bf16[768,512]{1,0:T(8,128)(2,1)S(1)} %collective-permute-done.14.down_far_ref) | copy-start | bytes 2359300
  693.0 15.4 %collective-permute-start.16 = (bf16[1024,1280]{1,0:T(8,128)(2,1)S(1)}, bf16[1024,1280]{1,0:T(8,128)(2,1)S(1)}, u32[]{:S(2)}, u32[]{:S(2)}) collective-permute-start(bf16[1024,1280]{1,0:T(8,128)(2,1)S(1)} %slice.130), channel_id=1, source_target_pairs={{0,1},{1,0},{2,3},{3,2},{4,5},{5,4},{6,7},{7,6},{8,9},{9,8},{10,11... | collective-permute-start | bytes 7864328 | tf_op jit(solution)/shard_map/ppermute | solution.py:34
  (20 other events, 92.9 us)
